TPU v7x, 128 devices: a whole 4x4x4 slice. The times are simulated.
128 devices in a mesh: dp: 8 (over y, x_hi), cent: 16 (over z, x_lo, core).
Axes of the slice: x: 4 (x_hi: 2, x_lo: 2; x = x_hi * 2 + x_lo), y: 4, z: 4, core: 2. Of those that a mesh axis runs over, the one named last changes fastest.
Arguments:
- embeddings: float32 [8192, 768], P('dp'), may hold values from -6 to 6
- centroids_one: bfloat16 [65536, 768], P('cent'), may hold values from -6 to 6
- centroids_two: bfloat16 [4096, 768], P('dp'), may hold values from -6 to 6
Outputs:
- updated_one: float32 [65536, 768], P('cent', 'dp')
- mass_one: float32 [65536], P('cent')
- updated_two: float32 [4096, 768], P('dp')
- mass_two: float32 [4096], P('dp')
All inputs are finite; a program needn't handle non-finite values.
Results may differ from a plain program's by a relative error of at most 0.029.
The roundings to bfloat16 on the way count: a program that leaves them out, or rounds other values in their place, can miss the bound.
Values may be sent and summed in bfloat16 or wider, within the bound.
No kernel may reach another device: no remote copies, remote signals or barrier semaphores. Data moves between devices by JAX's collectives and lax.ppermute only.
A program may use at most 128 MiB of HBM per device.

v0:
```python
import jax
import jax.numpy as jnp
from jax import lax
from jax.sharding import PartitionSpec as P

PRIOR = 0.5


def against(left, right):
    return lax.dot_general(
        left, right, (((1,), (1,)), ((), ())), preferred_element_type=jnp.float32
    )


def over_rows(left, right):
    return lax.dot_general(
        left, right, (((0,), (0,)), ((), ())), preferred_element_type=jnp.float32
    )


def body(embeddings, centroids_one, centroids_two):
    low_rows = embeddings.astype(jnp.bfloat16)
    norms_one = jnp.sum(jnp.square(centroids_one.astype(jnp.float32)), axis=1)
    scores = 2.0 * against(low_rows, centroids_one) - norms_one[None, :]
    local_max = jnp.max(scores, axis=1)
    row_max = lax.pmax(local_max, "cent")
    powers = jnp.exp(scores - row_max[:, None])
    row_total = lax.psum(jnp.sum(powers, axis=1), "cent")
    weights = (powers / row_total[:, None]).astype(jnp.bfloat16)
    partial_value = over_rows(weights, low_rows)
    mass_part = jnp.sum(weights.astype(jnp.float32), axis=0)
    numerator, mass_one = lax.psum((partial_value, mass_part), "dp")
    updated_full = (numerator + PRIOR * centroids_one.astype(jnp.float32)) / (
        mass_one[:, None] + PRIOR
    )
    share_width = updated_full.shape[1] // lax.axis_size("dp")
    updated_one = lax.dynamic_slice_in_dim(
        updated_full, lax.axis_index("dp") * share_width, share_width, 1
    )
    points = updated_full.astype(jnp.bfloat16)
    norms_two = jnp.sum(jnp.square(centroids_two.astype(jnp.float32)), axis=1)
    scores_two = 2.0 * against(points, centroids_two) - norms_two[None, :]
    point_max = jnp.max(scores_two, axis=1)
    joint_max = lax.pmax(point_max, "dp")
    powers_two = jnp.exp(scores_two - joint_max[:, None])
    joint_total = lax.psum(jnp.sum(powers_two, axis=1), "dp")
    weights_two = (powers_two / joint_total[:, None]).astype(jnp.bfloat16)
    partial_two = over_rows(weights_two, points)
    mass_two_part = jnp.sum(weights_two.astype(jnp.float32), axis=0)
    numerator_two, mass_two = lax.psum((partial_two, mass_two_part), "cent")
    updated_two = (numerator_two + PRIOR * centroids_two.astype(jnp.float32)) / (
        mass_two[:, None] + PRIOR
    )
    return (updated_one, mass_one, updated_two, mass_two)


def solution(mesh):
    return jax.shard_map(
        body,
        mesh=mesh,
        in_specs=(P("dp", None), P("cent", None), P("dp", None)),
        out_specs=(P("cent", "dp"), P("cent"), P("dp", None), P("dp")),
        check_vma=False,
    )
```

profile of v0, /device:TPU:1, one launch (start us, length us, event | category | flops | bytes accessed | tf_op | source)
XLA Modules:
  0.0 845.0 jit_solution(932843439574432217)
XLA Ops:
  7.2 4.1 fusion.2
  11.3 13.1 %fusion = (f32[1024]{0:T(1024)S(1)}, f32[1024,4096]{1,0:T(8,128)}) fusion(f32[4096]{0:T(1024)S(1)} %fusion.2, bf16[4096,768]{1,0:T(8,128)(2,1)} %param.4, f32[1024,768]{1,0:T(8,128)} %param.3), kind=kOutput, calls=%fused_computation.6 | convolution fusion | flops 6455819264 | bytes 26234880 | tf_op jit(solution)/shard_map/dot_general | solution.py:10
  24.4 29.2 %pmax.14 = f32[1024]{0:T(1024)S(1)} all-reduce(f32[1024]{0:T(1024)S(1)} %get-tuple-element.12), channel_id=1, replica_groups=mesh['dp'=8,'cent'=16] {'cent'}, use_global_device_ids=true, to_apply=%region_2.0 | all-reduce | flops 1024 | bytes 8192 | tf_op jit(solution)/shard_map/pmax | solution.py:26
  53.6 7.8 fusion.1
  61.4 30.3 %psum.42 = f32[1024]{0:T(1024)S(1)} all-reduce(f32[1024]{0:T(1024)S(1)} %fusion.1), channel_id=1, replica_groups=mesh['dp'=8,'cent'=16] {'cent'}, use_global_device_ids=true, to_apply=%region_4.0 | all-reduce | flops 1024 | bytes 8192 | tf_op jit(solution)/shard_map/psum | solution.py:28
  91.8 8.4 convert_reduce_fusion
  100.2 10.0 %fusion.14 = f32[4096,768]{1,0:T(8,128)} fusion(bf16[1024,4096]{1,0:T(8,128)(2,1)S(1)} %get-tuple-element.11, f32[1024,768]{1,0:T(8,128)S(1)} %copy-done.5), kind=kOutput, calls=%fused_computation.26 | convolution fusion | flops 6443237376 | bytes 24117248 | tf_op jit(solution)/shard_map/dot_general | solution.py:16
  110.3 37.0 %psum.44 = f32[4096]{0:T(1024)S(1)} all-reduce(f32[4096]{0:T(1024)S(1)} %get-tuple-element.10), channel_id=1, replica_groups=mesh['dp'=8,'cent'=16] {'dp'}, use_global_device_ids=true, to_apply=%region_7.0 | all-reduce | flops 4096 | bytes 32768 | tf_op jit(solution)/shard_map/psum | solution.py:32
  147.3 0.2 fusion.11
  147.5 461.3 %all-reduce.3.cloned.1.call-done = f32[4096,768]{1,0:T(8,128)} async-done(((f32[4096,768]{1,0:T(8,128)}), f32[4096,768]{1,0:T(8,128)}) %all-reduce.3.cloned.1.call-update) | async-done | bytes 12582928 | tf_op jit(solution)/shard_map/psum | solution.py:32
  608.8 7.4 fusion.4
  616.3 6.3 fusion.5
  622.6 0.7 copy-done
  623.3 32.0 %pmax.15 = f32[4096]{0:T(1024)S(1)} all-reduce(f32[4096]{0:T(1024)S(1)} %get-tuple-element.14), channel_id=1, replica_groups=mesh['dp'=8,'cent'=16] {'dp'}, use_global_device_ids=true, to_apply=%region_10.0 | all-reduce | flops 4096 | bytes 32768 | tf_op jit(solution)/shard_map/pmax | solution.py:44
  655.3 4.4 fusion.6
  659.7 30.2 %psum.45 = f32[4096]{0:T(1024)S(1)} all-reduce(f32[4096]{0:T(1024)S(1)} %fusion.6), channel_id=1, replica_groups=mesh['dp'=8,'cent'=16] {'dp'}, use_global_device_ids=true, to_apply=%region_12.0 | all-reduce | flops 4096 | bytes 32768 | tf_op jit(solution)/shard_map/psum | solution.py:46
  689.8 5.2 convert_reduce_fusion.1
  695.0 1.8 copy-done.1
  696.8 4.6 fusion.7
  701.5 2.8 constant_dynamic-slice_fusion
  704.3 1.7 copy.7
  706.0 41.4 %psum.47 = f32[512]{0:T(512)S(1)} all-reduce(f32[512]{0:T(512)S(1)} %get-tuple-element.8), channel_id=1, replica_groups=mesh['dp'=8,'cent'=16] {'cent'}, use_global_device_ids=true, to_apply=%region_15.0 | all-reduce | flops 512 | bytes 4096 | tf_op jit(solution)/shard_map/psum | solution.py:50
  747.4 88.0 %all-reduce.5.cloned.1.call-done = f32[512,768]{1,0:T(8,128)} async-done(((f32[512,768]{1,0:T(8,128)}), f32[512,768]{1,0:T(8,128)}) %all-reduce.5.cloned.1.call-update) | async-done | bytes 1572880 | tf_op jit(solution)/shard_map/psum | solution.py:50
  835.4 2.8 fusion.13
  (16 shorter events, 0.1 us)
Async XLA Ops:
  7.2 601.7 %all-reduce.3.cloned.1.call-start = ((), (), s32[]{:S(2)}) async-start(), calls=%async_computation | async-start | bytes 25165824 | tf_op jit(solution)/shard_map/psum | solution.py:32
  91.8 8.4 copy-start.5
  110.2 37.0 %copy-start.2 = (bf16[512,768]{1,0:T(8,128)(2,1)S(1)}, bf16[512,768]{1,0:T(8,128)(2,1)}, u32[]{:S(2)}) copy-start(bf16[512,768]{1,0:T(8,128)(2,1)} %param.5) | copy-start | bytes 2359300
  110.2 725.2 %all-reduce.5.cloned.1.call-start = ((), (), s32[]{:S(2)}) async-start(), calls=%async_computation.1 | async-start | bytes 3145728 | tf_op jit(solution)/shard_map/psum | solution.py:50
  147.3 469.0 %copy-start.3 = (f32[4096]{0:T(1024)}, f32[4096]{0:T(1024)S(1)}, u32[]{:S(2)}) copy-start(f32[4096]{0:T(1024)S(1)} %psum.44) | copy-start | bytes 49156
  616.3 7.0 copy-start
  689.8 7.0 copy-start.1
  747.4 90.8 %copy-start.4 = (f32[512]{0:T(512)}, f32[512]{0:T(512)S(1)}, u32[]{:S(2)}) copy-start(f32[512]{0:T(512)S(1)} %psum.47) | copy-start | bytes 6148
Sparse Core Ops, SparseCore 0:
  110.4 498.4 all-reduce.2
  701.6 133.7 all-reduce.4
where the time goes:
time: 845 us
  waiting for transfers between devices  549 us (65%)
  blocking collectives  200 us (24%)
  other arithmetic  40.3 us (5%)
  matrix products  34.1 us (4%)
  between operations  14.1 us (2%)
    psum x1, waiting for transfers between devices, body(): numerator, mass_one = lax.psum((partial_value, mass_part), 'dp')  461 us
    psum x1, waiting for transfers between devices, body(): numerator_two, mass_two = lax.psum((partial_two, mass_two_part), 'cent')  88 us
    psum x1, blocking collectives, body(): numerator_two, mass_two = lax.psum((partial_two, mass_two_part), 'cent')  41.4 us
    psum x1, blocking collectives, body(): numerator, mass_one = lax.psum((partial_value, mass_part), 'dp')  37 us
    pmax x1, blocking collectives, body(): joint_max = lax.pmax(point_max, 'dp')  32 us
    psum x1, blocking collectives, body(): row_total = lax.psum(jnp.sum(powers, axis=1), 'cent')  30.3 us
    psum x1, blocking collectives, body(): joint_total = lax.psum(jnp.sum(powers_two, axis=1), 'dp')  30.2 us
    pmax x1, blocking collectives, body(): row_max = lax.pmax(local_max, 'cent')  29.2 us
  transfers between devices with their start and end apart: 2, of which 2 were waited for; matrix products, arithmetic and copies ran while one was open for 1% of the time, Pallas kernels for 0%

commit v1 on v0

v1 whole, which is shorter than its diff:
```python
import jax
import jax.numpy as jnp
from jax import lax
from jax.experimental import pallas as pl
from jax.experimental.pallas import tpu as pltpu
from jax.sharding import Mesh, PartitionSpec as P

PRIOR = 0.5
BF = jnp.bfloat16
F32 = jnp.float32
D = 768
TALL = 208
SMEM = pl.BlockSpec(memory_space=pltpu.SMEM)
VMEM = pl.BlockSpec(memory_space=pltpu.VMEM)


def nt(left, right):
    return lax.dot_general(left, right, (((1,), (1,)), ((), ())), preferred_element_type=F32)


def nn(left, right):
    return lax.dot_general(left, right, (((1,), (0,)), ((), ())), preferred_element_type=F32)


def shape(dims, dtype):
    return jax.ShapeDtypeStruct(dims, dtype)


def cost(flops, exps=0, size=1 << 20):
    return pl.CostEstimate(flops=flops, transcendentals=exps, bytes_accessed=size)


def square_norms(block):
    wide = block.astype(F32)
    return jnp.sum(wide * wide, axis=1, keepdims=True)


def fold_rows(block, op):
    parts = [block[i : i + 8] for i in range(0, block.shape[0], 8)]
    while len(parts) > 1:
        parts = [op(parts[i], parts[i + 1]) for i in range(0, len(parts) - 1, 2)] + (
            [parts[-1]] if len(parts) % 2 else []
        )
    return parts[0]


def lane_sums(w):
    wide = w.astype(F32)
    part = wide[:, 0:128]
    for j in range(128, wide.shape[1], 128):
        part = part + wide[:, j : j + 128]
    return jnp.sum(part, axis=1, keepdims=True)


def as_row(column):
    return jnp.broadcast_to(column, (column.shape[0], 128)).T[0:1, :]


def as_column(row):
    return jnp.broadcast_to(row, (128, row.shape[1])).T[:, 0:1]


def mass_rows(row):
    t = jnp.broadcast_to(row, (16, row.shape[1]))
    hi = t.astype(BF).astype(F32)
    mid = (t - hi).astype(BF).astype(F32)
    low = t - hi - mid
    at = lax.broadcasted_iota(jnp.int32, t.shape, 0)
    return jnp.where(at == 0, hi, jnp.where(at == 1, mid, jnp.where(at == 2, low, 0.0)))


def scores_step(cents, twice, norms, p_ref, scores):
    top = None
    for k in range(4):
        for h in range(2):
            at = k * 512 + h * 256
            n = norms[pl.ds(at, 256), :]
            s = nt(cents[k][pl.ds(h * 256, 256), :], twice) - jnp.concatenate([n, n], axis=1)
            scores[pl.ds(at, 256), :] = s
            t = fold_rows(s, jnp.maximum)
            top = t if top is None else jnp.maximum(top, t)
    m = jnp.max(top, axis=0, keepdims=True)
    total = None
    for at in range(0, 2048, 256):
        e = jnp.exp(scores[pl.ds(at, 256), :] - m)
        p_ref[pl.ds(at, 256), :] = e
        t = fold_rows(e, jnp.add)
        total = t if total is None else total + t
    return m, jnp.sum(total, axis=0, keepdims=True)


def put_stats(stat_ref, row, i, m, l):
    cols = pl.ds(pl.multiple_of(lax.rem(i, 2) * 256, 256), 256)
    stat_ref[pl.ds(row, 1), cols] = m
    stat_ref[pl.ds(4 + row, 1), cols] = l


def scores_near_kernel(idx, a_ref, b_ref, c0, c1, c2, c3, p_ref, x_ref, stat_ref, norms_ref, scores):
    i = pl.program_id(0)
    cents = (c0, c1, c2, c3)

    @pl.when(i == 0)
    def _():
        stat_ref[...] = jnp.zeros_like(stat_ref)
        for k in range(4):
            for h in range(2):
                n = square_norms(cents[k][pl.ds(h * 256, 256), :])
                norms_ref[pl.ds(k * 512 + h * 256, 256), :] = jnp.broadcast_to(n, (256, 128))

    x = jnp.where(i < 2, a_ref[...], b_ref[...])
    x_ref[...] = x
    m, l = scores_step(cents, x * 2, norms_ref, p_ref, scores)
    put_stats(stat_ref, idx[4 + i // 2], i, m, l)


def scores_far_kernel(idx, a_ref, b_ref, c0, c1, c2, c3, norms_ref, near_ref, p_old, x_old, p_ref, x_ref, stat_ref, scores):
    i = pl.program_id(0)

    @pl.when(i == 0)
    def _():
        stat_ref[...] = near_ref[...]

    x = jnp.where(i < 2, a_ref[...], b_ref[...])
    x_ref[...] = x
    m, l = scores_step((c0, c1, c2, c3), x * 2, norms_ref, p_ref, scores)
    put_stats(stat_ref, idx[6 + i // 2], i, m, l)


ANY = pl.BlockSpec(memory_space=pl.ANY)
ROW_IN = [
    pl.BlockSpec((256, D), lambda i, s: (jnp.minimum(i, 1), 0)),
    pl.BlockSpec((256, D), lambda i, s: (jnp.maximum(i - 2, 0), 0)),
]
CENTS_IN = [pl.BlockSpec((512, D), lambda i, s, k=k: (s[k], 0)) for k in range(4)]
WHOLE_STAT = pl.BlockSpec((8, 512), lambda i, s: (0, 0))
WHOLE_NORMS = pl.BlockSpec((2048, 128), lambda i, s: (0, 0))


def scores_near(idx, a, b, cents):
    return pl.pallas_call(
        scores_near_kernel,
        grid_spec=pltpu.PrefetchScalarGridSpec(
            num_scalar_prefetch=1,
            grid=(4,),
            in_specs=ROW_IN + CENTS_IN,
            out_specs=[
                pl.BlockSpec((2048, 256), lambda i, s: (0, i)),
                pl.BlockSpec((256, D), lambda i, s: (i, 0)),
                WHOLE_STAT,
                WHOLE_NORMS,
            ],
            scratch_shapes=[pltpu.VMEM((2048, 256), F32)],
        ),
        out_shape=[
            shape((2048, 2048), F32),
            shape((2048, D), BF),
            shape((8, 512), F32),
            shape((2048, 128), F32),
        ],
        cost_estimate=cost(2 * 2048 * 1024 * D, 2048 * 1024),
        name="scores_near",
    )(idx, a, b, cents, cents, cents, cents)


def scores_far(idx, a, b, cents, norms, near, p, x):
    return pl.pallas_call(
        scores_far_kernel,
        grid_spec=pltpu.PrefetchScalarGridSpec(
            num_scalar_prefetch=1,
            grid=(4,),
            in_specs=ROW_IN + CENTS_IN + [WHOLE_NORMS, WHOLE_STAT, ANY, ANY],
            out_specs=[
                pl.BlockSpec((2048, 256), lambda i, s: (0, 4 + i)),
                pl.BlockSpec((256, D), lambda i, s: (4 + i, 0)),
                WHOLE_STAT,
            ],
            scratch_shapes=[pltpu.VMEM((2048, 256), F32)],
        ),
        out_shape=[shape((2048, 2048), F32), shape((2048, D), BF), shape((8, 512), F32)],
        input_output_aliases={9: 0, 10: 1},
        cost_estimate=cost(2 * 2048 * 1024 * D, 2048 * 1024),
        name="scores_far",
    )(idx, a, b, cents, cents, cents, cents, norms, near, p, x)


def merge_all(stats):
    m = stats[0][0:4]
    for t in stats[1:]:
        m = jnp.maximum(m, t[0:4])
    total = None
    for t in stats:
        part = t[4:8] * jnp.exp(t[0:4] - m)
        total = part if total is None else total + part
    return m, total


def merge_cores(local, other):
    def kernel(a, b, o_ref):
        m, total = merge_all([a[...], b[...]])
        both = jnp.concatenate([m, total], axis=0)
        for i in range(16):
            o_ref[i] = both

    return pl.pallas_call(
        kernel, in_specs=[VMEM] * 2, out_shape=shape((16, 8, 512), F32), name="merge_cores"
    )(local, other)


def merge_last(idx, stats, local):
    def kernel(idx_ref, s_ref, l_ref, f_ref, tmp):
        m, total = merge_all([s_ref[i] for i in range(16)])
        tmp[0:4, :] = jnp.exp(l_ref[0:4, :] - m) / total
        for r in range(4):
            f_ref[:, r * 512 : (r + 1) * 512] = tmp[pl.ds(idx_ref[4 + r], 1), :]

    return pl.pallas_call(
        kernel,
        in_specs=[SMEM] + [VMEM] * 2,
        scratch_shapes=[pltpu.VMEM((8, 512), F32)],
        out_shape=shape((1, 2048), F32),
        name="merge_last",
    )(idx, stats, local)


def sums_one(p, factor, x, masses, first, count, dtype):
    def kernel(p_ref, f_ref, x_ref, old_ref, o_ref, mass_ref, acc, macc):
        j, i = pl.program_id(0), pl.program_id(1)
        w = (p_ref[...] * f_ref[...]).astype(BF)
        part = nn(w, x_ref[...])
        wide = w.astype(F32)
        lanes = wide[:, 0:128]
        for at in range(128, 1024, 128):
            lanes = lanes + wide[:, at : at + 128]

        @pl.when((i == 0) & (j == 0))
        def _():
            mass_ref[...] = old_ref[...]

        @pl.when(i == 0)
        def _():
            acc[...] = part
            macc[...] = lanes

        @pl.when(i == 1)
        def _():
            o_ref[...] = (acc[...] + part).astype(o_ref.dtype)
            mass = jnp.sum(macc[...] + lanes, axis=1, keepdims=True)
            mass_ref[pl.ds(first + 2 * j, 1), :] = as_row(mass)

    return pl.pallas_call(
        kernel,
        grid=(count, 2),
        in_specs=[
            pl.BlockSpec((512, 1024), lambda j, i: (first + 2 * j, i)),
            pl.BlockSpec((1, 1024), lambda j, i: (0, i)),
            pl.BlockSpec((1024, D), lambda j, i: (i, 0)),
            pl.BlockSpec((4, 512), lambda j, i: (0, 0)),
        ],
        out_specs=[
            pl.BlockSpec((512, D), lambda j, i: (j, 0)),
            pl.BlockSpec((4, 512), lambda j, i: (0, 0)),
        ],
        scratch_shapes=[pltpu.VMEM((512, D), F32), pltpu.VMEM((512, 128), F32)],
        out_shape=[shape((512 * count, D), dtype), shape((4, 512), F32)],
        name="sums_one",
    )(p, factor, x, masses)


def finish_one(idx, own, got, cents, masses, far_masses):
    def kernel(idx_ref, own_ref, g1, g2, g3, cents_ref, m0, m1, m2, m3, pts_ref, mass_ref):
        total = m0[...]
        for k, ref in ((1, m1), (2, m2), (3, m3)):
            t = ref[...]
            total = total + jnp.concatenate([t[k:], t[:k]], axis=0)
        mass_ref[...] = total
        i = pl.program_id(0)
        column = as_column(mass_ref[0:1, pl.ds(pl.multiple_of(i * 128, 128), 128)]) + PRIOR
        num = own_ref[...] + g1[...].astype(F32) + g2[...].astype(F32) + g3[...].astype(F32)
        num = num + PRIOR * cents_ref[...].astype(F32)
        pts_ref[...] = (num / column).astype(BF)

    rows = pl.BlockSpec((128, D), lambda i, s: (i, 0))
    small = pl.BlockSpec((4, 512), lambda i, s: (0, 0))
    return pl.pallas_call(
        kernel,
        grid_spec=pltpu.PrefetchScalarGridSpec(
            num_scalar_prefetch=1,
            grid=(4,),
            in_specs=[rows] * 4 + [pl.BlockSpec((128, D), lambda i, s: (s[0] * 4 + i, 0))] + [small] * 4,
            out_specs=[rows, small],
        ),
        out_shape=[shape((512, D), BF), shape((4, 512), F32)],
        name="finish_one",
    )(idx, own, *got, cents, masses, *far_masses)


def turn_points(points):
    def kernel(p_ref, o_ref):
        o_ref[...] = p_ref[...].astype(F32).T.astype(BF)

    return pl.pallas_call(
        kernel,
        grid=(6,),
        in_specs=[pl.BlockSpec((512, 128), lambda i: (0, i))],
        out_specs=pl.BlockSpec((128, 512), lambda i: (i, 0)),
        out_shape=shape((D, 512), BF),
        name="turn_points",
    )(points)


def gather_one(place, keep, take, totals, far_totals):
    def kernel(place_ref, keep_ref, take_ref, t_ref, f_ref, o_ref, m_ref):
        y, near = place_ref[0], place_ref[1]
        for ref, half in ((keep_ref, near), (take_ref, 1 - near)):
            for k in range(4):
                start = half * 2048 + lax.rem(y + 4 - k, 4) * 512
                o_ref[:, pl.ds(pl.multiple_of(start, 512), 512)] = ref[k].astype(F32)
        for ref, half in ((t_ref, near), (f_ref, 1 - near)):
            for j in range(4):
                m_ref[pl.ds(half * 4 + lax.rem(y + j, 4), 1), :] = ref[j : j + 1, :]

    return pl.pallas_call(
        kernel,
        in_specs=[SMEM] + [VMEM] * 4,
        out_shape=[shape((96, 4096), F32), shape((8, 512), F32)],
        name="gather_one",
    )(place, keep, take, totals, far_totals)


def norms_two(two):
    def kernel(c_ref, o_ref):
        o_ref[...] = jnp.broadcast_to(square_norms(c_ref[...]), (256, 128))

    return pl.pallas_call(
        kernel,
        grid=(8,),
        in_specs=[pl.BlockSpec((256, D), lambda i: (i, 0))],
        out_specs=pl.BlockSpec((256, 128), lambda i: (i, 0)),
        out_shape=shape((2048, 128), F32),
        name="norms_two",
    )(two)


def scores_two(slots, a, b, two, norms):
    def kernel(slots_ref, a_ref, b_ref, c_ref, n_ref, p_ref, stat_ref, scores):
        i = pl.program_id(0)
        twice = jnp.where(i < 2, a_ref[...], b_ref[...]) * 2
        top = None
        for d in range(8):
            here = pl.ds(pl.multiple_of(slots_ref[d] * 256, 256), 256)
            n = n_ref[here, :]
            s = nt(c_ref[here, :], twice) - jnp.concatenate([n, n], axis=1)
            scores[pl.ds(d * 256, 256), :] = s
            t = fold_rows(s, jnp.maximum)
            top = t if top is None else jnp.maximum(top, t)
        m = jnp.max(top, axis=0, keepdims=True)
        total = None
        for at in range(0, 2048, 256):
            e = jnp.exp(scores[pl.ds(at, 256), :] - m)
            p_ref[pl.ds(at, 256), :] = e
            t = fold_rows(e, jnp.add)
            total = t if total is None else total + t
        stat_ref[0:1, :] = m
        stat_ref[1:2, :] = jnp.sum(total, axis=0, keepdims=True)

    return pl.pallas_call(
        kernel,
        grid_spec=pltpu.PrefetchScalarGridSpec(
            num_scalar_prefetch=1,
            grid=(4,),
            in_specs=ROW_IN + [pl.BlockSpec((2048, D), lambda i, s: (0, 0)), WHOLE_NORMS],
            out_specs=[
                pl.BlockSpec((2048, 256), lambda i, s: (0, i)),
                pl.BlockSpec((2, 256), lambda i, s: (0, i)),
            ],
            scratch_shapes=[pltpu.VMEM((2048, 256), F32)],
        ),
        out_shape=[shape((2048, 1024), F32), shape((2, 1024), F32)],
        cost_estimate=cost(2 * 2048 * 1024 * D, 2048 * 1024),
        name="scores_two",
    )(slots, a, b, two, norms)


def sums_two(p, stat, other, a, b):
    def kernel(p_ref, s_ref, r_ref, a_ref, b_ref, o_ref, rows, factor):
        @pl.when(pl.program_id(0) == 0)
        def _():
            rows[0:512, :] = a_ref[...]
            rows[512:1024, :] = b_ref[...]
            theirs = jnp.concatenate([r_ref[:, 512:1024], r_ref[:, 0:512]], axis=1)
            mine = s_ref[...]
            m = jnp.maximum(mine[0:1], theirs[0:1])
            near = jnp.exp(mine[0:1] - m)
            total = mine[1:2] * near + theirs[1:2] * jnp.exp(theirs[0:1] - m)
            factor[0:1, :] = near / total

        w = (p_ref[...] * factor[0:1, :]).astype(BF)
        num = nn(w, rows[...])
        packed = mass_rows(as_row(lane_sums(w)))
        for q in range(8):
            for j in range(6):
                o_ref[q, j * 32 : j * 32 + 32, :] = num[q * 32 : q * 32 + 32, j * 128 : j * 128 + 128].astype(BF)
            lanes = packed[:, (q // 4) * 128 : (q // 4) * 128 + 128]
            turn = (128 - (q % 4) * 32) % 128
            o_ref[q, 192:TALL, :] = (pltpu.roll(lanes, turn, 1) if turn else lanes).astype(BF)

    whole = lambda r, c: pl.BlockSpec((r, c), lambda i: (0, 0))
    return pl.pallas_call(
        kernel,
        grid=(8,),
        in_specs=[pl.BlockSpec((256, 1024), lambda i: (i, 0)), whole(2, 1024), whole(2, 1024), whole(512, D), whole(512, D)],
        out_specs=pl.BlockSpec((8, TALL, 128), lambda i: (i, 0, 0)),
        scratch_shapes=[pltpu.VMEM((1024, D), BF), pltpu.VMEM((8, 1024), F32)],
        out_shape=shape((64, TALL, 128), BF),
        cost_estimate=cost(2 * 2048 * 1024 * D),
        name="sums_two",
    )(p, stat, other, a, b)


def finish_two(parts, cents):
    def kernel(x_ref, c_ref, o_ref, acc):
        i = pl.program_id(0)
        total = x_ref[0].astype(F32)
        for q in range(1, 8):
            total = total + x_ref[q].astype(F32)

        @pl.when(i == 0)
        def _():
            acc[...] = total

        @pl.when(i > 0)
        def _():
            acc[...] += total

        @pl.when(i == 7)
        def _():
            mass = acc[192:193, :] + acc[193:194, :] + acc[194:195, :]
            column = as_column(mass)[0:32] + PRIOR
            packed = mass_rows(mass).astype(BF)
            for j in range(6):
                num = acc[j * 32 : j * 32 + 32, :] + PRIOR * c_ref[:, j * 128 : j * 128 + 128].astype(F32)
                new = (num / column).astype(BF)
                for q in range(8):
                    o_ref[q, j * 32 : j * 32 + 32, :] = new
            for q in range(8):
                o_ref[q, 192:TALL, :] = packed

    return pl.pallas_call(
        kernel,
        grid=(8,),
        in_specs=[
            pl.BlockSpec((8, TALL, 128), lambda i: (i, 0, 0)),
            pl.BlockSpec((32, D), lambda i: (0, 0)),
        ],
        out_specs=pl.BlockSpec((8, TALL, 128), lambda i: (0, 0, 0)),
        scratch_shapes=[pltpu.VMEM((TALL, 128), F32)],
        out_shape=shape((8, TALL, 128), BF),
        name="finish_two",
    )(parts, cents)


def gather_two(core, mine, theirs):
    def kernel(core_ref, a_ref, b_ref, o_ref, m_ref):
        lane = lax.broadcasted_iota(jnp.int32, (16, 128), 1)
        for ref, half in ((a_ref, core_ref[0]), (b_ref, 1 - core_ref[0])):
            start = pl.multiple_of(half * 256, 256)
            for q in range(8):
                for j in range(6):
                    o_ref[pl.ds(start + q * 32, 32), j * 128 : j * 128 + 128] = ref[q, j * 32 : j * 32 + 32, :].astype(F32)
            for g in range(2):
                row = None
                for r in range(4):
                    t = ref[g * 4 + r, 192:TALL, :].astype(F32)
                    t = pltpu.roll(t, r * 32, 1) if r else t
                    row = t if row is None else jnp.where(lane >= r * 32, t, row)
                m_ref[:, pl.ds(start + g * 128, 128)] = row[0:1] + row[1:2] + row[2:3]

    return pl.pallas_call(
        kernel,
        in_specs=[SMEM] + [VMEM] * 2,
        out_shape=[shape((512, D), F32), shape((1, 512), F32)],
        name="gather_two",
    )(core, mine, theirs)


def shift_y(x, k):
    return lax.ppermute(x, "y", [(i, (i + k) % 4) for i in range(4)])


def shift_z(x, k):
    return lax.ppermute(x, "z", [(i, (i + k) % 4) for i in range(4)])


def flip(x, axis):
    return lax.ppermute(x, axis, [(0, 1), (1, 0)])


def flip_x(x):
    return lax.ppermute(x, ("xh", "xl"), [(0, 3), (1, 2), (2, 1), (3, 0)])


def after(x, *others):
    return lax.optimization_barrier((x,) + others)[0]


def body(embeddings, cents_one, cents_two):
    y = lax.axis_index("y").astype(jnp.int32)
    xh = lax.axis_index("xh").astype(jnp.int32)
    z = lax.axis_index("z").astype(jnp.int32)
    xl = lax.axis_index("xl").astype(jnp.int32)
    c = lax.axis_index("c").astype(jnp.int32)
    halves = jnp.stack([xh * 2 + c, xh * 2 + 1 - c, 2 - xh * 2 + c, 3 - xh * 2 - c])
    idx = jnp.concatenate([xh * 4 + (y + jnp.arange(4, dtype=jnp.int32)) % 4, halves])
    to = jnp.arange(8, dtype=jnp.int32)
    slots = (xh ^ (to % 2)) * 4 + (y - to // 2) % 4

    mine = lax.dynamic_slice_in_dim(embeddings, c * 512, 512, 0).astype(BF)
    far_mine = flip_x(mine)
    other = lax.dynamic_slice_in_dim(embeddings, (1 - c) * 512, 512, 0).astype(BF)
    p, x, near, norms = scores_near(idx, mine, other, cents_one)
    far_mine = after(far_mine, near)
    far_other = flip(far_mine, "c")
    p, x, local = scores_far(idx, far_mine, far_other, cents_one, norms, near, p, x)

    spread = merge_cores(local, flip(local, "c"))
    stats = lax.all_to_all(spread, ("xh", "z", "xl"), 0, 0, tiled=True)

    half_two = after(lax.dynamic_slice_in_dim(cents_two, c * 256, 256, 0), spread)
    around = [shift_y(half_two, k) for k in (1, 2, 3)]

    factor = merge_last(idx, stats, local)
    masses = jnp.zeros((4, 512), F32)
    part, masses = sums_one(p, factor, x, masses, 2, 1, BF)
    same_two = jnp.concatenate([half_two] + [after(t, part) for t in around], axis=0)
    got = {2: shift_y(part, 2)}
    part, masses = sums_one(p, factor, x, masses, 1, 2, BF)
    got[1], got[3] = shift_y(part[0:512], 1), shift_y(part[512:1024], 3)
    own, masses = sums_one(p, factor, x, masses, 0, 1, F32)

    far_two = after(flip_x(same_two), masses)
    two = jnp.concatenate([same_two, far_two], axis=0)
    norms = norms_two(two)

    points, totals = finish_one(
        idx, after(own, norms), [got[k] for k in (1, 2, 3)], cents_one, masses, [shift_y(masses, k) for k in (1, 2, 3)]
    )
    their_points = flip(points, "c")
    tall = turn_points(points)
    p2, stat2 = scores_two(slots, after(points, tall), their_points, two, norms)
    other2 = flip(stat2, "c")

    cut = lambda d: lax.dynamic_slice_in_dim(tall, ((y + d) % 4) * 192, 192, 0)
    cols = jnp.stack([cut(0)] + [shift_y(cut(k), k) for k in (1, 2, 3)]).reshape(4, 2, 96, 512)
    keep = lax.dynamic_index_in_dim(cols, xh, 1, keepdims=False)
    take = flip(lax.dynamic_index_in_dim(cols, 1 - xh, 1, keepdims=False), "xh")
    far_totals = flip(totals, "xh")

    packed = sums_two(p2, stat2, other2, points, their_points)
    packed = after(packed, take, far_totals)
    parts = lax.all_to_all(packed, ("y", "xh", "z", "xl"), 0, 0, tiled=True)
    turned_one, mass_one = gather_one(jnp.stack([y, xh]), keep, take, totals, far_totals)
    rows = lax.dynamic_slice_in_dim(cents_two, c * 256 + z * 64 + xl * 32, 32, 0)
    spread = finish_two(parts, after(rows, turned_one))
    block = lax.all_to_all(spread, ("z", "xl"), 0, 0, tiled=True)
    updated_two, mass_two = gather_two(c[None], block, flip(block, "c"))
    return turned_one.T, mass_one.reshape(4096), updated_two, mass_two.reshape(512)


def solution(mesh):
    fine = Mesh(mesh.devices.reshape(4, 2, 4, 2, 2), ("y", "xh", "z", "xl", "c"))
    dp, cent = ("y", "xh"), ("z", "xl", "c")
    return jax.shard_map(
        body,
        mesh=fine,
        in_specs=(P(dp, None), P(cent, None), P(dp, None)),
        out_specs=(P(cent, dp), P(cent), P(dp, None), P(dp)),
        check_vma=False,
    )
```

time: 845 us -> 257 us (0.30)
  waiting for transfers between devices: 549 us -> 75 us
  blocking collectives: 200 us -> 27 us
  Pallas kernels: 0 us -> 90.2 us
  starting transfers between devices: 0.08 us -> 39.9 us
  other arithmetic: 40.3 us -> 2.4 us
  matrix products: 34.1 us -> 0 us
  local copies, waits for them, and re-layouts: 7.02 us -> 20.4 us
  between operations: 14.1 us -> 0.81 us
    psum x2 -> x0, waiting for transfers between devices: 549 us -> none  [the longest x1 461 us: body(): numerator, mass_one = lax.psum((partial_value, mass_part), 'dp')]
    psum x4 -> x0, blocking collectives: 139 us -> none  [the longest x1 41.4 us: body(): numerator_two, mass_two = lax.psum((partial_two, mass_two_part), 'cent')]
    pallas_call x0 -> x15, Pallas kernels: none -> 90.2 us  [the longest x3 20.4 us: sums_one(): pl.pallas_call(kernel, grid=(count, 2), in_specs=[pl.BlockSpec((512, 1024...]
    pmax x2 -> x0, blocking collectives: 61.2 us -> none  [the longest x1 32 us: body(): joint_max = lax.pmax(point_max, 'dp')]
    all_to_all x0 -> x1, waiting for transfers between devices: none -> 38.3 us  [body(): parts = lax.all_to_all(packed, ('y', 'xh', 'z', 'xl'), 0, 0, tiled=True)]
    ppermute x0 -> x21, waiting for transfers between devices: none -> 36.7 us  [the longest x12 18.4 us: shift_y(): return lax.ppermute(x, 'y', [(i, (i + k) % 4) for i in range(4)])]
    dot_general x4 -> x0, matrix products: 34.1 us -> none  [the longest x2 19.4 us: against(): lax.dot_general(left, right, (((1,), (1,)), ((), ())), preferred_element_...]
    ppermute x0 -> x21, starting transfers between devices: none -> 33.1 us  [the longest x12 15.8 us: shift_y(): return lax.ppermute(x, 'y', [(i, (i + k) % 4) for i in range(4)])]
  transfers between devices with their start and end apart: 2 -> 22, of which waited for: 2 -> 10; matrix products, arithmetic and copies ran while one was open for 1% -> 5% of each run, Pallas kernels for 0% -> 26%
where the time goes in v1:
time: 257 us; the launch traced here: 256 us
  Pallas kernels  90.2 us (35%)
  waiting for transfers between devices  75 us (29%)
  starting transfers between devices  39.9 us (16%)
  blocking collectives  27 us (11%)
  local copies, waits for them, and re-layouts  20.4 us (8%)
    all_to_all x1, waiting for transfers between devices, body(): parts = lax.all_to_all(packed, ('y', 'xh', 'z', 'xl'), 0, 0, tiled=True)  38.3 us
    pallas_call x3, Pallas kernels, sums_one(): pl.pallas_call(kernel, grid=(count, 2), in_specs=[pl.BlockSpec((512, 1024...  20.4 us
    ppermute x12, waiting for transfers between devices, shift_y(): return lax.ppermute(x, 'y', [(i, (i + k) % 4) for i in range(4)])  18.4 us
    ppermute x12, starting transfers between devices, shift_y(): return lax.ppermute(x, 'y', [(i, (i + k) % 4) for i in range(4)])  15.8 us
    all_to_all x1, blocking collectives, body(): stats = lax.all_to_all(spread, ('xh', 'z', 'xl'), 0, 0, tiled=True)  15 us
    ppermute x2, waiting for transfers between devices, flip_x(): return lax.ppermute(x, ('xh', 'xl'), [(0, 3), (1, 2), (2, 1), (3, 0)])  14.5 us
    ppermute x7, starting transfers between devices, flip(): return lax.ppermute(x, axis, [(0, 1), (1, 0)])  12.8 us
    all_to_all x1, blocking collectives, body(): block = lax.all_to_all(spread, ('z', 'xl'), 0, 0, tiled=True)  12 us
  transfers between devices with their start and end apart: 22, of which 10 were waited for; matrix products, arithmetic and copies ran while one was open for 5% of the time, Pallas kernels for 26%

profile of v1, /device:TPU:1, one launch (start us, length us, event | category | flops | bytes accessed | tf_op | source)
XLA Modules:
  0.0 255.6 jit_solution(13191418962733087120)
XLA Ops:
  0.7 3.0 %dynamic-slice_convert_fusion = (bf16[512,768]{1,0:T(8,128)(2,1)}, bf16[512,768]{1,0:T(8,128)(2,1)S(1)}) fusion(f32[1024,768]{1,0:T(8,128)} %param.3, s32[]{:T(128)S(6)} %select_n.73, s32[]{:T(128)S(6)} %select_n.72), kind=kLoop, calls=%fused_computation.1 | loop fusion | bytes 3145736 | tf_op jit(solution)/shard_map/convert_element_type | solution.py:519
  3.6 3.3 %collective-permute-start = (bf16[512,768]{1,0:T(8,128)(2,1)S(1)}, bf16[512,768]{1,0:T(8,128)(2,1)S(1)}, u32[]{:S(2)}, u32[]{:S(2)}) collective-permute-start(bf16[512,768]{1,0:T(8,128)(2,1)S(1)} %get-tuple-element.67.a_ref), channel_id=1, source_target_pairs={{0,18},{2,16},{16,2},{18,0},{1,19},{3,17},{17,3},{19,1},{4,22},{6,... | collective-permute-start | bytes 2359304 | tf_op jit(solution)/shard_map/ppermute | solution.py:499
  7.6 10.5 %scores_near.1 = (f32[2048,2048]{1,0:T(8,128)}, bf16[2048,768]{1,0:T(8,128)(2,1)}, f32[8,512]{1,0:T(8,128)}, f32[2048,128]{1,0:T(8,128)}) custom-call(s32[8]{0:T(128)} %concatenate.11.idx.idx_ref, bf16[512,768]{1,0:T(8,128)(2,1)} %copy-done.1, bf16[512,768]{1,0:T(8,128)(2,1)} %get-tuple-element.66.b_ref, bf16[4096,768]{1,0:T(8,128)(2,1)} %cents_ref.1, ...), custom_call_target="tpu_custom_call" | custom-call | flops 3221225472 | bytes 1048576 | tf_op jit(solution)/shard_map/scores_near/pallas_call | solution.py:140
  18.1 5.7 %collective-permute-done.a_ref = bf16[512,768]{1,0:T(8,128)(2,1)S(1)} collective-permute-done((bf16[512,768]{1,0:T(8,128)(2,1)S(1)}, bf16[512,768]{1,0:T(8,128)(2,1)S(1)}, u32[]{:S(2)}, u32[]{:S(2)}) %collective-permute-start) | collective-permute-done | bytes 786464 | tf_op jit(solution)/shard_map/ppermute | solution.py:499
  28.3 10.3 %scores_far.1 = (f32[2048,2048]{1,0:T(8,128)}, bf16[2048,768]{1,0:T(8,128)(2,1)}, f32[8,512]{1,0:T(8,128)}) custom-call(s32[8]{0:T(128)} %concatenate.11.idx.idx_ref, bf16[512,768]{1,0:T(8,128)(2,1)} %copy-done.6, bf16[512,768]{1,0:T(8,128)(2,1)} %copy-done.7, bf16[4096,768]{1,0:T(8,128)(2,1)} %cents_ref.1, ...), custom_call_target="tpu_custom_call", output_to_operand_aliasing={{0}: (9, {}), {1}: (10, {})} | custom-call | flops 3221225472 | bytes 1048576 | tf_op jit(solution)/shard_map/scores_far/pallas_call | solution.py:166
  46.1 15.0 %all_to_all.15.s_ref = f32[16,8,512]{2,1,0:T(8,128)} all-to-all(f32[16,8,512]{2,1,0:T(8,128)} %merge_cores.1), channel_id=1, replica_groups=mesh['y'=4,'xh'=2,'z'=4,'xl'=2,'c'=2] {'xh','z','xl'}, dimensions={0} | all-to-all | bytes 524288 | tf_op jit(solution)/shard_map/all_to_all | solution.py:526
  63.3 5.4 %sums_one.3 = (bf16[512,768]{1,0:T(8,128)(2,1)}, f32[4,512]{1,0:T(4,128)}) custom-call(f32[2048,2048]{1,0:T(8,128)} %get-tuple-element.40.p_ref, f32[1,2048]{1,0:T(1,128)} %merge_last.1.f_ref, bf16[2048,768]{1,0:T(8,128)(2,1)} %get-tuple-element.42.x_ref, f32[4,512]{1,0:T(4,128)} %broadcast_in_dim.6.old_ref), custom_call_target="tpu_custom_call" | custom-call | tf_op jit(solution)/shard_map/sums_one/pallas_call | solution.py:250
  71.9 9.3 %sums_one.4 = (bf16[1024,768]{1,0:T(8,128)(2,1)}, f32[4,512]{1,0:T(4,128)}) custom-call(f32[2048,2048]{1,0:T(8,128)} %get-tuple-element.40.p_ref, f32[1,2048]{1,0:T(1,128)} %merge_last.1.f_ref, bf16[2048,768]{1,0:T(8,128)(2,1)} %get-tuple-element.42.x_ref, f32[4,512]{1,0:T(4,128)} %get-tuple-element.43.old_ref), custom_call_target="tpu_custom_call" | custom-call | tf_op jit(solution)/shard_map/sums_one/pallas_call | solution.py:250
  88.0 5.7 %sums_one.5 = (f32[512,768]{1,0:T(8,128)}, f32[4,512]{1,0:T(4,128)}) custom-call(f32[2048,2048]{1,0:T(8,128)} %get-tuple-element.40.p_ref, f32[1,2048]{1,0:T(1,128)} %merge_last.1.f_ref, bf16[2048,768]{1,0:T(8,128)(2,1)} %get-tuple-element.42.x_ref, f32[4,512]{1,0:T(4,128)} %get-tuple-element.44.old_ref), custom_call_target="tpu_custom_call" | custom-call | tf_op jit(solution)/shard_map/sums_one/pallas_call | solution.py:250
  96.6 8.9 %collective-permute-done.6 = bf16[1024,768]{1,0:T(8,128)(2,1)S(1)} collective-permute-done((bf16[1024,768]{1,0:T(8,128)(2,1)}, bf16[1024,768]{1,0:T(8,128)(2,1)S(1)}, u32[]{:S(2)}, u32[]{:S(2)}) %collective-permute-start.6) | collective-permute-done | bytes 1572896 | tf_op jit(solution)/shard_map/ppermute | solution.py:499
  107.7 9.2 %collective-permute-done.10.m1 = f32[4,512]{1,0:T(4,128)S(1)} collective-permute-done((f32[4,512]{1,0:T(4,128)}, f32[4,512]{1,0:T(4,128)S(1)}, u32[]{:S(2)}, u32[]{:S(2)}) %collective-permute-start.10) | collective-permute-done | bytes 8224 | tf_op jit(solution)/shard_map/ppermute | solution.py:487
  120.8 6.1 %norms_two.1.n_ref = f32[2048,128]{1,0:T(8,128)} custom-call(bf16[2048,768]{1,0:T(8,128)(2,1)} %constant_dynamic-update-slice_fusion.c_ref), custom_call_target="tpu_custom_call" | custom-call | tf_op jit(solution)/shard_map/norms_two/pallas_call | solution.py:334
  127.5 5.1 %finish_one.1 = (bf16[512,768]{1,0:T(8,128)(2,1)}, f32[4,512]{1,0:T(4,128)}) custom-call(s32[8]{0:T(128)} %concatenate.11.idx.idx_ref, f32[512,768]{1,0:T(8,128)} %get-tuple-element.53.own_ref, bf16[512,768]{1,0:T(8,128)(2,1)} %collective-permute-done.7.g1, bf16[512,768]{1,0:T(8,128)(2,1)} %collective-permute-done.8.g2, ...), custom_call_target="tpu_custom_call" | custom-call | tf_op jit(solution)/shard_map/finish_one/pallas_call | solution.py:284
  132.6 3.8 %collective-permute-start.18 = (bf16[512,768]{1,0:T(8,128)(2,1)}, bf16[512,768]{1,0:T(8,128)(2,1)S(1)}, u32[]{:S(2)}, u32[]{:S(2)}) collective-permute-start(bf16[512,768]{1,0:T(8,128)(2,1)} %get-tuple-element.59.p_ref.a_ref), channel_id=1, source_target_pairs={{0,1},{1,0},{2,3},{3,2},{4,5},{5,4},{6,7},{7,6},{8,9},{9,8},{10,11... | collective-permute-start | bytes 2359304 | tf_op jit(solution)/shard_map/ppermute | solution.py:495
  136.4 4.4 %turn_points.1 = bf16[768,512]{1,0:T(8,128)(2,1)} custom-call(bf16[512,768]{1,0:T(8,128)(2,1)} %get-tuple-element.59.p_ref.a_ref), custom_call_target="tpu_custom_call" | custom-call | tf_op jit(solution)/shard_map/turn_points/pallas_call | solution.py:301
  145.6 4.6 %collective-permute-done.14 = bf16[192,512]{1,0:T(8,128)(2,1)S(1)} collective-permute-done((bf16[192,512]{1,0:T(8,128)(2,1)S(1)}, bf16[192,512]{1,0:T(8,128)(2,1)S(1)}, u32[]{:S(2)}, u32[]{:S(2)}) %collective-permute-start.14) | collective-permute-done | bytes 196640 | tf_op jit(solution)/shard_map/ppermute | solution.py:487
  151.8 3.0 %collective-permute-done.13 = bf16[192,512]{1,0:T(8,128)(2,1)S(1)} collective-permute-done((bf16[192,512]{1,0:T(8,128)(2,1)S(1)}, bf16[192,512]{1,0:T(8,128)(2,1)S(1)}, u32[]{:S(2)}, u32[]{:S(2)}) %collective-permute-start.13) | collective-permute-done | bytes 196640 | tf_op jit(solution)/shard_map/ppermute | solution.py:487
  157.6 10.0 %scores_two.1 = (f32[2048,1024]{1,0:T(8,128)}, f32[2,1024]{1,0:T(2,128)}) custom-call(s32[8]{0:T(128)} %fusion.slots_ref, bf16[512,768]{1,0:T(8,128)(2,1)} %get-tuple-element.59.p_ref.a_ref, bf16[512,768]{1,0:T(8,128)(2,1)} %copy-done.5, bf16[2048,768]{1,0:T(8,128)(2,1)} %constant_dynamic-update-slice_fusion.c_ref, f32[2048,128]{1,0:T(8,128)} %norms_two.1.n_ref), custom_call_target="tpu_custom_call" | custom-call | flops 3221225472 | bytes 1048576 | tf_op jit(solution)/shard_map/scores_two/pallas_call | solution.py:366
  170.9 10.0 %sums_two.1 = bf16[64,208,128]{2,1,0:T(8,128)(2,1)} custom-call(f32[2048,1024]{1,0:T(8,128)} %get-tuple-element.60.p_ref, f32[2,1024]{1,0:T(2,128)} %get-tuple-element.61.s_ref, f32[2,1024]{1,0:T(2,128)} %copy-done.17, bf16[512,768]{1,0:T(8,128)(2,1)} %get-tuple-element.59.p_ref.a_ref, bf16[512,768]{1,0:T(8,128)(2,1)} %copy-done.5), custom_call_target="tpu_custom_call" | custom-call | flops 3221225472 | bytes 1048576 | tf_op jit(solution)/shard_map/sums_two/pallas_call | solution.py:408
  181.7 6.8 %all-to-all-start.1 = ((bf16[64,208,128]{2,1,0:T(8,128)(2,1)}), bf16[64,208,128]{2,1,0:T(8,128)(2,1)}, u32[]{:S(2)}, u32[]{:S(2)}) async-start(bf16[64,208,128]{2,1,0:T(8,128)(2,1)} %sums_two.1), calls=%async_computation.1 | async-start | bytes 6815744 | tf_op jit(solution)/shard_map/all_to_all | solution.py:560
  192.0 38.3 %all-to-all-done.1.x_ref = bf16[64,208,128]{2,1,0:T(8,128)(2,1)} async-done(((bf16[64,208,128]{2,1,0:T(8,128)(2,1)}), bf16[64,208,128]{2,1,0:T(8,128)(2,1)}, u32[]{:S(2)}, u32[]{:S(2)}) %all-to-all-start.1) | async-done | bytes 3407904 | tf_op jit(solution)/shard_map/all_to_all | solution.py:560
  230.4 5.5 %finish_two.1 = bf16[8,208,128]{2,1,0:T(8,128)(2,1)} custom-call(bf16[64,208,128]{2,1,0:T(8,128)(2,1)} %all-to-all-done.1.x_ref, bf16[32,768]{1,0:T(8,128)(2,1)} %constant_dynamic-slice_fusion.c_ref), custom_call_target="tpu_custom_call" | custom-call | tf_op jit(solution)/shard_map/finish_two/pallas_call | solution.py:448
  235.9 12.0 %all_to_all.16.a_ref = bf16[8,208,128]{2,1,0:T(8,128)(2,1)S(1)} all-to-all(bf16[8,208,128]{2,1,0:T(8,128)(2,1)} %finish_two.1), channel_id=1, replica_groups=mesh['y'=4,'xh'=2,'z'=4,'xl'=2,'c'=2] {'z','xl'}, dimensions={0} | all-to-all | bytes 851968 | tf_op jit(solution)/shard_map/all_to_all | solution.py:564
  247.9 3.1 %collective-permute-start.20 = (bf16[8,208,128]{2,1,0:T(8,128)(2,1)S(1)}, bf16[8,208,128]{2,1,0:T(8,128)(2,1)S(1)}, u32[]{:S(2)}, u32[]{:S(2)}) collective-permute-start(bf16[8,208,128]{2,1,0:T(8,128)(2,1)S(1)} %all_to_all.16.a_ref), channel_id=1, source_target_pairs={{0,1},{1,0},{2,3},{3,2},{4,5},{5,4},{6,7},{7,6},{8,9},{9,8},{10,11... | collective-permute-start | bytes 1277960 | tf_op jit(solution)/shard_map/ppermute | solution.py:495
  (92 shorter events, 55.8 us)
Async XLA Ops:
  0.6 38.4 %copy-start = (bf16[512,768]{1,0:T(8,128)(2,1)S(1)}, bf16[512,768]{1,0:T(8,128)(2,1)}, u32[]{:S(2)}) copy-start(bf16[512,768]{1,0:T(8,128)(2,1)} %param.5) | copy-start | bytes 2359300
  3.6 20.1 %collective-permute-start = (bf16[512,768]{1,0:T(8,128)(2,1)S(1)}, bf16[512,768]{1,0:T(8,128)(2,1)S(1)}, u32[]{:S(2)}, u32[]{:S(2)}) collective-permute-start(bf16[512,768]{1,0:T(8,128)(2,1)S(1)} %get-tuple-element.67.a_ref), channel_id=1, source_target_pairs={{0,18},{2,16},{16,2},{18,0},{1,19},{3,17},{17,3},{19,1},{4,22},{6,... | collective-permute-start | bytes 2359304 | tf_op jit(solution)/shard_map/ppermute | solution.py:499
  23.8 3.6 %collective-permute-start.1 = (bf16[512,768]{1,0:T(8,128)(2,1)S(1)}, bf16[512,768]{1,0:T(8,128)(2,1)S(1)}, u32[]{:S(2)}, u32[]{:S(2)}) collective-permute-start(bf16[512,768]{1,0:T(8,128)(2,1)S(1)} %collective-permute-done.a_ref), channel_id=1, source_target_pairs={{0,1},{1,0},{2,3},{3,2},{4,5},{5,4},{6,7},{7,6},{8,9},{9,8},{10,11... | collective-permute-start | bytes 2359304 | tf_op jit(solution)/shard_map/ppermute | solution.py:495
  38.5 1.5 collective-permute-start.2
  42.1 26.6 %collective-permute-start.5 = (bf16[256,768]{1,0:T(8,128)(2,1)S(1)}, bf16[256,768]{1,0:T(8,128)(2,1)S(1)}, u32[]{:S(2)}, u32[]{:S(2)}) collective-permute-start(bf16[256,768]{1,0:T(8,128)(2,1)S(1)} %constant_dynamic-slice_fusion.5), channel_id=1, source_target_pairs={{0,96},{32,0},{64,32},{96,64},{1,97},{33,1},{65,33},{97,65},{2,98}... | collective-permute-start | bytes 1179656 | tf_op jit(solution)/shard_map/ppermute | solution.py:487
  45.1 23.7 %collective-permute-start.4 = (bf16[256,768]{1,0:T(8,128)(2,1)S(1)}, bf16[256,768]{1,0:T(8,128)(2,1)S(1)}, u32[]{:S(2)}, u32[]{:S(2)}) collective-permute-start(bf16[256,768]{1,0:T(8,128)(2,1)S(1)} %constant_dynamic-slice_fusion.5), channel_id=1, source_target_pairs={{0,64},{32,96},{64,0},{96,32},{1,65},{33,97},{65,1},{97,33},{2,66}... | collective-permute-start | bytes 1179656 | tf_op jit(solution)/shard_map/ppermute | solution.py:487
  45.4 23.3 %collective-permute-start.3 = (bf16[256,768]{1,0:T(8,128)(2,1)S(1)}, bf16[256,768]{1,0:T(8,128)(2,1)S(1)}, u32[]{:S(2)}, u32[]{:S(2)}) collective-permute-start(bf16[256,768]{1,0:T(8,128)(2,1)S(1)} %constant_dynamic-slice_fusion.5), channel_id=1, source_target_pairs={{0,32},{32,64},{64,96},{96,0},{1,33},{33,65},{65,97},{97,1},{2,34}... | collective-permute-start | bytes 1179656 | tf_op jit(solution)/shard_map/ppermute | solution.py:487
  70.7 34.8 %collective-permute-start.6 = (bf16[1024,768]{1,0:T(8,128)(2,1)}, bf16[1024,768]{1,0:T(8,128)(2,1)S(1)}, u32[]{:S(2)}, u32[]{:S(2)}) collective-permute-start(bf16[1024,768]{1,0:T(8,128)(2,1)} %pad_maximum_fusion), channel_id=1, source_target_pairs={{0,18},{2,16},{16,2},{18,0},{1,19},{3,17},{17,3},{19,1},{4,22},{6,... | collective-permute-start | bytes 4718600 | tf_op jit(solution)/shard_map/ppermute | solution.py:499
  83.8 43.2 %collective-permute-start.7 = (bf16[512,768]{1,0:T(8,128)(2,1)}, bf16[512,768]{1,0:T(8,128)(2,1)}, u32[]{:S(2)}, u32[]{:S(2)}) collective-permute-start(bf16[512,768]{1,0:T(8,128)(2,1)} %get-tuple-element.69), channel_id=1, source_target_pairs={{0,32},{32,64},{64,96},{96,0},{1,33},{33,65},{65,97},{97,1},{2,34}... | collective-permute-start | bytes 2359304 | tf_op jit(solution)/shard_map/ppermute | solution.py:487
  85.4 41.6 %collective-permute-start.9 = (bf16[512,768]{1,0:T(8,128)(2,1)}, bf16[512,768]{1,0:T(8,128)(2,1)}, u32[]{:S(2)}, u32[]{:S(2)}) collective-permute-start(bf16[512,768]{1,0:T(8,128)(2,1)} %get-tuple-element.68), channel_id=1, source_target_pairs={{0,96},{32,0},{64,32},{96,64},{1,97},{33,1},{65,33},{97,65},{2,98}... | collective-permute-start | bytes 2359304 | tf_op jit(solution)/shard_map/ppermute | solution.py:487
  86.5 40.5 %collective-permute-start.8 = (bf16[512,768]{1,0:T(8,128)(2,1)}, bf16[512,768]{1,0:T(8,128)(2,1)}, u32[]{:S(2)}, u32[]{:S(2)}) collective-permute-start(bf16[512,768]{1,0:T(8,128)(2,1)} %get-tuple-element.47), channel_id=1, source_target_pairs={{0,64},{32,96},{64,0},{96,32},{1,65},{33,97},{65,1},{97,33},{2,66}... | collective-permute-start | bytes 2359304 | tf_op jit(solution)/shard_map/ppermute | solution.py:487
  93.7 23.2 %collective-permute-start.10 = (f32[4,512]{1,0:T(4,128)}, f32[4,512]{1,0:T(4,128)S(1)}, u32[]{:S(2)}, u32[]{:S(2)}) collective-permute-start(f32[4,512]{1,0:T(4,128)} %get-tuple-element.51.m0), channel_id=1, source_target_pairs={{0,32},{32,64},{64,96},{96,0},{1,33},{33,65},{65,97},{97,1},{2,34}... | collective-permute-start | bytes 24584 | tf_op jit(solution)/shard_map/ppermute | solution.py:487
  105.5 21.4 %collective-permute-start.11 = (f32[4,512]{1,0:T(4,128)}, f32[4,512]{1,0:T(4,128)S(1)}, u32[]{:S(2)}, u32[]{:S(2)}) collective-permute-start(f32[4,512]{1,0:T(4,128)} %get-tuple-element.51.m0), channel_id=1, source_target_pairs={{0,64},{32,96},{64,0},{96,32},{1,65},{33,97},{65,1},{97,33},{2,66}... | collective-permute-start | bytes 24584 | tf_op jit(solution)/shard_map/ppermute | solution.py:487
  116.9 10.0 %collective-permute-start.12 = (f32[4,512]{1,0:T(4,128)}, f32[4,512]{1,0:T(4,128)S(1)}, u32[]{:S(2)}, u32[]{:S(2)}) collective-permute-start(f32[4,512]{1,0:T(4,128)} %get-tuple-element.51.m0), channel_id=1, source_target_pairs={{0,96},{32,0},{64,32},{96,64},{1,97},{33,1},{65,33},{97,65},{2,98}... | collective-permute-start | bytes 24584 | tf_op jit(solution)/shard_map/ppermute | solution.py:487
  132.6 24.0 %collective-permute-start.18 = (bf16[512,768]{1,0:T(8,128)(2,1)}, bf16[512,768]{1,0:T(8,128)(2,1)S(1)}, u32[]{:S(2)}, u32[]{:S(2)}) collective-permute-start(bf16[512,768]{1,0:T(8,128)(2,1)} %get-tuple-element.59.p_ref.a_ref), channel_id=1, source_target_pairs={{0,1},{1,0},{2,3},{3,2},{4,5},{5,4},{6,7},{7,6},{8,9},{9,8},{10,11... | collective-permute-start | bytes 2359304 | tf_op jit(solution)/shard_map/ppermute | solution.py:495
  142.1 8.1 %collective-permute-start.14 = (bf16[192,512]{1,0:T(8,128)(2,1)S(1)}, bf16[192,512]{1,0:T(8,128)(2,1)S(1)}, u32[]{:S(2)}, u32[]{:S(2)}) collective-permute-start(bf16[192,512]{1,0:T(8,128)(2,1)S(1)} %get-tuple-element.74), channel_id=1, source_target_pairs={{0,64},{32,96},{64,0},{96,32},{1,65},{33,97},{65,1},{97,33},{2,66}... | collective-permute-start | bytes 589832 | tf_op jit(solution)/shard_map/ppermute | solution.py:487
  143.6 8.1 %collective-permute-start.15 = (bf16[192,512]{1,0:T(8,128)(2,1)S(1)}, bf16[192,512]{1,0:T(8,128)(2,1)S(1)}, u32[]{:S(2)}, u32[]{:S(2)}) collective-permute-start(bf16[192,512]{1,0:T(8,128)(2,1)S(1)} %get-tuple-element.73), channel_id=1, source_target_pairs={{0,96},{32,0},{64,32},{96,64},{1,97},{33,1},{65,33},{97,65},{2,98}... | collective-permute-start | bytes 589832 | tf_op jit(solution)/shard_map/ppermute | solution.py:487
  143.9 10.8 %collective-permute-start.13 = (bf16[192,512]{1,0:T(8,128)(2,1)S(1)}, bf16[192,512]{1,0:T(8,128)(2,1)S(1)}, u32[]{:S(2)}, u32[]{:S(2)}) collective-permute-start(bf16[192,512]{1,0:T(8,128)(2,1)S(1)} %get-tuple-element.75), channel_id=1, source_target_pairs={{0,32},{32,64},{64,96},{96,0},{1,33},{33,65},{65,97},{97,1},{2,34}... | collective-permute-start | bytes 589832 | tf_op jit(solution)/shard_map/ppermute | solution.py:487
  155.7 25.2 %collective-permute-start.16 = (bf16[4,96,512]{2,1,0:T(8,128)(2,1)S(1)}, bf16[4,96,512]{2,1,0:T(8,128)(2,1)S(1)}, u32[]{:S(2)}, u32[]{:S(2)}) collective-permute-start(bf16[4,96,512]{2,1,0:T(8,128)(2,1)S(1)} %get-tuple-element.70), channel_id=1, source_target_pairs={{0,16},{16,0},{1,17},{17,1},{2,18},{18,2},{3,19},{19,3},{4,20},{20... | collective-permute-start | bytes 1179656 | tf_op jit(solution)/shard_map/ppermute | solution.py:495
  167.5 2.8 %collective-permute-start.19 = (f32[2,1024]{1,0:T(2,128)}, f32[2,1024]{1,0:T(2,128)S(1)}, u32[]{:S(2)}, u32[]{:S(2)}) collective-permute-start(f32[2,1024]{1,0:T(2,128)} %get-tuple-element.61.s_ref), channel_id=1, source_target_pairs={{0,1},{1,0},{2,3},{3,2},{4,5},{5,4},{6,7},{7,6},{8,9},{9,8},{10,11... | collective-permute-start | bytes 24584 | tf_op jit(solution)/shard_map/ppermute | solution.py:495
  168.3 12.6 %collective-permute-start.17 = (f32[4,512]{1,0:T(4,128)S(1)}, f32[4,512]{1,0:T(4,128)S(1)}, u32[]{:S(2)}, u32[]{:S(2)}) collective-permute-start(f32[4,512]{1,0:T(4,128)S(1)} %copy-done.12), channel_id=1, source_target_pairs={{0,16},{16,0},{1,17},{17,1},{2,18},{18,2},{3,19},{19,3},{4,20},{20... | collective-permute-start | bytes 24584 | tf_op jit(solution)/shard_map/ppermute | solution.py:495
  181.7 48.7 %all-to-all-start.1 = ((bf16[64,208,128]{2,1,0:T(8,128)(2,1)}), bf16[64,208,128]{2,1,0:T(8,128)(2,1)}, u32[]{:S(2)}, u32[]{:S(2)}) async-start(bf16[64,208,128]{2,1,0:T(8,128)(2,1)} %sums_two.1), calls=%async_computation.1 | async-start | bytes 6815744 | tf_op jit(solution)/shard_map/all_to_all | solution.py:560
  192.0 59.0 %copy-start.11 = (f32[8,512]{1,0:T(8,128)S(1)}, f32[8,512]{1,0:T(8,128)}, u32[]{:S(2)}) copy-start(f32[8,512]{1,0:T(8,128)} %get-tuple-element.58) | copy-start | bytes 49156
  247.9 4.5 %collective-permute-start.20 = (bf16[8,208,128]{2,1,0:T(8,128)(2,1)S(1)}, bf16[8,208,128]{2,1,0:T(8,128)(2,1)S(1)}, u32[]{:S(2)}, u32[]{:S(2)}) collective-permute-start(bf16[8,208,128]{2,1,0:T(8,128)(2,1)S(1)} %all_to_all.16.a_ref), channel_id=1, source_target_pairs={{0,1},{1,0},{2,3},{3,2},{4,5},{5,4},{6,7},{7,6},{8,9},{9,8},{10,11... | collective-permute-start | bytes 1277960 | tf_op jit(solution)/shard_map/ppermute | solution.py:495
  (16 other events, 48.1 us)

commit v2 on v1

--- a/solution.py
+++ b/solution.py
@@ -24,10 +24,6 @@
 
 def shape(dims, dtype):
     return jax.ShapeDtypeStruct(dims, dtype)
-
-
-def cost(flops, exps=0, size=1 << 20):
-    return pl.CostEstimate(flops=flops, transcendentals=exps, bytes_accessed=size)
 
 
 def square_norms(block):
@@ -157,7 +153,9 @@
             shape((8, 512), F32),
             shape((2048, 128), F32),
         ],
-        cost_estimate=cost(2 * 2048 * 1024 * D, 2048 * 1024),
+        cost_estimate=pl.CostEstimate(
+            flops=2 * 2048 * 1024 * D, transcendentals=2048 * 1024, bytes_accessed=24 << 20
+        ),
         name="scores_near",
     )(idx, a, b, cents, cents, cents, cents)
 
@@ -178,7 +176,6 @@
         ),
         out_shape=[shape((2048, 2048), F32), shape((2048, D), BF), shape((8, 512), F32)],
         input_output_aliases={9: 0, 10: 1},
-        cost_estimate=cost(2 * 2048 * 1024 * D, 2048 * 1024),
         name="scores_far",
     )(idx, a, b, cents, cents, cents, cents, norms, near, p, x)
 
@@ -222,46 +219,35 @@
     )(idx, stats, local)
 
 
-def sums_one(p, factor, x, masses, first, count, dtype):
-    def kernel(p_ref, f_ref, x_ref, old_ref, o_ref, mass_ref, acc, macc):
-        j, i = pl.program_id(0), pl.program_id(1)
+def sums_one(p, factor, x, masses, blocks, dtype):
+    first, step = blocks[0], blocks[-1] - blocks[0]
+
+    def kernel(p_ref, f_ref, x_ref, old_ref, *refs):
+        mass_ref = refs[-1]
         w = (p_ref[...] * f_ref[...]).astype(BF)
-        part = nn(w, x_ref[...])
-        wide = w.astype(F32)
-        lanes = wide[:, 0:128]
-        for at in range(128, 1024, 128):
-            lanes = lanes + wide[:, at : at + 128]
-
-        @pl.when((i == 0) & (j == 0))
-        def _():
-            mass_ref[...] = old_ref[...]
-
-        @pl.when(i == 0)
-        def _():
-            acc[...] = part
-            macc[...] = lanes
-
-        @pl.when(i == 1)
-        def _():
-            o_ref[...] = (acc[...] + part).astype(o_ref.dtype)
-            mass = jnp.sum(macc[...] + lanes, axis=1, keepdims=True)
-            mass_ref[pl.ds(first + 2 * j, 1), :] = as_row(mass)
-
-    return pl.pallas_call(
-        kernel,
-        grid=(count, 2),
+        sums = nn(w, x_ref[...])
+        mass = as_row(lane_sums(w))
+        for q, k in enumerate(blocks):
+
+            @pl.when(pl.program_id(0) == q)
+            def _(q=q, k=k):
+                if q == 0:
+                    mass_ref[...] = old_ref[...]
+                refs[q][...] = sums.astype(dtype)
+                mass_ref[k : k + 1, :] = mass
+
+    return pl.pallas_call(
+        kernel,
+        grid=(len(blocks),),
         in_specs=[
-            pl.BlockSpec((512, 1024), lambda j, i: (first + 2 * j, i)),
-            pl.BlockSpec((1, 1024), lambda j, i: (0, i)),
-            pl.BlockSpec((1024, D), lambda j, i: (i, 0)),
-            pl.BlockSpec((4, 512), lambda j, i: (0, 0)),
+            pl.BlockSpec((512, 2048), lambda j: (first + step * j, 0)),
+            pl.BlockSpec((1, 2048), lambda j: (0, 0)),
+            pl.BlockSpec((2048, D), lambda j: (0, 0)),
+            pl.BlockSpec((4, 512), lambda j: (0, 0)),
         ],
-        out_specs=[
-            pl.BlockSpec((512, D), lambda j, i: (j, 0)),
-            pl.BlockSpec((4, 512), lambda j, i: (0, 0)),
-        ],
-        scratch_shapes=[pltpu.VMEM((512, D), F32), pltpu.VMEM((512, 128), F32)],
-        out_shape=[shape((512 * count, D), dtype), shape((4, 512), F32)],
+        out_specs=[pl.BlockSpec((512, D), lambda j: (0, 0)) for k in blocks]
+        + [pl.BlockSpec((4, 512), lambda j: (0, 0))],
+        out_shape=[shape((512, D), dtype) for k in blocks] + [shape((4, 512), F32)],
         name="sums_one",
     )(p, factor, x, masses)
 
@@ -274,19 +260,19 @@
             total = total + jnp.concatenate([t[k:], t[:k]], axis=0)
         mass_ref[...] = total
         i = pl.program_id(0)
-        column = as_column(mass_ref[0:1, pl.ds(pl.multiple_of(i * 128, 128), 128)]) + PRIOR
+        column = as_column(mass_ref[0:1, pl.ds(pl.multiple_of(i * 256, 256), 256)]) + PRIOR
         num = own_ref[...] + g1[...].astype(F32) + g2[...].astype(F32) + g3[...].astype(F32)
         num = num + PRIOR * cents_ref[...].astype(F32)
         pts_ref[...] = (num / column).astype(BF)
 
-    rows = pl.BlockSpec((128, D), lambda i, s: (i, 0))
+    rows = pl.BlockSpec((256, D), lambda i, s: (i, 0))
     small = pl.BlockSpec((4, 512), lambda i, s: (0, 0))
     return pl.pallas_call(
         kernel,
         grid_spec=pltpu.PrefetchScalarGridSpec(
             num_scalar_prefetch=1,
-            grid=(4,),
-            in_specs=[rows] * 4 + [pl.BlockSpec((128, D), lambda i, s: (s[0] * 4 + i, 0))] + [small] * 4,
+            grid=(2,),
+            in_specs=[rows] * 4 + [pl.BlockSpec((256, D), lambda i, s: (s[0] * 2 + i, 0))] + [small] * 4,
             out_specs=[rows, small],
         ),
         out_shape=[shape((512, D), BF), shape((4, 512), F32)],
@@ -296,16 +282,10 @@
 
 def turn_points(points):
     def kernel(p_ref, o_ref):
-        o_ref[...] = p_ref[...].astype(F32).T.astype(BF)
-
-    return pl.pallas_call(
-        kernel,
-        grid=(6,),
-        in_specs=[pl.BlockSpec((512, 128), lambda i: (0, i))],
-        out_specs=pl.BlockSpec((128, 512), lambda i: (i, 0)),
-        out_shape=shape((D, 512), BF),
-        name="turn_points",
-    )(points)
+        for at in range(0, D, 128):
+            o_ref[pl.ds(at, 128), :] = p_ref[:, pl.ds(at, 128)].astype(F32).T.astype(BF)
+
+    return pl.pallas_call(kernel, in_specs=[VMEM], out_shape=shape((D, 512), BF), name="turn_points")(points)
 
 
 def gather_one(place, keep, take, totals, far_totals):
@@ -329,13 +309,13 @@
 
 def norms_two(two):
     def kernel(c_ref, o_ref):
-        o_ref[...] = jnp.broadcast_to(square_norms(c_ref[...]), (256, 128))
-
-    return pl.pallas_call(
-        kernel,
-        grid=(8,),
-        in_specs=[pl.BlockSpec((256, D), lambda i: (i, 0))],
-        out_specs=pl.BlockSpec((256, 128), lambda i: (i, 0)),
+        o_ref[...] = jnp.broadcast_to(square_norms(c_ref[...]), (1024, 128))
+
+    return pl.pallas_call(
+        kernel,
+        grid=(2,),
+        in_specs=[pl.BlockSpec((1024, D), lambda i: (i, 0))],
+        out_specs=pl.BlockSpec((1024, 128), lambda i: (i, 0)),
         out_shape=shape((2048, 128), F32),
         name="norms_two",
     )(two)
@@ -376,7 +356,6 @@
             scratch_shapes=[pltpu.VMEM((2048, 256), F32)],
         ),
         out_shape=[shape((2048, 1024), F32), shape((2, 1024), F32)],
-        cost_estimate=cost(2 * 2048 * 1024 * D, 2048 * 1024),
         name="scores_two",
     )(slots, a, b, two, norms)
 
@@ -397,7 +376,7 @@
         w = (p_ref[...] * factor[0:1, :]).astype(BF)
         num = nn(w, rows[...])
         packed = mass_rows(as_row(lane_sums(w)))
-        for q in range(8):
+        for q in range(32):
             for j in range(6):
                 o_ref[q, j * 32 : j * 32 + 32, :] = num[q * 32 : q * 32 + 32, j * 128 : j * 128 + 128].astype(BF)
             lanes = packed[:, (q // 4) * 128 : (q // 4) * 128 + 128]
@@ -407,12 +386,11 @@
     whole = lambda r, c: pl.BlockSpec((r, c), lambda i: (0, 0))
     return pl.pallas_call(
         kernel,
-        grid=(8,),
-        in_specs=[pl.BlockSpec((256, 1024), lambda i: (i, 0)), whole(2, 1024), whole(2, 1024), whole(512, D), whole(512, D)],
-        out_specs=pl.BlockSpec((8, TALL, 128), lambda i: (i, 0, 0)),
+        grid=(2,),
+        in_specs=[pl.BlockSpec((1024, 1024), lambda i: (i, 0)), whole(2, 1024), whole(2, 1024), whole(512, D), whole(512, D)],
+        out_specs=pl.BlockSpec((32, TALL, 128), lambda i: (i, 0, 0)),
         scratch_shapes=[pltpu.VMEM((1024, D), BF), pltpu.VMEM((8, 1024), F32)],
         out_shape=shape((64, TALL, 128), BF),
-        cost_estimate=cost(2 * 2048 * 1024 * D),
         name="sums_two",
     )(p, stat, other, a, b)
 
@@ -421,7 +399,7 @@
     def kernel(x_ref, c_ref, o_ref, acc):
         i = pl.program_id(0)
         total = x_ref[0].astype(F32)
-        for q in range(1, 8):
+        for q in range(1, 16):
             total = total + x_ref[q].astype(F32)
 
         @pl.when(i == 0)
@@ -432,7 +410,7 @@
         def _():
             acc[...] += total
 
-        @pl.when(i == 7)
+        @pl.when(i == 3)
         def _():
             mass = acc[192:193, :] + acc[193:194, :] + acc[194:195, :]
             column = as_column(mass)[0:32] + PRIOR
@@ -447,9 +425,9 @@
 
     return pl.pallas_call(
         kernel,
-        grid=(8,),
+        grid=(4,),
         in_specs=[
-            pl.BlockSpec((8, TALL, 128), lambda i: (i, 0, 0)),
+            pl.BlockSpec((16, TALL, 128), lambda i: (i, 0, 0)),
             pl.BlockSpec((32, D), lambda i: (0, 0)),
         ],
         out_specs=pl.BlockSpec((8, TALL, 128), lambda i: (0, 0, 0)),
@@ -516,27 +494,27 @@
 
     mine = lax.dynamic_slice_in_dim(embeddings, c * 512, 512, 0).astype(BF)
     far_mine = flip_x(mine)
+    half_two = lax.dynamic_slice_in_dim(cents_two, c * 256, 256, 0)
+    around = [shift_y(half_two, k) for k in (1, 2, 3)]
+
     other = lax.dynamic_slice_in_dim(embeddings, (1 - c) * 512, 512, 0).astype(BF)
     p, x, near, norms = scores_near(idx, mine, other, cents_one)
-    far_mine = after(far_mine, near)
+    far_mine = after(far_mine, near, around[0], around[2])
     far_other = flip(far_mine, "c")
     p, x, local = scores_far(idx, far_mine, far_other, cents_one, norms, near, p, x)
 
     spread = merge_cores(local, flip(local, "c"))
     stats = lax.all_to_all(spread, ("xh", "z", "xl"), 0, 0, tiled=True)
-
-    half_two = after(lax.dynamic_slice_in_dim(cents_two, c * 256, 256, 0), spread)
-    around = [shift_y(half_two, k) for k in (1, 2, 3)]
-
     factor = merge_last(idx, stats, local)
+
     masses = jnp.zeros((4, 512), F32)
-    part, masses = sums_one(p, factor, x, masses, 2, 1, BF)
+    part, masses = sums_one(p, factor, x, masses, (2,), BF)
+    got = {2: shift_y(part, 2)}
+    part1, part3, masses = sums_one(p, factor, x, masses, (1, 3), BF)
+    got[1], got[3] = shift_y(part1, 1), shift_y(part3, 3)
+    own, masses = sums_one(p, factor, x, after(masses, got[2]), (0,), F32)
+
     same_two = jnp.concatenate([half_two] + [after(t, part) for t in around], axis=0)
-    got = {2: shift_y(part, 2)}
-    part, masses = sums_one(p, factor, x, masses, 1, 2, BF)
-    got[1], got[3] = shift_y(part[0:512], 1), shift_y(part[512:1024], 3)
-    own, masses = sums_one(p, factor, x, masses, 0, 1, F32)
-
     far_two = after(flip_x(same_two), masses)
     two = jnp.concatenate([same_two, far_two], axis=0)
     norms = norms_two(two)
@@ -545,20 +523,18 @@
         idx, after(own, norms), [got[k] for k in (1, 2, 3)], cents_one, masses, [shift_y(masses, k) for k in (1, 2, 3)]
     )
     their_points = flip(points, "c")
-    tall = turn_points(points)
-    p2, stat2 = scores_two(slots, after(points, tall), their_points, two, norms)
-    other2 = flip(stat2, "c")
-
+    p2, stat2 = scores_two(slots, points, their_points, two, norms)
+    packed = sums_two(p2, stat2, flip(stat2, "c"), points, their_points)
+    parts = lax.all_to_all(packed, ("y", "xh", "z", "xl"), 0, 0, tiled=True)
+
+    late_points, late_totals = lax.optimization_barrier((points, totals, packed))[0:2]
+    tall = turn_points(late_points)
     cut = lambda d: lax.dynamic_slice_in_dim(tall, ((y + d) % 4) * 192, 192, 0)
     cols = jnp.stack([cut(0)] + [shift_y(cut(k), k) for k in (1, 2, 3)]).reshape(4, 2, 96, 512)
     keep = lax.dynamic_index_in_dim(cols, xh, 1, keepdims=False)
     take = flip(lax.dynamic_index_in_dim(cols, 1 - xh, 1, keepdims=False), "xh")
-    far_totals = flip(totals, "xh")
-
-    packed = sums_two(p2, stat2, other2, points, their_points)
-    packed = after(packed, take, far_totals)
-    parts = lax.all_to_all(packed, ("y", "xh", "z", "xl"), 0, 0, tiled=True)
-    turned_one, mass_one = gather_one(jnp.stack([y, xh]), keep, take, totals, far_totals)
+    turned_one, mass_one = gather_one(jnp.stack([y, xh]), keep, take, late_totals, flip(late_totals, "xh"))
+
     rows = lax.dynamic_slice_in_dim(cents_two, c * 256 + z * 64 + xl * 32, 32, 0)
     spread = finish_two(parts, after(rows, turned_one))
     block = lax.all_to_all(spread, ("z", "xl"), 0, 0, tiled=True)

time: 257 us -> 240 us (0.934)
  waiting for transfers between devices: 75 us -> 62 us
  Pallas kernels: 90.2 us -> 80 us
  other arithmetic: 2.4 us -> 5.04 us
    all_to_all x1, waiting for transfers between devices: 38.3 us -> 0.01 us  [body(): parts = lax.all_to_all(packed, ('y', 'xh', 'z', 'xl'), 0, 0, tiled=True)]
    ppermute x12, waiting for transfers between devices: 18.4 us -> 43.3 us  [shift_y(): return lax.ppermute(x, 'y', [(i, (i + k) % 4) for i in range(4)])]
    pallas_call x7, Pallas kernels: 46.4 us -> 37 us  [the longest x3 20.3 us: sums_one(): pl.pallas_call(kernel, grid=(len(blocks),), in_specs=[pl.BlockSpec((512,...]
    ppermute x7, waiting for transfers between devices: 3.72 us -> 10.9 us  [flip(): return lax.ppermute(x, axis, [(0, 1), (1, 0)])]
    ppermute x2, waiting for transfers between devices: 14.5 us -> 7.78 us  [flip_x(): return lax.ppermute(x, ('xh', 'xl'), [(0, 3), (1, 2), (2, 1), (3, 0)])]
    ppermute x12, starting transfers between devices: 15.8 us -> 20.5 us  [shift_y(): return lax.ppermute(x, 'y', [(i, (i + k) % 4) for i in range(4)])]
    unnamed x41 -> x31, local copies, waits for them, and re-layouts: 9.54 us -> 12.5 us
    slice x1 -> x0, local copies, waits for them, and re-layouts: 2.61 us -> none  [body(): got[1], got[3] = (shift_y(part[0:512], 1), shift_y(part[512:1024], 3))]
  transfers between devices with their start and end apart: 22 -> 22, of which waited for: 10 -> 11; matrix products, arithmetic and copies ran while one was open for 5% -> 6% of each run, Pallas kernels for 26% -> 22%
where the time goes in v2:
time: 240 us
  Pallas kernels  80 us (33%)
  waiting for transfers between devices  62 us (26%)
  starting transfers between devices  40.1 us (17%)
  blocking collectives  28.7 us (12%)
  local copies, waits for them, and re-layouts  22.8 us (10%)
  other arithmetic  5.04 us (2%)
    ppermute x12, waiting for transfers between devices, shift_y(): return lax.ppermute(x, 'y', [(i, (i + k) % 4) for i in range(4)])  43.3 us
    ppermute x12, starting transfers between devices, shift_y(): return lax.ppermute(x, 'y', [(i, (i + k) % 4) for i in range(4)])  20.5 us
    pallas_call x3, Pallas kernels, sums_one(): pl.pallas_call(kernel, grid=(len(blocks),), in_specs=[pl.BlockSpec((512,...  20.3 us
    all_to_all x1, blocking collectives, body(): stats = lax.all_to_all(spread, ('xh', 'z', 'xl'), 0, 0, tiled=True)  15.5 us
    all_to_all x1, blocking collectives, body(): block = lax.all_to_all(spread, ('z', 'xl'), 0, 0, tiled=True)  13.1 us
    unnamed x31, local copies, waits for them, and re-layouts  12.5 us
    ppermute x7, waiting for transfers between devices, flip(): return lax.ppermute(x, axis, [(0, 1), (1, 0)])  10.9 us
    ppermute x7, starting transfers between devices, flip(): return lax.ppermute(x, axis, [(0, 1), (1, 0)])  10.7 us
  transfers between devices with their start and end apart: 22, of which 11 were waited for; matrix products, arithmetic and copies ran while one was open for 6% of the time, Pallas kernels for 22%

profile of v2, /device:TPU:1, one launch (start us, length us, event | category | flops | bytes accessed | tf_op | source)
XLA Modules:
  0.0 239.5 jit_solution(12481307494130297065)
XLA Ops:
  0.6 3.2 %dynamic-slice_convert_fusion = (bf16[512,768]{1,0:T(8,128)(2,1)}, bf16[512,768]{1,0:T(8,128)(2,1)}) fusion(f32[1024,768]{1,0:T(8,128)} %param.3, s32[]{:T(128)S(6)} %select_n.73, s32[]{:T(128)S(6)} %select_n.72), kind=kLoop, calls=%fused_computation.1 | loop fusion | bytes 3145736 | tf_op jit(solution)/shard_map/convert_element_type | solution.py:500
  3.8 3.3 %collective-permute-start = (bf16[512,768]{1,0:T(8,128)(2,1)}, bf16[512,768]{1,0:T(8,128)(2,1)}, u32[]{:S(2)}, u32[]{:S(2)}) collective-permute-start(bf16[512,768]{1,0:T(8,128)(2,1)} %get-tuple-element.71.a_ref), channel_id=1, source_target_pairs={{0,18},{2,16},{16,2},{18,0},{1,19},{3,17},{17,3},{19,1},{4,22},{6,... | collective-permute-start | bytes 2359304 | tf_op jit(solution)/shard_map/ppermute | solution.py:477
  12.3 10.5 %scores_near.1 = (f32[2048,2048]{1,0:T(8,128)}, bf16[2048,768]{1,0:T(8,128)(2,1)}, f32[8,512]{1,0:T(8,128)}, f32[2048,128]{1,0:T(8,128)}) custom-call(s32[8]{0:T(128)} %concatenate.11.idx.idx_ref, bf16[512,768]{1,0:T(8,128)(2,1)} %get-tuple-element.71.a_ref, bf16[512,768]{1,0:T(8,128)(2,1)} %get-tuple-element.70.b_ref, bf16[4096,768]{1,0:T(8,128)(2,1)} %cents_ref.1, ...), custom_call_target="tpu_custom_call" | custom-call | flops 3221225472 | bytes 25165824 | tf_op jit(solution)/shard_map/scores_near/pallas_call | solution.py:136
  26.0 3.1 %collective-permute-start.6 = (bf16[256,768]{1,0:T(8,128)(2,1)}, bf16[256,768]{1,0:T(8,128)(2,1)}, u32[]{:S(2)}, u32[]{:S(2)}) collective-permute-start(bf16[256,768]{1,0:T(8,128)(2,1)} %get-tuple-element.69), channel_id=1, source_target_pairs={{0,64},{32,96},{64,0},{96,32},{1,65},{33,97},{65,1},{97,33},{2,66}... | collective-permute-start | bytes 1179656 | tf_op jit(solution)/shard_map/ppermute | solution.py:465
  29.1 10.3 %scores_far.1 = (f32[2048,2048]{1,0:T(8,128)}, bf16[2048,768]{1,0:T(8,128)(2,1)}, f32[8,512]{1,0:T(8,128)}) custom-call(s32[8]{0:T(128)} %concatenate.11.idx.idx_ref, bf16[512,768]{1,0:T(8,128)(2,1)} %collective-permute-done.a_ref, bf16[512,768]{1,0:T(8,128)(2,1)} %collective-permute-done.3.b_ref, ...), custom_call_target="tpu_custom_call", output_to_operand_aliasing={{0}: (9, {}), {1}: (10, {})} | custom-call | tf_op jit(solution)/shard_map/scores_far/pallas_call | solution.py:164
  42.9 15.5 %all_to_all.15.s_ref = f32[16,8,512]{2,1,0:T(8,128)} all-to-all(f32[16,8,512]{2,1,0:T(8,128)} %merge_cores.1), channel_id=1, replica_groups=mesh['y'=4,'xh'=2,'z'=4,'xl'=2,'c'=2] {'xh','z','xl'}, dimensions={0} | all-to-all | bytes 524288 | tf_op jit(solution)/shard_map/all_to_all | solution.py:507
  60.7 5.9 %sums_one.3 = (bf16[512,768]{1,0:T(8,128)(2,1)}, f32[4,512]{1,0:T(4,128)}) custom-call(f32[2048,2048]{1,0:T(8,128)} %get-tuple-element.41.p_ref, f32[1,2048]{1,0:T(1,128)} %merge_last.1.f_ref, bf16[2048,768]{1,0:T(8,128)(2,1)} %get-tuple-element.43.x_ref, f32[4,512]{1,0:T(4,128)} %broadcast_in_dim.6.old_ref), custom_call_target="tpu_custom_call" | custom-call | tf_op jit(solution)/shard_map/sums_one/pallas_call | solution.py:239
  72.2 8.3 %sums_one.4 = (bf16[512,768]{1,0:T(8,128)(2,1)}, bf16[512,768]{1,0:T(8,128)(2,1)}, f32[4,512]{1,0:T(4,128)}) custom-call(f32[2048,2048]{1,0:T(8,128)} %get-tuple-element.41.p_ref, f32[1,2048]{1,0:T(1,128)} %merge_last.1.f_ref, bf16[2048,768]{1,0:T(8,128)(2,1)} %get-tuple-element.43.x_ref, f32[4,512]{1,0:T(4,128)} %get-tuple-element.44.old_ref), custom_call_target="tpu_custom_call" | custom-call | tf_op jit(solution)/shard_map/sums_one/pallas_call | solution.py:239
  85.2 3.7 %collective-permute-done.5.g2 = bf16[512,768]{1,0:T(8,128)(2,1)} collective-permute-done((bf16[512,768]{1,0:T(8,128)(2,1)}, bf16[512,768]{1,0:T(8,128)(2,1)}, u32[]{:S(2)}, u32[]{:S(2)}) %collective-permute-start.5) | collective-permute-done | bytes 786464 | tf_op jit(solution)/shard_map/ppermute | solution.py:465
  89.0 6.1 %sums_one.5 = (f32[512,768]{1,0:T(8,128)}, f32[4,512]{1,0:T(4,128)}) custom-call(f32[2048,2048]{1,0:T(8,128)} %get-tuple-element.41.p_ref, f32[1,2048]{1,0:T(1,128)} %merge_last.1.f_ref, bf16[2048,768]{1,0:T(8,128)(2,1)} %get-tuple-element.43.x_ref, f32[4,512]{1,0:T(4,128)} %get-tuple-element.47.old_ref), custom_call_target="tpu_custom_call" | custom-call | tf_op jit(solution)/shard_map/sums_one/pallas_call | solution.py:239
  98.5 6.4 %collective-permute-done.7 = bf16[1024,768]{1,0:T(8,128)(2,1)} collective-permute-done((bf16[1024,768]{1,0:T(8,128)(2,1)}, bf16[1024,768]{1,0:T(8,128)(2,1)}, u32[]{:S(2)}, u32[]{:S(2)}) %collective-permute-start.7) | collective-permute-done | bytes 1572896 | tf_op jit(solution)/shard_map/ppermute | solution.py:477
  110.2 3.0 %norms_two.1.n_ref = f32[2048,128]{1,0:T(8,128)} custom-call(bf16[2048,768]{1,0:T(8,128)(2,1)} %copy-done), custom_call_target="tpu_custom_call" | custom-call | tf_op jit(solution)/shard_map/norms_two/pallas_call | solution.py:314
  114.5 4.2 %finish_one.1 = (bf16[512,768]{1,0:T(8,128)(2,1)}, f32[4,512]{1,0:T(4,128)}) custom-call(s32[8]{0:T(128)} %concatenate.11.idx.idx_ref, f32[512,768]{1,0:T(8,128)} %get-tuple-element.54.own_ref, bf16[512,768]{1,0:T(8,128)(2,1)} %collective-permute-done.8.g1, bf16[512,768]{1,0:T(8,128)(2,1)} %collective-permute-done.5.g2, ...), custom_call_target="tpu_custom_call" | custom-call | tf_op jit(solution)/shard_map/finish_one/pallas_call | solution.py:270
  118.6 2.7 %collective-permute-start.13 = (bf16[512,768]{1,0:T(8,128)(2,1)}, bf16[512,768]{1,0:T(8,128)(2,1)S(1)}, u32[]{:S(2)}, u32[]{:S(2)}) collective-permute-start(bf16[512,768]{1,0:T(8,128)(2,1)} %get-tuple-element.61.a_ref.p_ref), channel_id=1, source_target_pairs={{0,1},{1,0},{2,3},{3,2},{4,5},{5,4},{6,7},{7,6},{8,9},{9,8},{10,11... | collective-permute-start | bytes 2359304 | tf_op jit(solution)/shard_map/ppermute | solution.py:473
  124.3 10.1 %scores_two.1 = (f32[2048,1024]{1,0:T(8,128)}, f32[2,1024]{1,0:T(2,128)}) custom-call(s32[8]{0:T(128)} %fusion.slots_ref, bf16[512,768]{1,0:T(8,128)(2,1)} %get-tuple-element.61.a_ref.p_ref, bf16[512,768]{1,0:T(8,128)(2,1)} %copy-done.2, bf16[2048,768]{1,0:T(8,128)(2,1)} %copy-done, f32[2048,128]{1,0:T(8,128)} %norms_two.1.n_ref), custom_call_target="tpu_custom_call" | custom-call | tf_op jit(solution)/shard_map/scores_two/pallas_call | solution.py:346
  136.4 7.6 %sums_two.1 = bf16[64,208,128]{2,1,0:T(8,128)(2,1)} custom-call(f32[2048,1024]{1,0:T(8,128)} %get-tuple-element.59.p_ref, f32[2,1024]{1,0:T(2,128)} %get-tuple-element.60.s_ref, f32[2,1024]{1,0:T(2,128)} %copy-done.12, bf16[512,768]{1,0:T(8,128)(2,1)} %get-tuple-element.61.a_ref.p_ref, bf16[512,768]{1,0:T(8,128)(2,1)} %copy-done.2), custom_call_target="tpu_custom_call" | custom-call | tf_op jit(solution)/shard_map/sums_two/pallas_call | solution.py:387
  144.0 4.7 %all-to-all-start.1 = ((bf16[64,208,128]{2,1,0:T(8,128)(2,1)}), bf16[64,208,128]{2,1,0:T(8,128)(2,1)S(1)}, u32[]{:S(2)}, u32[]{:S(2)}) async-start(bf16[64,208,128]{2,1,0:T(8,128)(2,1)} %sums_two.1), calls=%async_computation.1 | async-start | bytes 6815744 | tf_op jit(solution)/shard_map/all_to_all | solution.py:528
  153.3 2.6 %collective-permute-start.16 = (bf16[192,512]{1,0:T(8,128)(2,1)}, bf16[192,512]{1,0:T(8,128)(2,1)}, u32[]{:S(2)}, u32[]{:S(2)}) collective-permute-start(bf16[192,512]{1,0:T(8,128)(2,1)} %get-tuple-element.76), channel_id=1, source_target_pairs={{0,64},{32,96},{64,0},{96,32},{1,65},{33,97},{65,1},{97,33},{2,66}... | collective-permute-start | bytes 589832 | tf_op jit(solution)/shard_map/ppermute | solution.py:465
  157.3 35.4 %collective-permute-done.16 = bf16[192,512]{1,0:T(8,128)(2,1)} collective-permute-done((bf16[192,512]{1,0:T(8,128)(2,1)}, bf16[192,512]{1,0:T(8,128)(2,1)}, u32[]{:S(2)}, u32[]{:S(2)}) %collective-permute-start.16) | collective-permute-done | bytes 196640 | tf_op jit(solution)/shard_map/ppermute | solution.py:465
  192.8 2.8 %collective-permute-done.17 = bf16[192,512]{1,0:T(8,128)(2,1)} collective-permute-done((bf16[192,512]{1,0:T(8,128)(2,1)}, bf16[192,512]{1,0:T(8,128)(2,1)}, u32[]{:S(2)}, u32[]{:S(2)}) %collective-permute-start.17) | collective-permute-done | bytes 196640 | tf_op jit(solution)/shard_map/ppermute | solution.py:465
  204.2 6.4 %collective-permute-done.19.f_ref = f32[4,512]{1,0:T(4,128)S(1)} collective-permute-done((f32[4,512]{1,0:T(4,128)S(1)}, f32[4,512]{1,0:T(4,128)S(1)}, u32[]{:S(2)}, u32[]{:S(2)}) %collective-permute-start.19) | collective-permute-done | bytes 8224 | tf_op jit(solution)/shard_map/ppermute | solution.py:473
  215.3 3.8 %finish_two.1 = bf16[8,208,128]{2,1,0:T(8,128)(2,1)} custom-call(bf16[64,208,128]{2,1,0:T(8,128)(2,1)} %copy-done.1, bf16[32,768]{1,0:T(8,128)(2,1)} %constant_dynamic-slice_fusion.c_ref), custom_call_target="tpu_custom_call" | custom-call | tf_op jit(solution)/shard_map/finish_two/pallas_call | solution.py:426
  219.1 13.1 %all_to_all.16.a_ref = bf16[8,208,128]{2,1,0:T(8,128)(2,1)S(1)} all-to-all(bf16[8,208,128]{2,1,0:T(8,128)(2,1)} %finish_two.1), channel_id=1, replica_groups=mesh['y'=4,'xh'=2,'z'=4,'xl'=2,'c'=2] {'z','xl'}, dimensions={0} | all-to-all | bytes 851968 | tf_op jit(solution)/shard_map/all_to_all | solution.py:540
  232.3 2.7 %collective-permute-start.20 = (bf16[8,208,128]{2,1,0:T(8,128)(2,1)S(1)}, bf16[8,208,128]{2,1,0:T(8,128)(2,1)S(1)}, u32[]{:S(2)}, u32[]{:S(2)}) collective-permute-start(bf16[8,208,128]{2,1,0:T(8,128)(2,1)S(1)} %all_to_all.16.a_ref), channel_id=1, source_target_pairs={{0,1},{1,0},{2,3},{3,2},{4,5},{5,4},{6,7},{7,6},{8,9},{9,8},{10,11... | collective-permute-start | bytes 1277960 | tf_op jit(solution)/shard_map/ppermute | solution.py:473
  (80 shorter events, 63.0 us)
Async XLA Ops:
  3.8 20.4 %collective-permute-start = (bf16[512,768]{1,0:T(8,128)(2,1)}, bf16[512,768]{1,0:T(8,128)(2,1)}, u32[]{:S(2)}, u32[]{:S(2)}) collective-permute-start(bf16[512,768]{1,0:T(8,128)(2,1)} %get-tuple-element.71.a_ref), channel_id=1, source_target_pairs={{0,18},{2,16},{16,2},{18,0},{1,19},{3,17},{17,3},{19,1},{4,22},{6,... | collective-permute-start | bytes 2359304 | tf_op jit(solution)/shard_map/ppermute | solution.py:477
  9.0 13.9 %collective-permute-start.1 = (bf16[256,768]{1,0:T(8,128)(2,1)}, bf16[256,768]{1,0:T(8,128)(2,1)}, u32[]{:S(2)}, u32[]{:S(2)}) collective-permute-start(bf16[256,768]{1,0:T(8,128)(2,1)} %get-tuple-element.69), channel_id=1, source_target_pairs={{0,32},{32,64},{64,96},{96,0},{1,33},{33,65},{65,97},{97,1},{2,34}... | collective-permute-start | bytes 1179656 | tf_op jit(solution)/shard_map/ppermute | solution.py:465
  10.3 12.6 %collective-permute-start.2 = (bf16[256,768]{1,0:T(8,128)(2,1)}, bf16[256,768]{1,0:T(8,128)(2,1)S(1)}, u32[]{:S(2)}, u32[]{:S(2)}) collective-permute-start(bf16[256,768]{1,0:T(8,128)(2,1)} %get-tuple-element.69), channel_id=1, source_target_pairs={{0,96},{32,0},{64,32},{96,64},{1,97},{33,1},{65,33},{97,65},{2,98}... | collective-permute-start | bytes 1179656 | tf_op jit(solution)/shard_map/ppermute | solution.py:465
  24.3 4.8 %collective-permute-start.3 = (bf16[512,768]{1,0:T(8,128)(2,1)}, bf16[512,768]{1,0:T(8,128)(2,1)}, u32[]{:S(2)}, u32[]{:S(2)}) collective-permute-start(bf16[512,768]{1,0:T(8,128)(2,1)} %collective-permute-done.a_ref), channel_id=1, source_target_pairs={{0,1},{1,0},{2,3},{3,2},{4,5},{5,4},{6,7},{7,6},{8,9},{9,8},{10,11... | collective-permute-start | bytes 2359304 | tf_op jit(solution)/shard_map/ppermute | solution.py:473
  26.0 40.6 %collective-permute-start.6 = (bf16[256,768]{1,0:T(8,128)(2,1)}, bf16[256,768]{1,0:T(8,128)(2,1)}, u32[]{:S(2)}, u32[]{:S(2)}) collective-permute-start(bf16[256,768]{1,0:T(8,128)(2,1)} %get-tuple-element.69), channel_id=1, source_target_pairs={{0,64},{32,96},{64,0},{96,32},{1,65},{33,97},{65,1},{97,33},{2,66}... | collective-permute-start | bytes 1179656 | tf_op jit(solution)/shard_map/ppermute | solution.py:465
  39.4 1.4 collective-permute-start.4
  69.0 35.9 %collective-permute-start.7 = (bf16[1024,768]{1,0:T(8,128)(2,1)}, bf16[1024,768]{1,0:T(8,128)(2,1)}, u32[]{:S(2)}, u32[]{:S(2)}) collective-permute-start(bf16[1024,768]{1,0:T(8,128)(2,1)} %pad_maximum_fusion), channel_id=1, source_target_pairs={{0,18},{2,16},{16,2},{18,0},{1,19},{3,17},{17,3},{19,1},{4,22},{6,... | collective-permute-start | bytes 4718600 | tf_op jit(solution)/shard_map/ppermute | solution.py:477
  69.9 19.1 %collective-permute-start.5 = (bf16[512,768]{1,0:T(8,128)(2,1)}, bf16[512,768]{1,0:T(8,128)(2,1)}, u32[]{:S(2)}, u32[]{:S(2)}) collective-permute-start(bf16[512,768]{1,0:T(8,128)(2,1)} %get-tuple-element.46), channel_id=1, source_target_pairs={{0,64},{32,96},{64,0},{96,32},{1,65},{33,97},{65,1},{97,33},{2,66}... | collective-permute-start | bytes 2359304 | tf_op jit(solution)/shard_map/ppermute | solution.py:465
  80.5 32.8 %collective-permute-start.8 = (bf16[512,768]{1,0:T(8,128)(2,1)}, bf16[512,768]{1,0:T(8,128)(2,1)}, u32[]{:S(2)}, u32[]{:S(2)}) collective-permute-start(bf16[512,768]{1,0:T(8,128)(2,1)} %get-tuple-element.55), channel_id=1, source_target_pairs={{0,32},{32,64},{64,96},{96,0},{1,33},{33,65},{65,97},{97,1},{2,34}... | collective-permute-start | bytes 2359304 | tf_op jit(solution)/shard_map/ppermute | solution.py:465
  80.9 32.4 %collective-permute-start.9 = (bf16[512,768]{1,0:T(8,128)(2,1)}, bf16[512,768]{1,0:T(8,128)(2,1)}, u32[]{:S(2)}, u32[]{:S(2)}) collective-permute-start(bf16[512,768]{1,0:T(8,128)(2,1)} %get-tuple-element.56), channel_id=1, source_target_pairs={{0,96},{32,0},{64,32},{96,64},{1,97},{33,1},{65,33},{97,65},{2,98}... | collective-permute-start | bytes 2359304 | tf_op jit(solution)/shard_map/ppermute | solution.py:465
  95.1 18.1 %collective-permute-start.10 = (f32[4,512]{1,0:T(4,128)}, f32[4,512]{1,0:T(4,128)S(1)}, u32[]{:S(2)}, u32[]{:S(2)}) collective-permute-start(f32[4,512]{1,0:T(4,128)} %get-tuple-element.52.m0), channel_id=1, source_target_pairs={{0,32},{32,64},{64,96},{96,0},{1,33},{33,65},{65,97},{97,1},{2,34}... | collective-permute-start | bytes 24584 | tf_op jit(solution)/shard_map/ppermute | solution.py:465
  95.9 17.4 %collective-permute-start.11 = (f32[4,512]{1,0:T(4,128)}, f32[4,512]{1,0:T(4,128)S(1)}, u32[]{:S(2)}, u32[]{:S(2)}) collective-permute-start(f32[4,512]{1,0:T(4,128)} %get-tuple-element.52.m0), channel_id=1, source_target_pairs={{0,64},{32,96},{64,0},{96,32},{1,65},{33,97},{65,1},{97,33},{2,66}... | collective-permute-start | bytes 24584 | tf_op jit(solution)/shard_map/ppermute | solution.py:465
  104.9 8.4 %collective-permute-start.12 = (f32[4,512]{1,0:T(4,128)}, f32[4,512]{1,0:T(4,128)S(1)}, u32[]{:S(2)}, u32[]{:S(2)}) collective-permute-start(f32[4,512]{1,0:T(4,128)} %get-tuple-element.52.m0), channel_id=1, source_target_pairs={{0,96},{32,0},{64,32},{96,64},{1,97},{33,1},{65,33},{97,65},{2,98}... | collective-permute-start | bytes 24584 | tf_op jit(solution)/shard_map/ppermute | solution.py:465
  118.6 4.8 %collective-permute-start.13 = (bf16[512,768]{1,0:T(8,128)(2,1)}, bf16[512,768]{1,0:T(8,128)(2,1)S(1)}, u32[]{:S(2)}, u32[]{:S(2)}) collective-permute-start(bf16[512,768]{1,0:T(8,128)(2,1)} %get-tuple-element.61.a_ref.p_ref), channel_id=1, source_target_pairs={{0,1},{1,0},{2,3},{3,2},{4,5},{5,4},{6,7},{7,6},{8,9},{9,8},{10,11... | collective-permute-start | bytes 2359304 | tf_op jit(solution)/shard_map/ppermute | solution.py:473
  134.4 1.4 collective-permute-start.14
  144.0 69.6 %all-to-all-start.1 = ((bf16[64,208,128]{2,1,0:T(8,128)(2,1)}), bf16[64,208,128]{2,1,0:T(8,128)(2,1)S(1)}, u32[]{:S(2)}, u32[]{:S(2)}) async-start(bf16[64,208,128]{2,1,0:T(8,128)(2,1)} %sums_two.1), calls=%async_computation.1 | async-start | bytes 6815744 | tf_op jit(solution)/shard_map/all_to_all | solution.py:528
  148.9 54.2 %copy-start.7 = (f32[4,512]{1,0:T(4,128)S(1)}, f32[4,512]{1,0:T(4,128)}, u32[]{:S(2)}) copy-start(f32[4,512]{1,0:T(4,128)} %get-tuple-element.62.t_ref) | copy-start | bytes 24580
  153.3 39.5 %collective-permute-start.16 = (bf16[192,512]{1,0:T(8,128)(2,1)}, bf16[192,512]{1,0:T(8,128)(2,1)}, u32[]{:S(2)}, u32[]{:S(2)}) collective-permute-start(bf16[192,512]{1,0:T(8,128)(2,1)} %get-tuple-element.76), channel_id=1, source_target_pairs={{0,64},{32,96},{64,0},{96,32},{1,65},{33,97},{65,1},{97,33},{2,66}... | collective-permute-start | bytes 589832 | tf_op jit(solution)/shard_map/ppermute | solution.py:465
  155.9 39.7 %collective-permute-start.17 = (bf16[192,512]{1,0:T(8,128)(2,1)}, bf16[192,512]{1,0:T(8,128)(2,1)}, u32[]{:S(2)}, u32[]{:S(2)}) collective-permute-start(bf16[192,512]{1,0:T(8,128)(2,1)} %get-tuple-element.75), channel_id=1, source_target_pairs={{0,96},{32,0},{64,32},{96,64},{1,97},{33,1},{65,33},{97,65},{2,98}... | collective-permute-start | bytes 589832 | tf_op jit(solution)/shard_map/ppermute | solution.py:465
  156.7 40.3 %collective-permute-start.15 = (bf16[192,512]{1,0:T(8,128)(2,1)}, bf16[192,512]{1,0:T(8,128)(2,1)}, u32[]{:S(2)}, u32[]{:S(2)}) collective-permute-start(bf16[192,512]{1,0:T(8,128)(2,1)} %get-tuple-element.77), channel_id=1, source_target_pairs={{0,32},{32,64},{64,96},{96,0},{1,33},{33,65},{65,97},{97,1},{2,34}... | collective-permute-start | bytes 589832 | tf_op jit(solution)/shard_map/ppermute | solution.py:465
  199.2 11.4 %collective-permute-start.18 = (bf16[4,96,512]{2,1,0:T(8,128)(2,1)}, bf16[4,96,512]{2,1,0:T(8,128)(2,1)}, u32[]{:S(2)}, u32[]{:S(2)}) collective-permute-start(bf16[4,96,512]{2,1,0:T(8,128)(2,1)} %get-tuple-element.72), channel_id=1, source_target_pairs={{0,16},{16,0},{1,17},{17,1},{2,18},{18,2},{3,19},{19,3},{4,20},{20... | collective-permute-start | bytes 1179656 | tf_op jit(solution)/shard_map/ppermute | solution.py:473
  203.1 7.6 %collective-permute-start.19 = (f32[4,512]{1,0:T(4,128)S(1)}, f32[4,512]{1,0:T(4,128)S(1)}, u32[]{:S(2)}, u32[]{:S(2)}) collective-permute-start(f32[4,512]{1,0:T(4,128)S(1)} %copy-done.7), channel_id=1, source_target_pairs={{0,16},{16,0},{1,17},{17,1},{2,18},{18,2},{3,19},{19,3},{4,20},{20... | collective-permute-start | bytes 24584 | tf_op jit(solution)/shard_map/ppermute | solution.py:473
  213.6 21.4 %copy-start.6 = (f32[8,512]{1,0:T(8,128)S(1)}, f32[8,512]{1,0:T(8,128)}, u32[]{:S(2)}) copy-start(f32[8,512]{1,0:T(8,128)} %get-tuple-element.64) | copy-start | bytes 49156
  232.3 4.1 %collective-permute-start.20 = (bf16[8,208,128]{2,1,0:T(8,128)(2,1)S(1)}, bf16[8,208,128]{2,1,0:T(8,128)(2,1)S(1)}, u32[]{:S(2)}, u32[]{:S(2)}) collective-permute-start(bf16[8,208,128]{2,1,0:T(8,128)(2,1)S(1)} %all_to_all.16.a_ref), channel_id=1, source_target_pairs={{0,1},{1,0},{2,3},{3,2},{4,5},{5,4},{6,7},{7,6},{8,9},{9,8},{10,11... | collective-permute-start | bytes 1277960 | tf_op jit(solution)/shard_map/ppermute | solution.py:473
  (11 other events, 12.7 us)

commit v3 on v2

--- a/solution.py
+++ b/solution.py
@@ -91,7 +91,7 @@
     stat_ref[pl.ds(4 + row, 1), cols] = l
 
 
-def scores_near_kernel(idx, a_ref, b_ref, c0, c1, c2, c3, p_ref, x_ref, stat_ref, norms_ref, scores):
+def scores_near_kernel(idx, e_ref, c0, c1, c2, c3, p_ref, x_ref, stat_ref, norms_ref, scores):
     i = pl.program_id(0)
     cents = (c0, c1, c2, c3)
 
@@ -103,7 +103,7 @@
                 n = square_norms(cents[k][pl.ds(h * 256, 256), :])
                 norms_ref[pl.ds(k * 512 + h * 256, 256), :] = jnp.broadcast_to(n, (256, 128))
 
-    x = jnp.where(i < 2, a_ref[...], b_ref[...])
+    x = e_ref[...].astype(BF)
     x_ref[...] = x
     m, l = scores_step(cents, x * 2, norms_ref, p_ref, scores)
     put_stats(stat_ref, idx[4 + i // 2], i, m, l)
@@ -132,13 +132,13 @@
 WHOLE_NORMS = pl.BlockSpec((2048, 128), lambda i, s: (0, 0))
 
 
-def scores_near(idx, a, b, cents):
+def scores_near(idx, embeddings, cents):
     return pl.pallas_call(
         scores_near_kernel,
         grid_spec=pltpu.PrefetchScalarGridSpec(
             num_scalar_prefetch=1,
             grid=(4,),
-            in_specs=ROW_IN + CENTS_IN,
+            in_specs=[pl.BlockSpec((256, D), lambda i, s: (s[8 + i // 2] * 2 + i % 2, 0))] + CENTS_IN,
             out_specs=[
                 pl.BlockSpec((2048, 256), lambda i, s: (0, i)),
                 pl.BlockSpec((256, D), lambda i, s: (i, 0)),
@@ -157,7 +157,7 @@
             flops=2 * 2048 * 1024 * D, transcendentals=2048 * 1024, bytes_accessed=24 << 20
         ),
         name="scores_near",
-    )(idx, a, b, cents, cents, cents, cents)
+    )(idx, embeddings, cents, cents, cents, cents)
 
 
 def scores_far(idx, a, b, cents, norms, near, p, x):
@@ -280,64 +280,83 @@
     )(idx, own, *got, cents, masses, *far_masses)
 
 
-def turn_points(points):
-    def kernel(p_ref, o_ref):
+def turn_points(points, totals):
+    def kernel(p_ref, t_ref, o_ref, tall):
         for at in range(0, D, 128):
-            o_ref[pl.ds(at, 128), :] = p_ref[:, pl.ds(at, 128)].astype(F32).T.astype(BF)
-
-    return pl.pallas_call(kernel, in_specs=[VMEM], out_shape=shape((D, 512), BF), name="turn_points")(points)
-
-
-def gather_one(place, keep, take, totals, far_totals):
-    def kernel(place_ref, keep_ref, take_ref, t_ref, f_ref, o_ref, m_ref):
-        y, near = place_ref[0], place_ref[1]
-        for ref, half in ((keep_ref, near), (take_ref, 1 - near)):
-            for k in range(4):
-                start = half * 2048 + lax.rem(y + 4 - k, 4) * 512
-                o_ref[:, pl.ds(pl.multiple_of(start, 512), 512)] = ref[k].astype(F32)
-        for ref, half in ((t_ref, near), (f_ref, 1 - near)):
-            for j in range(4):
-                m_ref[pl.ds(half * 4 + lax.rem(y + j, 4), 1), :] = ref[j : j + 1, :]
-
-    return pl.pallas_call(
-        kernel,
-        in_specs=[SMEM] + [VMEM] * 4,
+            tall[pl.ds(at, 128), :] = p_ref[:, pl.ds(at, 128)].astype(F32).T.astype(BF)
+        packed = mass_rows(t_ref[0:1, :]).astype(BF)
+        for d in range(8):
+            o_ref[d, 0:96, :] = tall[pl.ds(d * 96, 96), :]
+            o_ref[d, 96:112, :] = packed
+
+    return pl.pallas_call(
+        kernel,
+        in_specs=[VMEM] * 2,
+        scratch_shapes=[pltpu.VMEM((D, 512), BF)],
+        out_shape=shape((8, 112, 512), BF),
+        cost_estimate=pl.CostEstimate(flops=0, transcendentals=0, bytes_accessed=24 << 20),
+        name="turn_points",
+    )(points, totals)
+
+
+def gather_one(parts):
+    def kernel(x_ref, o_ref, m_ref):
+        for s in range(8):
+            block = (s % 2) * 4 + s // 2
+            o_ref[:, block * 512 : block * 512 + 512] = x_ref[s, 0:96, :].astype(F32)
+            t = x_ref[s, 96:112, :].astype(F32)
+            m_ref[block : block + 1, :] = t[0:1] + t[1:2] + t[2:3]
+
+    return pl.pallas_call(
+        kernel,
+        in_specs=[VMEM],
         out_shape=[shape((96, 4096), F32), shape((8, 512), F32)],
         name="gather_one",
-    )(place, keep, take, totals, far_totals)
-
-
-def norms_two(two):
+    )(parts)
+
+
+def join_near(blocks):
+    def kernel(a, b, c, d, o_ref, n_ref):
+        for at, ref in zip(range(0, 1024, 256), (a, b, c, d)):
+            block = ref[...]
+            o_ref[pl.ds(at, 256), :] = block
+            n_ref[pl.ds(at, 256), :] = jnp.broadcast_to(square_norms(block), (256, 128))
+
+    return pl.pallas_call(
+        kernel,
+        in_specs=[VMEM] * 4,
+        out_shape=[shape((1024, D), BF), shape((1024, 128), F32)],
+        name="join_near",
+    )(*blocks)
+
+
+def norms_far(block):
     def kernel(c_ref, o_ref):
         o_ref[...] = jnp.broadcast_to(square_norms(c_ref[...]), (1024, 128))
 
     return pl.pallas_call(
-        kernel,
-        grid=(2,),
-        in_specs=[pl.BlockSpec((1024, D), lambda i: (i, 0))],
-        out_specs=pl.BlockSpec((1024, 128), lambda i: (i, 0)),
-        out_shape=shape((2048, 128), F32),
-        name="norms_two",
-    )(two)
-
-
-def scores_two(slots, a, b, two, norms):
-    def kernel(slots_ref, a_ref, b_ref, c_ref, n_ref, p_ref, stat_ref, scores):
+        kernel, in_specs=[VMEM], out_shape=shape((1024, 128), F32), name="norms_far"
+    )(block)
+
+
+def scores_two(places, a, b, near, far, near_norms, far_norms):
+    def kernel(places_ref, a_ref, b_ref, near_ref, far_ref, nn_ref, fn_ref, p_ref, stat_ref, scores):
         i = pl.program_id(0)
         twice = jnp.where(i < 2, a_ref[...], b_ref[...]) * 2
         top = None
-        for d in range(8):
-            here = pl.ds(pl.multiple_of(slots_ref[d] * 256, 256), 256)
+        for slot in range(8):
+            c_ref, n_ref = ((near_ref, nn_ref), (far_ref, fn_ref))[slot // 4]
+            here = pl.ds((slot % 4) * 256, 256)
             n = n_ref[here, :]
             s = nt(c_ref[here, :], twice) - jnp.concatenate([n, n], axis=1)
-            scores[pl.ds(d * 256, 256), :] = s
+            scores[pl.ds(slot * 256, 256), :] = s
             t = fold_rows(s, jnp.maximum)
             top = t if top is None else jnp.maximum(top, t)
         m = jnp.max(top, axis=0, keepdims=True)
         total = None
-        for at in range(0, 2048, 256):
-            e = jnp.exp(scores[pl.ds(at, 256), :] - m)
-            p_ref[pl.ds(at, 256), :] = e
+        for slot in range(8):
+            e = jnp.exp(scores[pl.ds(slot * 256, 256), :] - m)
+            p_ref[pl.ds(pl.multiple_of(places_ref[slot] * 256, 256), 256), :] = e
             t = fold_rows(e, jnp.add)
             total = t if total is None else total + t
         stat_ref[0:1, :] = m
@@ -348,7 +367,9 @@
         grid_spec=pltpu.PrefetchScalarGridSpec(
             num_scalar_prefetch=1,
             grid=(4,),
-            in_specs=ROW_IN + [pl.BlockSpec((2048, D), lambda i, s: (0, 0)), WHOLE_NORMS],
+            in_specs=ROW_IN
+            + [pl.BlockSpec((1024, D), lambda i, s: (0, 0))] * 2
+            + [pl.BlockSpec((1024, 128), lambda i, s: (0, 0))] * 2,
             out_specs=[
                 pl.BlockSpec((2048, 256), lambda i, s: (0, i)),
                 pl.BlockSpec((2, 256), lambda i, s: (0, i)),
@@ -357,7 +378,7 @@
         ),
         out_shape=[shape((2048, 1024), F32), shape((2, 1024), F32)],
         name="scores_two",
-    )(slots, a, b, two, norms)
+    )(places, a, b, near, far, near_norms, far_norms)
 
 
 def sums_two(p, stat, other, a, b):
@@ -395,46 +416,22 @@
     )(p, stat, other, a, b)
 
 
-def finish_two(parts, cents):
-    def kernel(x_ref, c_ref, o_ref, acc):
-        i = pl.program_id(0)
-        total = x_ref[0].astype(F32)
-        for q in range(1, 16):
-            total = total + x_ref[q].astype(F32)
-
-        @pl.when(i == 0)
-        def _():
-            acc[...] = total
-
-        @pl.when(i > 0)
-        def _():
-            acc[...] += total
-
-        @pl.when(i == 3)
-        def _():
-            mass = acc[192:193, :] + acc[193:194, :] + acc[194:195, :]
-            column = as_column(mass)[0:32] + PRIOR
-            packed = mass_rows(mass).astype(BF)
-            for j in range(6):
-                num = acc[j * 32 : j * 32 + 32, :] + PRIOR * c_ref[:, j * 128 : j * 128 + 128].astype(F32)
-                new = (num / column).astype(BF)
-                for q in range(8):
-                    o_ref[q, j * 32 : j * 32 + 32, :] = new
+def finish_two(total, cents):
+    def kernel(x_ref, c_ref, o_ref):
+        mass = x_ref[192:193, :] + x_ref[193:194, :] + x_ref[194:195, :]
+        column = as_column(mass)[0:32] + PRIOR
+        packed = mass_rows(mass).astype(BF)
+        for j in range(6):
+            num = x_ref[j * 32 : j * 32 + 32, :] + PRIOR * c_ref[:, j * 128 : j * 128 + 128].astype(F32)
+            new = (num / column).astype(BF)
             for q in range(8):
-                o_ref[q, 192:TALL, :] = packed
-
-    return pl.pallas_call(
-        kernel,
-        grid=(4,),
-        in_specs=[
-            pl.BlockSpec((16, TALL, 128), lambda i: (i, 0, 0)),
-            pl.BlockSpec((32, D), lambda i: (0, 0)),
-        ],
-        out_specs=pl.BlockSpec((8, TALL, 128), lambda i: (0, 0, 0)),
-        scratch_shapes=[pltpu.VMEM((TALL, 128), F32)],
-        out_shape=shape((8, TALL, 128), BF),
-        name="finish_two",
-    )(parts, cents)
+                o_ref[q, j * 32 : j * 32 + 32, :] = new
+        for q in range(8):
+            o_ref[q, 192:TALL, :] = packed
+
+    return pl.pallas_call(
+        kernel, in_specs=[VMEM] * 2, out_shape=shape((8, TALL, 128), BF), name="finish_two"
+    )(total, cents)
 
 
 def gather_two(core, mine, theirs):
@@ -488,24 +485,24 @@
     xl = lax.axis_index("xl").astype(jnp.int32)
     c = lax.axis_index("c").astype(jnp.int32)
     halves = jnp.stack([xh * 2 + c, xh * 2 + 1 - c, 2 - xh * 2 + c, 3 - xh * 2 - c])
-    idx = jnp.concatenate([xh * 4 + (y + jnp.arange(4, dtype=jnp.int32)) % 4, halves])
-    to = jnp.arange(8, dtype=jnp.int32)
-    slots = (xh ^ (to % 2)) * 4 + (y - to // 2) % 4
+    idx = jnp.concatenate([xh * 4 + (y + jnp.arange(4, dtype=jnp.int32)) % 4, halves, jnp.stack([c, 1 - c])])
+    slot = jnp.arange(8, dtype=jnp.int32)
+    places = (y - slot) % 4 * 2 + (xh ^ (slot // 4))
 
     mine = lax.dynamic_slice_in_dim(embeddings, c * 512, 512, 0).astype(BF)
     far_mine = flip_x(mine)
     half_two = lax.dynamic_slice_in_dim(cents_two, c * 256, 256, 0)
     around = [shift_y(half_two, k) for k in (1, 2, 3)]
 
-    other = lax.dynamic_slice_in_dim(embeddings, (1 - c) * 512, 512, 0).astype(BF)
-    p, x, near, norms = scores_near(idx, mine, other, cents_one)
+    p, x, near, norms = scores_near(idx, embeddings, cents_one)
     far_mine = after(far_mine, near, around[0], around[2])
     far_other = flip(far_mine, "c")
     p, x, local = scores_far(idx, far_mine, far_other, cents_one, norms, near, p, x)
 
     spread = merge_cores(local, flip(local, "c"))
     stats = lax.all_to_all(spread, ("xh", "z", "xl"), 0, 0, tiled=True)
-    factor = merge_last(idx, stats, local)
+    near_two, near_norms = join_near([after(half_two, spread)] + around)
+    factor = merge_last(idx, stats, after(local, near_norms))
 
     masses = jnp.zeros((4, 512), F32)
     part, masses = sums_one(p, factor, x, masses, (2,), BF)
@@ -514,29 +511,22 @@
     got[1], got[3] = shift_y(part1, 1), shift_y(part3, 3)
     own, masses = sums_one(p, factor, x, after(masses, got[2]), (0,), F32)
 
-    same_two = jnp.concatenate([half_two] + [after(t, part) for t in around], axis=0)
-    far_two = after(flip_x(same_two), masses)
-    two = jnp.concatenate([same_two, far_two], axis=0)
-    norms = norms_two(two)
+    far_two = after(flip_x(after(near_two, part)), masses)
+    far_norms = norms_far(far_two)
 
     points, totals = finish_one(
-        idx, after(own, norms), [got[k] for k in (1, 2, 3)], cents_one, masses, [shift_y(masses, k) for k in (1, 2, 3)]
+        idx, after(own, far_norms), [got[k] for k in (1, 2, 3)], cents_one, masses, [shift_y(masses, k) for k in (1, 2, 3)]
     )
     their_points = flip(points, "c")
-    p2, stat2 = scores_two(slots, points, their_points, two, norms)
+    tall = turn_points(points, totals)
+    columns = lax.all_to_all(tall, ("y", "xh"), 0, 0, tiled=True)
+    p2, stat2 = scores_two(places, after(points, tall), their_points, near_two, far_two, near_norms, far_norms)
     packed = sums_two(p2, stat2, flip(stat2, "c"), points, their_points)
-    parts = lax.all_to_all(packed, ("y", "xh", "z", "xl"), 0, 0, tiled=True)
-
-    late_points, late_totals = lax.optimization_barrier((points, totals, packed))[0:2]
-    tall = turn_points(late_points)
-    cut = lambda d: lax.dynamic_slice_in_dim(tall, ((y + d) % 4) * 192, 192, 0)
-    cols = jnp.stack([cut(0)] + [shift_y(cut(k), k) for k in (1, 2, 3)]).reshape(4, 2, 96, 512)
-    keep = lax.dynamic_index_in_dim(cols, xh, 1, keepdims=False)
-    take = flip(lax.dynamic_index_in_dim(cols, 1 - xh, 1, keepdims=False), "xh")
-    turned_one, mass_one = gather_one(jnp.stack([y, xh]), keep, take, late_totals, flip(late_totals, "xh"))
-
+    parts = lax.all_to_all(after(packed, columns), ("y", "xh", "z", "xl"), 0, 0, tiled=True)
+    turned_one, mass_one = gather_one(columns)
+    total = jnp.sum(parts.astype(F32), axis=0)
     rows = lax.dynamic_slice_in_dim(cents_two, c * 256 + z * 64 + xl * 32, 32, 0)
-    spread = finish_two(parts, after(rows, turned_one))
+    spread = finish_two(total, after(rows, turned_one))
     block = lax.all_to_all(spread, ("z", "xl"), 0, 0, tiled=True)
     updated_two, mass_two = gather_two(c[None], block, flip(block, "c"))
     return turned_one.T, mass_one.reshape(4096), updated_two, mass_two.reshape(512)

time: 240 us -> 221 us (0.921)
  blocking collectives: 28.7 us -> 12 us
  local copies, waits for them, and re-layouts: 22.8 us -> 10.6 us
  starting transfers between devices: 40.1 us -> 48 us
    all_to_all x1 -> x3, waiting for transfers between devices: 0.01 us -> 44.1 us  [the longest x1 38.8 us: body(): lax.all_to_all(after(packed, columns), ('y', 'xh', 'z', 'xl'), 0, 0, tile...]
    ppermute x12 -> x9, waiting for transfers between devices: 43.3 us -> 6.27 us  [shift_y(): return lax.ppermute(x, 'y', [(i, (i + k) % 4) for i in range(4)])]
    all_to_all x1 -> x0, blocking collectives: 15.5 us -> none  [body(): stats = lax.all_to_all(spread, ('xh', 'z', 'xl'), 0, 0, tiled=True)]
    all_to_all x1 -> x3, starting transfers between devices: 4.74 us -> 20.2 us  [the longest x1 9.3 us: body(): lax.all_to_all(after(packed, columns), ('y', 'xh', 'z', 'xl'), 0, 0, tile...]
    ppermute x7 -> x5, waiting for transfers between devices: 10.9 us -> 4.26 us  [flip(): return lax.ppermute(x, axis, [(0, 1), (1, 0)])]
    unnamed x31 -> x41, local copies, waits for them, and re-layouts: 12.5 us -> 7.19 us
    ppermute x12 -> x9, starting transfers between devices: 20.5 us -> 15.2 us  [shift_y(): return lax.ppermute(x, 'y', [(i, (i + k) % 4) for i in range(4)])]
    reduce_sum x0 -> x1, other arithmetic: none -> 3.08 us  [body(): total = jnp.sum(parts.astype(F32), axis=0)]
  transfers between devices with their start and end apart: 22 -> 19, of which waited for: 11 -> 9; matrix products, arithmetic and copies ran while one was open for 6% -> 1% of each run, Pallas kernels for 22% -> 29%
where the time goes in v3:
time: 221 us; the launch traced here: 220 us
  Pallas kernels  81.3 us (37%)
  waiting for transfers between devices  63.7 us (29%)
  starting transfers between devices  48 us (22%)
  blocking collectives  12 us (5%)
  local copies, waits for them, and re-layouts  10.6 us (5%)
  other arithmetic  3.61 us (2%)
    all_to_all x1, waiting for transfers between devices, body(): lax.all_to_all(after(packed, columns), ('y', 'xh', 'z', 'xl'), 0, 0, tile...  38.8 us
    pallas_call x3, Pallas kernels, sums_one(): pl.pallas_call(kernel, grid=(len(blocks),), in_specs=[pl.BlockSpec((512,...  20.5 us
    ppermute x9, starting transfers between devices, shift_y(): return lax.ppermute(x, 'y', [(i, (i + k) % 4) for i in range(4)])  15.2 us
    all_to_all x1, blocking collectives, body(): block = lax.all_to_all(spread, ('z', 'xl'), 0, 0, tiled=True)  12 us
    pallas_call x1, Pallas kernels, scores_near(): pl.pallas_call(scores_near_kernel, grid_spec=pltpu.PrefetchScalarGridSpec...  10.9 us
    pallas_call x1, Pallas kernels, scores_two(): pl.pallas_call(kernel, grid_spec=pltpu.PrefetchScalarGridSpec(num_scalar_...  10.3 us
    pallas_call x1, Pallas kernels, scores_far(): pl.pallas_call(scores_far_kernel, grid_spec=pltpu.PrefetchScalarGridSpec(...  10.3 us
    all_to_all x1, starting transfers between devices, body(): lax.all_to_all(after(packed, columns), ('y', 'xh', 'z', 'xl'), 0, 0, tile...  9.3 us
  transfers between devices with their start and end apart: 19, of which 9 were waited for; matrix products, arithmetic and copies ran while one was open for 1% of the time, Pallas kernels for 29%

profile of v3, /device:TPU:1, one launch (start us, length us, event | category | flops | bytes accessed | tf_op | source)
XLA Modules:
  0.0 220.1 jit_solution(6768261505025348173)
XLA Ops:
  2.2 3.4 %collective-permute-start = (bf16[512,768]{1,0:T(8,128)(2,1)S(1)}, bf16[512,768]{1,0:T(8,128)(2,1)S(1)}, u32[]{:S(2)}, u32[]{:S(2)}) collective-permute-start(bf16[512,768]{1,0:T(8,128)(2,1)S(1)} %dynamic-slice_convert_fusion), channel_id=1, source_target_pairs={{0,18},{2,16},{16,2},{18,0},{1,19},{3,17},{17,3},{19,1},{4,22},{6,... | collective-permute-start | bytes 2359304 | tf_op jit(solution)/shard_map/ppermute | solution.py:474
  9.1 10.9 %scores_near.1 = (f32[2048,2048]{1,0:T(8,128)}, bf16[2048,768]{1,0:T(8,128)(2,1)}, f32[8,512]{1,0:T(8,128)}, f32[2048,128]{1,0:T(8,128)}) custom-call(s32[10]{0:T(128)} %concatenate.3.idx.idx_ref, f32[1024,768]{1,0:T(8,128)} %e_ref.1, bf16[4096,768]{1,0:T(8,128)(2,1)} %cents_ref.1, bf16[4096,768]{1,0:T(8,128)(2,1)} %cents_ref.1, ...), custom_call_target="tpu_custom_call" | custom-call | flops 3221225472 | bytes 25165824 | tf_op jit(solution)/shard_map/scores_near/pallas_call | solution.py:136
  24.1 3.1 %collective-permute-start.5 = (bf16[256,768]{1,0:T(8,128)(2,1)S(1)}, bf16[256,768]{1,0:T(8,128)(2,1)}, u32[]{:S(2)}, u32[]{:S(2)}) collective-permute-start(bf16[256,768]{1,0:T(8,128)(2,1)S(1)} %constant_dynamic-slice_fusion.1.a), channel_id=1, source_target_pairs={{0,64},{32,96},{64,0},{96,32},{1,65},{33,97},{65,1},{97,33},{2,66}... | collective-permute-start | bytes 1179656 | tf_op jit(solution)/shard_map/ppermute | solution.py:462
  28.1 10.3 %scores_far.1 = (f32[2048,2048]{1,0:T(8,128)}, bf16[2048,768]{1,0:T(8,128)(2,1)}, f32[8,512]{1,0:T(8,128)}) custom-call(s32[10]{0:T(128)} %concatenate.3.idx.idx_ref, bf16[512,768]{1,0:T(8,128)(2,1)} %copy-done.9, bf16[512,768]{1,0:T(8,128)(2,1)} %copy-done.10, bf16[4096,768]{1,0:T(8,128)(2,1)} %cents_ref.1, ...), custom_call_target="tpu_custom_call", output_to_operand_aliasing={{0}: (9, {}), {1}: (10, {})} | custom-call | tf_op jit(solution)/shard_map/scores_far/pallas_call | solution.py:164
  42.0 7.3 %all-to-all-start = ((f32[16,8,512]{2,1,0:T(8,128)}), f32[16,8,512]{2,1,0:T(8,128)S(1)}, u32[]{:S(2)}, u32[]{:S(2)}) async-start(f32[16,8,512]{2,1,0:T(8,128)} %merge_cores.1), calls=%async_computation | async-start | bytes 524288 | tf_op jit(solution)/shard_map/all_to_all | solution.py:503
  49.3 2.9 %join_near.1 = (bf16[1024,768]{1,0:T(8,128)(2,1)}, f32[1024,128]{1,0:T(8,128)}) custom-call(bf16[256,768]{1,0:T(8,128)(2,1)} %copy-done.6, bf16[256,768]{1,0:T(8,128)(2,1)} %copy-done.12, bf16[256,768]{1,0:T(8,128)(2,1)} %collective-permute-done.5.c, bf16[256,768]{1,0:T(8,128)(2,1)} %copy-done.13), custom_call_target="tpu_custom_call" | custom-call | tf_op jit(solution)/shard_map/join_near/pallas_call | solution.py:325
  52.2 5.2 %all-to-all-done.s_ref = f32[16,8,512]{2,1,0:T(8,128)S(1)} async-done(((f32[16,8,512]{2,1,0:T(8,128)}), f32[16,8,512]{2,1,0:T(8,128)S(1)}, u32[]{:S(2)}, u32[]{:S(2)}) %all-to-all-start) | async-done | bytes 262176 | tf_op jit(solution)/shard_map/all_to_all | solution.py:503
  60.4 5.9 %sums_one.3 = (bf16[512,768]{1,0:T(8,128)(2,1)}, f32[4,512]{1,0:T(4,128)}) custom-call(f32[2048,2048]{1,0:T(8,128)} %get-tuple-element.43.p_ref, f32[1,2048]{1,0:T(1,128)} %merge_last.1.f_ref, bf16[2048,768]{1,0:T(8,128)(2,1)} %get-tuple-element.48.x_ref, f32[4,512]{1,0:T(4,128)} %broadcast_in_dim.4.old_ref), custom_call_target="tpu_custom_call" | custom-call | tf_op jit(solution)/shard_map/sums_one/pallas_call | solution.py:239
  69.1 8.2 %sums_one.4 = (bf16[512,768]{1,0:T(8,128)(2,1)}, bf16[512,768]{1,0:T(8,128)(2,1)}, f32[4,512]{1,0:T(4,128)}) custom-call(f32[2048,2048]{1,0:T(8,128)} %get-tuple-element.43.p_ref, f32[1,2048]{1,0:T(1,128)} %merge_last.1.f_ref, bf16[2048,768]{1,0:T(8,128)(2,1)} %get-tuple-element.48.x_ref, f32[4,512]{1,0:T(4,128)} %get-tuple-element.49.old_ref), custom_call_target="tpu_custom_call" | custom-call | tf_op jit(solution)/shard_map/sums_one/pallas_call | solution.py:239
  79.9 6.3 %collective-permute-done.6.g2 = bf16[512,768]{1,0:T(8,128)(2,1)S(1)} collective-permute-done((bf16[512,768]{1,0:T(8,128)(2,1)}, bf16[512,768]{1,0:T(8,128)(2,1)S(1)}, u32[]{:S(2)}, u32[]{:S(2)}) %collective-permute-start.6) | collective-permute-done | bytes 786464 | tf_op jit(solution)/shard_map/ppermute | solution.py:462
  86.2 6.4 %sums_one.5 = (f32[512,768]{1,0:T(8,128)}, f32[4,512]{1,0:T(4,128)}) custom-call(f32[2048,2048]{1,0:T(8,128)} %get-tuple-element.43.p_ref, f32[1,2048]{1,0:T(1,128)} %merge_last.1.f_ref, bf16[2048,768]{1,0:T(8,128)(2,1)} %get-tuple-element.48.x_ref, f32[4,512]{1,0:T(4,128)} %get-tuple-element.52.old_ref), custom_call_target="tpu_custom_call" | custom-call | tf_op jit(solution)/shard_map/sums_one/pallas_call | solution.py:239
  93.0 2.5 %collective-permute-start.11 = (f32[4,512]{1,0:T(4,128)}, f32[4,512]{1,0:T(4,128)S(1)}, u32[]{:S(2)}, u32[]{:S(2)}) collective-permute-start(f32[4,512]{1,0:T(4,128)} %get-tuple-element.56.m0), channel_id=1, source_target_pairs={{0,64},{32,96},{64,0},{96,32},{1,65},{33,97},{65,1},{97,33},{2,66}... | collective-permute-start | bytes 24584 | tf_op jit(solution)/shard_map/ppermute | solution.py:462
  95.5 6.7 %collective-permute-done.7.c_ref.far_ref = bf16[1024,768]{1,0:T(8,128)(2,1)S(1)} collective-permute-done((bf16[1024,768]{1,0:T(8,128)(2,1)}, bf16[1024,768]{1,0:T(8,128)(2,1)S(1)}, u32[]{:S(2)}, u32[]{:S(2)}) %collective-permute-start.7) | collective-permute-done | bytes 1572896 | tf_op jit(solution)/shard_map/ppermute | solution.py:474
  103.9 2.6 %norms_far.1.fn_ref = f32[1024,128]{1,0:T(8,128)} custom-call(bf16[1024,768]{1,0:T(8,128)(2,1)} %copy-done.2), custom_call_target="tpu_custom_call" | custom-call | tf_op jit(solution)/shard_map/norms_far/pallas_call | solution.py:337
  107.7 4.2 %finish_one.1 = (bf16[512,768]{1,0:T(8,128)(2,1)}, f32[4,512]{1,0:T(4,128)}) custom-call(s32[10]{0:T(128)} %concatenate.3.idx.idx_ref, f32[512,768]{1,0:T(8,128)} %get-tuple-element.58.own_ref, bf16[512,768]{1,0:T(8,128)(2,1)} %collective-permute-done.8.g1, bf16[512,768]{1,0:T(8,128)(2,1)} %copy-done.8, bf16[512,768]{1,0:T(8,128)(2,1)} %collective-permute-done.9.g3, ...), custom_call_target="tpu_custom_call" | custom-call | tf_op jit(solution)/shard_map/finish_one/pallas_call | solution.py:270
  114.3 3.6 %all-to-all-start.1 = ((bf16[8,112,512]{2,1,0:T(8,128)(2,1)}), bf16[8,112,512]{2,1,0:T(8,128)(2,1)S(1)}, u32[]{:S(2)}, u32[]{:S(2)}) async-start(bf16[8,112,512]{2,1,0:T(8,128)(2,1)} %turn_points.1), calls=%async_computation.1 | async-start | bytes 1835008 | tf_op jit(solution)/shard_map/all_to_all | solution.py:522
  117.9 2.7 %collective-permute-start.13 = (bf16[512,768]{1,0:T(8,128)(2,1)S(1)}, bf16[512,768]{1,0:T(8,128)(2,1)S(1)}, u32[]{:S(2)}, u32[]{:S(2)}) collective-permute-start(bf16[512,768]{1,0:T(8,128)(2,1)S(1)} %copy-done.1), channel_id=1, source_target_pairs={{0,1},{1,0},{2,3},{3,2},{4,5},{5,4},{6,7},{7,6},{8,9},{9,8},{10,11... | collective-permute-start | bytes 2359304 | tf_op jit(solution)/shard_map/ppermute | solution.py:470
  123.3 10.3 %scores_two.1 = (f32[2048,1024]{1,0:T(8,128)}, f32[2,1024]{1,0:T(2,128)}) custom-call(s32[8]{0:T(128)} %fusion.1.places_ref, bf16[512,768]{1,0:T(8,128)(2,1)} %get-tuple-element.65.p_ref.a_ref, bf16[512,768]{1,0:T(8,128)(2,1)} %copy-done.4, bf16[1024,768]{1,0:T(8,128)(2,1)} %get-tuple-element.55.near_ref, bf16[1024,768]{1,0:T(8,128)(2,1)} %copy-done.2, ...), custom_call_target="tpu_custom_call" | custom-call | tf_op jit(solution)/shard_map/scores_two/pallas_call | solution.py:365
  135.7 7.6 %sums_two.1 = bf16[64,208,128]{2,1,0:T(8,128)(2,1)} custom-call(f32[2048,1024]{1,0:T(8,128)} %get-tuple-element.66.p_ref, f32[2,1024]{1,0:T(2,128)} %get-tuple-element.67.s_ref, f32[2,1024]{1,0:T(2,128)} %copy-done.19, bf16[512,768]{1,0:T(8,128)(2,1)} %get-tuple-element.65.p_ref.a_ref, bf16[512,768]{1,0:T(8,128)(2,1)} %copy-done.4), custom_call_target="tpu_custom_call" | custom-call | tf_op jit(solution)/shard_map/sums_two/pallas_call | solution.py:408
  144.2 9.3 %all-to-all-start.2 = ((bf16[64,208,128]{2,1,0:T(8,128)(2,1)}), bf16[64,208,128]{2,1,0:T(8,128)(2,1)}, u32[]{:S(2)}, u32[]{:S(2)}) async-start(bf16[64,208,128]{2,1,0:T(8,128)(2,1)} %sums_two.1), calls=%async_computation.2 | async-start | bytes 6815744 | tf_op jit(solution)/shard_map/all_to_all | solution.py:525
  156.6 38.8 %all-to-all-done.2 = bf16[64,208,128]{2,1,0:T(8,128)(2,1)} async-done(((bf16[64,208,128]{2,1,0:T(8,128)(2,1)}), bf16[64,208,128]{2,1,0:T(8,128)(2,1)}, u32[]{:S(2)}, u32[]{:S(2)}) %all-to-all-start.2) | async-done | bytes 3407904 | tf_op jit(solution)/shard_map/all_to_all | solution.py:525
  195.4 3.1 %convert_reduce_fusion.x_ref = f32[208,128]{1,0:T(8,128)} fusion(bf16[64,208,128]{2,1,0:T(8,128)(2,1)} %all-to-all-done.2), kind=kLoop, calls=%fused_computation | loop fusion | flops 3381248 | bytes 3514368 | tf_op jit(solution)/shard_map/reduce_sum | solution.py:527
  200.3 12.0 %all_to_all.20.a_ref = bf16[8,208,128]{2,1,0:T(8,128)(2,1)S(1)} all-to-all(bf16[8,208,128]{2,1,0:T(8,128)(2,1)} %finish_two.1), channel_id=1, replica_groups=mesh['y'=4,'xh'=2,'z'=4,'xl'=2,'c'=2] {'z','xl'}, dimensions={0} | all-to-all | bytes 851968 | tf_op jit(solution)/shard_map/all_to_all | solution.py:530
  212.4 3.1 %collective-permute-start.15 = (bf16[8,208,128]{2,1,0:T(8,128)(2,1)S(1)}, bf16[8,208,128]{2,1,0:T(8,128)(2,1)S(1)}, u32[]{:S(2)}, u32[]{:S(2)}) collective-permute-start(bf16[8,208,128]{2,1,0:T(8,128)(2,1)S(1)} %all_to_all.20.a_ref), channel_id=1, source_target_pairs={{0,1},{1,0},{2,3},{3,2},{4,5},{5,4},{6,7},{7,6},{8,9},{9,8},{10,11... | collective-permute-start | bytes 1277960 | tf_op jit(solution)/shard_map/ppermute | solution.py:470
  (80 shorter events, 43.0 us)
Async XLA Ops:
  2.2 20.2 %collective-permute-start = (bf16[512,768]{1,0:T(8,128)(2,1)S(1)}, bf16[512,768]{1,0:T(8,128)(2,1)S(1)}, u32[]{:S(2)}, u32[]{:S(2)}) collective-permute-start(bf16[512,768]{1,0:T(8,128)(2,1)S(1)} %dynamic-slice_convert_fusion), channel_id=1, source_target_pairs={{0,18},{2,16},{16,2},{18,0},{1,19},{3,17},{17,3},{19,1},{4,22},{6,... | collective-permute-start | bytes 2359304 | tf_op jit(solution)/shard_map/ppermute | solution.py:474
  5.6 18.5 %copy-start.6 = (bf16[256,768]{1,0:T(8,128)(2,1)}, bf16[256,768]{1,0:T(8,128)(2,1)S(1)}, u32[]{:S(2)}) copy-start(bf16[256,768]{1,0:T(8,128)(2,1)S(1)} %constant_dynamic-slice_fusion.1.a) | copy-start | bytes 1179652
  5.6 14.3 %collective-permute-start.1 = (bf16[256,768]{1,0:T(8,128)(2,1)S(1)}, bf16[256,768]{1,0:T(8,128)(2,1)S(1)}, u32[]{:S(2)}, u32[]{:S(2)}) collective-permute-start(bf16[256,768]{1,0:T(8,128)(2,1)S(1)} %constant_dynamic-slice_fusion.1.a), channel_id=1, source_target_pairs={{0,32},{32,64},{64,96},{96,0},{1,33},{33,65},{65,97},{97,1},{2,34}... | collective-permute-start | bytes 1179656 | tf_op jit(solution)/shard_map/ppermute | solution.py:462
  7.0 13.0 %collective-permute-start.2 = (bf16[256,768]{1,0:T(8,128)(2,1)S(1)}, bf16[256,768]{1,0:T(8,128)(2,1)S(1)}, u32[]{:S(2)}, u32[]{:S(2)}) collective-permute-start(bf16[256,768]{1,0:T(8,128)(2,1)S(1)} %constant_dynamic-slice_fusion.1.a), channel_id=1, source_target_pairs={{0,96},{32,0},{64,32},{96,64},{1,97},{33,1},{65,33},{97,65},{2,98}... | collective-permute-start | bytes 1179656 | tf_op jit(solution)/shard_map/ppermute | solution.py:462
  20.0 18.4 %copy-start.12 = (bf16[256,768]{1,0:T(8,128)(2,1)}, bf16[256,768]{1,0:T(8,128)(2,1)S(1)}, u32[]{:S(2)}) copy-start(bf16[256,768]{1,0:T(8,128)(2,1)S(1)} %collective-permute-done.1.b) | copy-start | bytes 1179652
  20.0 18.4 %copy-start.13 = (bf16[256,768]{1,0:T(8,128)(2,1)}, bf16[256,768]{1,0:T(8,128)(2,1)S(1)}, u32[]{:S(2)}) copy-start(bf16[256,768]{1,0:T(8,128)(2,1)S(1)} %collective-permute-done.2.d) | copy-start | bytes 1179652
  22.4 4.8 %collective-permute-start.3 = (bf16[512,768]{1,0:T(8,128)(2,1)S(1)}, bf16[512,768]{1,0:T(8,128)(2,1)S(1)}, u32[]{:S(2)}, u32[]{:S(2)}) collective-permute-start(bf16[512,768]{1,0:T(8,128)(2,1)S(1)} %collective-permute-done.a_ref), channel_id=1, source_target_pairs={{0,1},{1,0},{2,3},{3,2},{4,5},{5,4},{6,7},{7,6},{8,9},{9,8},{10,11... | collective-permute-start | bytes 2359304 | tf_op jit(solution)/shard_map/ppermute | solution.py:470
  24.1 25.2 %collective-permute-start.5 = (bf16[256,768]{1,0:T(8,128)(2,1)S(1)}, bf16[256,768]{1,0:T(8,128)(2,1)}, u32[]{:S(2)}, u32[]{:S(2)}) collective-permute-start(bf16[256,768]{1,0:T(8,128)(2,1)S(1)} %constant_dynamic-slice_fusion.1.a), channel_id=1, source_target_pairs={{0,64},{32,96},{64,0},{96,32},{1,65},{33,97},{65,1},{97,33},{2,66}... | collective-permute-start | bytes 1179656 | tf_op jit(solution)/shard_map/ppermute | solution.py:462
  38.4 1.5 collective-permute-start.4
  42.0 15.5 %all-to-all-start = ((f32[16,8,512]{2,1,0:T(8,128)}), f32[16,8,512]{2,1,0:T(8,128)S(1)}, u32[]{:S(2)}, u32[]{:S(2)}) async-start(f32[16,8,512]{2,1,0:T(8,128)} %merge_cores.1), calls=%async_computation | async-start | bytes 524288 | tf_op jit(solution)/shard_map/all_to_all | solution.py:503
  66.3 35.9 %collective-permute-start.7 = (bf16[1024,768]{1,0:T(8,128)(2,1)}, bf16[1024,768]{1,0:T(8,128)(2,1)S(1)}, u32[]{:S(2)}, u32[]{:S(2)}) collective-permute-start(bf16[1024,768]{1,0:T(8,128)(2,1)} %get-tuple-element.55.near_ref), channel_id=1, source_target_pairs={{0,18},{2,16},{16,2},{18,0},{1,19},{3,17},{17,3},{19,1},{4,22},{6,... | collective-permute-start | bytes 4718600 | tf_op jit(solution)/shard_map/ppermute | solution.py:474
  67.2 19.0 %collective-permute-start.6 = (bf16[512,768]{1,0:T(8,128)(2,1)}, bf16[512,768]{1,0:T(8,128)(2,1)S(1)}, u32[]{:S(2)}, u32[]{:S(2)}) collective-permute-start(bf16[512,768]{1,0:T(8,128)(2,1)} %get-tuple-element.51), channel_id=1, source_target_pairs={{0,64},{32,96},{64,0},{96,32},{1,65},{33,97},{65,1},{97,33},{2,66}... | collective-permute-start | bytes 2359304 | tf_op jit(solution)/shard_map/ppermute | solution.py:462
  77.2 29.3 %collective-permute-start.8 = (bf16[512,768]{1,0:T(8,128)(2,1)}, bf16[512,768]{1,0:T(8,128)(2,1)}, u32[]{:S(2)}, u32[]{:S(2)}) collective-permute-start(bf16[512,768]{1,0:T(8,128)(2,1)} %get-tuple-element.59), channel_id=1, source_target_pairs={{0,32},{32,64},{64,96},{96,0},{1,33},{33,65},{65,97},{97,1},{2,34}... | collective-permute-start | bytes 2359304 | tf_op jit(solution)/shard_map/ppermute | solution.py:462
  77.6 28.9 %collective-permute-start.9 = (bf16[512,768]{1,0:T(8,128)(2,1)}, bf16[512,768]{1,0:T(8,128)(2,1)}, u32[]{:S(2)}, u32[]{:S(2)}) collective-permute-start(bf16[512,768]{1,0:T(8,128)(2,1)} %get-tuple-element.60), channel_id=1, source_target_pairs={{0,96},{32,0},{64,32},{96,64},{1,97},{33,1},{65,33},{97,65},{2,98}... | collective-permute-start | bytes 2359304 | tf_op jit(solution)/shard_map/ppermute | solution.py:462
  86.2 6.4 %copy-start.8 = (bf16[512,768]{1,0:T(8,128)(2,1)}, bf16[512,768]{1,0:T(8,128)(2,1)S(1)}, u32[]{:S(2)}) copy-start(bf16[512,768]{1,0:T(8,128)(2,1)S(1)} %collective-permute-done.6.g2) | copy-start | bytes 2359300
  92.6 13.9 %collective-permute-start.10 = (f32[4,512]{1,0:T(4,128)}, f32[4,512]{1,0:T(4,128)S(1)}, u32[]{:S(2)}, u32[]{:S(2)}) collective-permute-start(f32[4,512]{1,0:T(4,128)} %get-tuple-element.56.m0), channel_id=1, source_target_pairs={{0,32},{32,64},{64,96},{96,0},{1,33},{33,65},{65,97},{97,1},{2,34}... | collective-permute-start | bytes 24584 | tf_op jit(solution)/shard_map/ppermute | solution.py:462
  93.0 13.5 %collective-permute-start.11 = (f32[4,512]{1,0:T(4,128)}, f32[4,512]{1,0:T(4,128)S(1)}, u32[]{:S(2)}, u32[]{:S(2)}) collective-permute-start(f32[4,512]{1,0:T(4,128)} %get-tuple-element.56.m0), channel_id=1, source_target_pairs={{0,64},{32,96},{64,0},{96,32},{1,65},{33,97},{65,1},{97,33},{2,66}... | collective-permute-start | bytes 24584 | tf_op jit(solution)/shard_map/ppermute | solution.py:462
  102.2 4.4 %collective-permute-start.12 = (f32[4,512]{1,0:T(4,128)}, f32[4,512]{1,0:T(4,128)S(1)}, u32[]{:S(2)}, u32[]{:S(2)}) collective-permute-start(f32[4,512]{1,0:T(4,128)} %get-tuple-element.56.m0), channel_id=1, source_target_pairs={{0,96},{32,0},{64,32},{96,64},{1,97},{33,1},{65,33},{97,65},{2,98}... | collective-permute-start | bytes 24584 | tf_op jit(solution)/shard_map/ppermute | solution.py:462
  114.3 29.0 %all-to-all-start.1 = ((bf16[8,112,512]{2,1,0:T(8,128)(2,1)}), bf16[8,112,512]{2,1,0:T(8,128)(2,1)S(1)}, u32[]{:S(2)}, u32[]{:S(2)}) async-start(bf16[8,112,512]{2,1,0:T(8,128)(2,1)} %turn_points.1), calls=%async_computation.1 | async-start | bytes 1835008 | tf_op jit(solution)/shard_map/all_to_all | solution.py:522
  117.9 4.6 %collective-permute-start.13 = (bf16[512,768]{1,0:T(8,128)(2,1)S(1)}, bf16[512,768]{1,0:T(8,128)(2,1)S(1)}, u32[]{:S(2)}, u32[]{:S(2)}) collective-permute-start(bf16[512,768]{1,0:T(8,128)(2,1)S(1)} %copy-done.1), channel_id=1, source_target_pairs={{0,1},{1,0},{2,3},{3,2},{4,5},{5,4},{6,7},{7,6},{8,9},{9,8},{10,11... | collective-permute-start | bytes 2359304 | tf_op jit(solution)/shard_map/ppermute | solution.py:470
  133.7 1.4 collective-permute-start.14
  144.2 51.2 %all-to-all-start.2 = ((bf16[64,208,128]{2,1,0:T(8,128)(2,1)}), bf16[64,208,128]{2,1,0:T(8,128)(2,1)}, u32[]{:S(2)}, u32[]{:S(2)}) async-start(bf16[64,208,128]{2,1,0:T(8,128)(2,1)} %sums_two.1), calls=%async_computation.2 | async-start | bytes 6815744 | tf_op jit(solution)/shard_map/all_to_all | solution.py:525
  156.6 59.0 %copy-start.15 = (f32[8,512]{1,0:T(8,128)S(1)}, f32[8,512]{1,0:T(8,128)}, u32[]{:S(2)}) copy-start(f32[8,512]{1,0:T(8,128)} %get-tuple-element.64) | copy-start | bytes 49156
  212.4 4.5 %collective-permute-start.15 = (bf16[8,208,128]{2,1,0:T(8,128)(2,1)S(1)}, bf16[8,208,128]{2,1,0:T(8,128)(2,1)S(1)}, u32[]{:S(2)}, u32[]{:S(2)}) collective-permute-start(bf16[8,208,128]{2,1,0:T(8,128)(2,1)S(1)} %all_to_all.20.a_ref), channel_id=1, source_target_pairs={{0,1},{1,0},{2,3},{3,2},{4,5},{5,4},{6,7},{7,6},{8,9},{9,8},{10,11... | collective-permute-start | bytes 1277960 | tf_op jit(solution)/shard_map/ppermute | solution.py:470
  (15 other events, 29.2 us)

commit v4 on v3

--- a/solution.py
+++ b/solution.py
@@ -219,84 +219,99 @@
     )(idx, stats, local)
 
 
-def sums_one(p, factor, x, masses, blocks, dtype):
-    first, step = blocks[0], blocks[-1] - blocks[0]
-
-    def kernel(p_ref, f_ref, x_ref, old_ref, *refs):
-        mass_ref = refs[-1]
+def sums_far(p, factor, x, half):
+    def kernel(p_ref, f_ref, x_ref, *refs):
         w = (p_ref[...] * f_ref[...]).astype(BF)
-        sums = nn(w, x_ref[...])
-        mass = as_row(lane_sums(w))
-        for q, k in enumerate(blocks):
+        sums = nn(w, x_ref[...]).astype(BF)
+        packed = mass_rows(as_row(lane_sums(w))).astype(BF)
+        for q in range(3):
 
             @pl.when(pl.program_id(0) == q)
-            def _(q=q, k=k):
-                if q == 0:
-                    mass_ref[...] = old_ref[...]
-                refs[q][...] = sums.astype(dtype)
-                mass_ref[k : k + 1, :] = mass
-
-    return pl.pallas_call(
-        kernel,
-        grid=(len(blocks),),
+            def _(q=q):
+                refs[q][0:256, :] = sums
+                refs[q][256:272, 0:256] = packed
+                refs[q][256:272, 256:D] = jnp.zeros((16, D - 256), BF)
+
+    return pl.pallas_call(
+        kernel,
+        grid=(3,),
         in_specs=[
-            pl.BlockSpec((512, 2048), lambda j: (first + step * j, 0)),
+            pl.BlockSpec((256, 2048), lambda j: ((2 - j + 3 * (j // 2)) * 2 + half, 0)),
             pl.BlockSpec((1, 2048), lambda j: (0, 0)),
             pl.BlockSpec((2048, D), lambda j: (0, 0)),
-            pl.BlockSpec((4, 512), lambda j: (0, 0)),
         ],
-        out_specs=[pl.BlockSpec((512, D), lambda j: (0, 0)) for k in blocks]
-        + [pl.BlockSpec((4, 512), lambda j: (0, 0))],
-        out_shape=[shape((512, D), dtype) for k in blocks] + [shape((4, 512), F32)],
-        name="sums_one",
-    )(p, factor, x, masses)
-
-
-def finish_one(idx, own, got, cents, masses, far_masses):
-    def kernel(idx_ref, own_ref, g1, g2, g3, cents_ref, m0, m1, m2, m3, pts_ref, mass_ref):
-        total = m0[...]
-        for k, ref in ((1, m1), (2, m2), (3, m3)):
-            t = ref[...]
-            total = total + jnp.concatenate([t[k:], t[:k]], axis=0)
+        out_specs=[pl.BlockSpec((272, D), lambda j: (0, 0))] * 3,
+        out_shape=[shape((272, D), BF)] * 3,
+        name="sums_far",
+    )(p, factor, x)
+
+
+def sums_own(p, factor, x):
+    def kernel(p_ref, f_ref, x_ref, o_ref, m_ref):
+        w = (p_ref[...] * f_ref[...]).astype(BF)
+        o_ref[...] = nn(w, x_ref[...])
+        m_ref[...] = as_row(lane_sums(w))
+
+    return pl.pallas_call(
+        kernel,
+        grid=(1,),
+        in_specs=[
+            pl.BlockSpec((512, 2048), lambda j: (0, 0)),
+            pl.BlockSpec((1, 2048), lambda j: (0, 0)),
+            pl.BlockSpec((2048, D), lambda j: (0, 0)),
+        ],
+        out_specs=[pl.BlockSpec((512, D), lambda j: (0, 0)), pl.BlockSpec((1, 512), lambda j: (0, 0))],
+        out_shape=[shape((512, D), F32), shape((1, 512), F32)],
+        name="sums_own",
+    )(p, factor, x)
+
+
+def finish_one(idx, own, own_mass, got, cents, half):
+    def kernel(idx_ref, own_ref, m_ref, g1, g2, g3, cents_ref, pts_ref, mass_ref):
+        total = m_ref[...]
+        num = own_ref[...] + PRIOR * cents_ref[...].astype(F32)
+        for g in (g1, g2, g3):
+            extra = g[256:272, 0:256].astype(F32)
+            total = total + (extra[0:1] + extra[1:2] + extra[2:3])
+            num = num + g[0:256, :].astype(F32)
         mass_ref[...] = total
-        i = pl.program_id(0)
-        column = as_column(mass_ref[0:1, pl.ds(pl.multiple_of(i * 256, 256), 256)]) + PRIOR
-        num = own_ref[...] + g1[...].astype(F32) + g2[...].astype(F32) + g3[...].astype(F32)
-        num = num + PRIOR * cents_ref[...].astype(F32)
-        pts_ref[...] = (num / column).astype(BF)
-
-    rows = pl.BlockSpec((256, D), lambda i, s: (i, 0))
-    small = pl.BlockSpec((4, 512), lambda i, s: (0, 0))
+        pts_ref[...] = (num / (as_column(total) + PRIOR)).astype(BF)
+
     return pl.pallas_call(
         kernel,
         grid_spec=pltpu.PrefetchScalarGridSpec(
             num_scalar_prefetch=1,
-            grid=(2,),
-            in_specs=[rows] * 4 + [pl.BlockSpec((256, D), lambda i, s: (s[0] * 2 + i, 0))] + [small] * 4,
-            out_specs=[rows, small],
+            grid=(1,),
+            in_specs=[
+                pl.BlockSpec((256, D), lambda i, s: (half, 0)),
+                pl.BlockSpec((1, 256), lambda i, s: (0, half)),
+            ]
+            + [pl.BlockSpec((272, D), lambda i, s: (0, 0))] * 3
+            + [pl.BlockSpec((256, D), lambda i, s: (s[0] * 2 + half, 0))],
+            out_specs=[pl.BlockSpec((256, D), lambda i, s: (0, 0)), pl.BlockSpec((1, 256), lambda i, s: (0, 0))],
         ),
-        out_shape=[shape((512, D), BF), shape((4, 512), F32)],
+        out_shape=[shape((256, D), BF), shape((1, 256), F32)],
         name="finish_one",
-    )(idx, own, *got, cents, masses, *far_masses)
-
-
-def turn_points(points, totals):
-    def kernel(p_ref, t_ref, o_ref, tall):
-        for at in range(0, D, 128):
-            tall[pl.ds(at, 128), :] = p_ref[:, pl.ds(at, 128)].astype(F32).T.astype(BF)
-        packed = mass_rows(t_ref[0:1, :]).astype(BF)
+    )(idx, own, own_mass, *got, cents)
+
+
+def turn_points(points, masses):
+    def kernel(p0, p1, m0, m1, o_ref, tall):
+        for h, p_ref in enumerate((p0, p1)):
+            for at in range(0, D, 128):
+                tall[pl.ds(at, 128), h * 256 : h * 256 + 256] = p_ref[:, pl.ds(at, 128)].astype(F32).T.astype(BF)
+        packed = mass_rows(jnp.concatenate([m0[...], m1[...]], axis=1)).astype(BF)
         for d in range(8):
             o_ref[d, 0:96, :] = tall[pl.ds(d * 96, 96), :]
             o_ref[d, 96:112, :] = packed
 
     return pl.pallas_call(
         kernel,
-        in_specs=[VMEM] * 2,
+        in_specs=[VMEM] * 4,
         scratch_shapes=[pltpu.VMEM((D, 512), BF)],
         out_shape=shape((8, 112, 512), BF),
-        cost_estimate=pl.CostEstimate(flops=0, transcendentals=0, bytes_accessed=24 << 20),
         name="turn_points",
-    )(points, totals)
+    )(*points, *masses)
 
 
 def gather_one(parts):
@@ -315,40 +330,41 @@
     )(parts)
 
 
-def join_near(blocks):
-    def kernel(a, b, c, d, o_ref, n_ref):
-        for at, ref in zip(range(0, 1024, 256), (a, b, c, d)):
+def join_two(a, b):
+    def kernel(a_ref, b_ref, o_ref, n_ref):
+        for at, ref in ((0, a_ref), (256, b_ref)):
             block = ref[...]
-            o_ref[pl.ds(at, 256), :] = block
-            n_ref[pl.ds(at, 256), :] = jnp.broadcast_to(square_norms(block), (256, 128))
-
-    return pl.pallas_call(
-        kernel,
-        in_specs=[VMEM] * 4,
-        out_shape=[shape((1024, D), BF), shape((1024, 128), F32)],
-        name="join_near",
-    )(*blocks)
-
-
-def norms_far(block):
-    def kernel(c_ref, o_ref):
-        o_ref[...] = jnp.broadcast_to(square_norms(c_ref[...]), (1024, 128))
-
-    return pl.pallas_call(
-        kernel, in_specs=[VMEM], out_shape=shape((1024, 128), F32), name="norms_far"
+            o_ref[at : at + 256, :] = block
+            n_ref[at : at + 256, :] = jnp.broadcast_to(square_norms(block), (256, 128))
+
+    return pl.pallas_call(
+        kernel,
+        in_specs=[VMEM] * 2,
+        out_shape=[shape((512, D), BF), shape((512, 128), F32)],
+        name="join_two",
+    )(a, b)
+
+
+def norms_of(block):
+    def kernel(c_ref, n_ref):
+        n_ref[...] = jnp.broadcast_to(square_norms(c_ref[...]), (512, 128))
+
+    return pl.pallas_call(
+        kernel, in_specs=[VMEM], out_shape=shape((512, 128), F32), name="norms_of"
     )(block)
 
 
-def scores_two(places, a, b, near, far, near_norms, far_norms):
-    def kernel(places_ref, a_ref, b_ref, near_ref, far_ref, nn_ref, fn_ref, p_ref, stat_ref, scores):
+def scores_two(places, own, theirs, two, norms, half, old=()):
+    def kernel(places_ref, a_ref, b_ref, *refs):
+        cents, ns = refs[0:4], refs[4:8]
+        p_ref, stat_ref, scores = refs[-3:]
         i = pl.program_id(0)
-        twice = jnp.where(i < 2, a_ref[...], b_ref[...]) * 2
+        twice = jnp.where(i == 0, a_ref[...], b_ref[...]) * 2
         top = None
         for slot in range(8):
-            c_ref, n_ref = ((near_ref, nn_ref), (far_ref, fn_ref))[slot // 4]
-            here = pl.ds((slot % 4) * 256, 256)
-            n = n_ref[here, :]
-            s = nt(c_ref[here, :], twice) - jnp.concatenate([n, n], axis=1)
+            here = pl.ds((slot % 2) * 256, 256)
+            n = ns[slot // 2][here, :]
+            s = nt(cents[slot // 2][here, :], twice) - jnp.concatenate([n, n], axis=1)
             scores[pl.ds(slot * 256, 256), :] = s
             t = fold_rows(s, jnp.maximum)
             top = t if top is None else jnp.maximum(top, t)
@@ -359,35 +375,39 @@
             p_ref[pl.ds(pl.multiple_of(places_ref[slot] * 256, 256), 256), :] = e
             t = fold_rows(e, jnp.add)
             total = t if total is None else total + t
-        stat_ref[0:1, :] = m
-        stat_ref[1:2, :] = jnp.sum(total, axis=0, keepdims=True)
-
+
+        @pl.when(i == 0)
+        def _():
+            stat_ref[...] = refs[9][...] if old else jnp.zeros_like(stat_ref)
+
+        cols = pl.ds(pl.multiple_of((half * 2 + i) * 256, 256), 256)
+        stat_ref[0:1, cols] = m
+        stat_ref[1:2, cols] = jnp.sum(total, axis=0, keepdims=True)
+
+    whole = lambda r, c: pl.BlockSpec((r, c), lambda i, s: (0, 0))
     return pl.pallas_call(
         kernel,
         grid_spec=pltpu.PrefetchScalarGridSpec(
             num_scalar_prefetch=1,
-            grid=(4,),
-            in_specs=ROW_IN
-            + [pl.BlockSpec((1024, D), lambda i, s: (0, 0))] * 2
-            + [pl.BlockSpec((1024, 128), lambda i, s: (0, 0))] * 2,
-            out_specs=[
-                pl.BlockSpec((2048, 256), lambda i, s: (0, i)),
-                pl.BlockSpec((2, 256), lambda i, s: (0, i)),
-            ],
+            grid=(2,),
+            in_specs=[whole(256, D)] * 2 + [whole(512, D)] * 4 + [whole(512, 128)] * 4
+            + ([ANY, whole(2, 1024)] if old else []),
+            out_specs=[pl.BlockSpec((2048, 256), lambda i, s: (0, half * 2 + i)), whole(2, 1024)],
             scratch_shapes=[pltpu.VMEM((2048, 256), F32)],
         ),
         out_shape=[shape((2048, 1024), F32), shape((2, 1024), F32)],
+        input_output_aliases={11: 0} if old else {},
         name="scores_two",
-    )(places, a, b, near, far, near_norms, far_norms)
-
-
-def sums_two(p, stat, other, a, b):
-    def kernel(p_ref, s_ref, r_ref, a_ref, b_ref, o_ref, rows, factor):
+    )(places, own, theirs, *two, *norms, *old)
+
+
+def sums_two(p, stat, other, points):
+    def kernel(p_ref, s_ref, r_ref, x0, x1, x2, x3, o_ref, rows, factor):
         @pl.when(pl.program_id(0) == 0)
         def _():
-            rows[0:512, :] = a_ref[...]
-            rows[512:1024, :] = b_ref[...]
-            theirs = jnp.concatenate([r_ref[:, 512:1024], r_ref[:, 0:512]], axis=1)
+            for at, ref in zip(range(0, 1024, 256), (x0, x1, x2, x3)):
+                rows[at : at + 256, :] = ref[...]
+            theirs = jnp.concatenate([r_ref[:, at : at + 256] for at in (256, 0, 768, 512)], axis=1)
             mine = s_ref[...]
             m = jnp.maximum(mine[0:1], theirs[0:1])
             near = jnp.exp(mine[0:1] - m)
@@ -408,12 +428,12 @@
     return pl.pallas_call(
         kernel,
         grid=(2,),
-        in_specs=[pl.BlockSpec((1024, 1024), lambda i: (i, 0)), whole(2, 1024), whole(2, 1024), whole(512, D), whole(512, D)],
+        in_specs=[pl.BlockSpec((1024, 1024), lambda i: (i, 0)), whole(2, 1024), whole(2, 1024)] + [whole(256, D)] * 4,
         out_specs=pl.BlockSpec((32, TALL, 128), lambda i: (i, 0, 0)),
         scratch_shapes=[pltpu.VMEM((1024, D), BF), pltpu.VMEM((8, 1024), F32)],
         out_shape=shape((64, TALL, 128), BF),
         name="sums_two",
-    )(p, stat, other, a, b)
+    )(p, stat, other, *points)
 
 
 def finish_two(total, cents):
@@ -495,33 +515,36 @@
     around = [shift_y(half_two, k) for k in (1, 2, 3)]
 
     p, x, near, norms = scores_near(idx, embeddings, cents_one)
-    far_mine = after(far_mine, near, around[0], around[2])
+    near_a, norms_a = join_two(after(half_two, near), around[0])
+    far_mine = after(far_mine, near, norms_a, around[2])
     far_other = flip(far_mine, "c")
+    far_a = flip_x(after(near_a, far_mine))
     p, x, local = scores_far(idx, far_mine, far_other, cents_one, norms, near, p, x)
 
     spread = merge_cores(local, flip(local, "c"))
     stats = lax.all_to_all(spread, ("xh", "z", "xl"), 0, 0, tiled=True)
-    near_two, near_norms = join_near([after(half_two, spread)] + around)
-    factor = merge_last(idx, stats, after(local, near_norms))
-
-    masses = jnp.zeros((4, 512), F32)
-    part, masses = sums_one(p, factor, x, masses, (2,), BF)
-    got = {2: shift_y(part, 2)}
-    part1, part3, masses = sums_one(p, factor, x, masses, (1, 3), BF)
-    got[1], got[3] = shift_y(part1, 1), shift_y(part3, 3)
-    own, masses = sums_one(p, factor, x, after(masses, got[2]), (0,), F32)
-
-    far_two = after(flip_x(after(near_two, part)), masses)
-    far_norms = norms_far(far_two)
-
-    points, totals = finish_one(
-        idx, after(own, far_norms), [got[k] for k in (1, 2, 3)], cents_one, masses, [shift_y(masses, k) for k in (1, 2, 3)]
-    )
-    their_points = flip(points, "c")
-    tall = turn_points(points, totals)
+    near_b, norms_b = join_two(after(around[1], spread), around[2])
+    norms_c = norms_of(after(far_a, spread))
+    factor = merge_last(idx, stats, after(local, norms_b, norms_c))
+
+    parts_0 = sums_far(p, factor, x, 0)
+    got_0 = [shift_y(part, k) for part, k in zip(parts_0, (2, 1, 3))]
+    far_b = flip_x(after(near_b, parts_0[0]))
+    parts_1 = sums_far(p, after(factor, parts_0[0]), x, 1)
+    own, own_mass = sums_own(p, after(factor, parts_1[0]), x)
+    got_1 = [shift_y(parts_1[0], 2)] + [shift_y(after(part, own_mass), k) for part, k in zip(parts_1[1:], (1, 3))]
+    two = (near_a, near_b, far_a, far_b)
+    norms_two = (norms_a, norms_b, norms_c, norms_of(after(far_b, own_mass)))
+
+    points_0, mass_0 = finish_one(idx, own, own_mass, got_0, cents_one, 0)
+    theirs_0 = flip(points_0, "c")
+    old = scores_two(places, points_0, theirs_0, two, norms_two, 0)
+    points_1, mass_1 = finish_one(idx, own, after(own_mass, old[1]), got_1, cents_one, 1)
+    theirs_1 = flip(points_1, "c")
+    tall = turn_points((points_0, points_1), (mass_0, mass_1))
     columns = lax.all_to_all(tall, ("y", "xh"), 0, 0, tiled=True)
-    p2, stat2 = scores_two(places, after(points, tall), their_points, near_two, far_two, near_norms, far_norms)
-    packed = sums_two(p2, stat2, flip(stat2, "c"), points, their_points)
+    p2, stat2 = scores_two(places, after(points_1, tall), theirs_1, two, norms_two, 1, tuple(old))
+    packed = sums_two(p2, stat2, flip(stat2, "c"), (points_0, theirs_0, points_1, theirs_1))
     parts = lax.all_to_all(after(packed, columns), ("y", "xh", "z", "xl"), 0, 0, tiled=True)
     turned_one, mass_one = gather_one(columns)
     total = jnp.sum(parts.astype(F32), axis=0)

time: 221 us -> 215 us (0.973)
  waiting for transfers between devices: 63.7 us -> 51.5 us
  Pallas kernels: 81.3 us -> 91.8 us
  starting transfers between devices: 48 us -> 41.1 us
  local copies, waits for them, and re-layouts: 10.6 us -> 13.5 us
    ppermute x2 -> x3, waiting for transfers between devices: 9.1 us -> 0.01 us  [flip_x(): return lax.ppermute(x, ('xh', 'xl'), [(0, 3), (1, 2), (2, 1), (3, 0)])]
    pallas_call x1 -> x2, Pallas kernels: 10.3 us -> 14.8 us  [scores_two(): pl.pallas_call(kernel, grid_spec=pltpu.PrefetchScalarGridSpec(num_scalar_...]
    ppermute x9, starting transfers between devices: 15.2 us -> 10.9 us  [shift_y(): return lax.ppermute(x, 'y', [(i, (i + k) % 4) for i in range(4)])]
    unnamed x41 -> x43, local copies, waits for them, and re-layouts: 7.19 us -> 10.7 us
    pallas_call x6 -> x8, Pallas kernels: 28.4 us -> 31.7 us  [the longest x2 14.7 us: sums_far(): pl.pallas_call(kernel, grid=(3,), in_specs=[pl.BlockSpec((256, 2048), lam...]
    pallas_call x1 -> x2, Pallas kernels: 4.16 us -> 6.8 us  [finish_one(): pl.pallas_call(kernel, grid_spec=pltpu.PrefetchScalarGridSpec(num_scalar_...]
    all_to_all x1, waiting for transfers between devices: 5.22 us -> 3 us  [body(): stats = lax.all_to_all(spread, ('xh', 'z', 'xl'), 0, 0, tiled=True)]
    ppermute x2 -> x3, starting transfers between devices: 4.27 us -> 5.94 us  [flip_x(): return lax.ppermute(x, ('xh', 'xl'), [(0, 3), (1, 2), (2, 1), (3, 0)])]
  transfers between devices with their start and end apart: 19 -> 21, of which waited for: 9 -> 7; matrix products, arithmetic and copies ran while one was open for 1% -> 1% of each run, Pallas kernels for 29% -> 34%
where the time goes in v4:
time: 215 us; the launch traced here: 214 us
  Pallas kernels  91.8 us (43%)
  waiting for transfers between devices  51.5 us (24%)
  starting transfers between devices  41.1 us (19%)
  local copies, waits for them, and re-layouts  13.5 us (6%)
  blocking collectives  12 us (6%)
  other arithmetic  3.66 us (2%)
    all_to_all x1, waiting for transfers between devices, body(): lax.all_to_all(after(packed, columns), ('y', 'xh', 'z', 'xl'), 0, 0, tile...  38.8 us
    pallas_call x2, Pallas kernels, scores_two(): pl.pallas_call(kernel, grid_spec=pltpu.PrefetchScalarGridSpec(num_scalar_...  14.8 us
    pallas_call x2, Pallas kernels, sums_far(): pl.pallas_call(kernel, grid=(3,), in_specs=[pl.BlockSpec((256, 2048), lam...  14.7 us
    all_to_all x1, blocking collectives, body(): block = lax.all_to_all(spread, ('z', 'xl'), 0, 0, tiled=True)  12 us
    pallas_call x1, Pallas kernels, scores_near(): pl.pallas_call(scores_near_kernel, grid_spec=pltpu.PrefetchScalarGridSpec...  10.9 us
    ppermute x9, starting transfers between devices, shift_y(): return lax.ppermute(x, 'y', [(i, (i + k) % 4) for i in range(4)])  10.9 us
    unnamed x43, local copies, waits for them, and re-layouts  10.7 us
    pallas_call x1, Pallas kernels, scores_far(): pl.pallas_call(scores_far_kernel, grid_spec=pltpu.PrefetchScalarGridSpec(...  10.2 us
  transfers between devices with their start and end apart: 21, of which 7 were waited for; matrix products, arithmetic and copies ran while one was open for 1% of the time, Pallas kernels for 34%

profile of v4, /device:TPU:1, one launch (start us, length us, event | category | flops | bytes accessed | tf_op | source)
XLA Modules:
  0.0 214.4 jit_solution(403806718435448266)
XLA Ops:
  2.2 3.4 %collective-permute-start = (bf16[512,768]{1,0:T(8,128)(2,1)S(1)}, bf16[512,768]{1,0:T(8,128)(2,1)S(1)}, u32[]{:S(2)}, u32[]{:S(2)}) collective-permute-start(bf16[512,768]{1,0:T(8,128)(2,1)S(1)} %dynamic-slice_convert_fusion), channel_id=1, source_target_pairs={{0,18},{2,16},{16,2},{18,0},{1,19},{3,17},{17,3},{19,1},{4,22},{6,... | collective-permute-start | bytes 2359304 | tf_op jit(solution)/shard_map/ppermute | solution.py:494
  9.1 10.9 %scores_near.1 = (f32[2048,2048]{1,0:T(8,128)}, bf16[2048,768]{1,0:T(8,128)(2,1)}, f32[8,512]{1,0:T(8,128)}, f32[2048,128]{1,0:T(8,128)}) custom-call(s32[10]{0:T(128)} %concatenate.3.idx.idx_ref, f32[1024,768]{1,0:T(8,128)} %e_ref.1, bf16[4096,768]{1,0:T(8,128)(2,1)} %cents_ref.3, bf16[4096,768]{1,0:T(8,128)(2,1)} %cents_ref.3, ...), custom_call_target="tpu_custom_call" | custom-call | flops 3221225472 | bytes 25165824 | tf_op jit(solution)/shard_map/scores_near/pallas_call | solution.py:136
  26.8 2.9 %collective-permute-start.5 = (bf16[256,768]{1,0:T(8,128)(2,1)}, bf16[256,768]{1,0:T(8,128)(2,1)}, u32[]{:S(2)}, u32[]{:S(2)}) collective-permute-start(bf16[256,768]{1,0:T(8,128)(2,1)} %copy-done.9), channel_id=1, source_target_pairs={{0,64},{32,96},{64,0},{96,32},{1,65},{33,97},{65,1},{97,33},{2,66}... | collective-permute-start | bytes 1179656 | tf_op jit(solution)/shard_map/ppermute | solution.py:482
  30.6 10.2 %scores_far.1 = (f32[2048,2048]{1,0:T(8,128)}, bf16[2048,768]{1,0:T(8,128)(2,1)}, f32[8,512]{1,0:T(8,128)}) custom-call(s32[10]{0:T(128)} %concatenate.3.idx.idx_ref, bf16[512,768]{1,0:T(8,128)(2,1)} %copy-done.11, bf16[512,768]{1,0:T(8,128)(2,1)} %copy-done.12, bf16[4096,768]{1,0:T(8,128)(2,1)} %cents_ref.3, ...), custom_call_target="tpu_custom_call", output_to_operand_aliasing={{0}: (9, {}), {1}: (10, {})} | custom-call | tf_op jit(solution)/shard_map/scores_far/pallas_call | solution.py:164
  44.7 5.1 %all-to-all-start = ((f32[16,8,512]{2,1,0:T(8,128)}), f32[16,8,512]{2,1,0:T(8,128)S(1)}, u32[]{:S(2)}, u32[]{:S(2)}) async-start(f32[16,8,512]{2,1,0:T(8,128)} %merge_cores.1), calls=%async_computation | async-start | bytes 524288 | tf_op jit(solution)/shard_map/all_to_all | solution.py:525
  55.0 3.0 %all-to-all-done.s_ref = f32[16,8,512]{2,1,0:T(8,128)S(1)} async-done(((f32[16,8,512]{2,1,0:T(8,128)}), f32[16,8,512]{2,1,0:T(8,128)S(1)}, u32[]{:S(2)}, u32[]{:S(2)}) %all-to-all-start) | async-done | bytes 262176 | tf_op jit(solution)/shard_map/all_to_all | solution.py:525
  60.3 7.5 %sums_far.2 = (bf16[272,768]{1,0:T(8,128)(2,1)}, bf16[272,768]{1,0:T(8,128)(2,1)}, bf16[272,768]{1,0:T(8,128)(2,1)}) custom-call(f32[2048,2048]{1,0:T(8,128)} %get-tuple-element.58.p_ref, f32[1,2048]{1,0:T(1,128)} %merge_last.1.f_ref, bf16[2048,768]{1,0:T(8,128)(2,1)} %get-tuple-element.66.x_ref), custom_call_target="tpu_custom_call" | custom-call | tf_op jit(solution)/shard_map/sums_far/pallas_call | solution.py:235
  72.7 7.3 %sums_far.3 = (bf16[272,768]{1,0:T(8,128)(2,1)}, bf16[272,768]{1,0:T(8,128)(2,1)}, bf16[272,768]{1,0:T(8,128)(2,1)}) custom-call(f32[2048,2048]{1,0:T(8,128)} %get-tuple-element.58.p_ref, f32[1,2048]{1,0:T(1,128)} %merge_last.1.f_ref, bf16[2048,768]{1,0:T(8,128)(2,1)} %get-tuple-element.66.x_ref), custom_call_target="tpu_custom_call" | custom-call | tf_op jit(solution)/shard_map/sums_far/pallas_call | solution.py:235
  80.4 6.1 %sums_own.1 = (f32[512,768]{1,0:T(8,128)}, f32[1,512]{1,0:T(1,128)}) custom-call(f32[2048,2048]{1,0:T(8,128)} %get-tuple-element.58.p_ref, f32[1,2048]{1,0:T(1,128)} %merge_last.1.f_ref, bf16[2048,768]{1,0:T(8,128)(2,1)} %get-tuple-element.66.x_ref), custom_call_target="tpu_custom_call" | custom-call | tf_op jit(solution)/shard_map/sums_own/pallas_call | solution.py:255
  87.2 4.8 %collective-permute-done.8.g2 = bf16[272,768]{1,0:T(8,128)(2,1)} collective-permute-done((bf16[272,768]{1,0:T(8,128)(2,1)}, bf16[272,768]{1,0:T(8,128)(2,1)}, u32[]{:S(2)}, u32[]{:S(2)}) %collective-permute-start.8) | collective-permute-done | bytes 417824 | tf_op jit(solution)/shard_map/ppermute | solution.py:482
  92.0 3.4 %finish_one.2 = (bf16[256,768]{1,0:T(8,128)(2,1)}, f32[1,256]{1,0:T(1,128)}) custom-call(s32[10]{0:T(128)} %concatenate.3.idx.idx_ref, f32[512,768]{1,0:T(8,128)} %get-tuple-element.71.own_ref, f32[1,512]{1,0:T(1,128)} %get-tuple-element.80.m_ref, bf16[272,768]{1,0:T(8,128)(2,1)} %copy-done.15, bf16[272,768]{1,0:T(8,128)(2,1)} %collective-permute-done.8.g2, ...), custom_call_target="tpu_custom_call" | custom-call | tf_op jit(solution)/shard_map/finish_one/pallas_call | solution.py:280
  100.9 7.4 %scores_two.2 = (f32[2048,1024]{1,0:T(8,128)}, f32[2,1024]{1,0:T(2,128)}) custom-call(s32[8]{0:T(128)} %fusion.1.places_ref, bf16[256,768]{1,0:T(8,128)(2,1)} %get-tuple-element.75.a_ref.p0.x0, bf16[256,768]{1,0:T(8,128)(2,1)} %copy-done.8, bf16[512,768]{1,0:T(8,128)(2,1)} %get-tuple-element.63.refs_0_, bf16[512,768]{1,0:T(8,128)(2,1)} %get-tuple-element.77.refs_1_, ...), custom_call_target="tpu_custom_call" | custom-call | tf_op jit(solution)/shard_map/scores_two/pallas_call | solution.py:388
  109.1 3.4 %finish_one.3 = (bf16[256,768]{1,0:T(8,128)(2,1)}, f32[1,256]{1,0:T(1,128)}) custom-call(s32[10]{0:T(128)} %concatenate.3.idx.idx_ref, f32[512,768]{1,0:T(8,128)} %get-tuple-element.71.own_ref, f32[1,512]{1,0:T(1,128)} %get-tuple-element.80.m_ref, bf16[272,768]{1,0:T(8,128)(2,1)} %copy-done.14, bf16[272,768]{1,0:T(8,128)(2,1)} %collective-permute-done.13.g2, ...), custom_call_target="tpu_custom_call" | custom-call | tf_op jit(solution)/shard_map/finish_one/pallas_call | solution.py:280
  112.5 2.4 %turn_points.1 = bf16[8,112,512]{2,1,0:T(8,128)(2,1)} custom-call(bf16[256,768]{1,0:T(8,128)(2,1)} %get-tuple-element.75.a_ref.p0.x0, bf16[256,768]{1,0:T(8,128)(2,1)} %get-tuple-element.90.p1.a_ref.x2, f32[1,256]{1,0:T(1,128)} %get-tuple-element.86.m0, f32[1,256]{1,0:T(1,128)} %get-tuple-element.87.m1), custom_call_target="tpu_custom_call" | custom-call | tf_op jit(solution)/shard_map/turn_points/pallas_call | solution.py:308
  114.9 3.6 %all-to-all-start.1 = ((bf16[8,112,512]{2,1,0:T(8,128)(2,1)}), bf16[8,112,512]{2,1,0:T(8,128)(2,1)S(1)}, u32[]{:S(2)}, u32[]{:S(2)}) async-start(bf16[8,112,512]{2,1,0:T(8,128)(2,1)} %turn_points.1), calls=%async_computation.1 | async-start | bytes 1835008 | tf_op jit(solution)/shard_map/all_to_all | solution.py:545
  121.0 7.3 %scores_two.3 = (f32[2048,1024]{1,0:T(8,128)}, f32[2,1024]{1,0:T(2,128)}) custom-call(s32[8]{0:T(128)} %fusion.1.places_ref, bf16[256,768]{1,0:T(8,128)(2,1)} %get-tuple-element.90.p1.a_ref.x2, bf16[256,768]{1,0:T(8,128)(2,1)} %copy-done.7, bf16[512,768]{1,0:T(8,128)(2,1)} %get-tuple-element.63.refs_0_, ...), custom_call_target="tpu_custom_call", output_to_operand_aliasing={{0}: (11, {})} | custom-call | tf_op jit(solution)/shard_map/scores_two/pallas_call | solution.py:388
  130.3 7.6 %sums_two.1 = bf16[64,208,128]{2,1,0:T(8,128)(2,1)} custom-call(f32[2048,1024]{1,0:T(8,128)} %get-tuple-element.92.p_ref, f32[2,1024]{1,0:T(2,128)} %get-tuple-element.93.s_ref, f32[2,1024]{1,0:T(2,128)} %copy-done.20, bf16[256,768]{1,0:T(8,128)(2,1)} %get-tuple-element.75.a_ref.p0.x0, bf16[256,768]{1,0:T(8,128)(2,1)} %copy-done.8, ...), custom_call_target="tpu_custom_call" | custom-call | tf_op jit(solution)/shard_map/sums_two/pallas_call | solution.py:428
  138.9 8.9 %all-to-all-start.2 = ((bf16[64,208,128]{2,1,0:T(8,128)(2,1)}), bf16[64,208,128]{2,1,0:T(8,128)(2,1)}, u32[]{:S(2)}, u32[]{:S(2)}) async-start(bf16[64,208,128]{2,1,0:T(8,128)(2,1)} %sums_two.1), calls=%async_computation.2 | async-start | bytes 6815744 | tf_op jit(solution)/shard_map/all_to_all | solution.py:548
  148.4 2.4 %gather_one.1 = (f32[96,4096]{1,0:T(8,128)}, f32[8,512]{1,0:T(8,128)}) custom-call(bf16[8,112,512]{2,1,0:T(8,128)(2,1)} %copy-done.3), custom_call_target="tpu_custom_call" | custom-call | tf_op jit(solution)/shard_map/gather_one/pallas_call | solution.py:325
  150.8 38.8 %all-to-all-done.2 = bf16[64,208,128]{2,1,0:T(8,128)(2,1)} async-done(((bf16[64,208,128]{2,1,0:T(8,128)(2,1)}), bf16[64,208,128]{2,1,0:T(8,128)(2,1)}, u32[]{:S(2)}, u32[]{:S(2)}) %all-to-all-start.2) | async-done | bytes 3407904 | tf_op jit(solution)/shard_map/all_to_all | solution.py:548
  189.7 3.1 %convert_reduce_fusion.x_ref = f32[208,128]{1,0:T(8,128)} fusion(bf16[64,208,128]{2,1,0:T(8,128)(2,1)} %all-to-all-done.2), kind=kLoop, calls=%fused_computation | loop fusion | flops 3381248 | bytes 3514368 | tf_op jit(solution)/shard_map/reduce_sum | solution.py:550
  194.6 12.0 %all_to_all.20.a_ref = bf16[8,208,128]{2,1,0:T(8,128)(2,1)S(1)} all-to-all(bf16[8,208,128]{2,1,0:T(8,128)(2,1)} %finish_two.1), channel_id=1, replica_groups=mesh['y'=4,'xh'=2,'z'=4,'xl'=2,'c'=2] {'z','xl'}, dimensions={0} | all-to-all | bytes 851968 | tf_op jit(solution)/shard_map/all_to_all | solution.py:553
  206.6 3.1 %collective-permute-start.17 = (bf16[8,208,128]{2,1,0:T(8,128)(2,1)S(1)}, bf16[8,208,128]{2,1,0:T(8,128)(2,1)S(1)}, u32[]{:S(2)}, u32[]{:S(2)}) collective-permute-start(bf16[8,208,128]{2,1,0:T(8,128)(2,1)S(1)} %all_to_all.20.a_ref), channel_id=1, source_target_pairs={{0,1},{1,0},{2,3},{3,2},{4,5},{5,4},{6,7},{7,6},{8,9},{9,8},{10,11... | collective-permute-start | bytes 1277960 | tf_op jit(solution)/shard_map/ppermute | solution.py:490
  212.0 2.4 %gather_two.1 = (f32[512,768]{1,0:T(8,128)}, f32[1,512]{1,0:T(1,128)}) custom-call(s32[1]{0:T(128)} %bitcast.4.core_ref, bf16[8,208,128]{2,1,0:T(8,128)(2,1)} %copy-done.6, bf16[8,208,128]{2,1,0:T(8,128)(2,1)} %copy-done.13), custom_call_target="tpu_custom_call" | custom-call | tf_op jit(solution)/shard_map/gather_two/pallas_call | solution.py:473
  (89 shorter events, 46.4 us)
Async XLA Ops:
  2.2 20.8 %collective-permute-start = (bf16[512,768]{1,0:T(8,128)(2,1)S(1)}, bf16[512,768]{1,0:T(8,128)(2,1)S(1)}, u32[]{:S(2)}, u32[]{:S(2)}) collective-permute-start(bf16[512,768]{1,0:T(8,128)(2,1)S(1)} %dynamic-slice_convert_fusion), channel_id=1, source_target_pairs={{0,18},{2,16},{16,2},{18,0},{1,19},{3,17},{17,3},{19,1},{4,22},{6,... | collective-permute-start | bytes 2359304 | tf_op jit(solution)/shard_map/ppermute | solution.py:494
  5.6 14.4 %copy-start.9 = (bf16[256,768]{1,0:T(8,128)(2,1)}, bf16[256,768]{1,0:T(8,128)(2,1)S(1)}, u32[]{:S(2)}) copy-start(bf16[256,768]{1,0:T(8,128)(2,1)S(1)} %constant_dynamic-slice_fusion.1.a_ref) | copy-start | bytes 1179652
  5.6 14.4 %collective-permute-start.1 = (bf16[256,768]{1,0:T(8,128)(2,1)S(1)}, bf16[256,768]{1,0:T(8,128)(2,1)S(1)}, u32[]{:S(2)}, u32[]{:S(2)}) collective-permute-start(bf16[256,768]{1,0:T(8,128)(2,1)S(1)} %constant_dynamic-slice_fusion.1.a_ref), channel_id=1, source_target_pairs={{0,32},{32,64},{64,96},{96,0},{1,33},{33,65},{65,97},{97,1},{2,34}... | collective-permute-start | bytes 1179656 | tf_op jit(solution)/shard_map/ppermute | solution.py:482
  7.0 16.0 %collective-permute-start.2 = (bf16[256,768]{1,0:T(8,128)(2,1)S(1)}, bf16[256,768]{1,0:T(8,128)(2,1)S(1)}, u32[]{:S(2)}, u32[]{:S(2)}) collective-permute-start(bf16[256,768]{1,0:T(8,128)(2,1)S(1)} %constant_dynamic-slice_fusion.1.a_ref), channel_id=1, source_target_pairs={{0,96},{32,0},{64,32},{96,64},{1,97},{33,1},{65,33},{97,65},{2,98}... | collective-permute-start | bytes 1179656 | tf_op jit(solution)/shard_map/ppermute | solution.py:482
  23.8 6.0 %collective-permute-start.3 = (bf16[512,768]{1,0:T(8,128)(2,1)S(1)}, bf16[512,768]{1,0:T(8,128)(2,1)S(1)}, u32[]{:S(2)}, u32[]{:S(2)}) collective-permute-start(bf16[512,768]{1,0:T(8,128)(2,1)S(1)} %collective-permute-done.a_ref), channel_id=1, source_target_pairs={{0,1},{1,0},{2,3},{3,2},{4,5},{5,4},{6,7},{7,6},{8,9},{9,8},{10,11... | collective-permute-start | bytes 2359304 | tf_op jit(solution)/shard_map/ppermute | solution.py:490
  25.1 24.7 %collective-permute-start.6 = (bf16[512,768]{1,0:T(8,128)(2,1)}, bf16[512,768]{1,0:T(8,128)(2,1)S(1)}, u32[]{:S(2)}, u32[]{:S(2)}) collective-permute-start(bf16[512,768]{1,0:T(8,128)(2,1)} %get-tuple-element.63.refs_0_), channel_id=1, source_target_pairs={{0,18},{2,16},{16,2},{18,0},{1,19},{3,17},{17,3},{19,1},{4,22},{6,... | collective-permute-start | bytes 2359304 | tf_op jit(solution)/shard_map/ppermute | solution.py:494
  26.8 23.0 %collective-permute-start.5 = (bf16[256,768]{1,0:T(8,128)(2,1)}, bf16[256,768]{1,0:T(8,128)(2,1)}, u32[]{:S(2)}, u32[]{:S(2)}) collective-permute-start(bf16[256,768]{1,0:T(8,128)(2,1)} %copy-done.9), channel_id=1, source_target_pairs={{0,64},{32,96},{64,0},{96,32},{1,65},{33,97},{65,1},{97,33},{2,66}... | collective-permute-start | bytes 1179656 | tf_op jit(solution)/shard_map/ppermute | solution.py:482
  40.9 1.7 collective-permute-start.4
  44.7 13.3 %all-to-all-start = ((f32[16,8,512]{2,1,0:T(8,128)}), f32[16,8,512]{2,1,0:T(8,128)S(1)}, u32[]{:S(2)}, u32[]{:S(2)}) async-start(f32[16,8,512]{2,1,0:T(8,128)} %merge_cores.1), calls=%async_computation | async-start | bytes 524288 | tf_op jit(solution)/shard_map/all_to_all | solution.py:525
  60.3 11.5 %copy-start.5 = (bf16[512,768]{1,0:T(8,128)(2,1)S(1)}, bf16[512,768]{1,0:T(8,128)(2,1)}, u32[]{:S(2)}) copy-start(bf16[512,768]{1,0:T(8,128)(2,1)} %get-tuple-element.77.refs_1_) | copy-start | bytes 2359300
  67.8 18.8 %collective-permute-start.7 = (bf16[272,768]{1,0:T(8,128)(2,1)}, bf16[272,768]{1,0:T(8,128)(2,1)S(1)}, u32[]{:S(2)}, u32[]{:S(2)}) collective-permute-start(bf16[272,768]{1,0:T(8,128)(2,1)} %get-tuple-element.67), channel_id=1, source_target_pairs={{0,64},{32,96},{64,0},{96,32},{1,65},{33,97},{65,1},{97,33},{2,66}... | collective-permute-start | bytes 1253384 | tf_op jit(solution)/shard_map/ppermute | solution.py:482
  69.1 22.9 %collective-permute-start.8 = (bf16[272,768]{1,0:T(8,128)(2,1)}, bf16[272,768]{1,0:T(8,128)(2,1)}, u32[]{:S(2)}, u32[]{:S(2)}) collective-permute-start(bf16[272,768]{1,0:T(8,128)(2,1)} %get-tuple-element.73), channel_id=1, source_target_pairs={{0,32},{32,64},{64,96},{96,0},{1,33},{33,65},{65,97},{97,1},{2,34}... | collective-permute-start | bytes 1253384 | tf_op jit(solution)/shard_map/ppermute | solution.py:482
  69.5 22.5 %collective-permute-start.9 = (bf16[272,768]{1,0:T(8,128)(2,1)}, bf16[272,768]{1,0:T(8,128)(2,1)}, u32[]{:S(2)}, u32[]{:S(2)}) collective-permute-start(bf16[272,768]{1,0:T(8,128)(2,1)} %get-tuple-element.74), channel_id=1, source_target_pairs={{0,96},{32,0},{64,32},{96,64},{1,97},{33,1},{65,33},{97,65},{2,98}... | collective-permute-start | bytes 1253384 | tf_op jit(solution)/shard_map/ppermute | solution.py:482
  71.8 25.4 %collective-permute-start.11 = (bf16[512,768]{1,0:T(8,128)(2,1)S(1)}, bf16[512,768]{1,0:T(8,128)(2,1)S(1)}, u32[]{:S(2)}, u32[]{:S(2)}) collective-permute-start(bf16[512,768]{1,0:T(8,128)(2,1)S(1)} %copy-done.5), channel_id=1, source_target_pairs={{0,18},{2,16},{16,2},{18,0},{1,19},{3,17},{17,3},{19,1},{4,22},{6,... | collective-permute-start | bytes 2359304 | tf_op jit(solution)/shard_map/ppermute | solution.py:494
  80.0 28.4 %collective-permute-start.12 = (bf16[272,768]{1,0:T(8,128)(2,1)}, bf16[272,768]{1,0:T(8,128)(2,1)S(1)}, u32[]{:S(2)}, u32[]{:S(2)}) collective-permute-start(bf16[272,768]{1,0:T(8,128)(2,1)} %get-tuple-element.69), channel_id=1, source_target_pairs={{0,64},{32,96},{64,0},{96,32},{1,65},{33,97},{65,1},{97,33},{2,66}... | collective-permute-start | bytes 1253384 | tf_op jit(solution)/shard_map/ppermute | solution.py:482
  86.5 21.8 %collective-permute-start.13 = (bf16[272,768]{1,0:T(8,128)(2,1)}, bf16[272,768]{1,0:T(8,128)(2,1)}, u32[]{:S(2)}, u32[]{:S(2)}) collective-permute-start(bf16[272,768]{1,0:T(8,128)(2,1)} %get-tuple-element.82), channel_id=1, source_target_pairs={{0,32},{32,64},{64,96},{96,0},{1,33},{33,65},{65,97},{97,1},{2,34}... | collective-permute-start | bytes 1253384 | tf_op jit(solution)/shard_map/ppermute | solution.py:482
  92.0 16.4 %collective-permute-start.14 = (bf16[272,768]{1,0:T(8,128)(2,1)}, bf16[272,768]{1,0:T(8,128)(2,1)}, u32[]{:S(2)}, u32[]{:S(2)}) collective-permute-start(bf16[272,768]{1,0:T(8,128)(2,1)} %get-tuple-element.84), channel_id=1, source_target_pairs={{0,96},{32,0},{64,32},{96,64},{1,97},{33,1},{65,33},{97,65},{2,98}... | collective-permute-start | bytes 1253384 | tf_op jit(solution)/shard_map/ppermute | solution.py:482
  95.4 4.7 %collective-permute-start.10 = (bf16[256,768]{1,0:T(8,128)(2,1)}, bf16[256,768]{1,0:T(8,128)(2,1)S(1)}, u32[]{:S(2)}, u32[]{:S(2)}) collective-permute-start(bf16[256,768]{1,0:T(8,128)(2,1)} %get-tuple-element.75.a_ref.p0.x0), channel_id=1, source_target_pairs={{0,1},{1,0},{2,3},{3,2},{4,5},{5,4},{6,7},{7,6},{8,9},{9,8},{10,11... | collective-permute-start | bytes 1179656 | tf_op jit(solution)/shard_map/ppermute | solution.py:490
  114.9 23.1 %all-to-all-start.1 = ((bf16[8,112,512]{2,1,0:T(8,128)(2,1)}), bf16[8,112,512]{2,1,0:T(8,128)(2,1)S(1)}, u32[]{:S(2)}, u32[]{:S(2)}) async-start(bf16[8,112,512]{2,1,0:T(8,128)(2,1)} %turn_points.1), calls=%async_computation.1 | async-start | bytes 1835008 | tf_op jit(solution)/shard_map/all_to_all | solution.py:545
  118.5 1.8 collective-permute-start.15
  128.4 1.4 collective-permute-start.16
  138.9 50.8 %all-to-all-start.2 = ((bf16[64,208,128]{2,1,0:T(8,128)(2,1)}), bf16[64,208,128]{2,1,0:T(8,128)(2,1)}, u32[]{:S(2)}, u32[]{:S(2)}) async-start(bf16[64,208,128]{2,1,0:T(8,128)(2,1)} %sums_two.1), calls=%async_computation.2 | async-start | bytes 6815744 | tf_op jit(solution)/shard_map/all_to_all | solution.py:548
  150.8 59.0 %copy-start.19 = (f32[8,512]{1,0:T(8,128)S(1)}, f32[8,512]{1,0:T(8,128)}, u32[]{:S(2)}) copy-start(f32[8,512]{1,0:T(8,128)} %get-tuple-element.89) | copy-start | bytes 49156
  206.6 4.5 %collective-permute-start.17 = (bf16[8,208,128]{2,1,0:T(8,128)(2,1)S(1)}, bf16[8,208,128]{2,1,0:T(8,128)(2,1)S(1)}, u32[]{:S(2)}, u32[]{:S(2)}) collective-permute-start(bf16[8,208,128]{2,1,0:T(8,128)(2,1)S(1)} %all_to_all.20.a_ref), channel_id=1, source_target_pairs={{0,1},{1,0},{2,3},{3,2},{4,5},{5,4},{6,7},{7,6},{8,9},{9,8},{10,11... | collective-permute-start | bytes 1277960 | tf_op jit(solution)/shard_map/ppermute | solution.py:490
  (18 other events, 37.0 us)

commit v5 on v4

--- a/solution.py
+++ b/solution.py
@@ -246,23 +246,40 @@
     )(p, factor, x)
 
 
-def sums_own(p, factor, x):
-    def kernel(p_ref, f_ref, x_ref, o_ref, m_ref):
+def sums_rest(p, factor, x):
+    def kernel(p_ref, f_ref, x_ref, g2, g1, g3, own_ref, m_ref):
         w = (p_ref[...] * f_ref[...]).astype(BF)
-        o_ref[...] = nn(w, x_ref[...])
-        m_ref[...] = as_row(lane_sums(w))
-
-    return pl.pallas_call(
-        kernel,
-        grid=(1,),
+        sums = nn(w, x_ref[...])
+        mass = as_row(lane_sums(w))
+        j = pl.program_id(0)
+        for q, ref in enumerate((g2, g1, g3)):
+
+            @pl.when(j == q)
+            def _(ref=ref):
+                ref[0:256, :] = sums.astype(BF)
+                ref[256:272, 0:256] = mass_rows(mass).astype(BF)
+                ref[256:272, 256:D] = jnp.zeros((16, D - 256), BF)
+
+        @pl.when(j >= 3)
+        def _():
+            own_ref[...] = sums
+            m_ref[...] = mass
+
+    return pl.pallas_call(
+        kernel,
+        grid=(5,),
         in_specs=[
-            pl.BlockSpec((512, 2048), lambda j: (0, 0)),
+            pl.BlockSpec((256, 2048), lambda j: (jnp.where(j < 3, (2 - j + 3 * (j // 2)) * 2 + 1, j - 3), 0)),
             pl.BlockSpec((1, 2048), lambda j: (0, 0)),
             pl.BlockSpec((2048, D), lambda j: (0, 0)),
         ],
-        out_specs=[pl.BlockSpec((512, D), lambda j: (0, 0)), pl.BlockSpec((1, 512), lambda j: (0, 0))],
-        out_shape=[shape((512, D), F32), shape((1, 512), F32)],
-        name="sums_own",
+        out_specs=[pl.BlockSpec((272, D), lambda j: (0, 0))] * 3
+        + [
+            pl.BlockSpec((256, D), lambda j: (jnp.maximum(j - 3, 0), 0)),
+            pl.BlockSpec((1, 256), lambda j: (0, jnp.maximum(j - 3, 0))),
+        ],
+        out_shape=[shape((272, D), BF)] * 3 + [shape((512, D), F32), shape((1, 512), F32)],
+        name="sums_rest",
     )(p, factor, x)
 
 
@@ -295,39 +312,41 @@
     )(idx, own, own_mass, *got, cents)
 
 
-def turn_points(points, masses):
-    def kernel(p0, p1, m0, m1, o_ref, tall):
+def turn_points(owners, points, masses):
+    def kernel(owners_ref, p0, p1, m0, m1, *refs):
+        tall = refs[8]
         for h, p_ref in enumerate((p0, p1)):
             for at in range(0, D, 128):
                 tall[pl.ds(at, 128), h * 256 : h * 256 + 256] = p_ref[:, pl.ds(at, 128)].astype(F32).T.astype(BF)
         packed = mass_rows(jnp.concatenate([m0[...], m1[...]], axis=1)).astype(BF)
-        for d in range(8):
-            o_ref[d, 0:96, :] = tall[pl.ds(d * 96, 96), :]
-            o_ref[d, 96:112, :] = packed
-
-    return pl.pallas_call(
-        kernel,
-        in_specs=[VMEM] * 4,
+        for r in range(8):
+            refs[r][0:96, :] = tall[pl.ds(pl.multiple_of(owners_ref[r] * 96, 32), 96), :]
+            refs[r][96:112, :] = packed
+
+    return pl.pallas_call(
+        kernel,
+        in_specs=[SMEM] + [VMEM] * 4,
         scratch_shapes=[pltpu.VMEM((D, 512), BF)],
-        out_shape=shape((8, 112, 512), BF),
+        out_shape=[shape((112, 512), BF)] * 8,
         name="turn_points",
-    )(*points, *masses)
-
-
-def gather_one(parts):
-    def kernel(x_ref, o_ref, m_ref):
-        for s in range(8):
-            block = (s % 2) * 4 + s // 2
-            o_ref[:, block * 512 : block * 512 + 512] = x_ref[s, 0:96, :].astype(F32)
-            t = x_ref[s, 96:112, :].astype(F32)
-            m_ref[block : block + 1, :] = t[0:1] + t[1:2] + t[2:3]
-
-    return pl.pallas_call(
-        kernel,
-        in_specs=[VMEM],
+    )(owners, *points, *masses)
+
+
+def gather_one(sources, pieces):
+    def kernel(sources_ref, *refs):
+        o_ref, m_ref = refs[8:]
+        for r in range(8):
+            block = sources_ref[r]
+            o_ref[:, pl.ds(pl.multiple_of(block * 512, 512), 512)] = refs[r][0:96, :].astype(F32)
+            t = refs[r][96:112, :].astype(F32)
+            m_ref[pl.ds(block, 1), :] = t[0:1] + t[1:2] + t[2:3]
+
+    return pl.pallas_call(
+        kernel,
+        in_specs=[SMEM] + [VMEM] * 8,
         out_shape=[shape((96, 4096), F32), shape((8, 512), F32)],
         name="gather_one",
-    )(parts)
+    )(sources, *pieces)
 
 
 def join_two(a, b):
@@ -530,9 +549,8 @@
     parts_0 = sums_far(p, factor, x, 0)
     got_0 = [shift_y(part, k) for part, k in zip(parts_0, (2, 1, 3))]
     far_b = flip_x(after(near_b, parts_0[0]))
-    parts_1 = sums_far(p, after(factor, parts_0[0]), x, 1)
-    own, own_mass = sums_own(p, after(factor, parts_1[0]), x)
-    got_1 = [shift_y(parts_1[0], 2)] + [shift_y(after(part, own_mass), k) for part, k in zip(parts_1[1:], (1, 3))]
+    *parts_1, own, own_mass = sums_rest(p, after(factor, parts_0[0]), x)
+    got_1 = [shift_y(part, k) for part, k in zip(parts_1, (2, 1, 3))]
     two = (near_a, near_b, far_a, far_b)
     norms_two = (norms_a, norms_b, norms_c, norms_of(after(far_b, own_mass)))
 
@@ -541,17 +559,23 @@
     old = scores_two(places, points_0, theirs_0, two, norms_two, 0)
     points_1, mass_1 = finish_one(idx, own, after(own_mass, old[1]), got_1, cents_one, 1)
     theirs_1 = flip(points_1, "c")
-    tall = turn_points((points_0, points_1), (mass_0, mass_1))
-    columns = lax.all_to_all(tall, ("y", "xh"), 0, 0, tiled=True)
-    p2, stat2 = scores_two(places, after(points_1, tall), theirs_1, two, norms_two, 1, tuple(old))
+    p2, stat2 = scores_two(places, points_1, theirs_1, two, norms_two, 1, tuple(old))
     packed = sums_two(p2, stat2, flip(stat2, "c"), (points_0, theirs_0, points_1, theirs_1))
-    parts = lax.all_to_all(after(packed, columns), ("y", "xh", "z", "xl"), 0, 0, tiled=True)
-    turned_one, mass_one = gather_one(columns)
-    total = jnp.sum(parts.astype(F32), axis=0)
+    parts = lax.all_to_all(packed, ("y", "xh", "z", "xl"), 0, 0, tiled=True)
+    late_0, late_1 = after(points_0, packed), after(points_1, packed)
+    owners = (y + slot) % 4 * 2 + (xh ^ (slot // 4))
+    sources = (y - slot) % 4 + (xh ^ (slot // 4)) * 4
+    tall = turn_points(owners, (late_0, late_1), (mass_0, mass_1))
+    pieces = [tall[0]]
+    for r in range(1, 8):
+        pairs = [(a * 2 + h, (a + r) % 4 * 2 + (h ^ (r // 4))) for a in range(4) for h in range(2)]
+        pieces.append(lax.ppermute(tall[r], ("y", "xh"), pairs))
+    turned_one, mass_one = gather_one(sources, pieces)
+    total = jnp.sum(after(parts, tall[0]).astype(F32), axis=0)
     rows = lax.dynamic_slice_in_dim(cents_two, c * 256 + z * 64 + xl * 32, 32, 0)
-    spread = finish_two(total, after(rows, turned_one))
-    block = lax.all_to_all(spread, ("z", "xl"), 0, 0, tiled=True)
-    updated_two, mass_two = gather_two(c[None], block, flip(block, "c"))
+    spread = finish_two(total, after(rows, *pieces[1:5]))
+    block = after(lax.all_to_all(spread, ("z", "xl"), 0, 0, tiled=True), *pieces[5:])
+    updated_two, mass_two = gather_two(after(c[None], turned_one), block, flip(block, "c"))
     return turned_one.T, mass_one.reshape(4096), updated_two, mass_two.reshape(512)
 
 

time: 215 us -> 220 us (1.023)
  starting transfers between devices: 41.1 us -> 56.2 us
  blocking collectives: 12 us -> 0 us
  waiting for transfers between devices: 51.5 us -> 54.8 us
  Pallas kernels: 91.8 us -> 88.7 us
    ppermute x0 -> x7, waiting for transfers between devices: none -> 39.3 us  [body(): pieces.append(lax.ppermute(tall[r], ('y', 'xh'), pairs))]
    all_to_all x2, waiting for transfers between devices: 38.8 us -> 0.01 us  [the longest x1 0.01 us: body(): lax.all_to_all(spread, ('z', 'xl'), 0, 0, tiled=True)]
    ppermute x0 -> x7, starting transfers between devices: none -> 17.6 us  [body(): pieces.append(lax.ppermute(tall[r], ('y', 'xh'), pairs))]
    all_to_all x1 -> x0, blocking collectives: 12 us -> none  [body(): block = lax.all_to_all(spread, ('z', 'xl'), 0, 0, tiled=True)]
    pallas_call x2 -> x1, Pallas kernels: 14.7 us -> 7.45 us  [sums_far(): pl.pallas_call(kernel, grid=(3,), in_specs=[pl.BlockSpec((256, 2048), lam...]
    pallas_call x3, Pallas kernels: 10.9 us -> 15.1 us  [the longest x1 10.3 us: sums_rest(): pl.pallas_call(kernel, grid=(5,), in_specs=[pl.BlockSpec((256, 2048), lam...]
    ppermute x9, waiting for transfers between devices: 4.83 us -> 8.23 us  [shift_y(): return lax.ppermute(x, 'y', [(i, (i + k) % 4) for i in range(4)])]
    unnamed x43 -> x55, local copies, waits for them, and re-layouts: 10.7 us -> 10.4 us
  transfers between devices with their start and end apart: 21 -> 28, of which waited for: 7 -> 9; matrix products, arithmetic and copies ran while one was open for 1% -> 2% of each run, Pallas kernels for 34% -> 26%
where the time goes in v5:
time: 220 us; the launch traced here: 219 us
  Pallas kernels  88.7 us (40%)
  starting transfers between devices  56.2 us (26%)
  waiting for transfers between devices  54.8 us (25%)
  local copies, waits for them, and re-layouts  13.2 us (6%)
  other arithmetic  4.77 us (2%)
    ppermute x7, waiting for transfers between devices, body(): pieces.append(lax.ppermute(tall[r], ('y', 'xh'), pairs))  39.3 us
    ppermute x7, starting transfers between devices, body(): pieces.append(lax.ppermute(tall[r], ('y', 'xh'), pairs))  17.6 us
    pallas_call x2, Pallas kernels, scores_two(): pl.pallas_call(kernel, grid_spec=pltpu.PrefetchScalarGridSpec(num_scalar_...  14.7 us
    pallas_call x1, Pallas kernels, scores_near(): pl.pallas_call(scores_near_kernel, grid_spec=pltpu.PrefetchScalarGridSpec...  10.9 us
    ppermute x9, starting transfers between devices, shift_y(): return lax.ppermute(x, 'y', [(i, (i + k) % 4) for i in range(4)])  10.6 us
    unnamed x55, local copies, waits for them, and re-layouts  10.4 us
    pallas_call x1, Pallas kernels, scores_far(): pl.pallas_call(scores_far_kernel, grid_spec=pltpu.PrefetchScalarGridSpec(...  10.3 us
    pallas_call x1, Pallas kernels, sums_rest(): pl.pallas_call(kernel, grid=(5,), in_specs=[pl.BlockSpec((256, 2048), lam...  10.3 us
  transfers between devices with their start and end apart: 28, of which 9 were waited for; matrix products, arithmetic and copies ran while one was open for 2% of the time, Pallas kernels for 26%

profile of v5, /device:TPU:1, one launch (start us, length us, event | category | flops | bytes accessed | tf_op | source)
XLA Modules:
  0.0 218.6 jit_solution(17156327327690765672)
XLA Ops:
  2.2 3.4 %collective-permute-start = (bf16[512,768]{1,0:T(8,128)(2,1)S(1)}, bf16[512,768]{1,0:T(8,128)(2,1)S(1)}, u32[]{:S(2)}, u32[]{:S(2)}) collective-permute-start(bf16[512,768]{1,0:T(8,128)(2,1)S(1)} %dynamic-slice_convert_fusion), channel_id=1, source_target_pairs={{0,18},{2,16},{16,2},{18,0},{1,19},{3,17},{17,3},{19,1},{4,22},{6,... | collective-permute-start | bytes 2359304 | tf_op jit(solution)/shard_map/ppermute | solution.py:513
  9.1 10.9 %scores_near.1 = (f32[2048,2048]{1,0:T(8,128)}, bf16[2048,768]{1,0:T(8,128)(2,1)}, f32[8,512]{1,0:T(8,128)}, f32[2048,128]{1,0:T(8,128)}) custom-call(s32[10]{0:T(128)} %concatenate.3.idx.idx_ref, f32[1024,768]{1,0:T(8,128)} %e_ref.1, bf16[4096,768]{1,0:T(8,128)(2,1)} %cents_ref.3, bf16[4096,768]{1,0:T(8,128)(2,1)} %cents_ref.3, ...), custom_call_target="tpu_custom_call" | custom-call | flops 3221225472 | bytes 25165824 | tf_op jit(solution)/shard_map/scores_near/pallas_call | solution.py:136
  26.8 2.9 %collective-permute-start.5 = (bf16[256,768]{1,0:T(8,128)(2,1)}, bf16[256,768]{1,0:T(8,128)(2,1)}, u32[]{:S(2)}, u32[]{:S(2)}) collective-permute-start(bf16[256,768]{1,0:T(8,128)(2,1)} %copy-done.7), channel_id=1, source_target_pairs={{0,64},{32,96},{64,0},{96,32},{1,65},{33,97},{65,1},{97,33},{2,66}... | collective-permute-start | bytes 1179656 | tf_op jit(solution)/shard_map/ppermute | solution.py:501
  30.6 10.3 %scores_far.1 = (f32[2048,2048]{1,0:T(8,128)}, bf16[2048,768]{1,0:T(8,128)(2,1)}, f32[8,512]{1,0:T(8,128)}) custom-call(s32[10]{0:T(128)} %concatenate.3.idx.idx_ref, bf16[512,768]{1,0:T(8,128)(2,1)} %copy-done.9, bf16[512,768]{1,0:T(8,128)(2,1)} %copy-done.10, bf16[4096,768]{1,0:T(8,128)(2,1)} %cents_ref.3, ...), custom_call_target="tpu_custom_call", output_to_operand_aliasing={{0}: (9, {}), {1}: (10, {})} | custom-call | tf_op jit(solution)/shard_map/scores_far/pallas_call | solution.py:164
  44.8 5.1 %all-to-all-start = ((f32[16,8,512]{2,1,0:T(8,128)}), f32[16,8,512]{2,1,0:T(8,128)S(1)}, u32[]{:S(2)}, u32[]{:S(2)}) async-start(f32[16,8,512]{2,1,0:T(8,128)} %merge_cores.1), calls=%async_computation | async-start | bytes 524288 | tf_op jit(solution)/shard_map/all_to_all | solution.py:544
  55.1 3.0 %all-to-all-done.s_ref = f32[16,8,512]{2,1,0:T(8,128)S(1)} async-done(((f32[16,8,512]{2,1,0:T(8,128)}), f32[16,8,512]{2,1,0:T(8,128)S(1)}, u32[]{:S(2)}, u32[]{:S(2)}) %all-to-all-start) | async-done | bytes 262176 | tf_op jit(solution)/shard_map/all_to_all | solution.py:544
  60.4 7.5 %sums_far.1 = (bf16[272,768]{1,0:T(8,128)(2,1)}, bf16[272,768]{1,0:T(8,128)(2,1)}, bf16[272,768]{1,0:T(8,128)(2,1)}) custom-call(f32[2048,2048]{1,0:T(8,128)} %get-tuple-element.66.p_ref, f32[1,2048]{1,0:T(1,128)} %merge_last.1.f_ref, bf16[2048,768]{1,0:T(8,128)(2,1)} %get-tuple-element.74.x_ref), custom_call_target="tpu_custom_call" | custom-call | tf_op jit(solution)/shard_map/sums_far/pallas_call | solution.py:235
  72.8 10.3 %sums_rest.1 = (bf16[272,768]{1,0:T(8,128)(2,1)}, bf16[272,768]{1,0:T(8,128)(2,1)}, bf16[272,768]{1,0:T(8,128)(2,1)}, f32[512,768]{1,0:T(8,128)}, f32[1,512]{1,0:T(1,128)}) custom-call(f32[2048,2048]{1,0:T(8,128)} %get-tuple-element.66.p_ref, f32[1,2048]{1,0:T(1,128)} %merge_last.1.f_ref, bf16[2048,768]{1,0:T(8,128)(2,1)} %get-tuple-element.74.x_ref), custom_call_target="tpu_custom_call" | custom-call | tf_op jit(solution)/shard_map/sums_rest/pallas_call | solution.py:268
  83.9 8.2 %collective-permute-done.8.g2 = bf16[272,768]{1,0:T(8,128)(2,1)} collective-permute-done((bf16[272,768]{1,0:T(8,128)(2,1)}, bf16[272,768]{1,0:T(8,128)(2,1)}, u32[]{:S(2)}, u32[]{:S(2)}) %collective-permute-start.8) | collective-permute-done | bytes 417824 | tf_op jit(solution)/shard_map/ppermute | solution.py:501
  92.1 3.4 %finish_one.2 = (bf16[256,768]{1,0:T(8,128)(2,1)}, f32[1,256]{1,0:T(1,128)}) custom-call(s32[10]{0:T(128)} %concatenate.3.idx.idx_ref, f32[512,768]{1,0:T(8,128)} %get-tuple-element.77.own_ref, f32[1,512]{1,0:T(1,128)} %get-tuple-element.86.m_ref, bf16[272,768]{1,0:T(8,128)(2,1)} %collective-permute-done.7.g1, bf16[272,768]{1,0:T(8,128)(2,1)} %collective-permute-done.8.g2, ...), custom_call_target="tpu_custom_call" | custom-call | tf_op jit(solution)/shard_map/finish_one/pallas_call | solution.py:297
  100.9 7.3 %scores_two.2 = (f32[2048,1024]{1,0:T(8,128)}, f32[2,1024]{1,0:T(2,128)}) custom-call(s32[8]{0:T(128)} %multiply_add_fusion.places_ref, bf16[256,768]{1,0:T(8,128)(2,1)} %get-tuple-element.94.a_ref.x0.p0, bf16[256,768]{1,0:T(8,128)(2,1)} %copy-done.6, bf16[512,768]{1,0:T(8,128)(2,1)} %get-tuple-element.71.refs_0_, ...), custom_call_target="tpu_custom_call" | custom-call | tf_op jit(solution)/shard_map/scores_two/pallas_call | solution.py:407
  109.0 3.4 %finish_one.3 = (bf16[256,768]{1,0:T(8,128)(2,1)}, f32[1,256]{1,0:T(1,128)}) custom-call(s32[10]{0:T(128)} %concatenate.3.idx.idx_ref, f32[512,768]{1,0:T(8,128)} %get-tuple-element.77.own_ref, f32[1,512]{1,0:T(1,128)} %get-tuple-element.86.m_ref, bf16[272,768]{1,0:T(8,128)(2,1)} %copy-done.12, bf16[272,768]{1,0:T(8,128)(2,1)} %collective-permute-done.13.g2, ...), custom_call_target="tpu_custom_call" | custom-call | tf_op jit(solution)/shard_map/finish_one/pallas_call | solution.py:297
  115.1 7.4 %scores_two.3 = (f32[2048,1024]{1,0:T(8,128)}, f32[2,1024]{1,0:T(2,128)}) custom-call(s32[8]{0:T(128)} %multiply_add_fusion.places_ref, bf16[256,768]{1,0:T(8,128)(2,1)} %get-tuple-element.95.a_ref.x2.p1, bf16[256,768]{1,0:T(8,128)(2,1)} %copy-done.5, bf16[512,768]{1,0:T(8,128)(2,1)} %get-tuple-element.71.refs_0_, ...), custom_call_target="tpu_custom_call", output_to_operand_aliasing={{0}: (11, {})} | custom-call | tf_op jit(solution)/shard_map/scores_two/pallas_call | solution.py:407
  124.5 7.6 %sums_two.1 = bf16[64,208,128]{2,1,0:T(8,128)(2,1)} custom-call(f32[2048,1024]{1,0:T(8,128)} %get-tuple-element.92.p_ref, f32[2,1024]{1,0:T(2,128)} %get-tuple-element.93.s_ref, f32[2,1024]{1,0:T(2,128)} %copy-done.23, bf16[256,768]{1,0:T(8,128)(2,1)} %get-tuple-element.94.a_ref.x0.p0, bf16[256,768]{1,0:T(8,128)(2,1)} %copy-done.6, ...), custom_call_target="tpu_custom_call" | custom-call | tf_op jit(solution)/shard_map/sums_two/pallas_call | solution.py:447
  132.1 5.6 %all-to-all-start.1 = ((bf16[64,208,128]{2,1,0:T(8,128)(2,1)}), bf16[64,208,128]{2,1,0:T(8,128)(2,1)}, u32[]{:S(2)}, u32[]{:S(2)}) async-start(bf16[64,208,128]{2,1,0:T(8,128)(2,1)} %sums_two.1), calls=%async_computation.1 | async-start | bytes 6815744 | tf_op jit(solution)/shard_map/all_to_all | solution.py:564
  145.3 2.7 %collective-permute-start.20 = (bf16[112,512]{1,0:T(8,128)(2,1)}, bf16[112,512]{1,0:T(8,128)(2,1)S(1)}, u32[]{:S(2)}, u32[]{:S(2)}) collective-permute-start(bf16[112,512]{1,0:T(8,128)(2,1)} %get-tuple-element.102), channel_id=1, source_target_pairs={{0,16},{16,0},{32,48},{48,32},{64,80},{80,64},{96,112},{112,96},{1... | collective-permute-start | bytes 344072 | tf_op jit(solution)/shard_map/ppermute | solution.py:572
  148.6 30.9 %collective-permute-done.17.refs_1_ = bf16[112,512]{1,0:T(8,128)(2,1)S(1)} collective-permute-done((bf16[112,512]{1,0:T(8,128)(2,1)}, bf16[112,512]{1,0:T(8,128)(2,1)S(1)}, u32[]{:S(2)}, u32[]{:S(2)}) %collective-permute-start.17) | collective-permute-done | bytes 114720 | tf_op jit(solution)/shard_map/ppermute | solution.py:572
  179.5 3.2 %collective-permute-done.18.refs_2_ = bf16[112,512]{1,0:T(8,128)(2,1)S(1)} collective-permute-done((bf16[112,512]{1,0:T(8,128)(2,1)}, bf16[112,512]{1,0:T(8,128)(2,1)S(1)}, u32[]{:S(2)}, u32[]{:S(2)}) %collective-permute-start.18) | collective-permute-done | bytes 114720 | tf_op jit(solution)/shard_map/ppermute | solution.py:572
  182.7 3.2 %convert_reduce_fusion.x_ref = f32[208,128]{1,0:T(8,128)} fusion(bf16[64,208,128]{2,1,0:T(8,128)(2,1)} %all-to-all-done.1), kind=kLoop, calls=%fused_computation | loop fusion | flops 3381248 | bytes 3514368 | tf_op jit(solution)/shard_map/reduce_sum | solution.py:574
  187.8 5.0 %all-to-all-start.2 = ((bf16[8,208,128]{2,1,0:T(8,128)(2,1)}), bf16[8,208,128]{2,1,0:T(8,128)(2,1)S(1)}, u32[]{:S(2)}, u32[]{:S(2)}) async-start(bf16[8,208,128]{2,1,0:T(8,128)(2,1)} %finish_two.1), calls=%async_computation.2 | async-start | bytes 851968 | tf_op jit(solution)/shard_map/all_to_all | solution.py:577
  192.7 3.1 %collective-permute-start.21 = (bf16[112,512]{1,0:T(8,128)(2,1)S(1)}, bf16[112,512]{1,0:T(8,128)(2,1)S(1)}, u32[]{:S(2)}, u32[]{:S(2)}) collective-permute-start(bf16[112,512]{1,0:T(8,128)(2,1)S(1)} %copy-done.26), channel_id=1, source_target_pairs={{0,48},{16,32},{32,80},{48,64},{64,112},{80,96},{96,16},{112,0},{1... | collective-permute-start | bytes 344072 | tf_op jit(solution)/shard_map/ppermute | solution.py:572
  198.6 4.4 %collective-permute-start.23 = (bf16[112,512]{1,0:T(8,128)(2,1)S(1)}, bf16[112,512]{1,0:T(8,128)(2,1)S(1)}, u32[]{:S(2)}, u32[]{:S(2)}) collective-permute-start(bf16[112,512]{1,0:T(8,128)(2,1)S(1)} %copy-done.24), channel_id=1, source_target_pairs={{0,112},{16,96},{32,16},{48,0},{64,48},{80,32},{96,80},{112,64},{1... | collective-permute-start | bytes 344072 | tf_op jit(solution)/shard_map/ppermute | solution.py:572
  203.8 4.3 %collective-permute-done.22.refs_6_ = bf16[112,512]{1,0:T(8,128)(2,1)S(1)} collective-permute-done((bf16[112,512]{1,0:T(8,128)(2,1)S(1)}, bf16[112,512]{1,0:T(8,128)(2,1)S(1)}, u32[]{:S(2)}, u32[]{:S(2)}) %collective-permute-start.22) | collective-permute-done | bytes 114720 | tf_op jit(solution)/shard_map/ppermute | solution.py:572
  208.2 2.9 %collective-permute-start.24 = (bf16[8,208,128]{2,1,0:T(8,128)(2,1)S(1)}, bf16[8,208,128]{2,1,0:T(8,128)(2,1)S(1)}, u32[]{:S(2)}, u32[]{:S(2)}) collective-permute-start(bf16[8,208,128]{2,1,0:T(8,128)(2,1)S(1)} %all-to-all-done.2.a_ref), channel_id=1, source_target_pairs={{0,1},{1,0},{2,3},{3,2},{4,5},{5,4},{6,7},{7,6},{8,9},{9,8},{10,11... | collective-permute-start | bytes 1277960 | tf_op jit(solution)/shard_map/ppermute | solution.py:509
  (115 shorter events, 61.8 us)
Async XLA Ops:
  2.2 20.8 %collective-permute-start = (bf16[512,768]{1,0:T(8,128)(2,1)S(1)}, bf16[512,768]{1,0:T(8,128)(2,1)S(1)}, u32[]{:S(2)}, u32[]{:S(2)}) collective-permute-start(bf16[512,768]{1,0:T(8,128)(2,1)S(1)} %dynamic-slice_convert_fusion), channel_id=1, source_target_pairs={{0,18},{2,16},{16,2},{18,0},{1,19},{3,17},{17,3},{19,1},{4,22},{6,... | collective-permute-start | bytes 2359304 | tf_op jit(solution)/shard_map/ppermute | solution.py:513
  5.6 14.4 %collective-permute-start.1 = (bf16[256,768]{1,0:T(8,128)(2,1)S(1)}, bf16[256,768]{1,0:T(8,128)(2,1)S(1)}, u32[]{:S(2)}, u32[]{:S(2)}) collective-permute-start(bf16[256,768]{1,0:T(8,128)(2,1)S(1)} %constant_dynamic-slice_fusion.1.a_ref), channel_id=1, source_target_pairs={{0,32},{32,64},{64,96},{96,0},{1,33},{33,65},{65,97},{97,1},{2,34}... | collective-permute-start | bytes 1179656 | tf_op jit(solution)/shard_map/ppermute | solution.py:501
  7.0 16.0 %collective-permute-start.2 = (bf16[256,768]{1,0:T(8,128)(2,1)S(1)}, bf16[256,768]{1,0:T(8,128)(2,1)S(1)}, u32[]{:S(2)}, u32[]{:S(2)}) collective-permute-start(bf16[256,768]{1,0:T(8,128)(2,1)S(1)} %constant_dynamic-slice_fusion.1.a_ref), channel_id=1, source_target_pairs={{0,96},{32,0},{64,32},{96,64},{1,97},{33,1},{65,33},{97,65},{2,98}... | collective-permute-start | bytes 1179656 | tf_op jit(solution)/shard_map/ppermute | solution.py:501
  23.7 6.0 %collective-permute-start.3 = (bf16[512,768]{1,0:T(8,128)(2,1)S(1)}, bf16[512,768]{1,0:T(8,128)(2,1)S(1)}, u32[]{:S(2)}, u32[]{:S(2)}) collective-permute-start(bf16[512,768]{1,0:T(8,128)(2,1)S(1)} %collective-permute-done.a_ref), channel_id=1, source_target_pairs={{0,1},{1,0},{2,3},{3,2},{4,5},{5,4},{6,7},{7,6},{8,9},{9,8},{10,11... | collective-permute-start | bytes 2359304 | tf_op jit(solution)/shard_map/ppermute | solution.py:509
  25.1 24.8 %collective-permute-start.6 = (bf16[512,768]{1,0:T(8,128)(2,1)}, bf16[512,768]{1,0:T(8,128)(2,1)S(1)}, u32[]{:S(2)}, u32[]{:S(2)}) collective-permute-start(bf16[512,768]{1,0:T(8,128)(2,1)} %get-tuple-element.71.refs_0_), channel_id=1, source_target_pairs={{0,18},{2,16},{16,2},{18,0},{1,19},{3,17},{17,3},{19,1},{4,22},{6,... | collective-permute-start | bytes 2359304 | tf_op jit(solution)/shard_map/ppermute | solution.py:513
  26.8 23.1 %collective-permute-start.5 = (bf16[256,768]{1,0:T(8,128)(2,1)}, bf16[256,768]{1,0:T(8,128)(2,1)}, u32[]{:S(2)}, u32[]{:S(2)}) collective-permute-start(bf16[256,768]{1,0:T(8,128)(2,1)} %copy-done.7), channel_id=1, source_target_pairs={{0,64},{32,96},{64,0},{96,32},{1,65},{33,97},{65,1},{97,33},{2,66}... | collective-permute-start | bytes 1179656 | tf_op jit(solution)/shard_map/ppermute | solution.py:501
  44.8 13.3 %all-to-all-start = ((f32[16,8,512]{2,1,0:T(8,128)}), f32[16,8,512]{2,1,0:T(8,128)S(1)}, u32[]{:S(2)}, u32[]{:S(2)}) async-start(f32[16,8,512]{2,1,0:T(8,128)} %merge_cores.1), calls=%async_computation | async-start | bytes 524288 | tf_op jit(solution)/shard_map/all_to_all | solution.py:544
  67.9 15.6 %collective-permute-start.7 = (bf16[272,768]{1,0:T(8,128)(2,1)}, bf16[272,768]{1,0:T(8,128)(2,1)}, u32[]{:S(2)}, u32[]{:S(2)}) collective-permute-start(bf16[272,768]{1,0:T(8,128)(2,1)} %get-tuple-element.75), channel_id=1, source_target_pairs={{0,64},{32,96},{64,0},{96,32},{1,65},{33,97},{65,1},{97,33},{2,66}... | collective-permute-start | bytes 1253384 | tf_op jit(solution)/shard_map/ppermute | solution.py:501
  69.2 22.9 %collective-permute-start.8 = (bf16[272,768]{1,0:T(8,128)(2,1)}, bf16[272,768]{1,0:T(8,128)(2,1)}, u32[]{:S(2)}, u32[]{:S(2)}) collective-permute-start(bf16[272,768]{1,0:T(8,128)(2,1)} %get-tuple-element.79), channel_id=1, source_target_pairs={{0,32},{32,64},{64,96},{96,0},{1,33},{33,65},{65,97},{97,1},{2,34}... | collective-permute-start | bytes 1253384 | tf_op jit(solution)/shard_map/ppermute | solution.py:501
  69.6 22.5 %collective-permute-start.9 = (bf16[272,768]{1,0:T(8,128)(2,1)}, bf16[272,768]{1,0:T(8,128)(2,1)}, u32[]{:S(2)}, u32[]{:S(2)}) collective-permute-start(bf16[272,768]{1,0:T(8,128)(2,1)} %get-tuple-element.80), channel_id=1, source_target_pairs={{0,96},{32,0},{64,32},{96,64},{1,97},{33,1},{65,33},{97,65},{2,98}... | collective-permute-start | bytes 1253384 | tf_op jit(solution)/shard_map/ppermute | solution.py:501
  71.9 25.4 %collective-permute-start.11 = (bf16[512,768]{1,0:T(8,128)(2,1)S(1)}, bf16[512,768]{1,0:T(8,128)(2,1)S(1)}, u32[]{:S(2)}, u32[]{:S(2)}) collective-permute-start(bf16[512,768]{1,0:T(8,128)(2,1)S(1)} %copy-done.3), channel_id=1, source_target_pairs={{0,18},{2,16},{16,2},{18,0},{1,19},{3,17},{17,3},{19,1},{4,22},{6,... | collective-permute-start | bytes 2359304 | tf_op jit(solution)/shard_map/ppermute | solution.py:513
  83.0 25.2 %collective-permute-start.12 = (bf16[272,768]{1,0:T(8,128)(2,1)}, bf16[272,768]{1,0:T(8,128)(2,1)S(1)}, u32[]{:S(2)}, u32[]{:S(2)}) collective-permute-start(bf16[272,768]{1,0:T(8,128)(2,1)} %get-tuple-element.87), channel_id=1, source_target_pairs={{0,64},{32,96},{64,0},{96,32},{1,65},{33,97},{65,1},{97,33},{2,66}... | collective-permute-start | bytes 1253384 | tf_op jit(solution)/shard_map/ppermute | solution.py:501
  83.5 24.8 %collective-permute-start.13 = (bf16[272,768]{1,0:T(8,128)(2,1)}, bf16[272,768]{1,0:T(8,128)(2,1)}, u32[]{:S(2)}, u32[]{:S(2)}) collective-permute-start(bf16[272,768]{1,0:T(8,128)(2,1)} %get-tuple-element.88), channel_id=1, source_target_pairs={{0,32},{32,64},{64,96},{96,0},{1,33},{33,65},{65,97},{97,1},{2,34}... | collective-permute-start | bytes 1253384 | tf_op jit(solution)/shard_map/ppermute | solution.py:501
  92.1 16.2 %collective-permute-start.14 = (bf16[272,768]{1,0:T(8,128)(2,1)}, bf16[272,768]{1,0:T(8,128)(2,1)}, u32[]{:S(2)}, u32[]{:S(2)}) collective-permute-start(bf16[272,768]{1,0:T(8,128)(2,1)} %get-tuple-element.89), channel_id=1, source_target_pairs={{0,96},{32,0},{64,32},{96,64},{1,97},{33,1},{65,33},{97,65},{2,98}... | collective-permute-start | bytes 1253384 | tf_op jit(solution)/shard_map/ppermute | solution.py:501
  132.1 50.6 %all-to-all-start.1 = ((bf16[64,208,128]{2,1,0:T(8,128)(2,1)}), bf16[64,208,128]{2,1,0:T(8,128)(2,1)}, u32[]{:S(2)}, u32[]{:S(2)}) async-start(bf16[64,208,128]{2,1,0:T(8,128)(2,1)} %sums_two.1), calls=%async_computation.1 | async-start | bytes 6815744 | tf_op jit(solution)/shard_map/all_to_all | solution.py:564
  140.6 38.9 %collective-permute-start.17 = (bf16[112,512]{1,0:T(8,128)(2,1)}, bf16[112,512]{1,0:T(8,128)(2,1)S(1)}, u32[]{:S(2)}, u32[]{:S(2)}) collective-permute-start(bf16[112,512]{1,0:T(8,128)(2,1)} %get-tuple-element.99), channel_id=1, source_target_pairs={{0,32},{16,48},{32,64},{48,80},{64,96},{80,112},{96,0},{112,16},{1... | collective-permute-start | bytes 344072 | tf_op jit(solution)/shard_map/ppermute | solution.py:572
  141.6 41.1 %collective-permute-start.18 = (bf16[112,512]{1,0:T(8,128)(2,1)}, bf16[112,512]{1,0:T(8,128)(2,1)S(1)}, u32[]{:S(2)}, u32[]{:S(2)}) collective-permute-start(bf16[112,512]{1,0:T(8,128)(2,1)} %get-tuple-element.100), channel_id=1, source_target_pairs={{0,64},{16,80},{32,96},{48,112},{64,0},{80,16},{96,32},{112,48},{1... | collective-permute-start | bytes 344072 | tf_op jit(solution)/shard_map/ppermute | solution.py:572
  144.2 38.5 %collective-permute-start.19 = (bf16[112,512]{1,0:T(8,128)(2,1)}, bf16[112,512]{1,0:T(8,128)(2,1)S(1)}, u32[]{:S(2)}, u32[]{:S(2)}) collective-permute-start(bf16[112,512]{1,0:T(8,128)(2,1)} %get-tuple-element.101), channel_id=1, source_target_pairs={{0,96},{16,112},{32,0},{48,16},{64,32},{80,48},{96,64},{112,80},{1... | collective-permute-start | bytes 344072 | tf_op jit(solution)/shard_map/ppermute | solution.py:572
  145.3 37.5 %collective-permute-start.20 = (bf16[112,512]{1,0:T(8,128)(2,1)}, bf16[112,512]{1,0:T(8,128)(2,1)S(1)}, u32[]{:S(2)}, u32[]{:S(2)}) collective-permute-start(bf16[112,512]{1,0:T(8,128)(2,1)} %get-tuple-element.102), channel_id=1, source_target_pairs={{0,16},{16,0},{32,48},{48,32},{64,80},{80,64},{96,112},{112,96},{1... | collective-permute-start | bytes 344072 | tf_op jit(solution)/shard_map/ppermute | solution.py:572
  187.8 20.4 %all-to-all-start.2 = ((bf16[8,208,128]{2,1,0:T(8,128)(2,1)}), bf16[8,208,128]{2,1,0:T(8,128)(2,1)S(1)}, u32[]{:S(2)}, u32[]{:S(2)}) async-start(bf16[8,208,128]{2,1,0:T(8,128)(2,1)} %finish_two.1), calls=%async_computation.2 | async-start | bytes 851968 | tf_op jit(solution)/shard_map/all_to_all | solution.py:577
  192.7 11.1 %collective-permute-start.21 = (bf16[112,512]{1,0:T(8,128)(2,1)S(1)}, bf16[112,512]{1,0:T(8,128)(2,1)S(1)}, u32[]{:S(2)}, u32[]{:S(2)}) collective-permute-start(bf16[112,512]{1,0:T(8,128)(2,1)S(1)} %copy-done.26), channel_id=1, source_target_pairs={{0,48},{16,32},{32,80},{48,64},{64,112},{80,96},{96,16},{112,0},{1... | collective-permute-start | bytes 344072 | tf_op jit(solution)/shard_map/ppermute | solution.py:572
  195.9 12.2 %collective-permute-start.22 = (bf16[112,512]{1,0:T(8,128)(2,1)S(1)}, bf16[112,512]{1,0:T(8,128)(2,1)S(1)}, u32[]{:S(2)}, u32[]{:S(2)}) collective-permute-start(bf16[112,512]{1,0:T(8,128)(2,1)S(1)} %copy-done.25), channel_id=1, source_target_pairs={{0,80},{16,64},{32,112},{48,96},{64,16},{80,0},{96,48},{112,32},{1... | collective-permute-start | bytes 344072 | tf_op jit(solution)/shard_map/ppermute | solution.py:572
  198.6 9.6 %collective-permute-start.23 = (bf16[112,512]{1,0:T(8,128)(2,1)S(1)}, bf16[112,512]{1,0:T(8,128)(2,1)S(1)}, u32[]{:S(2)}, u32[]{:S(2)}) collective-permute-start(bf16[112,512]{1,0:T(8,128)(2,1)S(1)} %copy-done.24), channel_id=1, source_target_pairs={{0,112},{16,96},{32,16},{48,0},{64,48},{80,32},{96,80},{112,64},{1... | collective-permute-start | bytes 344072 | tf_op jit(solution)/shard_map/ppermute | solution.py:572
  208.2 7.3 %collective-permute-start.24 = (bf16[8,208,128]{2,1,0:T(8,128)(2,1)S(1)}, bf16[8,208,128]{2,1,0:T(8,128)(2,1)S(1)}, u32[]{:S(2)}, u32[]{:S(2)}) collective-permute-start(bf16[8,208,128]{2,1,0:T(8,128)(2,1)S(1)} %all-to-all-done.2.a_ref), channel_id=1, source_target_pairs={{0,1},{1,0},{2,3},{3,2},{4,5},{5,4},{6,7},{7,6},{8,9},{9,8},{10,11... | collective-permute-start | bytes 1277960 | tf_op jit(solution)/shard_map/ppermute | solution.py:509
  (31 other events, 361.6 us)

commit v6 on v5

--- a/solution.py
+++ b/solution.py
@@ -313,53 +313,70 @@
 
 
 def turn_points(owners, points, masses):
-    def kernel(owners_ref, p0, p1, m0, m1, *refs):
-        tall = refs[8]
+    def kernel(owners_ref, p0, p1, m0, m1, keep_ref, give_ref, tall):
         for h, p_ref in enumerate((p0, p1)):
             for at in range(0, D, 128):
                 tall[pl.ds(at, 128), h * 256 : h * 256 + 256] = p_ref[:, pl.ds(at, 128)].astype(F32).T.astype(BF)
         packed = mass_rows(jnp.concatenate([m0[...], m1[...]], axis=1)).astype(BF)
         for r in range(8):
-            refs[r][0:96, :] = tall[pl.ds(pl.multiple_of(owners_ref[r] * 96, 32), 96), :]
-            refs[r][96:112, :] = packed
+            ref = (keep_ref, give_ref)[r // 4]
+            ref[r % 4, 0:96, :] = tall[pl.ds(pl.multiple_of(owners_ref[r] * 96, 32), 96), :]
+            ref[r % 4, 96:112, :] = packed
 
     return pl.pallas_call(
         kernel,
         in_specs=[SMEM] + [VMEM] * 4,
         scratch_shapes=[pltpu.VMEM((D, 512), BF)],
-        out_shape=[shape((112, 512), BF)] * 8,
+        out_shape=[shape((4, 112, 512), BF)] * 2,
         name="turn_points",
     )(owners, *points, *masses)
 
 
-def gather_one(sources, pieces):
-    def kernel(sources_ref, *refs):
-        o_ref, m_ref = refs[8:]
+def pair_pieces(keep, take):
+    def kernel(k_ref, t_ref, *refs):
+        for k, ref in enumerate(refs, 1):
+            ref[0] = k_ref[k]
+            ref[1] = t_ref[k]
+
+    return pl.pallas_call(
+        kernel, in_specs=[VMEM] * 2, out_shape=[shape((2, 112, 512), BF)] * 3, name="pair_pieces"
+    )(keep, take)
+
+
+def gather_one(sources, keep, take, pieces):
+    def kernel(sources_ref, k_ref, t_ref, r1, r2, r3, o_ref, m_ref):
         for r in range(8):
+            b, k = r // 4, r % 4
+            piece = (r1, r2, r3)[k - 1].at[b] if k else (k_ref, t_ref)[b].at[0]
             block = sources_ref[r]
-            o_ref[:, pl.ds(pl.multiple_of(block * 512, 512), 512)] = refs[r][0:96, :].astype(F32)
-            t = refs[r][96:112, :].astype(F32)
+            o_ref[:, pl.ds(pl.multiple_of(block * 512, 512), 512)] = piece[0:96, :].astype(F32)
+            t = piece[96:112, :].astype(F32)
             m_ref[pl.ds(block, 1), :] = t[0:1] + t[1:2] + t[2:3]
 
     return pl.pallas_call(
         kernel,
-        in_specs=[SMEM] + [VMEM] * 8,
+        in_specs=[SMEM] + [VMEM] * 5,
         out_shape=[shape((96, 4096), F32), shape((8, 512), F32)],
         name="gather_one",
-    )(sources, *pieces)
-
-
-def join_two(a, b):
+    )(sources, keep, take, *pieces)
+
+
+def join_two(a, b, rows):
     def kernel(a_ref, b_ref, o_ref, n_ref):
+        if rows > 512:
+            o_ref[512:rows, 512:D] = jnp.zeros((rows - 512, D - 512), BF)
         for at, ref in ((0, a_ref), (256, b_ref)):
             block = ref[...]
+            n = square_norms(block)
             o_ref[at : at + 256, :] = block
-            n_ref[at : at + 256, :] = jnp.broadcast_to(square_norms(block), (256, 128))
+            n_ref[at : at + 256, :] = jnp.broadcast_to(n, (256, 128))
+            if rows > 512:
+                o_ref[512:rows, at : at + 256] = mass_rows(as_row(n)).astype(BF)
 
     return pl.pallas_call(
         kernel,
         in_specs=[VMEM] * 2,
-        out_shape=[shape((512, D), BF), shape((512, 128), F32)],
+        out_shape=[shape((rows, D), BF), shape((512, 128), F32)],
         name="join_two",
     )(a, b)
 
@@ -375,9 +392,16 @@
 
 def scores_two(places, own, theirs, two, norms, half, old=()):
     def kernel(places_ref, a_ref, b_ref, *refs):
-        cents, ns = refs[0:4], refs[4:8]
-        p_ref, stat_ref, scores = refs[-3:]
+        cents, ns = refs[0:4], (*refs[4:7], refs[-1])
+        p_ref, stat_ref, scores, far_norms = refs[-4:]
         i = pl.program_id(0)
+
+        @pl.when(i == 0)
+        def _():
+            row = cents[3][512:528, 0:512].astype(F32)
+            row = row[0:1] + row[1:2] + row[2:3]
+            far_norms[...] = jnp.broadcast_to(row, (128, 512)).T
+
         twice = jnp.where(i == 0, a_ref[...], b_ref[...]) * 2
         top = None
         for slot in range(8):
@@ -397,7 +421,7 @@
 
         @pl.when(i == 0)
         def _():
-            stat_ref[...] = refs[9][...] if old else jnp.zeros_like(stat_ref)
+            stat_ref[...] = refs[8][...] if old else jnp.zeros_like(stat_ref)
 
         cols = pl.ds(pl.multiple_of((half * 2 + i) * 256, 256), 256)
         stat_ref[0:1, cols] = m
@@ -409,13 +433,13 @@
         grid_spec=pltpu.PrefetchScalarGridSpec(
             num_scalar_prefetch=1,
             grid=(2,),
-            in_specs=[whole(256, D)] * 2 + [whole(512, D)] * 4 + [whole(512, 128)] * 4
+            in_specs=[whole(256, D)] * 2 + [whole(t.shape[0], D) for t in two] + [whole(512, 128)] * 3
             + ([ANY, whole(2, 1024)] if old else []),
             out_specs=[pl.BlockSpec((2048, 256), lambda i, s: (0, half * 2 + i)), whole(2, 1024)],
-            scratch_shapes=[pltpu.VMEM((2048, 256), F32)],
+            scratch_shapes=[pltpu.VMEM((2048, 256), F32), pltpu.VMEM((512, 128), F32)],
         ),
         out_shape=[shape((2048, 1024), F32), shape((2, 1024), F32)],
-        input_output_aliases={11: 0} if old else {},
+        input_output_aliases={10: 0} if old else {},
         name="scores_two",
     )(places, own, theirs, *two, *norms, *old)
 
@@ -534,7 +558,7 @@
     around = [shift_y(half_two, k) for k in (1, 2, 3)]
 
     p, x, near, norms = scores_near(idx, embeddings, cents_one)
-    near_a, norms_a = join_two(after(half_two, near), around[0])
+    near_a, norms_a = join_two(after(half_two, near), around[0], 512)
     far_mine = after(far_mine, near, norms_a, around[2])
     far_other = flip(far_mine, "c")
     far_a = flip_x(after(near_a, far_mine))
@@ -542,7 +566,7 @@
 
     spread = merge_cores(local, flip(local, "c"))
     stats = lax.all_to_all(spread, ("xh", "z", "xl"), 0, 0, tiled=True)
-    near_b, norms_b = join_two(after(around[1], spread), around[2])
+    near_b, norms_b = join_two(after(around[1], spread), around[2], 528)
     norms_c = norms_of(after(far_a, spread))
     factor = merge_last(idx, stats, after(local, norms_b, norms_c))
 
@@ -552,30 +576,30 @@
     *parts_1, own, own_mass = sums_rest(p, after(factor, parts_0[0]), x)
     got_1 = [shift_y(part, k) for part, k in zip(parts_1, (2, 1, 3))]
     two = (near_a, near_b, far_a, far_b)
-    norms_two = (norms_a, norms_b, norms_c, norms_of(after(far_b, own_mass)))
+    norms_two = (norms_a, norms_b, norms_c)
 
     points_0, mass_0 = finish_one(idx, own, own_mass, got_0, cents_one, 0)
     theirs_0 = flip(points_0, "c")
     old = scores_two(places, points_0, theirs_0, two, norms_two, 0)
     points_1, mass_1 = finish_one(idx, own, after(own_mass, old[1]), got_1, cents_one, 1)
     theirs_1 = flip(points_1, "c")
-    p2, stat2 = scores_two(places, points_1, theirs_1, two, norms_two, 1, tuple(old))
-    packed = sums_two(p2, stat2, flip(stat2, "c"), (points_0, theirs_0, points_1, theirs_1))
-    parts = lax.all_to_all(packed, ("y", "xh", "z", "xl"), 0, 0, tiled=True)
-    late_0, late_1 = after(points_0, packed), after(points_1, packed)
     owners = (y + slot) % 4 * 2 + (xh ^ (slot // 4))
     sources = (y - slot) % 4 + (xh ^ (slot // 4)) * 4
-    tall = turn_points(owners, (late_0, late_1), (mass_0, mass_1))
-    pieces = [tall[0]]
-    for r in range(1, 8):
-        pairs = [(a * 2 + h, (a + r) % 4 * 2 + (h ^ (r // 4))) for a in range(4) for h in range(2)]
-        pieces.append(lax.ppermute(tall[r], ("y", "xh"), pairs))
-    turned_one, mass_one = gather_one(sources, pieces)
-    total = jnp.sum(after(parts, tall[0]).astype(F32), axis=0)
+    keep, give = turn_points(owners, (points_0, points_1), (mass_0, mass_1))
+    take = flip(give, "xh")
+
+    p2, stat2 = scores_two(places, after(points_1, give), theirs_1, two, norms_two, 1, tuple(old))
+    packed = sums_two(p2, stat2, flip(stat2, "c"), (points_0, theirs_0, points_1, theirs_1))
+    packed = after(packed, take)
+    parts = lax.all_to_all(packed, ("y", "xh", "z", "xl"), 0, 0, tiled=True)
+    pairs = pair_pieces(after(keep, packed), take)
+    pieces = [shift_y(t, k) for t, k in zip(pairs, (1, 2, 3))]
+    turned_one, mass_one = gather_one(sources, keep, take, pieces)
+    total = jnp.sum(after(parts, pairs[0]).astype(F32), axis=0)
     rows = lax.dynamic_slice_in_dim(cents_two, c * 256 + z * 64 + xl * 32, 32, 0)
-    spread = finish_two(total, after(rows, *pieces[1:5]))
-    block = after(lax.all_to_all(spread, ("z", "xl"), 0, 0, tiled=True), *pieces[5:])
-    updated_two, mass_two = gather_two(after(c[None], turned_one), block, flip(block, "c"))
+    spread = finish_two(total, after(rows, *pieces))
+    block = after(lax.all_to_all(spread, ("z", "xl"), 0, 0, tiled=True), turned_one)
+    updated_two, mass_two = gather_two(c[None], block, flip(block, "c"))
     return turned_one.T, mass_one.reshape(4096), updated_two, mass_two.reshape(512)
 
 

time: 220 us -> 218 us (level)
  starting transfers between devices: 56.2 us -> 47.9 us
  waiting for transfers between devices: 54.8 us -> 61.3 us
    ppermute x9 -> x12, waiting for transfers between devices: 8.23 us -> 50.4 us  [shift_y(): return lax.ppermute(x, 'y', [(i, (i + k) % 4) for i in range(4)])]
    ppermute x7 -> x0, waiting for transfers between devices: 39.3 us -> none  [body(): pieces.append(lax.ppermute(tall[r], ('y', 'xh'), pairs))]
    ppermute x7 -> x0, starting transfers between devices: 17.6 us -> none  [body(): pieces.append(lax.ppermute(tall[r], ('y', 'xh'), pairs))]
    ppermute x9 -> x12, starting transfers between devices: 10.6 us -> 15.3 us  [shift_y(): return lax.ppermute(x, 'y', [(i, (i + k) % 4) for i in range(4)])]
    all_to_all x1, waiting for transfers between devices: 0.01 us -> 3.88 us  [body(): lax.all_to_all(spread, ('z', 'xl'), 0, 0, tiled=True)]
    pallas_call x3 -> x4, Pallas kernels: 6.86 us -> 9.15 us  [the longest x2 4.48 us: join_two(): pl.pallas_call(kernel, in_specs=[VMEM] * 2, out_shape=[shape((rows, D), B...]
    ppermute x6 -> x7, starting transfers between devices: 6.32 us -> 7.96 us  [flip(): return lax.ppermute(x, axis, [(0, 1), (1, 0)])]
    unnamed x55 -> x43, local copies, waits for them, and re-layouts: 10.4 us -> 10.6 us
  transfers between devices with their start and end apart: 28 -> 25, of which waited for: 9 -> 11; matrix products, arithmetic and copies ran while one was open for 2% -> 2% of each run, Pallas kernels for 26% -> 32%
where the time goes in v6:
time: 218 us; the launch traced here: 217 us
  Pallas kernels  89.1 us (41%)
  waiting for transfers between devices  61.3 us (28%)
  starting transfers between devices  47.9 us (22%)
  local copies, waits for them, and re-layouts  13.4 us (6%)
  other arithmetic  4.89 us (2%)
    ppermute x12, waiting for transfers between devices, shift_y(): return lax.ppermute(x, 'y', [(i, (i + k) % 4) for i in range(4)])  50.4 us
    ppermute x12, starting transfers between devices, shift_y(): return lax.ppermute(x, 'y', [(i, (i + k) % 4) for i in range(4)])  15.3 us
    pallas_call x2, Pallas kernels, scores_two(): pl.pallas_call(kernel, grid_spec=pltpu.PrefetchScalarGridSpec(num_scalar_...  14.9 us
    pallas_call x1, Pallas kernels, scores_near(): pl.pallas_call(scores_near_kernel, grid_spec=pltpu.PrefetchScalarGridSpec...  10.9 us
    unnamed x43, local copies, waits for them, and re-layouts  10.6 us
    pallas_call x1, Pallas kernels, scores_far(): pl.pallas_call(scores_far_kernel, grid_spec=pltpu.PrefetchScalarGridSpec(...  10.3 us
    pallas_call x1, Pallas kernels, sums_rest(): pl.pallas_call(kernel, grid=(5,), in_specs=[pl.BlockSpec((256, 2048), lam...  10.3 us
    ppermute x7, starting transfers between devices, flip(): return lax.ppermute(x, axis, [(0, 1), (1, 0)])  7.96 us
  transfers between devices with their start and end apart: 25, of which 11 were waited for; matrix products, arithmetic and copies ran while one was open for 2% of the time, Pallas kernels for 32%

profile of v6, /device:TPU:1, one launch (start us, length us, event | category | flops | bytes accessed | tf_op | source)
XLA Modules:
  0.0 217.3 jit_solution(10648606262522099658)
XLA Ops:
  2.2 3.4 %collective-permute-start = (bf16[512,768]{1,0:T(8,128)(2,1)S(1)}, bf16[512,768]{1,0:T(8,128)(2,1)S(1)}, u32[]{:S(2)}, u32[]{:S(2)}) collective-permute-start(bf16[512,768]{1,0:T(8,128)(2,1)S(1)} %dynamic-slice_convert_fusion), channel_id=1, source_target_pairs={{0,18},{2,16},{16,2},{18,0},{1,19},{3,17},{17,3},{19,1},{4,22},{6,... | collective-permute-start | bytes 2359304 | tf_op jit(solution)/shard_map/ppermute | solution.py:537
  9.2 10.9 %scores_near.1 = (f32[2048,2048]{1,0:T(8,128)}, bf16[2048,768]{1,0:T(8,128)(2,1)}, f32[8,512]{1,0:T(8,128)}, f32[2048,128]{1,0:T(8,128)}) custom-call(s32[10]{0:T(128)} %concatenate.3.idx.idx_ref, f32[1024,768]{1,0:T(8,128)} %e_ref.1, bf16[4096,768]{1,0:T(8,128)(2,1)} %cents_ref.3, bf16[4096,768]{1,0:T(8,128)(2,1)} %cents_ref.3, ...), custom_call_target="tpu_custom_call" | custom-call | flops 3221225472 | bytes 25165824 | tf_op jit(solution)/shard_map/scores_near/pallas_call | solution.py:136
  26.8 2.9 %collective-permute-start.5 = (bf16[256,768]{1,0:T(8,128)(2,1)}, bf16[256,768]{1,0:T(8,128)(2,1)}, u32[]{:S(2)}, u32[]{:S(2)}) collective-permute-start(bf16[256,768]{1,0:T(8,128)(2,1)} %copy-done.8), channel_id=1, source_target_pairs={{0,64},{32,96},{64,0},{96,32},{1,65},{33,97},{65,1},{97,33},{2,66}... | collective-permute-start | bytes 1179656 | tf_op jit(solution)/shard_map/ppermute | solution.py:525
  30.6 10.3 %scores_far.1 = (f32[2048,2048]{1,0:T(8,128)}, bf16[2048,768]{1,0:T(8,128)(2,1)}, f32[8,512]{1,0:T(8,128)}) custom-call(s32[10]{0:T(128)} %concatenate.3.idx.idx_ref, bf16[512,768]{1,0:T(8,128)(2,1)} %copy-done.10, bf16[512,768]{1,0:T(8,128)(2,1)} %copy-done.11, bf16[4096,768]{1,0:T(8,128)(2,1)} %cents_ref.3, ...), custom_call_target="tpu_custom_call", output_to_operand_aliasing={{0}: (9, {}), {1}: (10, {})} | custom-call | tf_op jit(solution)/shard_map/scores_far/pallas_call | solution.py:164
  44.8 5.1 %all-to-all-start = ((f32[16,8,512]{2,1,0:T(8,128)}), f32[16,8,512]{2,1,0:T(8,128)S(1)}, u32[]{:S(2)}, u32[]{:S(2)}) async-start(f32[16,8,512]{2,1,0:T(8,128)} %merge_cores.1), calls=%async_computation | async-start | bytes 524288 | tf_op jit(solution)/shard_map/all_to_all | solution.py:568
  55.2 2.8 %all-to-all-done.s_ref = f32[16,8,512]{2,1,0:T(8,128)S(1)} async-done(((f32[16,8,512]{2,1,0:T(8,128)}), f32[16,8,512]{2,1,0:T(8,128)S(1)}, u32[]{:S(2)}, u32[]{:S(2)}) %all-to-all-start) | async-done | bytes 262176 | tf_op jit(solution)/shard_map/all_to_all | solution.py:568
  60.4 7.4 %sums_far.1 = (bf16[272,768]{1,0:T(8,128)(2,1)}, bf16[272,768]{1,0:T(8,128)(2,1)}, bf16[272,768]{1,0:T(8,128)(2,1)}) custom-call(f32[2048,2048]{1,0:T(8,128)} %get-tuple-element.62.p_ref, f32[1,2048]{1,0:T(1,128)} %merge_last.1.f_ref, bf16[2048,768]{1,0:T(8,128)(2,1)} %get-tuple-element.70.x_ref), custom_call_target="tpu_custom_call" | custom-call | tf_op jit(solution)/shard_map/sums_far/pallas_call | solution.py:235
  72.7 10.3 %sums_rest.1 = (bf16[272,768]{1,0:T(8,128)(2,1)}, bf16[272,768]{1,0:T(8,128)(2,1)}, bf16[272,768]{1,0:T(8,128)(2,1)}, f32[512,768]{1,0:T(8,128)}, f32[1,512]{1,0:T(1,128)}) custom-call(f32[2048,2048]{1,0:T(8,128)} %get-tuple-element.62.p_ref, f32[1,2048]{1,0:T(1,128)} %merge_last.1.f_ref, bf16[2048,768]{1,0:T(8,128)(2,1)} %get-tuple-element.70.x_ref), custom_call_target="tpu_custom_call" | custom-call | tf_op jit(solution)/shard_map/sums_rest/pallas_call | solution.py:268
  83.8 8.2 %collective-permute-done.8.g2 = bf16[272,768]{1,0:T(8,128)(2,1)} collective-permute-done((bf16[272,768]{1,0:T(8,128)(2,1)}, bf16[272,768]{1,0:T(8,128)(2,1)}, u32[]{:S(2)}, u32[]{:S(2)}) %collective-permute-start.8) | collective-permute-done | bytes 417824 | tf_op jit(solution)/shard_map/ppermute | solution.py:525
  92.0 3.4 %finish_one.2 = (bf16[256,768]{1,0:T(8,128)(2,1)}, f32[1,256]{1,0:T(1,128)}) custom-call(s32[10]{0:T(128)} %concatenate.3.idx.idx_ref, f32[512,768]{1,0:T(8,128)} %get-tuple-element.73.own_ref, f32[1,512]{1,0:T(1,128)} %get-tuple-element.81.m_ref, bf16[272,768]{1,0:T(8,128)(2,1)} %collective-permute-done.7.g1, bf16[272,768]{1,0:T(8,128)(2,1)} %collective-permute-done.8.g2, ...), custom_call_target="tpu_custom_call" | custom-call | tf_op jit(solution)/shard_map/finish_one/pallas_call | solution.py:297
  99.9 7.4 %scores_two.2 = (f32[2048,1024]{1,0:T(8,128)}, f32[2,1024]{1,0:T(2,128)}) custom-call(s32[8]{0:T(128)} %multiply_add_fusion.places_ref, bf16[256,768]{1,0:T(8,128)(2,1)} %get-tuple-element.77.a_ref.p0.x0, bf16[256,768]{1,0:T(8,128)(2,1)} %copy-done.7, bf16[512,768]{1,0:T(8,128)(2,1)} %get-tuple-element.67.refs_0_, ...), custom_call_target="tpu_custom_call" | custom-call | tf_op jit(solution)/shard_map/scores_two/pallas_call | solution.py:431
  108.1 3.4 %finish_one.3 = (bf16[256,768]{1,0:T(8,128)(2,1)}, f32[1,256]{1,0:T(1,128)}) custom-call(s32[10]{0:T(128)} %concatenate.3.idx.idx_ref, f32[512,768]{1,0:T(8,128)} %get-tuple-element.73.own_ref, f32[1,512]{1,0:T(1,128)} %get-tuple-element.81.m_ref, bf16[272,768]{1,0:T(8,128)(2,1)} %copy-done.13, bf16[272,768]{1,0:T(8,128)(2,1)} %collective-permute-done.13.g2, ...), custom_call_target="tpu_custom_call" | custom-call | tf_op jit(solution)/shard_map/finish_one/pallas_call | solution.py:297
  117.5 7.5 %scores_two.3 = (f32[2048,1024]{1,0:T(8,128)}, f32[2,1024]{1,0:T(2,128)}) custom-call(s32[8]{0:T(128)} %multiply_add_fusion.places_ref, bf16[256,768]{1,0:T(8,128)(2,1)} %get-tuple-element.90.p1.a_ref.x2, bf16[256,768]{1,0:T(8,128)(2,1)} %copy-done.6, bf16[512,768]{1,0:T(8,128)(2,1)} %get-tuple-element.67.refs_0_, ...), custom_call_target="tpu_custom_call", output_to_operand_aliasing={{0}: (10, {})} | custom-call | tf_op jit(solution)/shard_map/scores_two/pallas_call | solution.py:431
  127.0 7.6 %sums_two.1 = bf16[64,208,128]{2,1,0:T(8,128)(2,1)} custom-call(f32[2048,1024]{1,0:T(8,128)} %get-tuple-element.92.p_ref, f32[2,1024]{1,0:T(2,128)} %get-tuple-element.93.s_ref, f32[2,1024]{1,0:T(2,128)} %copy-done.20, bf16[256,768]{1,0:T(8,128)(2,1)} %get-tuple-element.77.a_ref.p0.x0, bf16[256,768]{1,0:T(8,128)(2,1)} %copy-done.7, ...), custom_call_target="tpu_custom_call" | custom-call | tf_op jit(solution)/shard_map/sums_two/pallas_call | solution.py:471
  135.4 7.3 %all-to-all-start.1 = ((bf16[64,208,128]{2,1,0:T(8,128)(2,1)}), bf16[64,208,128]{2,1,0:T(8,128)(2,1)}, u32[]{:S(2)}, u32[]{:S(2)}) async-start(bf16[64,208,128]{2,1,0:T(8,128)(2,1)} %sums_two.1), calls=%async_computation.1 | async-start | bytes 6815744 | tf_op jit(solution)/shard_map/all_to_all | solution.py:594
  145.6 2.6 %collective-permute-start.19 = (bf16[2,112,512]{2,1,0:T(8,128)(2,1)}, bf16[2,112,512]{2,1,0:T(8,128)(2,1)S(1)}, u32[]{:S(2)}, u32[]{:S(2)}) collective-permute-start(bf16[2,112,512]{2,1,0:T(8,128)(2,1)} %get-tuple-element.97), channel_id=1, source_target_pairs={{0,64},{32,96},{64,0},{96,32},{1,65},{33,97},{65,1},{97,33},{2,66}... | collective-permute-start | bytes 688136 | tf_op jit(solution)/shard_map/ppermute | solution.py:525
  149.9 37.0 %collective-permute-done.18.r1 = bf16[2,112,512]{2,1,0:T(8,128)(2,1)S(1)} collective-permute-done((bf16[2,112,512]{2,1,0:T(8,128)(2,1)}, bf16[2,112,512]{2,1,0:T(8,128)(2,1)S(1)}, u32[]{:S(2)}, u32[]{:S(2)}) %collective-permute-start.18) | collective-permute-done | bytes 229408 | tf_op jit(solution)/shard_map/ppermute | solution.py:525
  186.9 4.4 %collective-permute-done.19.r2 = bf16[2,112,512]{2,1,0:T(8,128)(2,1)S(1)} collective-permute-done((bf16[2,112,512]{2,1,0:T(8,128)(2,1)}, bf16[2,112,512]{2,1,0:T(8,128)(2,1)S(1)}, u32[]{:S(2)}, u32[]{:S(2)}) %collective-permute-start.19) | collective-permute-done | bytes 229408 | tf_op jit(solution)/shard_map/ppermute | solution.py:525
  191.4 3.3 %convert_reduce_fusion.x_ref = f32[208,128]{1,0:T(8,128)} fusion(bf16[64,208,128]{2,1,0:T(8,128)(2,1)} %all-to-all-done.1), kind=kLoop, calls=%fused_computation | loop fusion | flops 3381248 | bytes 3514368 | tf_op jit(solution)/shard_map/reduce_sum | solution.py:598
  196.5 6.3 %all-to-all-start.2 = ((bf16[8,208,128]{2,1,0:T(8,128)(2,1)}), bf16[8,208,128]{2,1,0:T(8,128)(2,1)S(1)}, u32[]{:S(2)}, u32[]{:S(2)}) async-start(bf16[8,208,128]{2,1,0:T(8,128)(2,1)} %finish_two.1), calls=%async_computation.2 | async-start | bytes 851968 | tf_op jit(solution)/shard_map/all_to_all | solution.py:601
  203.3 2.7 %gather_one.1 = (f32[96,4096]{1,0:T(8,128)}, f32[8,512]{1,0:T(8,128)}) custom-call(s32[8]{0:T(128)} %multiply_add_fusion.1.sources_ref, bf16[4,112,512]{2,1,0:T(8,128)(2,1)} %get-tuple-element.95.k_ref, bf16[4,112,512]{2,1,0:T(8,128)(2,1)} %copy-done.4, bf16[2,112,512]{2,1,0:T(8,128)(2,1)} %copy-done.16, bf16[2,112,512]{2,1,0:T(8,128)(2,1)} %copy-done.17, ...), custom_call_target="tpu_custom_call" | custom-call | tf_op jit(solution)/shard_map/gather_one/pallas_call | solution.py:356
  206.0 3.9 %all-to-all-done.2.a_ref = bf16[8,208,128]{2,1,0:T(8,128)(2,1)S(1)} async-done(((bf16[8,208,128]{2,1,0:T(8,128)(2,1)}), bf16[8,208,128]{2,1,0:T(8,128)(2,1)S(1)}, u32[]{:S(2)}, u32[]{:S(2)}) %all-to-all-start.2) | async-done | bytes 426016 | tf_op jit(solution)/shard_map/all_to_all | solution.py:601
  209.9 2.9 %collective-permute-start.21 = (bf16[8,208,128]{2,1,0:T(8,128)(2,1)S(1)}, bf16[8,208,128]{2,1,0:T(8,128)(2,1)S(1)}, u32[]{:S(2)}, u32[]{:S(2)}) collective-permute-start(bf16[8,208,128]{2,1,0:T(8,128)(2,1)S(1)} %all-to-all-done.2.a_ref), channel_id=1, source_target_pairs={{0,1},{1,0},{2,3},{3,2},{4,5},{5,4},{6,7},{7,6},{8,9},{9,8},{10,11... | collective-permute-start | bytes 1277960 | tf_op jit(solution)/shard_map/ppermute | solution.py:533
  215.0 2.4 %gather_two.1 = (f32[512,768]{1,0:T(8,128)}, f32[1,512]{1,0:T(1,128)}) custom-call(s32[1]{0:T(128)} %bitcast.4.core_ref, bf16[8,208,128]{2,1,0:T(8,128)(2,1)} %copy-done.5, bf16[8,208,128]{2,1,0:T(8,128)(2,1)} %copy-done.12), custom_call_target="tpu_custom_call" | custom-call | tf_op jit(solution)/shard_map/gather_two/pallas_call | solution.py:516
  (97 shorter events, 53.3 us)
Async XLA Ops:
  2.2 20.7 %collective-permute-start = (bf16[512,768]{1,0:T(8,128)(2,1)S(1)}, bf16[512,768]{1,0:T(8,128)(2,1)S(1)}, u32[]{:S(2)}, u32[]{:S(2)}) collective-permute-start(bf16[512,768]{1,0:T(8,128)(2,1)S(1)} %dynamic-slice_convert_fusion), channel_id=1, source_target_pairs={{0,18},{2,16},{16,2},{18,0},{1,19},{3,17},{17,3},{19,1},{4,22},{6,... | collective-permute-start | bytes 2359304 | tf_op jit(solution)/shard_map/ppermute | solution.py:537
  5.6 14.4 %collective-permute-start.1 = (bf16[256,768]{1,0:T(8,128)(2,1)S(1)}, bf16[256,768]{1,0:T(8,128)(2,1)S(1)}, u32[]{:S(2)}, u32[]{:S(2)}) collective-permute-start(bf16[256,768]{1,0:T(8,128)(2,1)S(1)} %constant_dynamic-slice_fusion.1.a_ref), channel_id=1, source_target_pairs={{0,32},{32,64},{64,96},{96,0},{1,33},{33,65},{65,97},{97,1},{2,34}... | collective-permute-start | bytes 1179656 | tf_op jit(solution)/shard_map/ppermute | solution.py:525
  7.0 15.9 %collective-permute-start.2 = (bf16[256,768]{1,0:T(8,128)(2,1)S(1)}, bf16[256,768]{1,0:T(8,128)(2,1)S(1)}, u32[]{:S(2)}, u32[]{:S(2)}) collective-permute-start(bf16[256,768]{1,0:T(8,128)(2,1)S(1)} %constant_dynamic-slice_fusion.1.a_ref), channel_id=1, source_target_pairs={{0,96},{32,0},{64,32},{96,64},{1,97},{33,1},{65,33},{97,65},{2,98}... | collective-permute-start | bytes 1179656 | tf_op jit(solution)/shard_map/ppermute | solution.py:525
  23.7 6.0 %collective-permute-start.3 = (bf16[512,768]{1,0:T(8,128)(2,1)S(1)}, bf16[512,768]{1,0:T(8,128)(2,1)S(1)}, u32[]{:S(2)}, u32[]{:S(2)}) collective-permute-start(bf16[512,768]{1,0:T(8,128)(2,1)S(1)} %collective-permute-done.a_ref), channel_id=1, source_target_pairs={{0,1},{1,0},{2,3},{3,2},{4,5},{5,4},{6,7},{7,6},{8,9},{9,8},{10,11... | collective-permute-start | bytes 2359304 | tf_op jit(solution)/shard_map/ppermute | solution.py:533
  25.1 24.8 %collective-permute-start.6 = (bf16[512,768]{1,0:T(8,128)(2,1)}, bf16[512,768]{1,0:T(8,128)(2,1)S(1)}, u32[]{:S(2)}, u32[]{:S(2)}) collective-permute-start(bf16[512,768]{1,0:T(8,128)(2,1)} %get-tuple-element.67.refs_0_), channel_id=1, source_target_pairs={{0,18},{2,16},{16,2},{18,0},{1,19},{3,17},{17,3},{19,1},{4,22},{6,... | collective-permute-start | bytes 2359304 | tf_op jit(solution)/shard_map/ppermute | solution.py:537
  26.8 23.1 %collective-permute-start.5 = (bf16[256,768]{1,0:T(8,128)(2,1)}, bf16[256,768]{1,0:T(8,128)(2,1)}, u32[]{:S(2)}, u32[]{:S(2)}) collective-permute-start(bf16[256,768]{1,0:T(8,128)(2,1)} %copy-done.8), channel_id=1, source_target_pairs={{0,64},{32,96},{64,0},{96,32},{1,65},{33,97},{65,1},{97,33},{2,66}... | collective-permute-start | bytes 1179656 | tf_op jit(solution)/shard_map/ppermute | solution.py:525
  40.9 1.7 collective-permute-start.4
  44.8 13.3 %all-to-all-start = ((f32[16,8,512]{2,1,0:T(8,128)}), f32[16,8,512]{2,1,0:T(8,128)S(1)}, u32[]{:S(2)}, u32[]{:S(2)}) async-start(f32[16,8,512]{2,1,0:T(8,128)} %merge_cores.1), calls=%async_computation | async-start | bytes 524288 | tf_op jit(solution)/shard_map/all_to_all | solution.py:568
  67.8 15.6 %collective-permute-start.7 = (bf16[272,768]{1,0:T(8,128)(2,1)}, bf16[272,768]{1,0:T(8,128)(2,1)}, u32[]{:S(2)}, u32[]{:S(2)}) collective-permute-start(bf16[272,768]{1,0:T(8,128)(2,1)} %get-tuple-element.71), channel_id=1, source_target_pairs={{0,64},{32,96},{64,0},{96,32},{1,65},{33,97},{65,1},{97,33},{2,66}... | collective-permute-start | bytes 1253384 | tf_op jit(solution)/shard_map/ppermute | solution.py:525
  69.2 22.9 %collective-permute-start.8 = (bf16[272,768]{1,0:T(8,128)(2,1)}, bf16[272,768]{1,0:T(8,128)(2,1)}, u32[]{:S(2)}, u32[]{:S(2)}) collective-permute-start(bf16[272,768]{1,0:T(8,128)(2,1)} %get-tuple-element.75), channel_id=1, source_target_pairs={{0,32},{32,64},{64,96},{96,0},{1,33},{33,65},{65,97},{97,1},{2,34}... | collective-permute-start | bytes 1253384 | tf_op jit(solution)/shard_map/ppermute | solution.py:525
  69.6 22.5 %collective-permute-start.9 = (bf16[272,768]{1,0:T(8,128)(2,1)}, bf16[272,768]{1,0:T(8,128)(2,1)}, u32[]{:S(2)}, u32[]{:S(2)}) collective-permute-start(bf16[272,768]{1,0:T(8,128)(2,1)} %get-tuple-element.76), channel_id=1, source_target_pairs={{0,96},{32,0},{64,32},{96,64},{1,97},{33,1},{65,33},{97,65},{2,98}... | collective-permute-start | bytes 1253384 | tf_op jit(solution)/shard_map/ppermute | solution.py:525
  71.8 26.4 %collective-permute-start.11 = (bf16[528,768]{1,0:T(8,128)(2,1)S(1)}, bf16[528,768]{1,0:T(8,128)(2,1)S(1)}, u32[]{:S(2)}, u32[]{:S(2)}) collective-permute-start(bf16[528,768]{1,0:T(8,128)(2,1)S(1)} %copy-done.2), channel_id=1, source_target_pairs={{0,18},{2,16},{16,2},{18,0},{1,19},{3,17},{17,3},{19,1},{4,22},{6,... | collective-permute-start | bytes 2433032 | tf_op jit(solution)/shard_map/ppermute | solution.py:537
  83.0 24.3 %collective-permute-start.12 = (bf16[272,768]{1,0:T(8,128)(2,1)}, bf16[272,768]{1,0:T(8,128)(2,1)S(1)}, u32[]{:S(2)}, u32[]{:S(2)}) collective-permute-start(bf16[272,768]{1,0:T(8,128)(2,1)} %get-tuple-element.82), channel_id=1, source_target_pairs={{0,64},{32,96},{64,0},{96,32},{1,65},{33,97},{65,1},{97,33},{2,66}... | collective-permute-start | bytes 1253384 | tf_op jit(solution)/shard_map/ppermute | solution.py:525
  83.4 24.6 %collective-permute-start.13 = (bf16[272,768]{1,0:T(8,128)(2,1)}, bf16[272,768]{1,0:T(8,128)(2,1)}, u32[]{:S(2)}, u32[]{:S(2)}) collective-permute-start(bf16[272,768]{1,0:T(8,128)(2,1)} %get-tuple-element.83), channel_id=1, source_target_pairs={{0,32},{32,64},{64,96},{96,0},{1,33},{33,65},{65,97},{97,1},{2,34}... | collective-permute-start | bytes 1253384 | tf_op jit(solution)/shard_map/ppermute | solution.py:525
  92.0 16.0 %collective-permute-start.14 = (bf16[272,768]{1,0:T(8,128)(2,1)}, bf16[272,768]{1,0:T(8,128)(2,1)}, u32[]{:S(2)}, u32[]{:S(2)}) collective-permute-start(bf16[272,768]{1,0:T(8,128)(2,1)} %get-tuple-element.84), channel_id=1, source_target_pairs={{0,96},{32,0},{64,32},{96,64},{1,97},{33,1},{65,33},{97,65},{2,98}... | collective-permute-start | bytes 1253384 | tf_op jit(solution)/shard_map/ppermute | solution.py:525
  95.4 2.8 %collective-permute-start.10 = (bf16[256,768]{1,0:T(8,128)(2,1)}, bf16[256,768]{1,0:T(8,128)(2,1)S(1)}, u32[]{:S(2)}, u32[]{:S(2)}) collective-permute-start(bf16[256,768]{1,0:T(8,128)(2,1)} %get-tuple-element.77.a_ref.p0.x0), channel_id=1, source_target_pairs={{0,1},{1,0},{2,3},{3,2},{4,5},{5,4},{6,7},{7,6},{8,9},{9,8},{10,11... | collective-permute-start | bytes 1179656 | tf_op jit(solution)/shard_map/ppermute | solution.py:533
  113.8 20.7 %collective-permute-start.15 = (bf16[4,112,512]{2,1,0:T(8,128)(2,1)}, bf16[4,112,512]{2,1,0:T(8,128)(2,1)S(1)}, u32[]{:S(2)}, u32[]{:S(2)}) collective-permute-start(bf16[4,112,512]{2,1,0:T(8,128)(2,1)} %get-tuple-element.89), channel_id=1, source_target_pairs={{0,16},{16,0},{1,17},{17,1},{2,18},{18,2},{3,19},{19,3},{4,20},{20... | collective-permute-start | bytes 1376264 | tf_op jit(solution)/shard_map/ppermute | solution.py:533
  114.4 2.3 %collective-permute-start.16 = (bf16[256,768]{1,0:T(8,128)(2,1)}, bf16[256,768]{1,0:T(8,128)(2,1)S(1)}, u32[]{:S(2)}, u32[]{:S(2)}) collective-permute-start(bf16[256,768]{1,0:T(8,128)(2,1)} %get-tuple-element.90.p1.a_ref.x2), channel_id=1, source_target_pairs={{0,1},{1,0},{2,3},{3,2},{4,5},{5,4},{6,7},{7,6},{8,9},{9,8},{10,11... | collective-permute-start | bytes 1179656 | tf_op jit(solution)/shard_map/ppermute | solution.py:533
  135.4 56.0 %all-to-all-start.1 = ((bf16[64,208,128]{2,1,0:T(8,128)(2,1)}), bf16[64,208,128]{2,1,0:T(8,128)(2,1)}, u32[]{:S(2)}, u32[]{:S(2)}) async-start(bf16[64,208,128]{2,1,0:T(8,128)(2,1)} %sums_two.1), calls=%async_computation.1 | async-start | bytes 6815744 | tf_op jit(solution)/shard_map/all_to_all | solution.py:594
  144.7 42.3 %collective-permute-start.18 = (bf16[2,112,512]{2,1,0:T(8,128)(2,1)}, bf16[2,112,512]{2,1,0:T(8,128)(2,1)S(1)}, u32[]{:S(2)}, u32[]{:S(2)}) collective-permute-start(bf16[2,112,512]{2,1,0:T(8,128)(2,1)} %get-tuple-element.96), channel_id=1, source_target_pairs={{0,32},{32,64},{64,96},{96,0},{1,33},{33,65},{65,97},{97,1},{2,34}... | collective-permute-start | bytes 688136 | tf_op jit(solution)/shard_map/ppermute | solution.py:525
  145.6 45.8 %collective-permute-start.19 = (bf16[2,112,512]{2,1,0:T(8,128)(2,1)}, bf16[2,112,512]{2,1,0:T(8,128)(2,1)S(1)}, u32[]{:S(2)}, u32[]{:S(2)}) collective-permute-start(bf16[2,112,512]{2,1,0:T(8,128)(2,1)} %get-tuple-element.97), channel_id=1, source_target_pairs={{0,64},{32,96},{64,0},{96,32},{1,65},{33,97},{65,1},{97,33},{2,66}... | collective-permute-start | bytes 688136 | tf_op jit(solution)/shard_map/ppermute | solution.py:525
  148.2 43.2 %collective-permute-start.20 = (bf16[2,112,512]{2,1,0:T(8,128)(2,1)}, bf16[2,112,512]{2,1,0:T(8,128)(2,1)S(1)}, u32[]{:S(2)}, u32[]{:S(2)}) collective-permute-start(bf16[2,112,512]{2,1,0:T(8,128)(2,1)} %get-tuple-element.98), channel_id=1, source_target_pairs={{0,96},{32,0},{64,32},{96,64},{1,97},{33,1},{65,33},{97,65},{2,98}... | collective-permute-start | bytes 688136 | tf_op jit(solution)/shard_map/ppermute | solution.py:525
  196.5 13.4 %all-to-all-start.2 = ((bf16[8,208,128]{2,1,0:T(8,128)(2,1)}), bf16[8,208,128]{2,1,0:T(8,128)(2,1)S(1)}, u32[]{:S(2)}, u32[]{:S(2)}) async-start(bf16[8,208,128]{2,1,0:T(8,128)(2,1)} %finish_two.1), calls=%async_computation.2 | async-start | bytes 851968 | tf_op jit(solution)/shard_map/all_to_all | solution.py:601
  209.9 4.3 %collective-permute-start.21 = (bf16[8,208,128]{2,1,0:T(8,128)(2,1)S(1)}, bf16[8,208,128]{2,1,0:T(8,128)(2,1)S(1)}, u32[]{:S(2)}, u32[]{:S(2)}) collective-permute-start(bf16[8,208,128]{2,1,0:T(8,128)(2,1)S(1)} %all-to-all-done.2.a_ref), channel_id=1, source_target_pairs={{0,1},{1,0},{2,3},{3,2},{4,5},{5,4},{6,7},{7,6},{8,9},{9,8},{10,11... | collective-permute-start | bytes 1277960 | tf_op jit(solution)/shard_map/ppermute | solution.py:533
  (22 other events, 92.8 us)

commit v7 on v6

--- a/solution.py
+++ b/solution.py
@@ -219,12 +219,14 @@
     )(idx, stats, local)
 
 
-def sums_far(p, factor, x, half):
+def sums_far(p, factor, x, blocks, half):
+    first, step = blocks[0], blocks[-1] - blocks[0]
+
     def kernel(p_ref, f_ref, x_ref, *refs):
         w = (p_ref[...] * f_ref[...]).astype(BF)
         sums = nn(w, x_ref[...]).astype(BF)
         packed = mass_rows(as_row(lane_sums(w))).astype(BF)
-        for q in range(3):
+        for q in range(len(blocks)):
 
             @pl.when(pl.program_id(0) == q)
             def _(q=q):
@@ -234,14 +236,14 @@
 
     return pl.pallas_call(
         kernel,
-        grid=(3,),
+        grid=(len(blocks),),
         in_specs=[
-            pl.BlockSpec((256, 2048), lambda j: ((2 - j + 3 * (j // 2)) * 2 + half, 0)),
+            pl.BlockSpec((256, 2048), lambda j: ((first + step * j) * 2 + half, 0)),
             pl.BlockSpec((1, 2048), lambda j: (0, 0)),
             pl.BlockSpec((2048, D), lambda j: (0, 0)),
         ],
-        out_specs=[pl.BlockSpec((272, D), lambda j: (0, 0))] * 3,
-        out_shape=[shape((272, D), BF)] * 3,
+        out_specs=[pl.BlockSpec((272, D), lambda j: (0, 0)) for k in blocks],
+        out_shape=[shape((272, D), BF) for k in blocks],
         name="sums_far",
     )(p, factor, x)
 
@@ -570,10 +572,11 @@
     norms_c = norms_of(after(far_a, spread))
     factor = merge_last(idx, stats, after(local, norms_b, norms_c))
 
-    parts_0 = sums_far(p, factor, x, 0)
+    parts_0 = sums_far(p, factor, x, (2,), 0)
+    parts_0 += sums_far(p, after(factor, parts_0[0]), x, (1, 3), 0)
     got_0 = [shift_y(part, k) for part, k in zip(parts_0, (2, 1, 3))]
-    far_b = flip_x(after(near_b, parts_0[0]))
-    *parts_1, own, own_mass = sums_rest(p, after(factor, parts_0[0]), x)
+    far_b = flip_x(after(near_b, parts_0[1]))
+    *parts_1, own, own_mass = sums_rest(p, after(factor, parts_0[1]), x)
     got_1 = [shift_y(part, k) for part, k in zip(parts_1, (2, 1, 3))]
     two = (near_a, near_b, far_a, far_b)
     norms_two = (norms_a, norms_b, norms_c)
@@ -593,12 +596,12 @@
     packed = after(packed, take)
     parts = lax.all_to_all(packed, ("y", "xh", "z", "xl"), 0, 0, tiled=True)
     pairs = pair_pieces(after(keep, packed), take)
-    pieces = [shift_y(t, k) for t, k in zip(pairs, (1, 2, 3))]
-    turned_one, mass_one = gather_one(sources, keep, take, pieces)
     total = jnp.sum(after(parts, pairs[0]).astype(F32), axis=0)
     rows = lax.dynamic_slice_in_dim(cents_two, c * 256 + z * 64 + xl * 32, 32, 0)
-    spread = finish_two(total, after(rows, *pieces))
-    block = after(lax.all_to_all(spread, ("z", "xl"), 0, 0, tiled=True), turned_one)
+    spread = finish_two(total, rows)
+    pieces = [shift_y(after(t, spread), k) for t, k in zip(pairs, (1, 2, 3))]
+    turned_one, mass_one = gather_one(sources, keep, take, pieces)
+    block = after(lax.all_to_all(spread, ("z", "xl"), 0, 0, tiled=True), *pieces)
     updated_two, mass_two = gather_two(c[None], block, flip(block, "c"))
     return turned_one.T, mass_one.reshape(4096), updated_two, mass_two.reshape(512)
 

time: 218 us -> 217 us (level)
  waiting for transfers between devices: 61.3 us -> 56 us
  Pallas kernels: 89.1 us -> 91.5 us
    ppermute x12, waiting for transfers between devices: 50.4 us -> 9.84 us  [shift_y(): return lax.ppermute(x, 'y', [(i, (i + k) % 4) for i in range(4)])]
    all_to_all x1, waiting for transfers between devices: 0.01 us -> 39.2 us  [body(): parts = lax.all_to_all(packed, ('y', 'xh', 'z', 'xl'), 0, 0, tiled=True)]
    all_to_all x1, waiting for transfers between devices: 3.88 us -> 0.01 us  [body(): lax.all_to_all(spread, ('z', 'xl'), 0, 0, tiled=True)]
    pallas_call x1 -> x2, Pallas kernels: 7.41 us -> 9.87 us  [sums_far(): pl.pallas_call(kernel, grid=(len(blocks),), in_specs=[pl.BlockSpec((256,...]
    ppermute x7, starting transfers between devices: 7.96 us -> 10.4 us  [flip(): return lax.ppermute(x, axis, [(0, 1), (1, 0)])]
    unnamed x43 -> x49, local copies, waits for them, and re-layouts: 10.6 us -> 10.5 us
  transfers between devices with their start and end apart: 25 -> 25, of which waited for: 11 -> 10; matrix products, arithmetic and copies ran while one was open for 2% -> 2% of each run, Pallas kernels for 32% -> 35%
where the time goes in v7:
time: 217 us; the launch traced here: 216 us
  Pallas kernels  91.5 us (42%)
  waiting for transfers between devices  56 us (26%)
  starting transfers between devices  49.1 us (23%)
  local copies, waits for them, and re-layouts  13.3 us (6%)
  other arithmetic  4.8 us (2%)
    all_to_all x1, waiting for transfers between devices, body(): parts = lax.all_to_all(packed, ('y', 'xh', 'z', 'xl'), 0, 0, tiled=True)  39.2 us
    ppermute x12, starting transfers between devices, shift_y(): return lax.ppermute(x, 'y', [(i, (i + k) % 4) for i in range(4)])  17.2 us
    pallas_call x2, Pallas kernels, scores_two(): pl.pallas_call(kernel, grid_spec=pltpu.PrefetchScalarGridSpec(num_scalar_...  14.9 us
    pallas_call x1, Pallas kernels, scores_near(): pl.pallas_call(scores_near_kernel, grid_spec=pltpu.PrefetchScalarGridSpec...  10.9 us
    unnamed x49, local copies, waits for them, and re-layouts  10.5 us
    ppermute x7, starting transfers between devices, flip(): return lax.ppermute(x, axis, [(0, 1), (1, 0)])  10.4 us
    pallas_call x1, Pallas kernels, sums_rest(): pl.pallas_call(kernel, grid=(5,), in_specs=[pl.BlockSpec((256, 2048), lam...  10.3 us
    pallas_call x1, Pallas kernels, scores_far(): pl.pallas_call(scores_far_kernel, grid_spec=pltpu.PrefetchScalarGridSpec(...  10.2 us
  transfers between devices with their start and end apart: 25, of which 10 were waited for; matrix products, arithmetic and copies ran while one was open for 2% of the time, Pallas kernels for 35%

profile of v7, /device:TPU:1, one launch (start us, length us, event | category | flops | bytes accessed | tf_op | source)
XLA Modules:
  0.0 215.5 jit_solution(15964658988730183826)
XLA Ops:
  2.2 3.4 %collective-permute-start = (bf16[512,768]{1,0:T(8,128)(2,1)S(1)}, bf16[512,768]{1,0:T(8,128)(2,1)S(1)}, u32[]{:S(2)}, u32[]{:S(2)}) collective-permute-start(bf16[512,768]{1,0:T(8,128)(2,1)S(1)} %dynamic-slice_convert_fusion), channel_id=1, source_target_pairs={{0,18},{2,16},{16,2},{18,0},{1,19},{3,17},{17,3},{19,1},{4,22},{6,... | collective-permute-start | bytes 2359304 | tf_op jit(solution)/shard_map/ppermute | solution.py:539
  9.1 10.9 %scores_near.1 = (f32[2048,2048]{1,0:T(8,128)}, bf16[2048,768]{1,0:T(8,128)(2,1)}, f32[8,512]{1,0:T(8,128)}, f32[2048,128]{1,0:T(8,128)}) custom-call(s32[10]{0:T(128)} %concatenate.3.idx.idx_ref, f32[1024,768]{1,0:T(8,128)} %e_ref.1, bf16[4096,768]{1,0:T(8,128)(2,1)} %cents_ref.3, bf16[4096,768]{1,0:T(8,128)(2,1)} %cents_ref.3, ...), custom_call_target="tpu_custom_call" | custom-call | flops 3221225472 | bytes 25165824 | tf_op jit(solution)/shard_map/scores_near/pallas_call | solution.py:136
  26.8 2.9 %collective-permute-start.5 = (bf16[256,768]{1,0:T(8,128)(2,1)}, bf16[256,768]{1,0:T(8,128)(2,1)}, u32[]{:S(2)}, u32[]{:S(2)}) collective-permute-start(bf16[256,768]{1,0:T(8,128)(2,1)} %copy-done.8), channel_id=1, source_target_pairs={{0,64},{32,96},{64,0},{96,32},{1,65},{33,97},{65,1},{97,33},{2,66}... | collective-permute-start | bytes 1179656 | tf_op jit(solution)/shard_map/ppermute | solution.py:527
  30.6 10.2 %scores_far.1 = (f32[2048,2048]{1,0:T(8,128)}, bf16[2048,768]{1,0:T(8,128)(2,1)}, f32[8,512]{1,0:T(8,128)}) custom-call(s32[10]{0:T(128)} %concatenate.3.idx.idx_ref, bf16[512,768]{1,0:T(8,128)(2,1)} %copy-done.10, bf16[512,768]{1,0:T(8,128)(2,1)} %copy-done.11, bf16[4096,768]{1,0:T(8,128)(2,1)} %cents_ref.3, ...), custom_call_target="tpu_custom_call", output_to_operand_aliasing={{0}: (9, {}), {1}: (10, {})} | custom-call | tf_op jit(solution)/shard_map/scores_far/pallas_call | solution.py:164
  44.7 5.1 %all-to-all-start = ((f32[16,8,512]{2,1,0:T(8,128)}), f32[16,8,512]{2,1,0:T(8,128)S(1)}, u32[]{:S(2)}, u32[]{:S(2)}) async-start(f32[16,8,512]{2,1,0:T(8,128)} %merge_cores.1), calls=%async_computation | async-start | bytes 524288 | tf_op jit(solution)/shard_map/all_to_all | solution.py:570
  55.2 2.8 %all-to-all-done.s_ref = f32[16,8,512]{2,1,0:T(8,128)S(1)} async-done(((f32[16,8,512]{2,1,0:T(8,128)}), f32[16,8,512]{2,1,0:T(8,128)S(1)}, u32[]{:S(2)}, u32[]{:S(2)}) %all-to-all-start) | async-done | bytes 262176 | tf_op jit(solution)/shard_map/all_to_all | solution.py:570
  60.3 4.3 %sums_far.2 = bf16[272,768]{1,0:T(8,128)(2,1)} custom-call(f32[2048,2048]{1,0:T(8,128)} %get-tuple-element.64.p_ref, f32[1,2048]{1,0:T(1,128)} %merge_last.1.f_ref, bf16[2048,768]{1,0:T(8,128)(2,1)} %get-tuple-element.72.x_ref), custom_call_target="tpu_custom_call" | custom-call | tf_op jit(solution)/shard_map/sums_far/pallas_call | solution.py:237
  66.0 5.5 %sums_far.3 = (bf16[272,768]{1,0:T(8,128)(2,1)}, bf16[272,768]{1,0:T(8,128)(2,1)}) custom-call(f32[2048,2048]{1,0:T(8,128)} %get-tuple-element.64.p_ref, f32[1,2048]{1,0:T(1,128)} %merge_last.1.f_ref, bf16[2048,768]{1,0:T(8,128)(2,1)} %get-tuple-element.72.x_ref), custom_call_target="tpu_custom_call" | custom-call | tf_op jit(solution)/shard_map/sums_far/pallas_call | solution.py:237
  75.1 10.3 %sums_rest.1 = (bf16[272,768]{1,0:T(8,128)(2,1)}, bf16[272,768]{1,0:T(8,128)(2,1)}, bf16[272,768]{1,0:T(8,128)(2,1)}, f32[512,768]{1,0:T(8,128)}, f32[1,512]{1,0:T(1,128)}) custom-call(f32[2048,2048]{1,0:T(8,128)} %get-tuple-element.64.p_ref, f32[1,2048]{1,0:T(1,128)} %merge_last.1.f_ref, bf16[2048,768]{1,0:T(8,128)(2,1)} %get-tuple-element.72.x_ref), custom_call_target="tpu_custom_call" | custom-call | tf_op jit(solution)/shard_map/sums_rest/pallas_call | solution.py:270
  88.5 3.4 %finish_one.2 = (bf16[256,768]{1,0:T(8,128)(2,1)}, f32[1,256]{1,0:T(1,128)}) custom-call(s32[10]{0:T(128)} %concatenate.3.idx.idx_ref, f32[512,768]{1,0:T(8,128)} %get-tuple-element.76.own_ref, f32[1,512]{1,0:T(1,128)} %get-tuple-element.83.m_ref, bf16[272,768]{1,0:T(8,128)(2,1)} %collective-permute-done.7.g1, bf16[272,768]{1,0:T(8,128)(2,1)} %collective-permute-done.8.g2, ...), custom_call_target="tpu_custom_call" | custom-call | tf_op jit(solution)/shard_map/finish_one/pallas_call | solution.py:299
  91.9 3.5 %collective-permute-start.10 = (bf16[256,768]{1,0:T(8,128)(2,1)}, bf16[256,768]{1,0:T(8,128)(2,1)S(1)}, u32[]{:S(2)}, u32[]{:S(2)}) collective-permute-start(bf16[256,768]{1,0:T(8,128)(2,1)} %get-tuple-element.79.a_ref.p0.x0), channel_id=1, source_target_pairs={{0,1},{1,0},{2,3},{3,2},{4,5},{5,4},{6,7},{7,6},{8,9},{9,8},{10,11... | collective-permute-start | bytes 1179656 | tf_op jit(solution)/shard_map/ppermute | solution.py:535
  98.6 7.5 %scores_two.2 = (f32[2048,1024]{1,0:T(8,128)}, f32[2,1024]{1,0:T(2,128)}) custom-call(s32[8]{0:T(128)} %multiply_add_fusion.places_ref, bf16[256,768]{1,0:T(8,128)(2,1)} %get-tuple-element.79.a_ref.p0.x0, bf16[256,768]{1,0:T(8,128)(2,1)} %copy-done.7, bf16[512,768]{1,0:T(8,128)(2,1)} %get-tuple-element.69.refs_0_, ...), custom_call_target="tpu_custom_call" | custom-call | tf_op jit(solution)/shard_map/scores_two/pallas_call | solution.py:433
  107.7 3.4 %finish_one.3 = (bf16[256,768]{1,0:T(8,128)(2,1)}, f32[1,256]{1,0:T(1,128)}) custom-call(s32[10]{0:T(128)} %concatenate.3.idx.idx_ref, f32[512,768]{1,0:T(8,128)} %get-tuple-element.76.own_ref, f32[1,512]{1,0:T(1,128)} %get-tuple-element.83.m_ref, bf16[272,768]{1,0:T(8,128)(2,1)} %copy-done.13, bf16[272,768]{1,0:T(8,128)(2,1)} %collective-permute-done.13.g2, ...), custom_call_target="tpu_custom_call" | custom-call | tf_op jit(solution)/shard_map/finish_one/pallas_call | solution.py:299
  117.8 7.4 %scores_two.3 = (f32[2048,1024]{1,0:T(8,128)}, f32[2,1024]{1,0:T(2,128)}) custom-call(s32[8]{0:T(128)} %multiply_add_fusion.places_ref, bf16[256,768]{1,0:T(8,128)(2,1)} %get-tuple-element.92.p1.a_ref.x2, bf16[256,768]{1,0:T(8,128)(2,1)} %copy-done.6, bf16[512,768]{1,0:T(8,128)(2,1)} %get-tuple-element.69.refs_0_, ...), custom_call_target="tpu_custom_call", output_to_operand_aliasing={{0}: (10, {})} | custom-call | tf_op jit(solution)/shard_map/scores_two/pallas_call | solution.py:433
  127.2 7.6 %sums_two.1 = bf16[64,208,128]{2,1,0:T(8,128)(2,1)} custom-call(f32[2048,1024]{1,0:T(8,128)} %get-tuple-element.94.p_ref, f32[2,1024]{1,0:T(2,128)} %get-tuple-element.95.s_ref, f32[2,1024]{1,0:T(2,128)} %copy-done.20, bf16[256,768]{1,0:T(8,128)(2,1)} %get-tuple-element.79.a_ref.p0.x0, bf16[256,768]{1,0:T(8,128)(2,1)} %copy-done.7, ...), custom_call_target="tpu_custom_call" | custom-call | tf_op jit(solution)/shard_map/sums_two/pallas_call | solution.py:473
  135.6 5.7 %all-to-all-start.1 = ((bf16[64,208,128]{2,1,0:T(8,128)(2,1)}), bf16[64,208,128]{2,1,0:T(8,128)(2,1)}, u32[]{:S(2)}, u32[]{:S(2)}) async-start(bf16[64,208,128]{2,1,0:T(8,128)(2,1)} %sums_two.1), calls=%async_computation.1 | async-start | bytes 6815744 | tf_op jit(solution)/shard_map/all_to_all | solution.py:597
  144.0 39.2 %all-to-all-done.1 = bf16[64,208,128]{2,1,0:T(8,128)(2,1)} async-done(((bf16[64,208,128]{2,1,0:T(8,128)(2,1)}), bf16[64,208,128]{2,1,0:T(8,128)(2,1)}, u32[]{:S(2)}, u32[]{:S(2)}) %all-to-all-start.1) | async-done | bytes 3407904 | tf_op jit(solution)/shard_map/all_to_all | solution.py:597
  183.2 3.1 %convert_reduce_fusion.x_ref = f32[208,128]{1,0:T(8,128)} fusion(bf16[64,208,128]{2,1,0:T(8,128)(2,1)} %all-to-all-done.1), kind=kLoop, calls=%fused_computation | loop fusion | flops 3381248 | bytes 3514368 | tf_op jit(solution)/shard_map/reduce_sum | solution.py:599
  188.1 4.9 %all-to-all-start.2 = ((bf16[8,208,128]{2,1,0:T(8,128)(2,1)}), bf16[8,208,128]{2,1,0:T(8,128)(2,1)S(1)}, u32[]{:S(2)}, u32[]{:S(2)}) async-start(bf16[8,208,128]{2,1,0:T(8,128)(2,1)} %finish_two.1), calls=%async_computation.2 | async-start | bytes 851968 | tf_op jit(solution)/shard_map/all_to_all | solution.py:604
  193.2 2.8 %collective-permute-start.19 = (bf16[2,112,512]{2,1,0:T(8,128)(2,1)S(1)}, bf16[2,112,512]{2,1,0:T(8,128)(2,1)S(1)}, u32[]{:S(2)}, u32[]{:S(2)}) collective-permute-start(bf16[2,112,512]{2,1,0:T(8,128)(2,1)S(1)} %copy-done.22), channel_id=1, source_target_pairs={{0,64},{32,96},{64,0},{96,32},{1,65},{33,97},{65,1},{97,33},{2,66}... | collective-permute-start | bytes 688136 | tf_op jit(solution)/shard_map/ppermute | solution.py:527
  199.2 6.1 %collective-permute-done.19.r2 = bf16[2,112,512]{2,1,0:T(8,128)(2,1)S(1)} collective-permute-done((bf16[2,112,512]{2,1,0:T(8,128)(2,1)S(1)}, bf16[2,112,512]{2,1,0:T(8,128)(2,1)S(1)}, u32[]{:S(2)}, u32[]{:S(2)}) %collective-permute-start.19) | collective-permute-done | bytes 229408 | tf_op jit(solution)/shard_map/ppermute | solution.py:527
  205.4 2.5 %collective-permute-start.21 = (bf16[8,208,128]{2,1,0:T(8,128)(2,1)S(1)}, bf16[8,208,128]{2,1,0:T(8,128)(2,1)S(1)}, u32[]{:S(2)}, u32[]{:S(2)}) collective-permute-start(bf16[8,208,128]{2,1,0:T(8,128)(2,1)S(1)} %all-to-all-done.2.a_ref), channel_id=1, source_target_pairs={{0,1},{1,0},{2,3},{3,2},{4,5},{5,4},{6,7},{7,6},{8,9},{9,8},{10,11... | collective-permute-start | bytes 1277960 | tf_op jit(solution)/shard_map/ppermute | solution.py:535
  208.4 2.7 %gather_one.1 = (f32[96,4096]{1,0:T(8,128)}, f32[8,512]{1,0:T(8,128)}) custom-call(s32[8]{0:T(128)} %multiply_add_fusion.1.sources_ref, bf16[4,112,512]{2,1,0:T(8,128)(2,1)} %get-tuple-element.97.k_ref, bf16[4,112,512]{2,1,0:T(8,128)(2,1)} %copy-done.4, bf16[2,112,512]{2,1,0:T(8,128)(2,1)} %copy-done.16, bf16[2,112,512]{2,1,0:T(8,128)(2,1)} %copy-done.17, ...), custom_call_target="tpu_custom_call" | custom-call | tf_op jit(solution)/shard_map/gather_one/pallas_call | solution.py:358
  213.2 2.4 %gather_two.1 = (f32[512,768]{1,0:T(8,128)}, f32[1,512]{1,0:T(1,128)}) custom-call(s32[1]{0:T(128)} %bitcast.4.core_ref, bf16[8,208,128]{2,1,0:T(8,128)(2,1)} %copy-done.5, bf16[8,208,128]{2,1,0:T(8,128)(2,1)} %copy-done.12), custom_call_target="tpu_custom_call" | custom-call | tf_op jit(solution)/shard_map/gather_two/pallas_call | solution.py:518
  (104 shorter events, 57.1 us)
Async XLA Ops:
  2.2 20.8 %collective-permute-start = (bf16[512,768]{1,0:T(8,128)(2,1)S(1)}, bf16[512,768]{1,0:T(8,128)(2,1)S(1)}, u32[]{:S(2)}, u32[]{:S(2)}) collective-permute-start(bf16[512,768]{1,0:T(8,128)(2,1)S(1)} %dynamic-slice_convert_fusion), channel_id=1, source_target_pairs={{0,18},{2,16},{16,2},{18,0},{1,19},{3,17},{17,3},{19,1},{4,22},{6,... | collective-permute-start | bytes 2359304 | tf_op jit(solution)/shard_map/ppermute | solution.py:539
  5.6 14.4 %collective-permute-start.1 = (bf16[256,768]{1,0:T(8,128)(2,1)S(1)}, bf16[256,768]{1,0:T(8,128)(2,1)S(1)}, u32[]{:S(2)}, u32[]{:S(2)}) collective-permute-start(bf16[256,768]{1,0:T(8,128)(2,1)S(1)} %constant_dynamic-slice_fusion.1.a_ref), channel_id=1, source_target_pairs={{0,32},{32,64},{64,96},{96,0},{1,33},{33,65},{65,97},{97,1},{2,34}... | collective-permute-start | bytes 1179656 | tf_op jit(solution)/shard_map/ppermute | solution.py:527
  7.0 16.0 %collective-permute-start.2 = (bf16[256,768]{1,0:T(8,128)(2,1)S(1)}, bf16[256,768]{1,0:T(8,128)(2,1)S(1)}, u32[]{:S(2)}, u32[]{:S(2)}) collective-permute-start(bf16[256,768]{1,0:T(8,128)(2,1)S(1)} %constant_dynamic-slice_fusion.1.a_ref), channel_id=1, source_target_pairs={{0,96},{32,0},{64,32},{96,64},{1,97},{33,1},{65,33},{97,65},{2,98}... | collective-permute-start | bytes 1179656 | tf_op jit(solution)/shard_map/ppermute | solution.py:527
  23.8 5.9 %collective-permute-start.3 = (bf16[512,768]{1,0:T(8,128)(2,1)S(1)}, bf16[512,768]{1,0:T(8,128)(2,1)S(1)}, u32[]{:S(2)}, u32[]{:S(2)}) collective-permute-start(bf16[512,768]{1,0:T(8,128)(2,1)S(1)} %collective-permute-done.a_ref), channel_id=1, source_target_pairs={{0,1},{1,0},{2,3},{3,2},{4,5},{5,4},{6,7},{7,6},{8,9},{9,8},{10,11... | collective-permute-start | bytes 2359304 | tf_op jit(solution)/shard_map/ppermute | solution.py:535
  25.1 24.7 %collective-permute-start.6 = (bf16[512,768]{1,0:T(8,128)(2,1)}, bf16[512,768]{1,0:T(8,128)(2,1)S(1)}, u32[]{:S(2)}, u32[]{:S(2)}) collective-permute-start(bf16[512,768]{1,0:T(8,128)(2,1)} %get-tuple-element.69.refs_0_), channel_id=1, source_target_pairs={{0,18},{2,16},{16,2},{18,0},{1,19},{3,17},{17,3},{19,1},{4,22},{6,... | collective-permute-start | bytes 2359304 | tf_op jit(solution)/shard_map/ppermute | solution.py:539
  26.8 23.1 %collective-permute-start.5 = (bf16[256,768]{1,0:T(8,128)(2,1)}, bf16[256,768]{1,0:T(8,128)(2,1)}, u32[]{:S(2)}, u32[]{:S(2)}) collective-permute-start(bf16[256,768]{1,0:T(8,128)(2,1)} %copy-done.8), channel_id=1, source_target_pairs={{0,64},{32,96},{64,0},{96,32},{1,65},{33,97},{65,1},{97,33},{2,66}... | collective-permute-start | bytes 1179656 | tf_op jit(solution)/shard_map/ppermute | solution.py:527
  40.9 1.8 collective-permute-start.4
  44.7 13.3 %all-to-all-start = ((f32[16,8,512]{2,1,0:T(8,128)}), f32[16,8,512]{2,1,0:T(8,128)S(1)}, u32[]{:S(2)}, u32[]{:S(2)}) async-start(f32[16,8,512]{2,1,0:T(8,128)} %merge_cores.1), calls=%async_computation | async-start | bytes 524288 | tf_op jit(solution)/shard_map/all_to_all | solution.py:570
  64.7 21.1 %collective-permute-start.7 = (bf16[272,768]{1,0:T(8,128)(2,1)}, bf16[272,768]{1,0:T(8,128)(2,1)}, u32[]{:S(2)}, u32[]{:S(2)}) collective-permute-start(bf16[272,768]{1,0:T(8,128)(2,1)} %sums_far.2), channel_id=1, source_target_pairs={{0,64},{32,96},{64,0},{96,32},{1,65},{33,97},{65,1},{97,33},{2,66}... | collective-permute-start | bytes 1253384 | tf_op jit(solution)/shard_map/ppermute | solution.py:527
  71.6 14.7 %collective-permute-start.8 = (bf16[272,768]{1,0:T(8,128)(2,1)}, bf16[272,768]{1,0:T(8,128)(2,1)}, u32[]{:S(2)}, u32[]{:S(2)}) collective-permute-start(bf16[272,768]{1,0:T(8,128)(2,1)} %get-tuple-element.74), channel_id=1, source_target_pairs={{0,32},{32,64},{64,96},{96,0},{1,33},{33,65},{65,97},{97,1},{2,34}... | collective-permute-start | bytes 1253384 | tf_op jit(solution)/shard_map/ppermute | solution.py:527
  72.0 16.5 %collective-permute-start.9 = (bf16[272,768]{1,0:T(8,128)(2,1)}, bf16[272,768]{1,0:T(8,128)(2,1)}, u32[]{:S(2)}, u32[]{:S(2)}) collective-permute-start(bf16[272,768]{1,0:T(8,128)(2,1)} %get-tuple-element.78), channel_id=1, source_target_pairs={{0,96},{32,0},{64,32},{96,64},{1,97},{33,1},{65,33},{97,65},{2,98}... | collective-permute-start | bytes 1253384 | tf_op jit(solution)/shard_map/ppermute | solution.py:527
  74.2 22.7 %collective-permute-start.11 = (bf16[528,768]{1,0:T(8,128)(2,1)S(1)}, bf16[528,768]{1,0:T(8,128)(2,1)S(1)}, u32[]{:S(2)}, u32[]{:S(2)}) collective-permute-start(bf16[528,768]{1,0:T(8,128)(2,1)S(1)} %copy-done.2), channel_id=1, source_target_pairs={{0,18},{2,16},{16,2},{18,0},{1,19},{3,17},{17,3},{19,1},{4,22},{6,... | collective-permute-start | bytes 2433032 | tf_op jit(solution)/shard_map/ppermute | solution.py:539
  85.4 20.6 %collective-permute-start.12 = (bf16[272,768]{1,0:T(8,128)(2,1)}, bf16[272,768]{1,0:T(8,128)(2,1)S(1)}, u32[]{:S(2)}, u32[]{:S(2)}) collective-permute-start(bf16[272,768]{1,0:T(8,128)(2,1)} %get-tuple-element.84), channel_id=1, source_target_pairs={{0,64},{32,96},{64,0},{96,32},{1,65},{33,97},{65,1},{97,33},{2,66}... | collective-permute-start | bytes 1253384 | tf_op jit(solution)/shard_map/ppermute | solution.py:527
  85.8 21.9 %collective-permute-start.13 = (bf16[272,768]{1,0:T(8,128)(2,1)}, bf16[272,768]{1,0:T(8,128)(2,1)}, u32[]{:S(2)}, u32[]{:S(2)}) collective-permute-start(bf16[272,768]{1,0:T(8,128)(2,1)} %get-tuple-element.85), channel_id=1, source_target_pairs={{0,32},{32,64},{64,96},{96,0},{1,33},{33,65},{65,97},{97,1},{2,34}... | collective-permute-start | bytes 1253384 | tf_op jit(solution)/shard_map/ppermute | solution.py:527
  86.2 21.5 %collective-permute-start.14 = (bf16[272,768]{1,0:T(8,128)(2,1)}, bf16[272,768]{1,0:T(8,128)(2,1)}, u32[]{:S(2)}, u32[]{:S(2)}) collective-permute-start(bf16[272,768]{1,0:T(8,128)(2,1)} %get-tuple-element.86), channel_id=1, source_target_pairs={{0,96},{32,0},{64,32},{96,64},{1,97},{33,1},{65,33},{97,65},{2,98}... | collective-permute-start | bytes 1253384 | tf_op jit(solution)/shard_map/ppermute | solution.py:527
  91.9 5.0 %collective-permute-start.10 = (bf16[256,768]{1,0:T(8,128)(2,1)}, bf16[256,768]{1,0:T(8,128)(2,1)S(1)}, u32[]{:S(2)}, u32[]{:S(2)}) collective-permute-start(bf16[256,768]{1,0:T(8,128)(2,1)} %get-tuple-element.79.a_ref.p0.x0), channel_id=1, source_target_pairs={{0,1},{1,0},{2,3},{3,2},{4,5},{5,4},{6,7},{7,6},{8,9},{9,8},{10,11... | collective-permute-start | bytes 1179656 | tf_op jit(solution)/shard_map/ppermute | solution.py:535
  113.5 21.3 %collective-permute-start.15 = (bf16[4,112,512]{2,1,0:T(8,128)(2,1)}, bf16[4,112,512]{2,1,0:T(8,128)(2,1)S(1)}, u32[]{:S(2)}, u32[]{:S(2)}) collective-permute-start(bf16[4,112,512]{2,1,0:T(8,128)(2,1)} %get-tuple-element.91), channel_id=1, source_target_pairs={{0,16},{16,0},{1,17},{17,1},{2,18},{18,2},{3,19},{19,3},{4,20},{20... | collective-permute-start | bytes 1376264 | tf_op jit(solution)/shard_map/ppermute | solution.py:535
  114.7 2.3 %collective-permute-start.16 = (bf16[256,768]{1,0:T(8,128)(2,1)}, bf16[256,768]{1,0:T(8,128)(2,1)S(1)}, u32[]{:S(2)}, u32[]{:S(2)}) collective-permute-start(bf16[256,768]{1,0:T(8,128)(2,1)} %get-tuple-element.92.p1.a_ref.x2), channel_id=1, source_target_pairs={{0,1},{1,0},{2,3},{3,2},{4,5},{5,4},{6,7},{7,6},{8,9},{9,8},{10,11... | collective-permute-start | bytes 1179656 | tf_op jit(solution)/shard_map/ppermute | solution.py:535
  135.6 47.6 %all-to-all-start.1 = ((bf16[64,208,128]{2,1,0:T(8,128)(2,1)}), bf16[64,208,128]{2,1,0:T(8,128)(2,1)}, u32[]{:S(2)}, u32[]{:S(2)}) async-start(bf16[64,208,128]{2,1,0:T(8,128)(2,1)} %sums_two.1), calls=%async_computation.1 | async-start | bytes 6815744 | tf_op jit(solution)/shard_map/all_to_all | solution.py:597
  188.1 17.2 %all-to-all-start.2 = ((bf16[8,208,128]{2,1,0:T(8,128)(2,1)}), bf16[8,208,128]{2,1,0:T(8,128)(2,1)S(1)}, u32[]{:S(2)}, u32[]{:S(2)}) async-start(bf16[8,208,128]{2,1,0:T(8,128)(2,1)} %finish_two.1), calls=%async_computation.2 | async-start | bytes 851968 | tf_op jit(solution)/shard_map/all_to_all | solution.py:604
  193.0 6.2 %collective-permute-start.18 = (bf16[2,112,512]{2,1,0:T(8,128)(2,1)S(1)}, bf16[2,112,512]{2,1,0:T(8,128)(2,1)S(1)}, u32[]{:S(2)}, u32[]{:S(2)}) collective-permute-start(bf16[2,112,512]{2,1,0:T(8,128)(2,1)S(1)} %copy-done.23), channel_id=1, source_target_pairs={{0,32},{32,64},{64,96},{96,0},{1,33},{33,65},{65,97},{97,1},{2,34}... | collective-permute-start | bytes 688136 | tf_op jit(solution)/shard_map/ppermute | solution.py:527
  193.2 12.1 %collective-permute-start.19 = (bf16[2,112,512]{2,1,0:T(8,128)(2,1)S(1)}, bf16[2,112,512]{2,1,0:T(8,128)(2,1)S(1)}, u32[]{:S(2)}, u32[]{:S(2)}) collective-permute-start(bf16[2,112,512]{2,1,0:T(8,128)(2,1)S(1)} %copy-done.22), channel_id=1, source_target_pairs={{0,64},{32,96},{64,0},{96,32},{1,65},{33,97},{65,1},{97,33},{2,66}... | collective-permute-start | bytes 688136 | tf_op jit(solution)/shard_map/ppermute | solution.py:527
  195.9 9.4 %collective-permute-start.20 = (bf16[2,112,512]{2,1,0:T(8,128)(2,1)S(1)}, bf16[2,112,512]{2,1,0:T(8,128)(2,1)S(1)}, u32[]{:S(2)}, u32[]{:S(2)}) collective-permute-start(bf16[2,112,512]{2,1,0:T(8,128)(2,1)S(1)} %copy-done.21), channel_id=1, source_target_pairs={{0,96},{32,0},{64,32},{96,64},{1,97},{33,1},{65,33},{97,65},{2,98}... | collective-permute-start | bytes 688136 | tf_op jit(solution)/shard_map/ppermute | solution.py:527
  205.4 7.0 %collective-permute-start.21 = (bf16[8,208,128]{2,1,0:T(8,128)(2,1)S(1)}, bf16[8,208,128]{2,1,0:T(8,128)(2,1)S(1)}, u32[]{:S(2)}, u32[]{:S(2)}) collective-permute-start(bf16[8,208,128]{2,1,0:T(8,128)(2,1)S(1)} %all-to-all-done.2.a_ref), channel_id=1, source_target_pairs={{0,1},{1,0},{2,3},{3,2},{4,5},{5,4},{6,7},{7,6},{8,9},{9,8},{10,11... | collective-permute-start | bytes 1277960 | tf_op jit(solution)/shard_map/ppermute | solution.py:535
  (25 other events, 219.8 us)

commit v8 on v7

--- a/solution.py
+++ b/solution.py
@@ -353,12 +353,12 @@
             block = sources_ref[r]
             o_ref[:, pl.ds(pl.multiple_of(block * 512, 512), 512)] = piece[0:96, :].astype(F32)
             t = piece[96:112, :].astype(F32)
-            m_ref[pl.ds(block, 1), :] = t[0:1] + t[1:2] + t[2:3]
+            m_ref[:, pl.ds(pl.multiple_of(block * 512, 512), 512)] = t[0:1] + t[1:2] + t[2:3]
 
     return pl.pallas_call(
         kernel,
         in_specs=[SMEM] + [VMEM] * 5,
-        out_shape=[shape((96, 4096), F32), shape((8, 512), F32)],
+        out_shape=[shape((96, 4096), F32), shape((1, 4096), F32)],
         name="gather_one",
     )(sources, keep, take, *pieces)
 

time: 217 us -> 215 us (level)
    unnamed x49 -> x48, local copies, waits for them, and re-layouts: 10.5 us -> 9.19 us
  transfers between devices with their start and end apart: 25 -> 25, of which waited for: 10 -> 10; matrix products, arithmetic and copies ran while one was open for 2% -> 1% of each run, Pallas kernels for 35% -> 35%
where the time goes in v8:
time: 215 us; the launch traced here: 214 us
  Pallas kernels  91.5 us (43%)
  waiting for transfers between devices  56 us (26%)
  starting transfers between devices  49.1 us (23%)
  local copies, waits for them, and re-layouts  12 us (6%)
  other arithmetic  4.8 us (2%)
    all_to_all x1, waiting for transfers between devices, body(): parts = lax.all_to_all(packed, ('y', 'xh', 'z', 'xl'), 0, 0, tiled=True)  39.2 us
    ppermute x12, starting transfers between devices, shift_y(): return lax.ppermute(x, 'y', [(i, (i + k) % 4) for i in range(4)])  17.2 us
    pallas_call x2, Pallas kernels, scores_two(): pl.pallas_call(kernel, grid_spec=pltpu.PrefetchScalarGridSpec(num_scalar_...  14.9 us
    pallas_call x1, Pallas kernels, scores_near(): pl.pallas_call(scores_near_kernel, grid_spec=pltpu.PrefetchScalarGridSpec...  10.9 us
    ppermute x7, starting transfers between devices, flip(): return lax.ppermute(x, axis, [(0, 1), (1, 0)])  10.4 us
    pallas_call x1, Pallas kernels, sums_rest(): pl.pallas_call(kernel, grid=(5,), in_specs=[pl.BlockSpec((256, 2048), lam...  10.3 us
    pallas_call x1, Pallas kernels, scores_far(): pl.pallas_call(scores_far_kernel, grid_spec=pltpu.PrefetchScalarGridSpec(...  10.2 us
    pallas_call x2, Pallas kernels, sums_far(): pl.pallas_call(kernel, grid=(len(blocks),), in_specs=[pl.BlockSpec((256,...  9.87 us
  transfers between devices with their start and end apart: 25, of which 10 were waited for; matrix products, arithmetic and copies ran while one was open for 1% of the time, Pallas kernels for 35%

profile of v8, /device:TPU:1, one launch (start us, length us, event | category | flops | bytes accessed | tf_op | source)
XLA Modules:
  0.0 214.2 jit_solution(12594423547061095208)
XLA Ops:
  2.2 3.4 %collective-permute-start = (bf16[512,768]{1,0:T(8,128)(2,1)S(1)}, bf16[512,768]{1,0:T(8,128)(2,1)S(1)}, u32[]{:S(2)}, u32[]{:S(2)}) collective-permute-start(bf16[512,768]{1,0:T(8,128)(2,1)S(1)} %dynamic-slice_convert_fusion), channel_id=1, source_target_pairs={{0,18},{2,16},{16,2},{18,0},{1,19},{3,17},{17,3},{19,1},{4,22},{6,... | collective-permute-start | bytes 2359304 | tf_op jit(solution)/shard_map/ppermute | solution.py:539
  9.1 10.9 %scores_near.1 = (f32[2048,2048]{1,0:T(8,128)}, bf16[2048,768]{1,0:T(8,128)(2,1)}, f32[8,512]{1,0:T(8,128)}, f32[2048,128]{1,0:T(8,128)}) custom-call(s32[10]{0:T(128)} %concatenate.3.idx.idx_ref, f32[1024,768]{1,0:T(8,128)} %e_ref.1, bf16[4096,768]{1,0:T(8,128)(2,1)} %cents_ref.3, bf16[4096,768]{1,0:T(8,128)(2,1)} %cents_ref.3, ...), custom_call_target="tpu_custom_call" | custom-call | flops 3221225472 | bytes 25165824 | tf_op jit(solution)/shard_map/scores_near/pallas_call | solution.py:136
  26.8 2.9 %collective-permute-start.5 = (bf16[256,768]{1,0:T(8,128)(2,1)}, bf16[256,768]{1,0:T(8,128)(2,1)}, u32[]{:S(2)}, u32[]{:S(2)}) collective-permute-start(bf16[256,768]{1,0:T(8,128)(2,1)} %copy-done.8), channel_id=1, source_target_pairs={{0,64},{32,96},{64,0},{96,32},{1,65},{33,97},{65,1},{97,33},{2,66}... | collective-permute-start | bytes 1179656 | tf_op jit(solution)/shard_map/ppermute | solution.py:527
  30.6 10.2 %scores_far.1 = (f32[2048,2048]{1,0:T(8,128)}, bf16[2048,768]{1,0:T(8,128)(2,1)}, f32[8,512]{1,0:T(8,128)}) custom-call(s32[10]{0:T(128)} %concatenate.3.idx.idx_ref, bf16[512,768]{1,0:T(8,128)(2,1)} %copy-done.10, bf16[512,768]{1,0:T(8,128)(2,1)} %copy-done.11, bf16[4096,768]{1,0:T(8,128)(2,1)} %cents_ref.3, ...), custom_call_target="tpu_custom_call", output_to_operand_aliasing={{0}: (9, {}), {1}: (10, {})} | custom-call | tf_op jit(solution)/shard_map/scores_far/pallas_call | solution.py:164
  44.7 5.1 %all-to-all-start = ((f32[16,8,512]{2,1,0:T(8,128)}), f32[16,8,512]{2,1,0:T(8,128)S(1)}, u32[]{:S(2)}, u32[]{:S(2)}) async-start(f32[16,8,512]{2,1,0:T(8,128)} %merge_cores.1), calls=%async_computation | async-start | bytes 524288 | tf_op jit(solution)/shard_map/all_to_all | solution.py:570
  55.2 2.8 %all-to-all-done.s_ref = f32[16,8,512]{2,1,0:T(8,128)S(1)} async-done(((f32[16,8,512]{2,1,0:T(8,128)}), f32[16,8,512]{2,1,0:T(8,128)S(1)}, u32[]{:S(2)}, u32[]{:S(2)}) %all-to-all-start) | async-done | bytes 262176 | tf_op jit(solution)/shard_map/all_to_all | solution.py:570
  60.3 4.3 %sums_far.2 = bf16[272,768]{1,0:T(8,128)(2,1)} custom-call(f32[2048,2048]{1,0:T(8,128)} %get-tuple-element.64.p_ref, f32[1,2048]{1,0:T(1,128)} %merge_last.1.f_ref, bf16[2048,768]{1,0:T(8,128)(2,1)} %get-tuple-element.72.x_ref), custom_call_target="tpu_custom_call" | custom-call | tf_op jit(solution)/shard_map/sums_far/pallas_call | solution.py:237
  66.0 5.5 %sums_far.3 = (bf16[272,768]{1,0:T(8,128)(2,1)}, bf16[272,768]{1,0:T(8,128)(2,1)}) custom-call(f32[2048,2048]{1,0:T(8,128)} %get-tuple-element.64.p_ref, f32[1,2048]{1,0:T(1,128)} %merge_last.1.f_ref, bf16[2048,768]{1,0:T(8,128)(2,1)} %get-tuple-element.72.x_ref), custom_call_target="tpu_custom_call" | custom-call | tf_op jit(solution)/shard_map/sums_far/pallas_call | solution.py:237
  75.1 10.3 %sums_rest.1 = (bf16[272,768]{1,0:T(8,128)(2,1)}, bf16[272,768]{1,0:T(8,128)(2,1)}, bf16[272,768]{1,0:T(8,128)(2,1)}, f32[512,768]{1,0:T(8,128)}, f32[1,512]{1,0:T(1,128)}) custom-call(f32[2048,2048]{1,0:T(8,128)} %get-tuple-element.64.p_ref, f32[1,2048]{1,0:T(1,128)} %merge_last.1.f_ref, bf16[2048,768]{1,0:T(8,128)(2,1)} %get-tuple-element.72.x_ref), custom_call_target="tpu_custom_call" | custom-call | tf_op jit(solution)/shard_map/sums_rest/pallas_call | solution.py:270
  88.5 3.4 %finish_one.2 = (bf16[256,768]{1,0:T(8,128)(2,1)}, f32[1,256]{1,0:T(1,128)}) custom-call(s32[10]{0:T(128)} %concatenate.3.idx.idx_ref, f32[512,768]{1,0:T(8,128)} %get-tuple-element.76.own_ref, f32[1,512]{1,0:T(1,128)} %get-tuple-element.83.m_ref, bf16[272,768]{1,0:T(8,128)(2,1)} %collective-permute-done.7.g1, bf16[272,768]{1,0:T(8,128)(2,1)} %collective-permute-done.8.g2, ...), custom_call_target="tpu_custom_call" | custom-call | tf_op jit(solution)/shard_map/finish_one/pallas_call | solution.py:299
  91.9 3.5 %collective-permute-start.10 = (bf16[256,768]{1,0:T(8,128)(2,1)}, bf16[256,768]{1,0:T(8,128)(2,1)S(1)}, u32[]{:S(2)}, u32[]{:S(2)}) collective-permute-start(bf16[256,768]{1,0:T(8,128)(2,1)} %get-tuple-element.79.a_ref.p0.x0), channel_id=1, source_target_pairs={{0,1},{1,0},{2,3},{3,2},{4,5},{5,4},{6,7},{7,6},{8,9},{9,8},{10,11... | collective-permute-start | bytes 1179656 | tf_op jit(solution)/shard_map/ppermute | solution.py:535
  98.6 7.5 %scores_two.2 = (f32[2048,1024]{1,0:T(8,128)}, f32[2,1024]{1,0:T(2,128)}) custom-call(s32[8]{0:T(128)} %multiply_add_fusion.places_ref, bf16[256,768]{1,0:T(8,128)(2,1)} %get-tuple-element.79.a_ref.p0.x0, bf16[256,768]{1,0:T(8,128)(2,1)} %copy-done.7, bf16[512,768]{1,0:T(8,128)(2,1)} %get-tuple-element.69.refs_0_, ...), custom_call_target="tpu_custom_call" | custom-call | tf_op jit(solution)/shard_map/scores_two/pallas_call | solution.py:433
  107.7 3.4 %finish_one.3 = (bf16[256,768]{1,0:T(8,128)(2,1)}, f32[1,256]{1,0:T(1,128)}) custom-call(s32[10]{0:T(128)} %concatenate.3.idx.idx_ref, f32[512,768]{1,0:T(8,128)} %get-tuple-element.76.own_ref, f32[1,512]{1,0:T(1,128)} %get-tuple-element.83.m_ref, bf16[272,768]{1,0:T(8,128)(2,1)} %copy-done.13, bf16[272,768]{1,0:T(8,128)(2,1)} %collective-permute-done.13.g2, ...), custom_call_target="tpu_custom_call" | custom-call | tf_op jit(solution)/shard_map/finish_one/pallas_call | solution.py:299
  117.8 7.4 %scores_two.3 = (f32[2048,1024]{1,0:T(8,128)}, f32[2,1024]{1,0:T(2,128)}) custom-call(s32[8]{0:T(128)} %multiply_add_fusion.places_ref, bf16[256,768]{1,0:T(8,128)(2,1)} %get-tuple-element.92.p1.a_ref.x2, bf16[256,768]{1,0:T(8,128)(2,1)} %copy-done.6, bf16[512,768]{1,0:T(8,128)(2,1)} %get-tuple-element.69.refs_0_, ...), custom_call_target="tpu_custom_call", output_to_operand_aliasing={{0}: (10, {})} | custom-call | tf_op jit(solution)/shard_map/scores_two/pallas_call | solution.py:433
  127.2 7.6 %sums_two.1 = bf16[64,208,128]{2,1,0:T(8,128)(2,1)} custom-call(f32[2048,1024]{1,0:T(8,128)} %get-tuple-element.94.p_ref, f32[2,1024]{1,0:T(2,128)} %get-tuple-element.95.s_ref, f32[2,1024]{1,0:T(2,128)} %copy-done.20, bf16[256,768]{1,0:T(8,128)(2,1)} %get-tuple-element.79.a_ref.p0.x0, bf16[256,768]{1,0:T(8,128)(2,1)} %copy-done.7, ...), custom_call_target="tpu_custom_call" | custom-call | tf_op jit(solution)/shard_map/sums_two/pallas_call | solution.py:473
  135.6 5.7 %all-to-all-start.1 = ((bf16[64,208,128]{2,1,0:T(8,128)(2,1)}), bf16[64,208,128]{2,1,0:T(8,128)(2,1)}, u32[]{:S(2)}, u32[]{:S(2)}) async-start(bf16[64,208,128]{2,1,0:T(8,128)(2,1)} %sums_two.1), calls=%async_computation.1 | async-start | bytes 6815744 | tf_op jit(solution)/shard_map/all_to_all | solution.py:597
  144.0 39.2 %all-to-all-done.1 = bf16[64,208,128]{2,1,0:T(8,128)(2,1)} async-done(((bf16[64,208,128]{2,1,0:T(8,128)(2,1)}), bf16[64,208,128]{2,1,0:T(8,128)(2,1)}, u32[]{:S(2)}, u32[]{:S(2)}) %all-to-all-start.1) | async-done | bytes 3407904 | tf_op jit(solution)/shard_map/all_to_all | solution.py:597
  183.2 3.1 %convert_reduce_fusion.x_ref = f32[208,128]{1,0:T(8,128)} fusion(bf16[64,208,128]{2,1,0:T(8,128)(2,1)} %all-to-all-done.1), kind=kLoop, calls=%fused_computation | loop fusion | flops 3381248 | bytes 3514368 | tf_op jit(solution)/shard_map/reduce_sum | solution.py:599
  188.1 4.9 %all-to-all-start.2 = ((bf16[8,208,128]{2,1,0:T(8,128)(2,1)}), bf16[8,208,128]{2,1,0:T(8,128)(2,1)S(1)}, u32[]{:S(2)}, u32[]{:S(2)}) async-start(bf16[8,208,128]{2,1,0:T(8,128)(2,1)} %finish_two.1), calls=%async_computation.2 | async-start | bytes 851968 | tf_op jit(solution)/shard_map/all_to_all | solution.py:604
  193.2 2.8 %collective-permute-start.19 = (bf16[2,112,512]{2,1,0:T(8,128)(2,1)S(1)}, bf16[2,112,512]{2,1,0:T(8,128)(2,1)S(1)}, u32[]{:S(2)}, u32[]{:S(2)}) collective-permute-start(bf16[2,112,512]{2,1,0:T(8,128)(2,1)S(1)} %copy-done.22), channel_id=1, source_target_pairs={{0,64},{32,96},{64,0},{96,32},{1,65},{33,97},{65,1},{97,33},{2,66}... | collective-permute-start | bytes 688136 | tf_op jit(solution)/shard_map/ppermute | solution.py:527
  199.2 6.1 %collective-permute-done.19.r2 = bf16[2,112,512]{2,1,0:T(8,128)(2,1)S(1)} collective-permute-done((bf16[2,112,512]{2,1,0:T(8,128)(2,1)S(1)}, bf16[2,112,512]{2,1,0:T(8,128)(2,1)S(1)}, u32[]{:S(2)}, u32[]{:S(2)}) %collective-permute-start.19) | collective-permute-done | bytes 229408 | tf_op jit(solution)/shard_map/ppermute | solution.py:527
  205.4 2.5 %collective-permute-start.21 = (bf16[8,208,128]{2,1,0:T(8,128)(2,1)S(1)}, bf16[8,208,128]{2,1,0:T(8,128)(2,1)S(1)}, u32[]{:S(2)}, u32[]{:S(2)}) collective-permute-start(bf16[8,208,128]{2,1,0:T(8,128)(2,1)S(1)} %all-to-all-done.2.a_ref), channel_id=1, source_target_pairs={{0,1},{1,0},{2,3},{3,2},{4,5},{5,4},{6,7},{7,6},{8,9},{9,8},{10,11... | collective-permute-start | bytes 1277960 | tf_op jit(solution)/shard_map/ppermute | solution.py:535
  208.4 2.7 %gather_one.1 = (f32[96,4096]{1,0:T(8,128)}, f32[1,4096]{1,0:T(1,128)}) custom-call(s32[8]{0:T(128)} %multiply_add_fusion.1.sources_ref, bf16[4,112,512]{2,1,0:T(8,128)(2,1)} %get-tuple-element.97.k_ref, bf16[4,112,512]{2,1,0:T(8,128)(2,1)} %copy-done.4, bf16[2,112,512]{2,1,0:T(8,128)(2,1)} %copy-done.16, bf16[2,112,512]{2,1,0:T(8,128)(2,1)} %copy-done.17, ...), custom_call_target="tpu_custom_call" | custom-call | tf_op jit(solution)/shard_map/gather_one/pallas_call | solution.py:358
  211.8 2.4 %gather_two.1 = (f32[512,768]{1,0:T(8,128)}, f32[1,512]{1,0:T(1,128)}) custom-call(s32[1]{0:T(128)} %bitcast.4.core_ref, bf16[8,208,128]{2,1,0:T(8,128)(2,1)} %copy-done.5, bf16[8,208,128]{2,1,0:T(8,128)(2,1)} %copy-done.12), custom_call_target="tpu_custom_call" | custom-call | tf_op jit(solution)/shard_map/gather_two/pallas_call | solution.py:518
  (103 shorter events, 55.8 us)
Async XLA Ops:
  2.2 20.8 %collective-permute-start = (bf16[512,768]{1,0:T(8,128)(2,1)S(1)}, bf16[512,768]{1,0:T(8,128)(2,1)S(1)}, u32[]{:S(2)}, u32[]{:S(2)}) collective-permute-start(bf16[512,768]{1,0:T(8,128)(2,1)S(1)} %dynamic-slice_convert_fusion), channel_id=1, source_target_pairs={{0,18},{2,16},{16,2},{18,0},{1,19},{3,17},{17,3},{19,1},{4,22},{6,... | collective-permute-start | bytes 2359304 | tf_op jit(solution)/shard_map/ppermute | solution.py:539
  5.6 14.4 %collective-permute-start.1 = (bf16[256,768]{1,0:T(8,128)(2,1)S(1)}, bf16[256,768]{1,0:T(8,128)(2,1)S(1)}, u32[]{:S(2)}, u32[]{:S(2)}) collective-permute-start(bf16[256,768]{1,0:T(8,128)(2,1)S(1)} %constant_dynamic-slice_fusion.1.a_ref), channel_id=1, source_target_pairs={{0,32},{32,64},{64,96},{96,0},{1,33},{33,65},{65,97},{97,1},{2,34}... | collective-permute-start | bytes 1179656 | tf_op jit(solution)/shard_map/ppermute | solution.py:527
  7.0 16.0 %collective-permute-start.2 = (bf16[256,768]{1,0:T(8,128)(2,1)S(1)}, bf16[256,768]{1,0:T(8,128)(2,1)S(1)}, u32[]{:S(2)}, u32[]{:S(2)}) collective-permute-start(bf16[256,768]{1,0:T(8,128)(2,1)S(1)} %constant_dynamic-slice_fusion.1.a_ref), channel_id=1, source_target_pairs={{0,96},{32,0},{64,32},{96,64},{1,97},{33,1},{65,33},{97,65},{2,98}... | collective-permute-start | bytes 1179656 | tf_op jit(solution)/shard_map/ppermute | solution.py:527
  23.8 5.9 %collective-permute-start.3 = (bf16[512,768]{1,0:T(8,128)(2,1)S(1)}, bf16[512,768]{1,0:T(8,128)(2,1)S(1)}, u32[]{:S(2)}, u32[]{:S(2)}) collective-permute-start(bf16[512,768]{1,0:T(8,128)(2,1)S(1)} %collective-permute-done.a_ref), channel_id=1, source_target_pairs={{0,1},{1,0},{2,3},{3,2},{4,5},{5,4},{6,7},{7,6},{8,9},{9,8},{10,11... | collective-permute-start | bytes 2359304 | tf_op jit(solution)/shard_map/ppermute | solution.py:535
  25.1 24.7 %collective-permute-start.6 = (bf16[512,768]{1,0:T(8,128)(2,1)}, bf16[512,768]{1,0:T(8,128)(2,1)S(1)}, u32[]{:S(2)}, u32[]{:S(2)}) collective-permute-start(bf16[512,768]{1,0:T(8,128)(2,1)} %get-tuple-element.69.refs_0_), channel_id=1, source_target_pairs={{0,18},{2,16},{16,2},{18,0},{1,19},{3,17},{17,3},{19,1},{4,22},{6,... | collective-permute-start | bytes 2359304 | tf_op jit(solution)/shard_map/ppermute | solution.py:539
  26.8 23.1 %collective-permute-start.5 = (bf16[256,768]{1,0:T(8,128)(2,1)}, bf16[256,768]{1,0:T(8,128)(2,1)}, u32[]{:S(2)}, u32[]{:S(2)}) collective-permute-start(bf16[256,768]{1,0:T(8,128)(2,1)} %copy-done.8), channel_id=1, source_target_pairs={{0,64},{32,96},{64,0},{96,32},{1,65},{33,97},{65,1},{97,33},{2,66}... | collective-permute-start | bytes 1179656 | tf_op jit(solution)/shard_map/ppermute | solution.py:527
  40.9 1.8 collective-permute-start.4
  44.7 13.3 %all-to-all-start = ((f32[16,8,512]{2,1,0:T(8,128)}), f32[16,8,512]{2,1,0:T(8,128)S(1)}, u32[]{:S(2)}, u32[]{:S(2)}) async-start(f32[16,8,512]{2,1,0:T(8,128)} %merge_cores.1), calls=%async_computation | async-start | bytes 524288 | tf_op jit(solution)/shard_map/all_to_all | solution.py:570
  64.7 21.1 %collective-permute-start.7 = (bf16[272,768]{1,0:T(8,128)(2,1)}, bf16[272,768]{1,0:T(8,128)(2,1)}, u32[]{:S(2)}, u32[]{:S(2)}) collective-permute-start(bf16[272,768]{1,0:T(8,128)(2,1)} %sums_far.2), channel_id=1, source_target_pairs={{0,64},{32,96},{64,0},{96,32},{1,65},{33,97},{65,1},{97,33},{2,66}... | collective-permute-start | bytes 1253384 | tf_op jit(solution)/shard_map/ppermute | solution.py:527
  71.6 14.7 %collective-permute-start.8 = (bf16[272,768]{1,0:T(8,128)(2,1)}, bf16[272,768]{1,0:T(8,128)(2,1)}, u32[]{:S(2)}, u32[]{:S(2)}) collective-permute-start(bf16[272,768]{1,0:T(8,128)(2,1)} %get-tuple-element.74), channel_id=1, source_target_pairs={{0,32},{32,64},{64,96},{96,0},{1,33},{33,65},{65,97},{97,1},{2,34}... | collective-permute-start | bytes 1253384 | tf_op jit(solution)/shard_map/ppermute | solution.py:527
  72.0 16.5 %collective-permute-start.9 = (bf16[272,768]{1,0:T(8,128)(2,1)}, bf16[272,768]{1,0:T(8,128)(2,1)}, u32[]{:S(2)}, u32[]{:S(2)}) collective-permute-start(bf16[272,768]{1,0:T(8,128)(2,1)} %get-tuple-element.78), channel_id=1, source_target_pairs={{0,96},{32,0},{64,32},{96,64},{1,97},{33,1},{65,33},{97,65},{2,98}... | collective-permute-start | bytes 1253384 | tf_op jit(solution)/shard_map/ppermute | solution.py:527
  74.2 22.7 %collective-permute-start.11 = (bf16[528,768]{1,0:T(8,128)(2,1)S(1)}, bf16[528,768]{1,0:T(8,128)(2,1)S(1)}, u32[]{:S(2)}, u32[]{:S(2)}) collective-permute-start(bf16[528,768]{1,0:T(8,128)(2,1)S(1)} %copy-done.2), channel_id=1, source_target_pairs={{0,18},{2,16},{16,2},{18,0},{1,19},{3,17},{17,3},{19,1},{4,22},{6,... | collective-permute-start | bytes 2433032 | tf_op jit(solution)/shard_map/ppermute | solution.py:539
  85.4 20.6 %collective-permute-start.12 = (bf16[272,768]{1,0:T(8,128)(2,1)}, bf16[272,768]{1,0:T(8,128)(2,1)S(1)}, u32[]{:S(2)}, u32[]{:S(2)}) collective-permute-start(bf16[272,768]{1,0:T(8,128)(2,1)} %get-tuple-element.84), channel_id=1, source_target_pairs={{0,64},{32,96},{64,0},{96,32},{1,65},{33,97},{65,1},{97,33},{2,66}... | collective-permute-start | bytes 1253384 | tf_op jit(solution)/shard_map/ppermute | solution.py:527
  85.8 21.9 %collective-permute-start.13 = (bf16[272,768]{1,0:T(8,128)(2,1)}, bf16[272,768]{1,0:T(8,128)(2,1)}, u32[]{:S(2)}, u32[]{:S(2)}) collective-permute-start(bf16[272,768]{1,0:T(8,128)(2,1)} %get-tuple-element.85), channel_id=1, source_target_pairs={{0,32},{32,64},{64,96},{96,0},{1,33},{33,65},{65,97},{97,1},{2,34}... | collective-permute-start | bytes 1253384 | tf_op jit(solution)/shard_map/ppermute | solution.py:527
  86.2 21.5 %collective-permute-start.14 = (bf16[272,768]{1,0:T(8,128)(2,1)}, bf16[272,768]{1,0:T(8,128)(2,1)}, u32[]{:S(2)}, u32[]{:S(2)}) collective-permute-start(bf16[272,768]{1,0:T(8,128)(2,1)} %get-tuple-element.86), channel_id=1, source_target_pairs={{0,96},{32,0},{64,32},{96,64},{1,97},{33,1},{65,33},{97,65},{2,98}... | collective-permute-start | bytes 1253384 | tf_op jit(solution)/shard_map/ppermute | solution.py:527
  91.9 5.0 %collective-permute-start.10 = (bf16[256,768]{1,0:T(8,128)(2,1)}, bf16[256,768]{1,0:T(8,128)(2,1)S(1)}, u32[]{:S(2)}, u32[]{:S(2)}) collective-permute-start(bf16[256,768]{1,0:T(8,128)(2,1)} %get-tuple-element.79.a_ref.p0.x0), channel_id=1, source_target_pairs={{0,1},{1,0},{2,3},{3,2},{4,5},{5,4},{6,7},{7,6},{8,9},{9,8},{10,11... | collective-permute-start | bytes 1179656 | tf_op jit(solution)/shard_map/ppermute | solution.py:535
  113.5 21.3 %collective-permute-start.15 = (bf16[4,112,512]{2,1,0:T(8,128)(2,1)}, bf16[4,112,512]{2,1,0:T(8,128)(2,1)S(1)}, u32[]{:S(2)}, u32[]{:S(2)}) collective-permute-start(bf16[4,112,512]{2,1,0:T(8,128)(2,1)} %get-tuple-element.91), channel_id=1, source_target_pairs={{0,16},{16,0},{1,17},{17,1},{2,18},{18,2},{3,19},{19,3},{4,20},{20... | collective-permute-start | bytes 1376264 | tf_op jit(solution)/shard_map/ppermute | solution.py:535
  114.7 2.3 %collective-permute-start.16 = (bf16[256,768]{1,0:T(8,128)(2,1)}, bf16[256,768]{1,0:T(8,128)(2,1)S(1)}, u32[]{:S(2)}, u32[]{:S(2)}) collective-permute-start(bf16[256,768]{1,0:T(8,128)(2,1)} %get-tuple-element.92.p1.a_ref.x2), channel_id=1, source_target_pairs={{0,1},{1,0},{2,3},{3,2},{4,5},{5,4},{6,7},{7,6},{8,9},{9,8},{10,11... | collective-permute-start | bytes 1179656 | tf_op jit(solution)/shard_map/ppermute | solution.py:535
  135.6 47.6 %all-to-all-start.1 = ((bf16[64,208,128]{2,1,0:T(8,128)(2,1)}), bf16[64,208,128]{2,1,0:T(8,128)(2,1)}, u32[]{:S(2)}, u32[]{:S(2)}) async-start(bf16[64,208,128]{2,1,0:T(8,128)(2,1)} %sums_two.1), calls=%async_computation.1 | async-start | bytes 6815744 | tf_op jit(solution)/shard_map/all_to_all | solution.py:597
  188.1 17.2 %all-to-all-start.2 = ((bf16[8,208,128]{2,1,0:T(8,128)(2,1)}), bf16[8,208,128]{2,1,0:T(8,128)(2,1)S(1)}, u32[]{:S(2)}, u32[]{:S(2)}) async-start(bf16[8,208,128]{2,1,0:T(8,128)(2,1)} %finish_two.1), calls=%async_computation.2 | async-start | bytes 851968 | tf_op jit(solution)/shard_map/all_to_all | solution.py:604
  193.0 6.2 %collective-permute-start.18 = (bf16[2,112,512]{2,1,0:T(8,128)(2,1)S(1)}, bf16[2,112,512]{2,1,0:T(8,128)(2,1)S(1)}, u32[]{:S(2)}, u32[]{:S(2)}) collective-permute-start(bf16[2,112,512]{2,1,0:T(8,128)(2,1)S(1)} %copy-done.23), channel_id=1, source_target_pairs={{0,32},{32,64},{64,96},{96,0},{1,33},{33,65},{65,97},{97,1},{2,34}... | collective-permute-start | bytes 688136 | tf_op jit(solution)/shard_map/ppermute | solution.py:527
  193.2 12.1 %collective-permute-start.19 = (bf16[2,112,512]{2,1,0:T(8,128)(2,1)S(1)}, bf16[2,112,512]{2,1,0:T(8,128)(2,1)S(1)}, u32[]{:S(2)}, u32[]{:S(2)}) collective-permute-start(bf16[2,112,512]{2,1,0:T(8,128)(2,1)S(1)} %copy-done.22), channel_id=1, source_target_pairs={{0,64},{32,96},{64,0},{96,32},{1,65},{33,97},{65,1},{97,33},{2,66}... | collective-permute-start | bytes 688136 | tf_op jit(solution)/shard_map/ppermute | solution.py:527
  195.9 9.4 %collective-permute-start.20 = (bf16[2,112,512]{2,1,0:T(8,128)(2,1)S(1)}, bf16[2,112,512]{2,1,0:T(8,128)(2,1)S(1)}, u32[]{:S(2)}, u32[]{:S(2)}) collective-permute-start(bf16[2,112,512]{2,1,0:T(8,128)(2,1)S(1)} %copy-done.21), channel_id=1, source_target_pairs={{0,96},{32,0},{64,32},{96,64},{1,97},{33,1},{65,33},{97,65},{2,98}... | collective-permute-start | bytes 688136 | tf_op jit(solution)/shard_map/ppermute | solution.py:527
  205.4 5.7 %collective-permute-start.21 = (bf16[8,208,128]{2,1,0:T(8,128)(2,1)S(1)}, bf16[8,208,128]{2,1,0:T(8,128)(2,1)S(1)}, u32[]{:S(2)}, u32[]{:S(2)}) collective-permute-start(bf16[8,208,128]{2,1,0:T(8,128)(2,1)S(1)} %all-to-all-done.2.a_ref), channel_id=1, source_target_pairs={{0,1},{1,0},{2,3},{3,2},{4,5},{5,4},{6,7},{7,6},{8,9},{9,8},{10,11... | collective-permute-start | bytes 1277960 | tf_op jit(solution)/shard_map/ppermute | solution.py:535
  (25 other events, 218.5 us)

commit v9 on v8

--- a/solution.py
+++ b/solution.py
@@ -598,8 +598,9 @@
     pairs = pair_pieces(after(keep, packed), take)
     total = jnp.sum(after(parts, pairs[0]).astype(F32), axis=0)
     rows = lax.dynamic_slice_in_dim(cents_two, c * 256 + z * 64 + xl * 32, 32, 0)
-    spread = finish_two(total, rows)
-    pieces = [shift_y(after(t, spread), k) for t, k in zip(pairs, (1, 2, 3))]
+    far_step = shift_y(pairs[1], 2)
+    spread = finish_two(total, after(rows, far_step))
+    pieces = [shift_y(after(pairs[0], spread), 1), far_step, shift_y(after(pairs[2], spread), 3)]
     turned_one, mass_one = gather_one(sources, keep, take, pieces)
     block = after(lax.all_to_all(spread, ("z", "xl"), 0, 0, tiled=True), *pieces)
     updated_two, mass_two = gather_two(c[None], block, flip(block, "c"))

time: 215 us -> 214 us (level)
  waiting for transfers between devices: 56 us -> 51.7 us
  starting transfers between devices: 49.1 us -> 52 us
    all_to_all x1, waiting for transfers between devices: 39.2 us -> 0.01 us  [body(): parts = lax.all_to_all(packed, ('y', 'xh', 'z', 'xl'), 0, 0, tiled=True)]
    ppermute x12, waiting for transfers between devices: 9.84 us -> 44.4 us  [shift_y(): return lax.ppermute(x, 'y', [(i, (i + k) % 4) for i in range(4)])]
    unnamed x48 -> x46, local copies, waits for them, and re-layouts: 9.19 us -> 9.22 us
  transfers between devices with their start and end apart: 25 -> 25, of which waited for: 10 -> 9; matrix products, arithmetic and copies ran while one was open for 1% -> 1% of each run, Pallas kernels for 35% -> 36%
where the time goes in v9:
time: 214 us; the launch traced here: 213 us
  Pallas kernels  91.6 us (43%)
  starting transfers between devices  52 us (24%)
  waiting for transfers between devices  51.7 us (24%)
  local copies, waits for them, and re-layouts  12 us (6%)
  other arithmetic  4.81 us (2%)
    ppermute x12, waiting for transfers between devices, shift_y(): return lax.ppermute(x, 'y', [(i, (i + k) % 4) for i in range(4)])  44.4 us
    ppermute x12, starting transfers between devices, shift_y(): return lax.ppermute(x, 'y', [(i, (i + k) % 4) for i in range(4)])  18.2 us
    pallas_call x2, Pallas kernels, scores_two(): pl.pallas_call(kernel, grid_spec=pltpu.PrefetchScalarGridSpec(num_scalar_...  14.9 us
    pallas_call x1, Pallas kernels, scores_near(): pl.pallas_call(scores_near_kernel, grid_spec=pltpu.PrefetchScalarGridSpec...  10.9 us
    ppermute x7, starting transfers between devices, flip(): return lax.ppermute(x, axis, [(0, 1), (1, 0)])  10.8 us
    pallas_call x1, Pallas kernels, sums_rest(): pl.pallas_call(kernel, grid=(5,), in_specs=[pl.BlockSpec((256, 2048), lam...  10.3 us
    pallas_call x1, Pallas kernels, scores_far(): pl.pallas_call(scores_far_kernel, grid_spec=pltpu.PrefetchScalarGridSpec(...  10.2 us
    pallas_call x2, Pallas kernels, sums_far(): pl.pallas_call(kernel, grid=(len(blocks),), in_specs=[pl.BlockSpec((256,...  9.86 us
  transfers between devices with their start and end apart: 25, of which 9 were waited for; matrix products, arithmetic and copies ran while one was open for 1% of the time, Pallas kernels for 36%

profile of v9, /device:TPU:1, one launch (start us, length us, event | category | flops | bytes accessed | tf_op | source)
XLA Modules:
  0.0 212.9 jit_solution(2206041381718932763)
XLA Ops:
  2.2 3.4 %collective-permute-start = (bf16[512,768]{1,0:T(8,128)(2,1)S(1)}, bf16[512,768]{1,0:T(8,128)(2,1)S(1)}, u32[]{:S(2)}, u32[]{:S(2)}) collective-permute-start(bf16[512,768]{1,0:T(8,128)(2,1)S(1)} %dynamic-slice_convert_fusion), channel_id=1, source_target_pairs={{0,18},{2,16},{16,2},{18,0},{1,19},{3,17},{17,3},{19,1},{4,22},{6,... | collective-permute-start | bytes 2359304 | tf_op jit(solution)/shard_map/ppermute | solution.py:539
  9.2 10.9 %scores_near.1 = (f32[2048,2048]{1,0:T(8,128)}, bf16[2048,768]{1,0:T(8,128)(2,1)}, f32[8,512]{1,0:T(8,128)}, f32[2048,128]{1,0:T(8,128)}) custom-call(s32[10]{0:T(128)} %concatenate.3.idx.idx_ref, f32[1024,768]{1,0:T(8,128)} %e_ref.1, bf16[4096,768]{1,0:T(8,128)(2,1)} %cents_ref.3, bf16[4096,768]{1,0:T(8,128)(2,1)} %cents_ref.3, ...), custom_call_target="tpu_custom_call" | custom-call | flops 3221225472 | bytes 25165824 | tf_op jit(solution)/shard_map/scores_near/pallas_call | solution.py:136
  26.8 2.9 %collective-permute-start.5 = (bf16[256,768]{1,0:T(8,128)(2,1)}, bf16[256,768]{1,0:T(8,128)(2,1)}, u32[]{:S(2)}, u32[]{:S(2)}) collective-permute-start(bf16[256,768]{1,0:T(8,128)(2,1)} %copy-done.8), channel_id=1, source_target_pairs={{0,64},{32,96},{64,0},{96,32},{1,65},{33,97},{65,1},{97,33},{2,66}... | collective-permute-start | bytes 1179656 | tf_op jit(solution)/shard_map/ppermute | solution.py:527
  30.6 10.2 %scores_far.1 = (f32[2048,2048]{1,0:T(8,128)}, bf16[2048,768]{1,0:T(8,128)(2,1)}, f32[8,512]{1,0:T(8,128)}) custom-call(s32[10]{0:T(128)} %concatenate.3.idx.idx_ref, bf16[512,768]{1,0:T(8,128)(2,1)} %copy-done.10, bf16[512,768]{1,0:T(8,128)(2,1)} %copy-done.11, bf16[4096,768]{1,0:T(8,128)(2,1)} %cents_ref.3, ...), custom_call_target="tpu_custom_call", output_to_operand_aliasing={{0}: (9, {}), {1}: (10, {})} | custom-call | tf_op jit(solution)/shard_map/scores_far/pallas_call | solution.py:164
  44.7 5.1 %all-to-all-start = ((f32[16,8,512]{2,1,0:T(8,128)}), f32[16,8,512]{2,1,0:T(8,128)S(1)}, u32[]{:S(2)}, u32[]{:S(2)}) async-start(f32[16,8,512]{2,1,0:T(8,128)} %merge_cores.1), calls=%async_computation | async-start | bytes 524288 | tf_op jit(solution)/shard_map/all_to_all | solution.py:570
  55.2 2.8 %all-to-all-done.s_ref = f32[16,8,512]{2,1,0:T(8,128)S(1)} async-done(((f32[16,8,512]{2,1,0:T(8,128)}), f32[16,8,512]{2,1,0:T(8,128)S(1)}, u32[]{:S(2)}, u32[]{:S(2)}) %all-to-all-start) | async-done | bytes 262176 | tf_op jit(solution)/shard_map/all_to_all | solution.py:570
  60.3 4.3 %sums_far.2 = bf16[272,768]{1,0:T(8,128)(2,1)} custom-call(f32[2048,2048]{1,0:T(8,128)} %get-tuple-element.64.p_ref, f32[1,2048]{1,0:T(1,128)} %merge_last.1.f_ref, bf16[2048,768]{1,0:T(8,128)(2,1)} %get-tuple-element.72.x_ref), custom_call_target="tpu_custom_call" | custom-call | tf_op jit(solution)/shard_map/sums_far/pallas_call | solution.py:237
  66.0 5.6 %sums_far.3 = (bf16[272,768]{1,0:T(8,128)(2,1)}, bf16[272,768]{1,0:T(8,128)(2,1)}) custom-call(f32[2048,2048]{1,0:T(8,128)} %get-tuple-element.64.p_ref, f32[1,2048]{1,0:T(1,128)} %merge_last.1.f_ref, bf16[2048,768]{1,0:T(8,128)(2,1)} %get-tuple-element.72.x_ref), custom_call_target="tpu_custom_call" | custom-call | tf_op jit(solution)/shard_map/sums_far/pallas_call | solution.py:237
  75.1 10.3 %sums_rest.1 = (bf16[272,768]{1,0:T(8,128)(2,1)}, bf16[272,768]{1,0:T(8,128)(2,1)}, bf16[272,768]{1,0:T(8,128)(2,1)}, f32[512,768]{1,0:T(8,128)}, f32[1,512]{1,0:T(1,128)}) custom-call(f32[2048,2048]{1,0:T(8,128)} %get-tuple-element.64.p_ref, f32[1,2048]{1,0:T(1,128)} %merge_last.1.f_ref, bf16[2048,768]{1,0:T(8,128)(2,1)} %get-tuple-element.72.x_ref), custom_call_target="tpu_custom_call" | custom-call | tf_op jit(solution)/shard_map/sums_rest/pallas_call | solution.py:270
  88.5 3.4 %finish_one.2 = (bf16[256,768]{1,0:T(8,128)(2,1)}, f32[1,256]{1,0:T(1,128)}) custom-call(s32[10]{0:T(128)} %concatenate.3.idx.idx_ref, f32[512,768]{1,0:T(8,128)} %get-tuple-element.76.own_ref, f32[1,512]{1,0:T(1,128)} %get-tuple-element.83.m_ref, bf16[272,768]{1,0:T(8,128)(2,1)} %collective-permute-done.7.g1, bf16[272,768]{1,0:T(8,128)(2,1)} %collective-permute-done.8.g2, ...), custom_call_target="tpu_custom_call" | custom-call | tf_op jit(solution)/shard_map/finish_one/pallas_call | solution.py:299
  91.9 3.5 %collective-permute-start.10 = (bf16[256,768]{1,0:T(8,128)(2,1)}, bf16[256,768]{1,0:T(8,128)(2,1)S(1)}, u32[]{:S(2)}, u32[]{:S(2)}) collective-permute-start(bf16[256,768]{1,0:T(8,128)(2,1)} %get-tuple-element.79.a_ref.p0.x0), channel_id=1, source_target_pairs={{0,1},{1,0},{2,3},{3,2},{4,5},{5,4},{6,7},{7,6},{8,9},{9,8},{10,11... | collective-permute-start | bytes 1179656 | tf_op jit(solution)/shard_map/ppermute | solution.py:535
  98.6 7.4 %scores_two.2 = (f32[2048,1024]{1,0:T(8,128)}, f32[2,1024]{1,0:T(2,128)}) custom-call(s32[8]{0:T(128)} %multiply_add_fusion.places_ref, bf16[256,768]{1,0:T(8,128)(2,1)} %get-tuple-element.79.a_ref.p0.x0, bf16[256,768]{1,0:T(8,128)(2,1)} %copy-done.7, bf16[512,768]{1,0:T(8,128)(2,1)} %get-tuple-element.69.refs_0_, ...), custom_call_target="tpu_custom_call" | custom-call | tf_op jit(solution)/shard_map/scores_two/pallas_call | solution.py:433
  107.8 3.4 %finish_one.3 = (bf16[256,768]{1,0:T(8,128)(2,1)}, f32[1,256]{1,0:T(1,128)}) custom-call(s32[10]{0:T(128)} %concatenate.3.idx.idx_ref, f32[512,768]{1,0:T(8,128)} %get-tuple-element.76.own_ref, f32[1,512]{1,0:T(1,128)} %get-tuple-element.83.m_ref, bf16[272,768]{1,0:T(8,128)(2,1)} %copy-done.13, bf16[272,768]{1,0:T(8,128)(2,1)} %collective-permute-done.13.g2, ...), custom_call_target="tpu_custom_call" | custom-call | tf_op jit(solution)/shard_map/finish_one/pallas_call | solution.py:299
  117.8 7.5 %scores_two.3 = (f32[2048,1024]{1,0:T(8,128)}, f32[2,1024]{1,0:T(2,128)}) custom-call(s32[8]{0:T(128)} %multiply_add_fusion.places_ref, bf16[256,768]{1,0:T(8,128)(2,1)} %get-tuple-element.92.p1.a_ref.x2, bf16[256,768]{1,0:T(8,128)(2,1)} %copy-done.6, bf16[512,768]{1,0:T(8,128)(2,1)} %get-tuple-element.69.refs_0_, ...), custom_call_target="tpu_custom_call", output_to_operand_aliasing={{0}: (10, {})} | custom-call | tf_op jit(solution)/shard_map/scores_two/pallas_call | solution.py:433
  127.3 7.6 %sums_two.1 = bf16[64,208,128]{2,1,0:T(8,128)(2,1)} custom-call(f32[2048,1024]{1,0:T(8,128)} %get-tuple-element.94.p_ref, f32[2,1024]{1,0:T(2,128)} %get-tuple-element.95.s_ref, f32[2,1024]{1,0:T(2,128)} %copy-done.20, bf16[256,768]{1,0:T(8,128)(2,1)} %get-tuple-element.79.a_ref.p0.x0, bf16[256,768]{1,0:T(8,128)(2,1)} %copy-done.7, ...), custom_call_target="tpu_custom_call" | custom-call | tf_op jit(solution)/shard_map/sums_two/pallas_call | solution.py:473
  135.7 5.7 %all-to-all-start.1 = ((bf16[64,208,128]{2,1,0:T(8,128)(2,1)}), bf16[64,208,128]{2,1,0:T(8,128)(2,1)}, u32[]{:S(2)}, u32[]{:S(2)}) async-start(bf16[64,208,128]{2,1,0:T(8,128)(2,1)} %sums_two.1), calls=%async_computation.1 | async-start | bytes 6815744 | tf_op jit(solution)/shard_map/all_to_all | solution.py:597
  143.4 2.5 %collective-permute-start.18 = (bf16[2,112,512]{2,1,0:T(8,128)(2,1)}, bf16[2,112,512]{2,1,0:T(8,128)(2,1)S(1)}, u32[]{:S(2)}, u32[]{:S(2)}) collective-permute-start(bf16[2,112,512]{2,1,0:T(8,128)(2,1)} %get-tuple-element.100), channel_id=1, source_target_pairs={{0,64},{32,96},{64,0},{96,32},{1,65},{33,97},{65,1},{97,33},{2,66}... | collective-permute-start | bytes 688136 | tf_op jit(solution)/shard_map/ppermute | solution.py:527
  146.6 38.7 %collective-permute-done.18.r2 = bf16[2,112,512]{2,1,0:T(8,128)(2,1)S(1)} collective-permute-done((bf16[2,112,512]{2,1,0:T(8,128)(2,1)}, bf16[2,112,512]{2,1,0:T(8,128)(2,1)S(1)}, u32[]{:S(2)}, u32[]{:S(2)}) %collective-permute-start.18) | collective-permute-done | bytes 229408 | tf_op jit(solution)/shard_map/ppermute | solution.py:527
  185.3 3.2 %convert_reduce_fusion.x_ref = f32[208,128]{1,0:T(8,128)} fusion(bf16[64,208,128]{2,1,0:T(8,128)(2,1)} %all-to-all-done.1), kind=kLoop, calls=%fused_computation | loop fusion | flops 3381248 | bytes 3514368 | tf_op jit(solution)/shard_map/reduce_sum | solution.py:599
  190.3 6.3 %all-to-all-start.2 = ((bf16[8,208,128]{2,1,0:T(8,128)(2,1)}), bf16[8,208,128]{2,1,0:T(8,128)(2,1)S(1)}, u32[]{:S(2)}, u32[]{:S(2)}) async-start(bf16[8,208,128]{2,1,0:T(8,128)(2,1)} %finish_two.1), calls=%async_computation.2 | async-start | bytes 851968 | tf_op jit(solution)/shard_map/all_to_all | solution.py:605
  196.7 2.6 %collective-permute-start.20 = (bf16[2,112,512]{2,1,0:T(8,128)(2,1)S(1)}, bf16[2,112,512]{2,1,0:T(8,128)(2,1)S(1)}, u32[]{:S(2)}, u32[]{:S(2)}) collective-permute-start(bf16[2,112,512]{2,1,0:T(8,128)(2,1)S(1)} %copy-done.21), channel_id=1, source_target_pairs={{0,96},{32,0},{64,32},{96,64},{1,97},{33,1},{65,33},{97,65},{2,98}... | collective-permute-start | bytes 688136 | tf_op jit(solution)/shard_map/ppermute | solution.py:527
  199.3 3.9 %collective-permute-done.19.r1 = bf16[2,112,512]{2,1,0:T(8,128)(2,1)S(1)} collective-permute-done((bf16[2,112,512]{2,1,0:T(8,128)(2,1)S(1)}, bf16[2,112,512]{2,1,0:T(8,128)(2,1)S(1)}, u32[]{:S(2)}, u32[]{:S(2)}) %collective-permute-start.19) | collective-permute-done | bytes 229408 | tf_op jit(solution)/shard_map/ppermute | solution.py:527
  203.6 2.9 %collective-permute-start.21 = (bf16[8,208,128]{2,1,0:T(8,128)(2,1)S(1)}, bf16[8,208,128]{2,1,0:T(8,128)(2,1)S(1)}, u32[]{:S(2)}, u32[]{:S(2)}) collective-permute-start(bf16[8,208,128]{2,1,0:T(8,128)(2,1)S(1)} %all-to-all-done.2.a_ref), channel_id=1, source_target_pairs={{0,1},{1,0},{2,3},{3,2},{4,5},{5,4},{6,7},{7,6},{8,9},{9,8},{10,11... | collective-permute-start | bytes 1277960 | tf_op jit(solution)/shard_map/ppermute | solution.py:535
  207.1 2.7 %gather_one.1 = (f32[96,4096]{1,0:T(8,128)}, f32[1,4096]{1,0:T(1,128)}) custom-call(s32[8]{0:T(128)} %multiply_add_fusion.1.sources_ref, bf16[4,112,512]{2,1,0:T(8,128)(2,1)} %get-tuple-element.97.k_ref, bf16[4,112,512]{2,1,0:T(8,128)(2,1)} %copy-done.4, bf16[2,112,512]{2,1,0:T(8,128)(2,1)} %copy-done.17, bf16[2,112,512]{2,1,0:T(8,128)(2,1)} %copy-done.16, ...), custom_call_target="tpu_custom_call" | custom-call | tf_op jit(solution)/shard_map/gather_one/pallas_call | solution.py:358
  (101 shorter events, 55.3 us)
Async XLA Ops:
  2.2 20.8 %collective-permute-start = (bf16[512,768]{1,0:T(8,128)(2,1)S(1)}, bf16[512,768]{1,0:T(8,128)(2,1)S(1)}, u32[]{:S(2)}, u32[]{:S(2)}) collective-permute-start(bf16[512,768]{1,0:T(8,128)(2,1)S(1)} %dynamic-slice_convert_fusion), channel_id=1, source_target_pairs={{0,18},{2,16},{16,2},{18,0},{1,19},{3,17},{17,3},{19,1},{4,22},{6,... | collective-permute-start | bytes 2359304 | tf_op jit(solution)/shard_map/ppermute | solution.py:539
  5.6 14.5 %collective-permute-start.1 = (bf16[256,768]{1,0:T(8,128)(2,1)S(1)}, bf16[256,768]{1,0:T(8,128)(2,1)S(1)}, u32[]{:S(2)}, u32[]{:S(2)}) collective-permute-start(bf16[256,768]{1,0:T(8,128)(2,1)S(1)} %constant_dynamic-slice_fusion.1.a_ref), channel_id=1, source_target_pairs={{0,32},{32,64},{64,96},{96,0},{1,33},{33,65},{65,97},{97,1},{2,34}... | collective-permute-start | bytes 1179656 | tf_op jit(solution)/shard_map/ppermute | solution.py:527
  7.0 16.0 %collective-permute-start.2 = (bf16[256,768]{1,0:T(8,128)(2,1)S(1)}, bf16[256,768]{1,0:T(8,128)(2,1)S(1)}, u32[]{:S(2)}, u32[]{:S(2)}) collective-permute-start(bf16[256,768]{1,0:T(8,128)(2,1)S(1)} %constant_dynamic-slice_fusion.1.a_ref), channel_id=1, source_target_pairs={{0,96},{32,0},{64,32},{96,64},{1,97},{33,1},{65,33},{97,65},{2,98}... | collective-permute-start | bytes 1179656 | tf_op jit(solution)/shard_map/ppermute | solution.py:527
  23.8 5.9 %collective-permute-start.3 = (bf16[512,768]{1,0:T(8,128)(2,1)S(1)}, bf16[512,768]{1,0:T(8,128)(2,1)S(1)}, u32[]{:S(2)}, u32[]{:S(2)}) collective-permute-start(bf16[512,768]{1,0:T(8,128)(2,1)S(1)} %collective-permute-done.a_ref), channel_id=1, source_target_pairs={{0,1},{1,0},{2,3},{3,2},{4,5},{5,4},{6,7},{7,6},{8,9},{9,8},{10,11... | collective-permute-start | bytes 2359304 | tf_op jit(solution)/shard_map/ppermute | solution.py:535
  25.2 24.7 %collective-permute-start.6 = (bf16[512,768]{1,0:T(8,128)(2,1)}, bf16[512,768]{1,0:T(8,128)(2,1)S(1)}, u32[]{:S(2)}, u32[]{:S(2)}) collective-permute-start(bf16[512,768]{1,0:T(8,128)(2,1)} %get-tuple-element.69.refs_0_), channel_id=1, source_target_pairs={{0,18},{2,16},{16,2},{18,0},{1,19},{3,17},{17,3},{19,1},{4,22},{6,... | collective-permute-start | bytes 2359304 | tf_op jit(solution)/shard_map/ppermute | solution.py:539
  26.8 23.1 %collective-permute-start.5 = (bf16[256,768]{1,0:T(8,128)(2,1)}, bf16[256,768]{1,0:T(8,128)(2,1)}, u32[]{:S(2)}, u32[]{:S(2)}) collective-permute-start(bf16[256,768]{1,0:T(8,128)(2,1)} %copy-done.8), channel_id=1, source_target_pairs={{0,64},{32,96},{64,0},{96,32},{1,65},{33,97},{65,1},{97,33},{2,66}... | collective-permute-start | bytes 1179656 | tf_op jit(solution)/shard_map/ppermute | solution.py:527
  40.9 1.7 collective-permute-start.4
  44.7 13.3 %all-to-all-start = ((f32[16,8,512]{2,1,0:T(8,128)}), f32[16,8,512]{2,1,0:T(8,128)S(1)}, u32[]{:S(2)}, u32[]{:S(2)}) async-start(f32[16,8,512]{2,1,0:T(8,128)} %merge_cores.1), calls=%async_computation | async-start | bytes 524288 | tf_op jit(solution)/shard_map/all_to_all | solution.py:570
  64.6 21.2 %collective-permute-start.7 = (bf16[272,768]{1,0:T(8,128)(2,1)}, bf16[272,768]{1,0:T(8,128)(2,1)}, u32[]{:S(2)}, u32[]{:S(2)}) collective-permute-start(bf16[272,768]{1,0:T(8,128)(2,1)} %sums_far.2), channel_id=1, source_target_pairs={{0,64},{32,96},{64,0},{96,32},{1,65},{33,97},{65,1},{97,33},{2,66}... | collective-permute-start | bytes 1253384 | tf_op jit(solution)/shard_map/ppermute | solution.py:527
  71.6 14.6 %collective-permute-start.8 = (bf16[272,768]{1,0:T(8,128)(2,1)}, bf16[272,768]{1,0:T(8,128)(2,1)}, u32[]{:S(2)}, u32[]{:S(2)}) collective-permute-start(bf16[272,768]{1,0:T(8,128)(2,1)} %get-tuple-element.74), channel_id=1, source_target_pairs={{0,32},{32,64},{64,96},{96,0},{1,33},{33,65},{65,97},{97,1},{2,34}... | collective-permute-start | bytes 1253384 | tf_op jit(solution)/shard_map/ppermute | solution.py:527
  72.0 16.5 %collective-permute-start.9 = (bf16[272,768]{1,0:T(8,128)(2,1)}, bf16[272,768]{1,0:T(8,128)(2,1)}, u32[]{:S(2)}, u32[]{:S(2)}) collective-permute-start(bf16[272,768]{1,0:T(8,128)(2,1)} %get-tuple-element.78), channel_id=1, source_target_pairs={{0,96},{32,0},{64,32},{96,64},{1,97},{33,1},{65,33},{97,65},{2,98}... | collective-permute-start | bytes 1253384 | tf_op jit(solution)/shard_map/ppermute | solution.py:527
  74.2 22.7 %collective-permute-start.11 = (bf16[528,768]{1,0:T(8,128)(2,1)S(1)}, bf16[528,768]{1,0:T(8,128)(2,1)S(1)}, u32[]{:S(2)}, u32[]{:S(2)}) collective-permute-start(bf16[528,768]{1,0:T(8,128)(2,1)S(1)} %copy-done.2), channel_id=1, source_target_pairs={{0,18},{2,16},{16,2},{18,0},{1,19},{3,17},{17,3},{19,1},{4,22},{6,... | collective-permute-start | bytes 2433032 | tf_op jit(solution)/shard_map/ppermute | solution.py:539
  85.4 20.6 %collective-permute-start.12 = (bf16[272,768]{1,0:T(8,128)(2,1)}, bf16[272,768]{1,0:T(8,128)(2,1)S(1)}, u32[]{:S(2)}, u32[]{:S(2)}) collective-permute-start(bf16[272,768]{1,0:T(8,128)(2,1)} %get-tuple-element.84), channel_id=1, source_target_pairs={{0,64},{32,96},{64,0},{96,32},{1,65},{33,97},{65,1},{97,33},{2,66}... | collective-permute-start | bytes 1253384 | tf_op jit(solution)/shard_map/ppermute | solution.py:527
  85.8 21.9 %collective-permute-start.13 = (bf16[272,768]{1,0:T(8,128)(2,1)}, bf16[272,768]{1,0:T(8,128)(2,1)}, u32[]{:S(2)}, u32[]{:S(2)}) collective-permute-start(bf16[272,768]{1,0:T(8,128)(2,1)} %get-tuple-element.85), channel_id=1, source_target_pairs={{0,32},{32,64},{64,96},{96,0},{1,33},{33,65},{65,97},{97,1},{2,34}... | collective-permute-start | bytes 1253384 | tf_op jit(solution)/shard_map/ppermute | solution.py:527
  86.2 21.5 %collective-permute-start.14 = (bf16[272,768]{1,0:T(8,128)(2,1)}, bf16[272,768]{1,0:T(8,128)(2,1)}, u32[]{:S(2)}, u32[]{:S(2)}) collective-permute-start(bf16[272,768]{1,0:T(8,128)(2,1)} %get-tuple-element.86), channel_id=1, source_target_pairs={{0,96},{32,0},{64,32},{96,64},{1,97},{33,1},{65,33},{97,65},{2,98}... | collective-permute-start | bytes 1253384 | tf_op jit(solution)/shard_map/ppermute | solution.py:527
  91.9 5.0 %collective-permute-start.10 = (bf16[256,768]{1,0:T(8,128)(2,1)}, bf16[256,768]{1,0:T(8,128)(2,1)S(1)}, u32[]{:S(2)}, u32[]{:S(2)}) collective-permute-start(bf16[256,768]{1,0:T(8,128)(2,1)} %get-tuple-element.79.a_ref.p0.x0), channel_id=1, source_target_pairs={{0,1},{1,0},{2,3},{3,2},{4,5},{5,4},{6,7},{7,6},{8,9},{9,8},{10,11... | collective-permute-start | bytes 1179656 | tf_op jit(solution)/shard_map/ppermute | solution.py:535
  113.6 21.4 %collective-permute-start.15 = (bf16[4,112,512]{2,1,0:T(8,128)(2,1)}, bf16[4,112,512]{2,1,0:T(8,128)(2,1)S(1)}, u32[]{:S(2)}, u32[]{:S(2)}) collective-permute-start(bf16[4,112,512]{2,1,0:T(8,128)(2,1)} %get-tuple-element.91), channel_id=1, source_target_pairs={{0,16},{16,0},{1,17},{17,1},{2,18},{18,2},{3,19},{19,3},{4,20},{20... | collective-permute-start | bytes 1376264 | tf_op jit(solution)/shard_map/ppermute | solution.py:535
  114.7 2.3 %collective-permute-start.16 = (bf16[256,768]{1,0:T(8,128)(2,1)}, bf16[256,768]{1,0:T(8,128)(2,1)S(1)}, u32[]{:S(2)}, u32[]{:S(2)}) collective-permute-start(bf16[256,768]{1,0:T(8,128)(2,1)} %get-tuple-element.92.p1.a_ref.x2), channel_id=1, source_target_pairs={{0,1},{1,0},{2,3},{3,2},{4,5},{5,4},{6,7},{7,6},{8,9},{9,8},{10,11... | collective-permute-start | bytes 1179656 | tf_op jit(solution)/shard_map/ppermute | solution.py:535
  135.7 49.5 %all-to-all-start.1 = ((bf16[64,208,128]{2,1,0:T(8,128)(2,1)}), bf16[64,208,128]{2,1,0:T(8,128)(2,1)}, u32[]{:S(2)}, u32[]{:S(2)}) async-start(bf16[64,208,128]{2,1,0:T(8,128)(2,1)} %sums_two.1), calls=%async_computation.1 | async-start | bytes 6815744 | tf_op jit(solution)/shard_map/all_to_all | solution.py:597
  143.4 41.8 %collective-permute-start.18 = (bf16[2,112,512]{2,1,0:T(8,128)(2,1)}, bf16[2,112,512]{2,1,0:T(8,128)(2,1)S(1)}, u32[]{:S(2)}, u32[]{:S(2)}) collective-permute-start(bf16[2,112,512]{2,1,0:T(8,128)(2,1)} %get-tuple-element.100), channel_id=1, source_target_pairs={{0,64},{32,96},{64,0},{96,32},{1,65},{33,97},{65,1},{97,33},{2,66}... | collective-permute-start | bytes 688136 | tf_op jit(solution)/shard_map/ppermute | solution.py:527
  190.3 13.4 %all-to-all-start.2 = ((bf16[8,208,128]{2,1,0:T(8,128)(2,1)}), bf16[8,208,128]{2,1,0:T(8,128)(2,1)S(1)}, u32[]{:S(2)}, u32[]{:S(2)}) async-start(bf16[8,208,128]{2,1,0:T(8,128)(2,1)} %finish_two.1), calls=%async_computation.2 | async-start | bytes 851968 | tf_op jit(solution)/shard_map/all_to_all | solution.py:605
  196.6 6.6 %collective-permute-start.19 = (bf16[2,112,512]{2,1,0:T(8,128)(2,1)S(1)}, bf16[2,112,512]{2,1,0:T(8,128)(2,1)S(1)}, u32[]{:S(2)}, u32[]{:S(2)}) collective-permute-start(bf16[2,112,512]{2,1,0:T(8,128)(2,1)S(1)} %copy-done.22), channel_id=1, source_target_pairs={{0,32},{32,64},{64,96},{96,0},{1,33},{33,65},{65,97},{97,1},{2,34}... | collective-permute-start | bytes 688136 | tf_op jit(solution)/shard_map/ppermute | solution.py:527
  196.7 6.5 %collective-permute-start.20 = (bf16[2,112,512]{2,1,0:T(8,128)(2,1)S(1)}, bf16[2,112,512]{2,1,0:T(8,128)(2,1)S(1)}, u32[]{:S(2)}, u32[]{:S(2)}) collective-permute-start(bf16[2,112,512]{2,1,0:T(8,128)(2,1)S(1)} %copy-done.21), channel_id=1, source_target_pairs={{0,96},{32,0},{64,32},{96,64},{1,97},{33,1},{65,33},{97,65},{2,98}... | collective-permute-start | bytes 688136 | tf_op jit(solution)/shard_map/ppermute | solution.py:527
  203.6 6.1 %collective-permute-start.21 = (bf16[8,208,128]{2,1,0:T(8,128)(2,1)S(1)}, bf16[8,208,128]{2,1,0:T(8,128)(2,1)S(1)}, u32[]{:S(2)}, u32[]{:S(2)}) collective-permute-start(bf16[8,208,128]{2,1,0:T(8,128)(2,1)S(1)} %all-to-all-done.2.a_ref), channel_id=1, source_target_pairs={{0,1},{1,0},{2,3},{3,2},{4,5},{5,4},{6,7},{7,6},{8,9},{9,8},{10,11... | collective-permute-start | bytes 1277960 | tf_op jit(solution)/shard_map/ppermute | solution.py:535
  (24 other events, 189.5 us)

commit v10 on v8

--- a/solution.py
+++ b/solution.py
@@ -598,8 +598,9 @@
     pairs = pair_pieces(after(keep, packed), take)
     total = jnp.sum(after(parts, pairs[0]).astype(F32), axis=0)
     rows = lax.dynamic_slice_in_dim(cents_two, c * 256 + z * 64 + xl * 32, 32, 0)
-    spread = finish_two(total, rows)
-    pieces = [shift_y(after(t, spread), k) for t, k in zip(pairs, (1, 2, 3))]
+    one_up, one_down = shift_y(pairs[0], 1), shift_y(pairs[2], 3)
+    spread = finish_two(total, after(rows, one_up, one_down))
+    pieces = [one_up, shift_y(after(pairs[1], spread), 2), one_down]
     turned_one, mass_one = gather_one(sources, keep, take, pieces)
     block = after(lax.all_to_all(spread, ("z", "xl"), 0, 0, tiled=True), *pieces)
     updated_two, mass_two = gather_two(c[None], block, flip(block, "c"))

time: 215 us -> 213 us (level)
    all_to_all x1, waiting for transfers between devices: 39.2 us -> 0.01 us  [body(): parts = lax.all_to_all(packed, ('y', 'xh', 'z', 'xl'), 0, 0, tiled=True)]
    ppermute x12, waiting for transfers between devices: 9.84 us -> 46.6 us  [shift_y(): return lax.ppermute(x, 'y', [(i, (i + k) % 4) for i in range(4)])]
    unnamed x48 -> x44, local copies, waits for them, and re-layouts: 9.19 us -> 9.16 us
  transfers between devices with their start and end apart: 25 -> 25, of which waited for: 10 -> 9; matrix products, arithmetic and copies ran while one was open for 1% -> 1% of each run, Pallas kernels for 35% -> 36%
where the time goes in v10:
time: 213 us; the launch traced here: 212 us
  Pallas kernels  91.5 us (43%)
  waiting for transfers between devices  53.9 us (25%)
  starting transfers between devices  49 us (23%)
  local copies, waits for them, and re-layouts  12.1 us (6%)
  other arithmetic  4.86 us (2%)
    ppermute x12, waiting for transfers between devices, shift_y(): return lax.ppermute(x, 'y', [(i, (i + k) % 4) for i in range(4)])  46.6 us
    ppermute x12, starting transfers between devices, shift_y(): return lax.ppermute(x, 'y', [(i, (i + k) % 4) for i in range(4)])  17 us
    pallas_call x2, Pallas kernels, scores_two(): pl.pallas_call(kernel, grid_spec=pltpu.PrefetchScalarGridSpec(num_scalar_...  14.9 us
    pallas_call x1, Pallas kernels, scores_near(): pl.pallas_call(scores_near_kernel, grid_spec=pltpu.PrefetchScalarGridSpec...  10.9 us
    pallas_call x1, Pallas kernels, scores_far(): pl.pallas_call(scores_far_kernel, grid_spec=pltpu.PrefetchScalarGridSpec(...  10.3 us
    pallas_call x1, Pallas kernels, sums_rest(): pl.pallas_call(kernel, grid=(5,), in_specs=[pl.BlockSpec((256, 2048), lam...  10.3 us
    ppermute x7, starting transfers between devices, flip(): return lax.ppermute(x, axis, [(0, 1), (1, 0)])  9.93 us
    pallas_call x2, Pallas kernels, sums_far(): pl.pallas_call(kernel, grid=(len(blocks),), in_specs=[pl.BlockSpec((256,...  9.87 us
  transfers between devices with their start and end apart: 25, of which 9 were waited for; matrix products, arithmetic and copies ran while one was open for 1% of the time, Pallas kernels for 36%

profile of v10, /device:TPU:1, one launch (start us, length us, event | category | flops | bytes accessed | tf_op | source)
XLA Modules:
  0.0 212.2 jit_solution(12852537371407986773)
XLA Ops:
  2.2 3.4 %collective-permute-start = (bf16[512,768]{1,0:T(8,128)(2,1)S(1)}, bf16[512,768]{1,0:T(8,128)(2,1)S(1)}, u32[]{:S(2)}, u32[]{:S(2)}) collective-permute-start(bf16[512,768]{1,0:T(8,128)(2,1)S(1)} %dynamic-slice_convert_fusion), channel_id=1, source_target_pairs={{0,18},{2,16},{16,2},{18,0},{1,19},{3,17},{17,3},{19,1},{4,22},{6,... | collective-permute-start | bytes 2359304 | tf_op jit(solution)/shard_map/ppermute | solution.py:539
  9.2 10.9 %scores_near.1 = (f32[2048,2048]{1,0:T(8,128)}, bf16[2048,768]{1,0:T(8,128)(2,1)}, f32[8,512]{1,0:T(8,128)}, f32[2048,128]{1,0:T(8,128)}) custom-call(s32[10]{0:T(128)} %concatenate.3.idx.idx_ref, f32[1024,768]{1,0:T(8,128)} %e_ref.1, bf16[4096,768]{1,0:T(8,128)(2,1)} %cents_ref.3, bf16[4096,768]{1,0:T(8,128)(2,1)} %cents_ref.3, ...), custom_call_target="tpu_custom_call" | custom-call | flops 3221225472 | bytes 25165824 | tf_op jit(solution)/shard_map/scores_near/pallas_call | solution.py:136
  26.8 2.9 %collective-permute-start.5 = (bf16[256,768]{1,0:T(8,128)(2,1)}, bf16[256,768]{1,0:T(8,128)(2,1)}, u32[]{:S(2)}, u32[]{:S(2)}) collective-permute-start(bf16[256,768]{1,0:T(8,128)(2,1)} %copy-done.8), channel_id=1, source_target_pairs={{0,64},{32,96},{64,0},{96,32},{1,65},{33,97},{65,1},{97,33},{2,66}... | collective-permute-start | bytes 1179656 | tf_op jit(solution)/shard_map/ppermute | solution.py:527
  30.6 10.3 %scores_far.1 = (f32[2048,2048]{1,0:T(8,128)}, bf16[2048,768]{1,0:T(8,128)(2,1)}, f32[8,512]{1,0:T(8,128)}) custom-call(s32[10]{0:T(128)} %concatenate.3.idx.idx_ref, bf16[512,768]{1,0:T(8,128)(2,1)} %copy-done.10, bf16[512,768]{1,0:T(8,128)(2,1)} %copy-done.11, bf16[4096,768]{1,0:T(8,128)(2,1)} %cents_ref.3, ...), custom_call_target="tpu_custom_call", output_to_operand_aliasing={{0}: (9, {}), {1}: (10, {})} | custom-call | tf_op jit(solution)/shard_map/scores_far/pallas_call | solution.py:164
  44.8 5.1 %all-to-all-start = ((f32[16,8,512]{2,1,0:T(8,128)}), f32[16,8,512]{2,1,0:T(8,128)S(1)}, u32[]{:S(2)}, u32[]{:S(2)}) async-start(f32[16,8,512]{2,1,0:T(8,128)} %merge_cores.1), calls=%async_computation | async-start | bytes 524288 | tf_op jit(solution)/shard_map/all_to_all | solution.py:570
  52.9 2.3 %join_two.3 = (bf16[528,768]{1,0:T(8,128)(2,1)}, f32[512,128]{1,0:T(8,128)}) custom-call(bf16[256,768]{1,0:T(8,128)(2,1)} %collective-permute-done.5.a_ref, bf16[256,768]{1,0:T(8,128)(2,1)} %copy-done.14), custom_call_target="tpu_custom_call" | custom-call | tf_op jit(solution)/shard_map/join_two/pallas_call | solution.py:378
  55.2 2.8 %all-to-all-done.s_ref = f32[16,8,512]{2,1,0:T(8,128)S(1)} async-done(((f32[16,8,512]{2,1,0:T(8,128)}), f32[16,8,512]{2,1,0:T(8,128)S(1)}, u32[]{:S(2)}, u32[]{:S(2)}) %all-to-all-start) | async-done | bytes 262176 | tf_op jit(solution)/shard_map/all_to_all | solution.py:570
  60.4 4.3 %sums_far.2 = bf16[272,768]{1,0:T(8,128)(2,1)} custom-call(f32[2048,2048]{1,0:T(8,128)} %get-tuple-element.63.p_ref, f32[1,2048]{1,0:T(1,128)} %merge_last.1.f_ref, bf16[2048,768]{1,0:T(8,128)(2,1)} %get-tuple-element.71.x_ref), custom_call_target="tpu_custom_call" | custom-call | tf_op jit(solution)/shard_map/sums_far/pallas_call | solution.py:237
  66.1 5.6 %sums_far.3 = (bf16[272,768]{1,0:T(8,128)(2,1)}, bf16[272,768]{1,0:T(8,128)(2,1)}) custom-call(f32[2048,2048]{1,0:T(8,128)} %get-tuple-element.63.p_ref, f32[1,2048]{1,0:T(1,128)} %merge_last.1.f_ref, bf16[2048,768]{1,0:T(8,128)(2,1)} %get-tuple-element.71.x_ref), custom_call_target="tpu_custom_call" | custom-call | tf_op jit(solution)/shard_map/sums_far/pallas_call | solution.py:237
  75.2 10.3 %sums_rest.1 = (bf16[272,768]{1,0:T(8,128)(2,1)}, bf16[272,768]{1,0:T(8,128)(2,1)}, bf16[272,768]{1,0:T(8,128)(2,1)}, f32[512,768]{1,0:T(8,128)}, f32[1,512]{1,0:T(1,128)}) custom-call(f32[2048,2048]{1,0:T(8,128)} %get-tuple-element.63.p_ref, f32[1,2048]{1,0:T(1,128)} %merge_last.1.f_ref, bf16[2048,768]{1,0:T(8,128)(2,1)} %get-tuple-element.71.x_ref), custom_call_target="tpu_custom_call" | custom-call | tf_op jit(solution)/shard_map/sums_rest/pallas_call | solution.py:270
  88.6 3.4 %finish_one.2 = (bf16[256,768]{1,0:T(8,128)(2,1)}, f32[1,256]{1,0:T(1,128)}) custom-call(s32[10]{0:T(128)} %concatenate.3.idx.idx_ref, f32[512,768]{1,0:T(8,128)} %get-tuple-element.75.own_ref, f32[1,512]{1,0:T(1,128)} %get-tuple-element.82.m_ref, bf16[272,768]{1,0:T(8,128)(2,1)} %collective-permute-done.7.g1, bf16[272,768]{1,0:T(8,128)(2,1)} %collective-permute-done.8.g2, ...), custom_call_target="tpu_custom_call" | custom-call | tf_op jit(solution)/shard_map/finish_one/pallas_call | solution.py:299
  92.0 3.4 %collective-permute-start.10 = (bf16[256,768]{1,0:T(8,128)(2,1)}, bf16[256,768]{1,0:T(8,128)(2,1)S(1)}, u32[]{:S(2)}, u32[]{:S(2)}) collective-permute-start(bf16[256,768]{1,0:T(8,128)(2,1)} %get-tuple-element.78.a_ref.p0.x0), channel_id=1, source_target_pairs={{0,1},{1,0},{2,3},{3,2},{4,5},{5,4},{6,7},{7,6},{8,9},{9,8},{10,11... | collective-permute-start | bytes 1179656 | tf_op jit(solution)/shard_map/ppermute | solution.py:535
  98.6 7.5 %scores_two.2 = (f32[2048,1024]{1,0:T(8,128)}, f32[2,1024]{1,0:T(2,128)}) custom-call(s32[8]{0:T(128)} %multiply_add_fusion.places_ref, bf16[256,768]{1,0:T(8,128)(2,1)} %get-tuple-element.78.a_ref.p0.x0, bf16[256,768]{1,0:T(8,128)(2,1)} %copy-done.7, bf16[512,768]{1,0:T(8,128)(2,1)} %get-tuple-element.68.refs_0_, ...), custom_call_target="tpu_custom_call" | custom-call | tf_op jit(solution)/shard_map/scores_two/pallas_call | solution.py:433
  107.8 3.4 %finish_one.3 = (bf16[256,768]{1,0:T(8,128)(2,1)}, f32[1,256]{1,0:T(1,128)}) custom-call(s32[10]{0:T(128)} %concatenate.3.idx.idx_ref, f32[512,768]{1,0:T(8,128)} %get-tuple-element.75.own_ref, f32[1,512]{1,0:T(1,128)} %get-tuple-element.82.m_ref, bf16[272,768]{1,0:T(8,128)(2,1)} %copy-done.13, bf16[272,768]{1,0:T(8,128)(2,1)} %collective-permute-done.13.g2, ...), custom_call_target="tpu_custom_call" | custom-call | tf_op jit(solution)/shard_map/finish_one/pallas_call | solution.py:299
  111.2 2.4 %turn_points.1 = (bf16[4,112,512]{2,1,0:T(8,128)(2,1)}, bf16[4,112,512]{2,1,0:T(8,128)(2,1)}) custom-call(s32[8]{0:T(128)} %fusion.2.owners_ref, bf16[256,768]{1,0:T(8,128)(2,1)} %get-tuple-element.78.a_ref.p0.x0, bf16[256,768]{1,0:T(8,128)(2,1)} %get-tuple-element.91.p1.a_ref.x2, f32[1,256]{1,0:T(1,128)} %get-tuple-element.87.m0, f32[1,256]{1,0:T(1,128)} %get-tuple-element.88.m1), custom_call_target="tpu_custom_call" | custom-call | tf_op jit(solution)/shard_map/turn_points/pallas_call | solution.py:328
  117.8 7.4 %scores_two.3 = (f32[2048,1024]{1,0:T(8,128)}, f32[2,1024]{1,0:T(2,128)}) custom-call(s32[8]{0:T(128)} %multiply_add_fusion.places_ref, bf16[256,768]{1,0:T(8,128)(2,1)} %get-tuple-element.91.p1.a_ref.x2, bf16[256,768]{1,0:T(8,128)(2,1)} %copy-done.6, bf16[512,768]{1,0:T(8,128)(2,1)} %get-tuple-element.68.refs_0_, ...), custom_call_target="tpu_custom_call", output_to_operand_aliasing={{0}: (10, {})} | custom-call | tf_op jit(solution)/shard_map/scores_two/pallas_call | solution.py:433
  127.3 7.6 %sums_two.1 = bf16[64,208,128]{2,1,0:T(8,128)(2,1)} custom-call(f32[2048,1024]{1,0:T(8,128)} %get-tuple-element.93.p_ref, f32[2,1024]{1,0:T(2,128)} %get-tuple-element.94.s_ref, f32[2,1024]{1,0:T(2,128)} %copy-done.20, bf16[256,768]{1,0:T(8,128)(2,1)} %get-tuple-element.78.a_ref.p0.x0, bf16[256,768]{1,0:T(8,128)(2,1)} %copy-done.7, ...), custom_call_target="tpu_custom_call" | custom-call | tf_op jit(solution)/shard_map/sums_two/pallas_call | solution.py:473
  135.7 5.7 %all-to-all-start.1 = ((bf16[64,208,128]{2,1,0:T(8,128)(2,1)}), bf16[64,208,128]{2,1,0:T(8,128)(2,1)}, u32[]{:S(2)}, u32[]{:S(2)}) async-start(bf16[64,208,128]{2,1,0:T(8,128)(2,1)} %sums_two.1), calls=%async_computation.1 | async-start | bytes 6815744 | tf_op jit(solution)/shard_map/all_to_all | solution.py:597
  146.7 38.7 %collective-permute-done.18.r1 = bf16[2,112,512]{2,1,0:T(8,128)(2,1)S(1)} collective-permute-done((bf16[2,112,512]{2,1,0:T(8,128)(2,1)}, bf16[2,112,512]{2,1,0:T(8,128)(2,1)S(1)}, u32[]{:S(2)}, u32[]{:S(2)}) %collective-permute-start.18) | collective-permute-done | bytes 229408 | tf_op jit(solution)/shard_map/ppermute | solution.py:527
  185.4 3.3 %convert_reduce_fusion.x_ref = f32[208,128]{1,0:T(8,128)} fusion(bf16[64,208,128]{2,1,0:T(8,128)(2,1)} %all-to-all-done.1), kind=kLoop, calls=%fused_computation | loop fusion | flops 3381248 | bytes 3514368 | tf_op jit(solution)/shard_map/reduce_sum | solution.py:599
  190.5 5.4 %all-to-all-start.2 = ((bf16[8,208,128]{2,1,0:T(8,128)(2,1)}), bf16[8,208,128]{2,1,0:T(8,128)(2,1)S(1)}, u32[]{:S(2)}, u32[]{:S(2)}) async-start(bf16[8,208,128]{2,1,0:T(8,128)(2,1)} %finish_two.1), calls=%async_computation.2 | async-start | bytes 851968 | tf_op jit(solution)/shard_map/all_to_all | solution.py:605
  197.3 6.2 %collective-permute-done.20.r2 = bf16[2,112,512]{2,1,0:T(8,128)(2,1)S(1)} collective-permute-done((bf16[2,112,512]{2,1,0:T(8,128)(2,1)S(1)}, bf16[2,112,512]{2,1,0:T(8,128)(2,1)S(1)}, u32[]{:S(2)}, u32[]{:S(2)}) %collective-permute-start.20) | collective-permute-done | bytes 229408 | tf_op jit(solution)/shard_map/ppermute | solution.py:527
  206.4 2.7 %gather_one.1 = (f32[96,4096]{1,0:T(8,128)}, f32[1,4096]{1,0:T(1,128)}) custom-call(s32[8]{0:T(128)} %multiply_add_fusion.1.sources_ref, bf16[4,112,512]{2,1,0:T(8,128)(2,1)} %get-tuple-element.96.k_ref, bf16[4,112,512]{2,1,0:T(8,128)(2,1)} %copy-done.4, bf16[2,112,512]{2,1,0:T(8,128)(2,1)} %copy-done.16, bf16[2,112,512]{2,1,0:T(8,128)(2,1)} %copy-done.18, ...), custom_call_target="tpu_custom_call" | custom-call | tf_op jit(solution)/shard_map/gather_one/pallas_call | solution.py:358
  209.8 2.4 %gather_two.1 = (f32[512,768]{1,0:T(8,128)}, f32[1,512]{1,0:T(1,128)}) custom-call(s32[1]{0:T(128)} %bitcast.4.core_ref, bf16[8,208,128]{2,1,0:T(8,128)(2,1)} %copy-done.5, bf16[8,208,128]{2,1,0:T(8,128)(2,1)} %copy-done.12), custom_call_target="tpu_custom_call" | custom-call | tf_op jit(solution)/shard_map/gather_two/pallas_call | solution.py:518
  (99 shorter events, 54.2 us)
Async XLA Ops:
  2.2 20.8 %collective-permute-start = (bf16[512,768]{1,0:T(8,128)(2,1)S(1)}, bf16[512,768]{1,0:T(8,128)(2,1)S(1)}, u32[]{:S(2)}, u32[]{:S(2)}) collective-permute-start(bf16[512,768]{1,0:T(8,128)(2,1)S(1)} %dynamic-slice_convert_fusion), channel_id=1, source_target_pairs={{0,18},{2,16},{16,2},{18,0},{1,19},{3,17},{17,3},{19,1},{4,22},{6,... | collective-permute-start | bytes 2359304 | tf_op jit(solution)/shard_map/ppermute | solution.py:539
  5.6 14.4 %collective-permute-start.1 = (bf16[256,768]{1,0:T(8,128)(2,1)S(1)}, bf16[256,768]{1,0:T(8,128)(2,1)S(1)}, u32[]{:S(2)}, u32[]{:S(2)}) collective-permute-start(bf16[256,768]{1,0:T(8,128)(2,1)S(1)} %constant_dynamic-slice_fusion.1.a_ref), channel_id=1, source_target_pairs={{0,32},{32,64},{64,96},{96,0},{1,33},{33,65},{65,97},{97,1},{2,34}... | collective-permute-start | bytes 1179656 | tf_op jit(solution)/shard_map/ppermute | solution.py:527
  7.0 16.0 %collective-permute-start.2 = (bf16[256,768]{1,0:T(8,128)(2,1)S(1)}, bf16[256,768]{1,0:T(8,128)(2,1)S(1)}, u32[]{:S(2)}, u32[]{:S(2)}) collective-permute-start(bf16[256,768]{1,0:T(8,128)(2,1)S(1)} %constant_dynamic-slice_fusion.1.a_ref), channel_id=1, source_target_pairs={{0,96},{32,0},{64,32},{96,64},{1,97},{33,1},{65,33},{97,65},{2,98}... | collective-permute-start | bytes 1179656 | tf_op jit(solution)/shard_map/ppermute | solution.py:527
  23.8 5.9 %collective-permute-start.3 = (bf16[512,768]{1,0:T(8,128)(2,1)S(1)}, bf16[512,768]{1,0:T(8,128)(2,1)S(1)}, u32[]{:S(2)}, u32[]{:S(2)}) collective-permute-start(bf16[512,768]{1,0:T(8,128)(2,1)S(1)} %collective-permute-done.a_ref), channel_id=1, source_target_pairs={{0,1},{1,0},{2,3},{3,2},{4,5},{5,4},{6,7},{7,6},{8,9},{9,8},{10,11... | collective-permute-start | bytes 2359304 | tf_op jit(solution)/shard_map/ppermute | solution.py:535
  25.2 24.8 %collective-permute-start.6 = (bf16[512,768]{1,0:T(8,128)(2,1)}, bf16[512,768]{1,0:T(8,128)(2,1)S(1)}, u32[]{:S(2)}, u32[]{:S(2)}) collective-permute-start(bf16[512,768]{1,0:T(8,128)(2,1)} %get-tuple-element.68.refs_0_), channel_id=1, source_target_pairs={{0,18},{2,16},{16,2},{18,0},{1,19},{3,17},{17,3},{19,1},{4,22},{6,... | collective-permute-start | bytes 2359304 | tf_op jit(solution)/shard_map/ppermute | solution.py:539
  26.8 23.1 %collective-permute-start.5 = (bf16[256,768]{1,0:T(8,128)(2,1)}, bf16[256,768]{1,0:T(8,128)(2,1)}, u32[]{:S(2)}, u32[]{:S(2)}) collective-permute-start(bf16[256,768]{1,0:T(8,128)(2,1)} %copy-done.8), channel_id=1, source_target_pairs={{0,64},{32,96},{64,0},{96,32},{1,65},{33,97},{65,1},{97,33},{2,66}... | collective-permute-start | bytes 1179656 | tf_op jit(solution)/shard_map/ppermute | solution.py:527
  40.9 1.7 collective-permute-start.4
  44.8 13.3 %all-to-all-start = ((f32[16,8,512]{2,1,0:T(8,128)}), f32[16,8,512]{2,1,0:T(8,128)S(1)}, u32[]{:S(2)}, u32[]{:S(2)}) async-start(f32[16,8,512]{2,1,0:T(8,128)} %merge_cores.1), calls=%async_computation | async-start | bytes 524288 | tf_op jit(solution)/shard_map/all_to_all | solution.py:570
  64.7 21.2 %collective-permute-start.7 = (bf16[272,768]{1,0:T(8,128)(2,1)}, bf16[272,768]{1,0:T(8,128)(2,1)}, u32[]{:S(2)}, u32[]{:S(2)}) collective-permute-start(bf16[272,768]{1,0:T(8,128)(2,1)} %sums_far.2), channel_id=1, source_target_pairs={{0,64},{32,96},{64,0},{96,32},{1,65},{33,97},{65,1},{97,33},{2,66}... | collective-permute-start | bytes 1253384 | tf_op jit(solution)/shard_map/ppermute | solution.py:527
  71.6 14.6 %collective-permute-start.8 = (bf16[272,768]{1,0:T(8,128)(2,1)}, bf16[272,768]{1,0:T(8,128)(2,1)}, u32[]{:S(2)}, u32[]{:S(2)}) collective-permute-start(bf16[272,768]{1,0:T(8,128)(2,1)} %get-tuple-element.73), channel_id=1, source_target_pairs={{0,32},{32,64},{64,96},{96,0},{1,33},{33,65},{65,97},{97,1},{2,34}... | collective-permute-start | bytes 1253384 | tf_op jit(solution)/shard_map/ppermute | solution.py:527
  72.0 16.5 %collective-permute-start.9 = (bf16[272,768]{1,0:T(8,128)(2,1)}, bf16[272,768]{1,0:T(8,128)(2,1)}, u32[]{:S(2)}, u32[]{:S(2)}) collective-permute-start(bf16[272,768]{1,0:T(8,128)(2,1)} %get-tuple-element.77), channel_id=1, source_target_pairs={{0,96},{32,0},{64,32},{96,64},{1,97},{33,1},{65,33},{97,65},{2,98}... | collective-permute-start | bytes 1253384 | tf_op jit(solution)/shard_map/ppermute | solution.py:527
  74.3 22.7 %collective-permute-start.11 = (bf16[528,768]{1,0:T(8,128)(2,1)S(1)}, bf16[528,768]{1,0:T(8,128)(2,1)S(1)}, u32[]{:S(2)}, u32[]{:S(2)}) collective-permute-start(bf16[528,768]{1,0:T(8,128)(2,1)S(1)} %copy-done.2), channel_id=1, source_target_pairs={{0,18},{2,16},{16,2},{18,0},{1,19},{3,17},{17,3},{19,1},{4,22},{6,... | collective-permute-start | bytes 2433032 | tf_op jit(solution)/shard_map/ppermute | solution.py:539
  85.5 20.6 %collective-permute-start.12 = (bf16[272,768]{1,0:T(8,128)(2,1)}, bf16[272,768]{1,0:T(8,128)(2,1)S(1)}, u32[]{:S(2)}, u32[]{:S(2)}) collective-permute-start(bf16[272,768]{1,0:T(8,128)(2,1)} %get-tuple-element.83), channel_id=1, source_target_pairs={{0,64},{32,96},{64,0},{96,32},{1,65},{33,97},{65,1},{97,33},{2,66}... | collective-permute-start | bytes 1253384 | tf_op jit(solution)/shard_map/ppermute | solution.py:527
  85.9 21.9 %collective-permute-start.13 = (bf16[272,768]{1,0:T(8,128)(2,1)}, bf16[272,768]{1,0:T(8,128)(2,1)}, u32[]{:S(2)}, u32[]{:S(2)}) collective-permute-start(bf16[272,768]{1,0:T(8,128)(2,1)} %get-tuple-element.84), channel_id=1, source_target_pairs={{0,32},{32,64},{64,96},{96,0},{1,33},{33,65},{65,97},{97,1},{2,34}... | collective-permute-start | bytes 1253384 | tf_op jit(solution)/shard_map/ppermute | solution.py:527
  86.3 21.5 %collective-permute-start.14 = (bf16[272,768]{1,0:T(8,128)(2,1)}, bf16[272,768]{1,0:T(8,128)(2,1)}, u32[]{:S(2)}, u32[]{:S(2)}) collective-permute-start(bf16[272,768]{1,0:T(8,128)(2,1)} %get-tuple-element.85), channel_id=1, source_target_pairs={{0,96},{32,0},{64,32},{96,64},{1,97},{33,1},{65,33},{97,65},{2,98}... | collective-permute-start | bytes 1253384 | tf_op jit(solution)/shard_map/ppermute | solution.py:527
  92.0 5.0 %collective-permute-start.10 = (bf16[256,768]{1,0:T(8,128)(2,1)}, bf16[256,768]{1,0:T(8,128)(2,1)S(1)}, u32[]{:S(2)}, u32[]{:S(2)}) collective-permute-start(bf16[256,768]{1,0:T(8,128)(2,1)} %get-tuple-element.78.a_ref.p0.x0), channel_id=1, source_target_pairs={{0,1},{1,0},{2,3},{3,2},{4,5},{5,4},{6,7},{7,6},{8,9},{9,8},{10,11... | collective-permute-start | bytes 1179656 | tf_op jit(solution)/shard_map/ppermute | solution.py:535
  113.6 21.3 %collective-permute-start.15 = (bf16[4,112,512]{2,1,0:T(8,128)(2,1)}, bf16[4,112,512]{2,1,0:T(8,128)(2,1)S(1)}, u32[]{:S(2)}, u32[]{:S(2)}) collective-permute-start(bf16[4,112,512]{2,1,0:T(8,128)(2,1)} %get-tuple-element.90), channel_id=1, source_target_pairs={{0,16},{16,0},{1,17},{17,1},{2,18},{18,2},{3,19},{19,3},{4,20},{20... | collective-permute-start | bytes 1376264 | tf_op jit(solution)/shard_map/ppermute | solution.py:535
  114.8 2.3 %collective-permute-start.16 = (bf16[256,768]{1,0:T(8,128)(2,1)}, bf16[256,768]{1,0:T(8,128)(2,1)S(1)}, u32[]{:S(2)}, u32[]{:S(2)}) collective-permute-start(bf16[256,768]{1,0:T(8,128)(2,1)} %get-tuple-element.91.p1.a_ref.x2), channel_id=1, source_target_pairs={{0,1},{1,0},{2,3},{3,2},{4,5},{5,4},{6,7},{7,6},{8,9},{9,8},{10,11... | collective-permute-start | bytes 1179656 | tf_op jit(solution)/shard_map/ppermute | solution.py:535
  135.7 49.7 %all-to-all-start.1 = ((bf16[64,208,128]{2,1,0:T(8,128)(2,1)}), bf16[64,208,128]{2,1,0:T(8,128)(2,1)}, u32[]{:S(2)}, u32[]{:S(2)}) async-start(bf16[64,208,128]{2,1,0:T(8,128)(2,1)} %sums_two.1), calls=%async_computation.1 | async-start | bytes 6815744 | tf_op jit(solution)/shard_map/all_to_all | solution.py:597
  143.4 42.0 %collective-permute-start.18 = (bf16[2,112,512]{2,1,0:T(8,128)(2,1)}, bf16[2,112,512]{2,1,0:T(8,128)(2,1)S(1)}, u32[]{:S(2)}, u32[]{:S(2)}) collective-permute-start(bf16[2,112,512]{2,1,0:T(8,128)(2,1)} %get-tuple-element.97), channel_id=1, source_target_pairs={{0,32},{32,64},{64,96},{96,0},{1,33},{33,65},{65,97},{97,1},{2,34}... | collective-permute-start | bytes 688136 | tf_op jit(solution)/shard_map/ppermute | solution.py:527
  144.3 41.1 %collective-permute-start.19 = (bf16[2,112,512]{2,1,0:T(8,128)(2,1)}, bf16[2,112,512]{2,1,0:T(8,128)(2,1)S(1)}, u32[]{:S(2)}, u32[]{:S(2)}) collective-permute-start(bf16[2,112,512]{2,1,0:T(8,128)(2,1)} %get-tuple-element.100), channel_id=1, source_target_pairs={{0,96},{32,0},{64,32},{96,64},{1,97},{33,1},{65,33},{97,65},{2,98}... | collective-permute-start | bytes 688136 | tf_op jit(solution)/shard_map/ppermute | solution.py:527
  190.5 13.3 %all-to-all-start.2 = ((bf16[8,208,128]{2,1,0:T(8,128)(2,1)}), bf16[8,208,128]{2,1,0:T(8,128)(2,1)S(1)}, u32[]{:S(2)}, u32[]{:S(2)}) async-start(bf16[8,208,128]{2,1,0:T(8,128)(2,1)} %finish_two.1), calls=%async_computation.2 | async-start | bytes 851968 | tf_op jit(solution)/shard_map/all_to_all | solution.py:605
  195.9 7.5 %collective-permute-start.20 = (bf16[2,112,512]{2,1,0:T(8,128)(2,1)S(1)}, bf16[2,112,512]{2,1,0:T(8,128)(2,1)S(1)}, u32[]{:S(2)}, u32[]{:S(2)}) collective-permute-start(bf16[2,112,512]{2,1,0:T(8,128)(2,1)S(1)} %copy-done.21), channel_id=1, source_target_pairs={{0,64},{32,96},{64,0},{96,32},{1,65},{33,97},{65,1},{97,33},{2,66}... | collective-permute-start | bytes 688136 | tf_op jit(solution)/shard_map/ppermute | solution.py:527
  203.8 5.2 %collective-permute-start.21 = (bf16[8,208,128]{2,1,0:T(8,128)(2,1)S(1)}, bf16[8,208,128]{2,1,0:T(8,128)(2,1)S(1)}, u32[]{:S(2)}, u32[]{:S(2)}) collective-permute-start(bf16[8,208,128]{2,1,0:T(8,128)(2,1)S(1)} %all-to-all-done.2.a_ref), channel_id=1, source_target_pairs={{0,1},{1,0},{2,3},{3,2},{4,5},{5,4},{6,7},{7,6},{8,9},{9,8},{10,11... | collective-permute-start | bytes 1277960 | tf_op jit(solution)/shard_map/ppermute | solution.py:535
  (23 other events, 150.0 us)
